TPU v7x, 128 devices: a whole 4x4x4 slice. The times are simulated.
128 devices in a mesh: req: 16 (over y, z), tp: 8 (over x, core).
Axes of the slice: x: 4, y: 4, z: 4, core: 2. Of those that a mesh axis runs over, the one named last changes fastest.
Arguments:
- hidden_in: bfloat16 [4096, 2048], P('req'), may hold values from -40 to 40
- recompute_pos: int32 [16, 256], replicated, may hold values from 0 to 16383, as said below
- req_lengths: int32 [16], replicated, may hold values from 1 to 32, as said below
- stretch_order: int32 [16, 32], replicated, may hold values from 0 to 511, as said below
- page_table: int32 [2, 512], replicated, may hold values from 0 to 31, as said below
- cached_key_pool: bfloat16 [512, 512, 1024], P('req', None, 'tp'), may hold values from -6 to 6
- cached_value_pool: bfloat16 [512, 512, 1024], P('req', None, 'tp'), may hold values from -6 to 6
- attn_gain: float32 [2048], replicated, may hold values from 0.5 to 2
- w_query: bfloat16 [2048, 2048], P(None, 'tp'), may hold values from -1 to 1
- w_key: bfloat16 [2048, 1024], P(None, 'tp'), may hold values from -1 to 1
- value_weight: bfloat16 [2048, 1024], P(None, 'tp'), may hold values from -0.125 to 0.125
- query_gain: float32 [128], replicated, may hold values from 0 to 20
- key_norm_gain: float32 [128], replicated, may hold values from 0 to 20
- w_out: bfloat16 [2048, 2048], P('tp'), may hold values from -0.5 to 0.5
- ffn_gain: float32 [2048], replicated, may hold values from 0.5 to 2
- w_gate: bfloat16 [2048, 6144], P(None, 'tp'), may hold values from -0.125 to 0.125
- w_up: bfloat16 [2048, 6144], P(None, 'tp'), may hold values from -0.125 to 0.125
- w_down: bfloat16 [6144, 2048], P('tp'), may hold values from -0.078125 to 0.078125
Outputs:
- layer_out: bfloat16 [4096, 2048], P('req')
Inputs may be any that keep to these rules, and one draw needn't show every extreme that they name: `req_lengths`: on each draw, the requests of one index along req (chosen anew each time) all have 32 stretches; the others have 1 to 32. `stretch_order`: every stretch id appears exactly once over all requests and places, places at or past a request's length included. `page_table`: every slot of every index along req holds exactly one stretch id, and each index holds exactly 2 of the 32 ids listed by the requests of any one index. `recompute_pos`: strictly increasing along a request, below 512 times the request's length; every request recomputes its first and its last position.
All inputs are finite; a program needn't handle non-finite values.
Results may differ from a plain program's by a relative error of at most 0.015.
The roundings to bfloat16 on the way count: a program that leaves them out, or rounds other values in their place, can miss the bound.
Values may be sent and summed in bfloat16 or wider, within the bound.
No kernel may reach another device: no remote copies, remote signals or barrier semaphores. Data moves between devices by JAX's collectives and lax.ppermute only.
A program may use at most 192 MiB of HBM per device.

v0:
```python
import jax
import jax.numpy as jnp
from jax import lax
from jax.sharding import PartitionSpec as P

STRETCH_TOKENS = 512
MOST_STRETCHES = 32
REQ_DEV = 1
RECOMPUTE_TOKENS = 256


eps_norm = 1e-06
rope_base = 1000000.0
floor_score = -1e30


def norm_rows(matrix, gain_vec):
    wide = matrix.astype(jnp.float32)
    factor = lax.rsqrt(jnp.mean(wide * wide, axis=-1, keepdims=True) + eps_norm)
    return wide * factor * gain_vec


def angles(position, head_size):
    half_dim = head_size // 2
    frequency = rope_base ** (-jnp.arange(half_dim, dtype=jnp.float32) / half_dim)
    return position.astype(jnp.float32)[..., None] * frequency


def rotate_halves(vector, angle_arg):
    half_dim = vector.shape[-1] // 2
    lower_half = vector[..., :half_dim]
    upper_half = vector[..., half_dim:]
    cosine = jnp.cos(angle_arg)
    sine_part = jnp.sin(angle_arg)
    return jnp.concatenate(
        [
            lower_half * cosine - upper_half * sine_part,
            upper_half * cosine + lower_half * sine_part,
        ],
        axis=-1,
    )


def rotary_heads(raw_proj, gain_vec, position, head_count):
    head_size = gain_vec.shape[0]
    split_heads = raw_proj.reshape(raw_proj.shape[0], head_count, head_size)
    normed = norm_rows(split_heads, gain_vec)
    return rotate_halves(normed, angles(position, head_size)[:, None, :]).astype(jnp.bfloat16)


def block_stats(grouped_heads, gathered_stretch_keys, values, live_mask):
    count_of_rows, key_heads, groups, head_size = grouped_heads.shape
    scores = jnp.einsum(
        "mhgd,khd->hgmk", grouped_heads, gathered_stretch_keys, preferred_element_type=jnp.float32
    ) * head_size ** (-0.5)
    row_peak = jnp.max(jnp.where(live_mask, scores, floor_score), axis=-1)
    weights = jnp.where(live_mask, jnp.exp(scores - row_peak[..., None]), 0.0)
    weight_sum = jnp.sum(weights, axis=-1)
    weighted = jnp.einsum(
        "hgmk,khd->mhgd", weights.astype(jnp.bfloat16), values, preferred_element_type=jnp.float32
    )
    head_total = key_heads * groups
    return (
        weighted.reshape(count_of_rows, head_total, head_size),
        row_peak.transpose(2, 0, 1).reshape(count_of_rows, head_total),
        weight_sum.transpose(2, 0, 1).reshape(count_of_rows, head_total),
    )


def merge_stats(weighted, row_peak, weight_sum):
    row_top = jnp.max(row_peak, axis=0)
    factor = jnp.exp(row_peak - row_top[None])
    merged = jnp.sum(weighted * factor[..., None], axis=0)
    total_sum = jnp.sum(weight_sum * factor, axis=0)
    result = (merged / total_sum[..., None]).astype(jnp.bfloat16)
    return result.reshape(result.shape[0], -1)


def swiglu(rows_in, w_gate, w_up):
    gate_proj = jnp.dot(rows_in, w_gate, preferred_element_type=jnp.float32)
    up_proj = jnp.dot(rows_in, w_up, preferred_element_type=jnp.float32)
    return (jax.nn.silu(gate_proj) * up_proj).astype(jnp.bfloat16)


def on_device(
    hidden_in,
    recompute_pos,
    req_lengths,
    stretch_order,
    page_table,
    cached_key_pool,
    cached_value_pool,
    attn_gain,
    w_query,
    w_key,
    value_weight,
    query_gain,
    key_norm_gain,
    w_out,
    ffn_gain,
    w_gate,
    w_up,
    w_down,
):
    req_count = lax.axis_size("req")
    my_index = lax.axis_index("req")
    head_size = query_gain.shape[0]
    query_heads = w_query.shape[1] // head_size
    key_heads = w_key.shape[1] // head_size
    groups = query_heads // key_heads
    count_of_rows = hidden_in.shape[0]
    local_reqs = REQ_DEV
    req_rows = RECOMPUTE_TOKENS
    entries = local_reqs * MOST_STRETCHES
    pair_cap = entries // req_count
    normed = norm_rows(hidden_in, attn_gain).astype(jnp.bfloat16)
    query_raw = jnp.dot(normed, w_query, preferred_element_type=jnp.float32)
    unnormed_keys = jnp.dot(normed, w_key, preferred_element_type=jnp.float32)
    recomputed_values = (
        jnp.dot(normed, value_weight, preferred_element_type=jnp.float32)
        .astype(jnp.bfloat16)
        .reshape(count_of_rows, key_heads, head_size)
    )
    my_positions = lax.dynamic_slice_in_dim(recompute_pos, my_index * local_reqs, local_reqs, 0)
    my_lengths = lax.dynamic_slice_in_dim(req_lengths, my_index * local_reqs, local_reqs, 0)
    flattened_position = my_positions.reshape(count_of_rows)
    queries = rotary_heads(query_raw, query_gain, flattened_position, query_heads)
    recomputed_keys = rotary_heads(unnormed_keys, key_norm_gain, flattened_position, key_heads)
    grouped_heads = queries.reshape(count_of_rows, key_heads, groups, head_size)
    row_owner = jnp.arange(count_of_rows) // req_rows
    own_mask = (row_owner[None, :] == row_owner[:, None]) & (
        flattened_position[None, :] <= flattened_position[:, None]
    )
    fresh_sum, fresh_peak, fresh_total = block_stats(
        grouped_heads, recomputed_keys, recomputed_values, own_mask
    )
    holder_table = page_table[0][stretch_order]
    slot_table = page_table[1][stretch_order]
    holder_hits = holder_table[:, :, None] == jnp.arange(req_count)[None, None, :]
    hit_counts = jnp.cumsum(holder_hits.astype(jnp.int32), axis=1)
    pair_rank = jnp.sum(jnp.where(holder_hits, hit_counts - 1, 0), axis=2)
    my_sends = (holder_table == my_index)[:, :, None] & (
        pair_rank[:, :, None] == jnp.arange(pair_cap)[None, None, :]
    )
    send_slot = jnp.sum(jnp.where(my_sends, slot_table[:, :, None], 0), axis=1)
    send_keys = cached_key_pool[send_slot]
    send_values = cached_value_pool[send_slot]
    got_keys, got_values = (
        lax.all_to_all(send_keys, "req", split_axis=0, concat_axis=0, tiled=True),
        lax.all_to_all(send_values, "req", split_axis=0, concat_axis=0, tiled=True),
    )
    my_holder = lax.dynamic_index_in_dim(holder_table, my_index, 0, keepdims=False)
    my_rank = lax.dynamic_index_in_dim(pair_rank, my_index, 0, keepdims=False)
    buffer = my_holder * pair_cap + my_rank
    position_shift_angle = angles(jnp.arange(MOST_STRETCHES) * STRETCH_TOKENS, head_size)[
        None, :, None, None, :
    ]
    gathered_stretch_keys = got_keys.reshape((req_count * pair_cap,) + got_keys.shape[2:])[buffer]
    gathered_stretch_keys = gathered_stretch_keys.reshape(
        local_reqs, MOST_STRETCHES, STRETCH_TOKENS, key_heads, head_size
    )
    gathered_stretch_keys = rotate_halves(
        gathered_stretch_keys.astype(jnp.float32), position_shift_angle
    ).astype(jnp.bfloat16)
    gathered_stretch_keys = gathered_stretch_keys.reshape(
        local_reqs, MOST_STRETCHES * STRETCH_TOKENS, key_heads, head_size
    )
    gathered_stretch_values = got_values.reshape((req_count * pair_cap,) + got_values.shape[2:])[
        buffer
    ]
    gathered_stretch_values = gathered_stretch_values.reshape(
        local_reqs, MOST_STRETCHES * STRETCH_TOKENS, key_heads, head_size
    )
    key_place = jnp.arange(MOST_STRETCHES * STRETCH_TOKENS)

    def cached_stats(packed):
        group_query, position, length, key_block, value_block = packed
        live_mask = (key_place[None, :] < position[:, None]) & (
            key_place[None, :] // STRETCH_TOKENS < length
        )
        return block_stats(group_query, key_block, value_block, live_mask)

    held_sum, held_peak, held_total = lax.map(
        cached_stats,
        (
            grouped_heads.reshape(local_reqs, req_rows, key_heads, groups, head_size),
            my_positions,
            my_lengths,
            gathered_stretch_keys,
            gathered_stretch_values,
        ),
    )
    attended = merge_stats(
        jnp.stack([held_sum.reshape(fresh_sum.shape), fresh_sum]),
        jnp.stack([held_peak.reshape(fresh_peak.shape), fresh_peak]),
        jnp.stack([held_total.reshape(fresh_total.shape), fresh_total]),
    )
    attn_out = lax.psum(
        jnp.dot(attended, w_out, preferred_element_type=jnp.float32).astype(jnp.bfloat16), "tp"
    ).astype(jnp.float32)
    residual = (hidden_in.astype(jnp.float32) + attn_out).astype(jnp.bfloat16)
    normed_ffn = norm_rows(residual, ffn_gain).astype(jnp.bfloat16)
    hidden = swiglu(normed_ffn, w_gate, w_up)
    ffn_out = lax.psum(
        jnp.dot(hidden, w_down, preferred_element_type=jnp.float32).astype(jnp.bfloat16), "tp"
    ).astype(jnp.float32)
    return (residual.astype(jnp.float32) + ffn_out).astype(jnp.bfloat16)


def solution(mesh):
    return jax.shard_map(
        on_device,
        mesh=mesh,
        in_specs=(
            P("req", None),
            P(),
            P(),
            P(),
            P(),
            P("req", None, "tp"),
            P("req", None, "tp"),
            P(),
            P(None, "tp"),
            P(None, "tp"),
            P(None, "tp"),
            P(),
            P(),
            P("tp", None),
            P(),
            P(None, "tp"),
            P(None, "tp"),
            P("tp", None),
        ),
        out_specs=P("req", None),
        check_vma=False,
    )
```

profile of v0, /device:TPU:1, one launch (start us, length us, event | category | flops | bytes accessed | tf_op | source)
XLA Modules:
  0.0 327.9 jit_solution(9940913370905346261)
XLA Ops:
  8.2 3.5 %gather_fusion = s32[512]{0:T(512)S(1)} fusion(s32[512]{0:T(512)S(1)} %bitcast.127, s32[1024]{0:T(1024)S(1)} %pad_clamp_fusion.2), kind=kCustom, calls=%fused_computation | custom fusion | bytes 6144 | tf_op jit(solution)/shard_map/gather | solution.py:137
  12.7 3.5 %gather_fusion.1 = s32[512]{0:T(512)S(1)} fusion(s32[512]{0:T(512)S(1)} %bitcast.126, s32[1024]{0:T(1024)S(1)} %pad_clamp_fusion.2), kind=kCustom, calls=%fused_computation.1 | custom fusion | bytes 6144 | tf_op jit(solution)/shard_map/gather | solution.py:138
  16.6 5.2 %gather_fusion.4 = bf16[32,512,128]{2,1,0:T(8,128)(2,1)} fusion(bf16[32,512,128]{2,1,0:T(8,128)(2,1)} %param.23, s32[1024]{0:T(1024)S(1)} %pad_clamp_fusion.1), kind=kCustom, calls=%fused_computation.4 | custom fusion | bytes 8388736 | tf_op jit(solution)/shard_map/gather | solution.py:146
  21.9 8.8 %all-to-all-start.1 = ((bf16[16,2,512,128]{3,2,1,0:T(8,128)(2,1)}), bf16[16,2,512,128]{3,2,1,0:T(8,128)(2,1)}, u32[]{:S(2)}, u32[]{:S(2)}) async-start(bf16[16,2,512,128]{3,2,1,0:T(8,128)(2,1)} %bitcast.128), calls=%async_computation.1 | async-start | bytes 8388608 | tf_op jit(solution)/shard_map/all_to_all | solution.py:149
  33.0 1.2 multiply_cosine_fusion
  34.2 1.5 fusion.13
  35.8 2.9 multiply_reduce_fusion
  38.7 1.1 copy.55
  41.0 1.3 fusion.51
  42.2 1.9 multiply_reduce_fusion.1
  44.8 5.3 %gather_fusion.2 = bf16[32,512,128]{2,1,0:T(8,128)(2,1)} fusion(bf16[32,512,128]{2,1,0:T(8,128)(2,1)} %param.24, s32[1024]{0:T(1024)S(1)} %pad_clamp_fusion.1), kind=kCustom, calls=%fused_computation.2 | custom fusion | bytes 8388736 | tf_op jit(solution)/shard_map/gather | solution.py:147
  50.9 1.1 subtract_convert_fusion.1
  53.3 2.9 convolution_bitcast_fusion
  56.3 10.0 %fusion.8 = pred[256,16384]{0,1:T(8,128)(4,1)} fusion(s32[256]{0:T(256)} %bitcast.138, pred[16384]{0:T(1024)(128)(4,1)S(1)} %copy-done.6), kind=kLoop, calls=%fused_computation.16 | loop fusion | flops 8388608 | bytes 4211712 | tf_op jit(solution)/shard_map/while/body/eval_jaxpr/and | solution.py:178
  66.3 24.7 %all-to-all-done.1 = bf16[16,2,512,128]{3,2,1,0:T(8,128)(2,1)} async-done(((bf16[16,2,512,128]{3,2,1,0:T(8,128)(2,1)}), bf16[16,2,512,128]{3,2,1,0:T(8,128)(2,1)}, u32[]{:S(2)}, u32[]{:S(2)}) %all-to-all-start.1) | async-done | bytes 4194336 | tf_op jit(solution)/shard_map/all_to_all | solution.py:149
  91.0 11.4 %all-to-all-start = ((bf16[16,2,512,128]{3,2,1,0:T(8,128)(2,1)}), bf16[16,2,512,128]{3,2,1,0:T(8,128)(2,1)}, u32[]{:S(2)}, u32[]{:S(2)}) async-start(bf16[16,2,512,128]{3,2,1,0:T(8,128)(2,1)} %bitcast.129), calls=%async_computation | async-start | bytes 8388608 | tf_op jit(solution)/shard_map/all_to_all | solution.py:150
  102.5 5.4 %gather_fusion.5 = bf16[32,512,128]{2,1,0:T(8,128)(2,1)} fusion(bf16[32,512,128]{2,1,0:T(8,128)(2,1)} %bitcast.11, s32[1024]{0:T(1024)} %pad_clamp_fusion), kind=kCustom, calls=%fused_computation.5 | custom fusion | bytes 8388736 | tf_op jit(solution)/shard_map/gather | solution.py:158
  107.8 3.2 bitcast_convert_fusion
  111.1 5.3 %subtract_convert_fusion = (bf16[1,32,512,1,64]{4,2,1,3,0:T(8,128)(2,1)}, bf16[1,32,512,1,64]{4,2,1,3,0:T(8,128)(2,1)}) fusion(f32[1,32,512,1,128]{4,2,1,3,0:T(8,128)S(1)} %bitcast_convert_fusion, f32[32,64]{1,0:T(8,128)S(1)} %copy-done.5, f32[32,64]{1,0:T(8,128)S(1)} %copy-done.4), kind=kLoop, calls=%fused_computation.19 | loop fusion | flops 8388608 | bytes 12599296 | tf_op jit(solution)/shard_map/convert.10
  116.3 19.4 %fusion = (f32[2,256]{1,0:T(2,128)S(1)}, f32[16384,256,2]{1,0,2:T(8,128)}) fusion(pred[256,16384]{0,1:T(8,128)(4,1)} %fusion.8, bf16[256,2,64]{2,0,1:T(8,128)(2,1)S(1)} %get-tuple-element.40, bf16[256,2,64]{2,0,1:T(8,128)(2,1)S(1)} %get-tuple-element.29, bf16[16384,64]{1,0:T(8,128)(2,1)} %bitcast.132, bf16[16384,64]{1,0:T(8,128)(2,1)} %bitcast.131), kind=kOutput, calls=%fused_computation.8 | convolution fusion | flops 2181299712 | bytes 42076160 | tf_op jit(solution)/shard_map/while/body/eval_jaxpr/mhgd,khd->hgmk/dot_general | solution.py:53
  135.8 15.1 %fusion.3 = f32[2,256]{1,0:T(2,128)S(1)} fusion(f32[16384,256,2]{1,0,2:T(8,128)} %get-tuple-element.58, f32[2,256]{1,0:T(2,128)S(1)} %get-tuple-element.57, pred[256,16384]{0,1:T(8,128)(4,1)} %fusion.8), kind=kLoop, calls=%fused_computation.11 | loop fusion | flops 33553920 | bytes 37752832 | tf_op jit(solution)/shard_map/while/body/eval_jaxpr/reduce_sum | solution.py:58
  150.9 3.0 all-to-all-done
  153.9 5.4 %gather_fusion.3 = bf16[32,512,128]{2,1,0:T(8,128)(2,1)} fusion(bf16[32,512,128]{2,1,0:T(8,128)(2,1)} %bitcast.4, s32[1024]{0:T(1024)} %pad_clamp_fusion), kind=kCustom, calls=%fused_computation.3 | custom fusion | bytes 8388736 | tf_op jit(solution)/shard_map/gather | solution.py:168
  159.3 16.8 %fusion.23 = f32[1,256,2,128]{1,3,2,0:T(8,128)} fusion(bf16[16384,128,1]{1,0,2:T(8,128)(2,1)} %bitcast.130, f32[16384,256,2]{1,0,2:T(8,128)} %get-tuple-element.58, f32[2,256]{1,0:T(2,128)S(1)} %get-tuple-element.57, pred[256,16384]{0,1:T(8,128)(4,1)} %fusion.8), kind=kOutput, calls=%fused_computation.47 | convolution fusion | flops 2181038080 | bytes 42207232 | tf_op jit(solution)/shard_map/while/body/eval_jaxpr/hgmk,khd->mhgd/dot_general | solution.py:59
  176.2 1.0 fusion.28
  177.3 2.7 convolution_convert_fusion
  180.2 63.4 %all-reduce.3.cloned.1.call-done = bf16[256,2048]{1,0:T(8,128)(2,1)} async-done(((bf16[256,2048]{1,0:T(8,128)(2,1)}), bf16[256,2048]{1,0:T(8,128)(2,1)}) %all-reduce.3.cloned.1.call-update) | async-done | bytes 1048592 | tf_op jit(solution)/shard_map/psum | solution.py:198
  243.6 2.0 fusion.17
  246.6 3.9 %fusion.34 = f32[256,768]{1,0:T(8,128)} fusion(bf16[2048,768]{1,0:T(8,128)(2,1)} %param.33, bf16[256,2048]{1,0:T(8,128)(2,1)S(1)} %get-tuple-element.24, f32[2048]{0:T(1024)S(1)} %copy-done.13, f32[256]{0:T(256)S(1)} %add_rsqrt_fusion.1), kind=kOutput, calls=%fused_computation.58 | convolution fusion | flops 807403520 | bytes 4989952 | tf_op jit(solution)/shard_map/dot_general | solution.py:80
  250.5 5.6 %convolution_convert_fusion.1 = bf16[256,2048]{1,0:T(8,128)(2,1)} fusion(bf16[768,2048]{1,0:T(8,128)(2,1)S(1)} %copy-done, bf16[2048,768]{1,0:T(8,128)(2,1)} %param.34, f32[256,768]{1,0:T(8,128)} %fusion.34, bf16[256,2048]{1,0:T(8,128)(2,1)} %copy-done.1, f32[2048]{0:T(1024)S(1)} %copy-done.13, f32[256]{0:T(256)S(1)} %add_rsqrt_fusion.1), kind=kOutput, calls=%fused_computation.32 | convolution fusion | flops 1614413824 | bytes 9184256 | tf_op jit(solution)/shard_map/dot_general | solution.py:205
  256.1 62.1 %all-reduce.5.cloned.1.call-done = bf16[256,2048]{1,0:T(8,128)(2,1)} async-done(((bf16[256,2048]{1,0:T(8,128)(2,1)}), bf16[256,2048]{1,0:T(8,128)(2,1)}) %all-reduce.5.cloned.1.call-update) | async-done | bytes 1048592 | tf_op jit(solution)/shard_map/psum | solution.py:204
  318.2 2.9 fusion.20
  (72 shorter events, 10.6 us)
Async XLA Ops:
  6.5 244.0 %copy-start = (bf16[768,2048]{1,0:T(8,128)(2,1)S(1)}, bf16[768,2048]{1,0:T(8,128)(2,1)}, u32[]{:S(2)}) copy-start(bf16[768,2048]{1,0:T(8,128)(2,1)} %param.35) | copy-start | bytes 9437188
  21.9 13.9 %copy-start.12 = (f32[2048]{0:T(1024)S(1)}, f32[2048]{0:T(1024)}, u32[]{:S(2)}) copy-start(f32[2048]{0:T(1024)} %param.25) | copy-start | bytes 24580
  21.9 69.1 %all-to-all-start.1 = ((bf16[16,2,512,128]{3,2,1,0:T(8,128)(2,1)}), bf16[16,2,512,128]{3,2,1,0:T(8,128)(2,1)}, u32[]{:S(2)}, u32[]{:S(2)}) async-start(bf16[16,2,512,128]{3,2,1,0:T(8,128)(2,1)} %bitcast.128), calls=%async_computation.1 | async-start | bytes 8388608 | tf_op jit(solution)/shard_map/all_to_all | solution.py:149
  30.7 9.7 %copy-start.14 = (s32[16]{0:T(128)S(1)}, s32[16]{0:T(128)}, u32[]{:S(2)}) copy-start(s32[16]{0:T(128)} %param.20) | copy-start | bytes 196
  30.7 13.5 %copy-start.11 = (f32[128]{0:T(128)S(1)}, f32[128]{0:T(128)}, u32[]{:S(2)}) copy-start(f32[128]{0:T(128)} %param.30) | copy-start | bytes 1540
  32.2 12.5 %copy-start.9 = (s32[1,256]{1,0:T(1,128)}, s32[1,256]{1,0:T(1,128)S(1)}, u32[]{:S(2)}) copy-start(s32[1,256]{1,0:T(1,128)S(1)} %constant_dynamic-slice_fusion) | copy-start | bytes 3076
  35.8 8.5 %copy-start.10 = (f32[256]{0:T(256)}, f32[256]{0:T(256)S(1)}, u32[]{:S(2)}) copy-start(f32[256]{0:T(256)S(1)} %add_rsqrt_fusion.3) | copy-start | bytes 3076
  50.1 6.2 %copy-start.6 = (pred[16384]{0:T(1024)(128)(4,1)S(1)}, pred[16384]{0:T(1024)(128)(4,1)}, u32[]{:S(2)}) copy-start(pred[16384]{0:T(1024)(128)(4,1)} %fusion.51) | copy-start | bytes 49156
  52.4 0.8 copy-start.2
  52.4 0.8 copy-start.7
  91.0 62.9 %all-to-all-start = ((bf16[16,2,512,128]{3,2,1,0:T(8,128)(2,1)}), bf16[16,2,512,128]{3,2,1,0:T(8,128)(2,1)}, u32[]{:S(2)}, u32[]{:S(2)}) async-start(bf16[16,2,512,128]{3,2,1,0:T(8,128)(2,1)} %bitcast.129), calls=%async_computation | async-start | bytes 8388608 | tf_op jit(solution)/shard_map/all_to_all | solution.py:150
  102.4 141.2 %all-reduce.3.cloned.1.call-start = ((), (), s32[]{:S(2)}) async-start(), calls=%async_computation.2 | async-start | bytes 2097152 | tf_op jit(solution)/shard_map/psum | solution.py:198
  107.8 3.2 copy-start.4
  107.8 3.2 copy-start.5
  116.3 19.4 %copy-start.8 = (f32[2,256]{1,0:T(2,128)S(1)}, f32[2,256]{1,0:T(2,128)}, u32[]{:S(2)}) copy-start(f32[2,256]{1,0:T(2,128)} %copy-done.7) | copy-start | bytes 6148
  159.3 16.9 %copy-start.3 = (f32[1,256,2,128]{1,3,2,0:T(8,128)S(1)}, f32[1,256,2,128]{1,3,2,0:T(8,128)}, u32[]{:S(2)}) copy-start(f32[1,256,2,128]{1,3,2,0:T(8,128)} %convolution_bitcast_fusion) | copy-start | bytes 786436
  176.2 70.5 %copy-start.13 = (f32[2048]{0:T(1024)S(1)}, f32[2048]{0:T(1024)}, u32[]{:S(2)}) copy-start(f32[2048]{0:T(1024)} %param.32) | copy-start | bytes 24580
  179.9 138.3 %all-reduce.5.cloned.1.call-start = ((), (), s32[]{:S(2)}) async-start(), calls=%async_computation.3 | async-start | bytes 2097152 | tf_op jit(solution)/shard_map/psum | solution.py:204
  245.7 1.0 copy-start.1
Sparse Core Ops, SparseCore 0:
  180.1 63.5 all-reduce.2
  256.2 61.9 all-reduce.4
where the time goes:
time: 330 us; the launch traced here: 328 us
  waiting for transfers between devices  153 us (46%)
  matrix products  56.5 us (17%)
  other arithmetic  50.2 us (15%)
  local copies, waits for them, and re-layouts  33.8 us (10%)
  starting transfers between devices  20.5 us (6%)
  between operations  13.7 us (4%)
    psum x1, waiting for transfers between devices, on_device(): lax.psum(jnp.dot(attended, w_out, preferred_element_type=jnp.float32).ast...  63.4 us
    psum x1, waiting for transfers between devices, on_device(): lax.psum(jnp.dot(hidden, w_down, preferred_element_type=jnp.float32).asty...  62.1 us
    all_to_all x1, waiting for transfers between devices, on_device(): lax.all_to_all(send_keys, 'req', split_axis=0, concat_axis=0, tiled=True)  24.7 us
    dot_general x2, matrix products, block_stats(): jnp.einsum('hgmk,khd->mhgd', weights.astype(jnp.bfloat16), values, prefer...  19.8 us
    dot_general x2, matrix products, block_stats(): jnp.einsum('mhgd,khd->hgmk', grouped_heads, gathered_stretch_keys, prefer...  19.8 us
    reduce_sum x2, other arithmetic, block_stats(): weight_sum = jnp.sum(weights, axis=-1)  15.2 us
    all_to_all x1, starting transfers between devices, on_device(): lax.all_to_all(send_values, 'req', split_axis=0, concat_axis=0, tiled=True)  11.4 us
    and x1, other arithmetic, cached_stats(): (key_place[None, :] < position[:, None]) & (key_place[None, :] // STRETCH...  10 us
  transfers between devices with their start and end apart: 4, of which 4 were waited for; matrix products, arithmetic and copies ran while one was open for 25% of the time, Pallas kernels for 0%

commit v1 on v0

--- a/solution.py
+++ b/solution.py
@@ -80,6 +80,24 @@
     gate_proj = jnp.dot(rows_in, w_gate, preferred_element_type=jnp.float32)
     up_proj = jnp.dot(rows_in, w_up, preferred_element_type=jnp.float32)
     return (jax.nn.silu(gate_proj) * up_proj).astype(jnp.bfloat16)
+
+
+def reduce_rows(terms, tp_count):
+    blocks = terms.reshape(tp_count, terms.shape[0] // tp_count, terms.shape[1])
+    got = lax.all_to_all(blocks, "tp", 0, 0, tiled=False)
+    return jnp.sum(got.astype(jnp.float32), axis=0)
+
+
+def gather_rows(rows, tp_count):
+    tp_index = lax.axis_index("tp")
+    parts = [rows]
+    for shift in range(1, tp_count):
+        pairs = [(i, (i + shift) % tp_count) for i in range(tp_count)]
+        parts.append(lax.ppermute(rows, "tp", pairs))
+    stacked = jnp.stack(parts)
+    source = (tp_index - jnp.arange(tp_count)) % tp_count
+    ordered = jnp.take(stacked, jnp.argsort(source), axis=0)
+    return ordered.reshape(tp_count * rows.shape[0], rows.shape[1])
 
 
 def on_device(
@@ -195,16 +213,18 @@
         jnp.stack([held_peak.reshape(fresh_peak.shape), fresh_peak]),
         jnp.stack([held_total.reshape(fresh_total.shape), fresh_total]),
     )
-    attn_out = lax.psum(
-        jnp.dot(attended, w_out, preferred_element_type=jnp.float32).astype(jnp.bfloat16), "tp"
-    ).astype(jnp.float32)
-    residual = (hidden_in.astype(jnp.float32) + attn_out).astype(jnp.bfloat16)
-    normed_ffn = norm_rows(residual, ffn_gain).astype(jnp.bfloat16)
+    tp_count = lax.axis_size("tp")
+    tp_index = lax.axis_index("tp")
+    block_rows = count_of_rows // tp_count
+    attn_terms = jnp.dot(attended, w_out, preferred_element_type=jnp.float32).astype(jnp.bfloat16)
+    attn_out = reduce_rows(attn_terms, tp_count)
+    my_hidden = lax.dynamic_slice_in_dim(hidden_in, tp_index * block_rows, block_rows, 0)
+    residual = (my_hidden.astype(jnp.float32) + attn_out).astype(jnp.bfloat16)
+    normed_ffn = gather_rows(norm_rows(residual, ffn_gain).astype(jnp.bfloat16), tp_count)
     hidden = swiglu(normed_ffn, w_gate, w_up)
-    ffn_out = lax.psum(
-        jnp.dot(hidden, w_down, preferred_element_type=jnp.float32).astype(jnp.bfloat16), "tp"
-    ).astype(jnp.float32)
-    return (residual.astype(jnp.float32) + ffn_out).astype(jnp.bfloat16)
+    down_terms = jnp.dot(hidden, w_down, preferred_element_type=jnp.float32).astype(jnp.bfloat16)
+    ffn_out = reduce_rows(down_terms, tp_count)
+    return gather_rows((residual.astype(jnp.float32) + ffn_out).astype(jnp.bfloat16), tp_count)
 
 
 def solution(mesh):

time: 330 us -> 279 us (0.85)
  waiting for transfers between devices: 153 us -> 56 us
  starting transfers between devices: 20.5 us -> 44.6 us
  blocking collectives: 0 us -> 17.9 us
  local copies, waits for them, and re-layouts: 33.8 us -> 48.8 us
  between operations: 13.7 us -> 0.35 us
  other arithmetic: 50.2 us -> 53.8 us
    psum x2 -> x0, waiting for transfers between devices: 126 us -> none  [the longest x1 63.4 us: on_device(): lax.psum(jnp.dot(attended, w_out, preferred_element_type=jnp.float32).ast...]
    all_to_all x0 -> x1, blocking collectives: none -> 17.9 us  [reduce_rows(): got = lax.all_to_all(blocks, 'tp', 0, 0, tiled=False)]
    ppermute x0 -> x14, starting transfers between devices: none -> 14.8 us  [gather_rows(): parts.append(lax.ppermute(rows, 'tp', pairs))]
    all_to_all x0 -> x1, waiting for transfers between devices: none -> 14 us  [reduce_rows(): got = lax.all_to_all(blocks, 'tp', 0, 0, tiled=False)]
    ppermute x0 -> x14, waiting for transfers between devices: none -> 14 us  [gather_rows(): parts.append(lax.ppermute(rows, 'tp', pairs))]
    all_to_all x0 -> x1, starting transfers between devices: none -> 9.58 us  [reduce_rows(): got = lax.all_to_all(blocks, 'tp', 0, 0, tiled=False)]
    unnamed x30 -> x42, local copies, waits for them, and re-layouts: 1.79 us -> 9.77 us
    gather x0 -> x2, local copies, waits for them, and re-layouts: none -> 5.65 us  [gather_rows(): ordered = jnp.take(stacked, jnp.argsort(source), axis=0)]
  transfers between devices with their start and end apart: 4 -> 17, of which waited for: 4 -> 7; matrix products, arithmetic and copies ran while one was open for 25% -> 33% of each run, Pallas kernels for 0% -> 0%
where the time goes in v1:
time: 279 us; the launch traced here: 278 us
  matrix products  56.4 us (20%)
  waiting for transfers between devices  56 us (20%)
  other arithmetic  53.8 us (19%)
  local copies, waits for them, and re-layouts  48.8 us (17%)
  starting transfers between devices  44.6 us (16%)
  blocking collectives  17.9 us (6%)
    all_to_all x1, waiting for transfers between devices, on_device(): lax.all_to_all(send_keys, 'req', split_axis=0, concat_axis=0, tiled=True)  24.8 us
    dot_general x2, matrix products, block_stats(): jnp.einsum('hgmk,khd->mhgd', weights.astype(jnp.bfloat16), values, prefer...  19.8 us
    dot_general x2, matrix products, block_stats(): jnp.einsum('mhgd,khd->hgmk', grouped_heads, gathered_stretch_keys, prefer...  19.8 us
    all_to_all x1, blocking collectives, reduce_rows(): got = lax.all_to_all(blocks, 'tp', 0, 0, tiled=False)  17.9 us
    reduce_sum x2, other arithmetic, block_stats(): weight_sum = jnp.sum(weights, axis=-1)  15.2 us
    ppermute x14, starting transfers between devices, gather_rows(): parts.append(lax.ppermute(rows, 'tp', pairs))  14.8 us
    all_to_all x1, waiting for transfers between devices, reduce_rows(): got = lax.all_to_all(blocks, 'tp', 0, 0, tiled=False)  14 us
    ppermute x14, waiting for transfers between devices, gather_rows(): parts.append(lax.ppermute(rows, 'tp', pairs))  14 us
  transfers between devices with their start and end apart: 17, of which 7 were waited for; matrix products, arithmetic and copies ran while one was open for 33% of the time, Pallas kernels for 0%

profile of v1, /device:TPU:1, one launch (start us, length us, event | category | flops | bytes accessed | tf_op | source)
XLA Modules:
  0.0 277.8 jit_solution(1655308337186719698)
XLA Ops:
  1.7 3.5 %gather_fusion = s32[512]{0:T(512)S(1)} fusion(s32[512]{0:T(512)S(1)} %bitcast.165, s32[1024]{0:T(1024)S(1)} %pad_clamp_fusion.3), kind=kCustom, calls=%fused_computation.2 | custom fusion | bytes 6144 | tf_op jit(solution)/shard_map/gather | solution.py:155
  6.2 3.5 %gather_fusion.1 = s32[512]{0:T(512)S(1)} fusion(s32[512]{0:T(512)S(1)} %bitcast.164, s32[1024]{0:T(1024)S(1)} %pad_clamp_fusion.3), kind=kCustom, calls=%fused_computation.3 | custom fusion | bytes 6144 | tf_op jit(solution)/shard_map/gather | solution.py:156
  10.1 5.2 %gather_fusion.4 = bf16[32,512,128]{2,1,0:T(8,128)(2,1)} fusion(bf16[32,512,128]{2,1,0:T(8,128)(2,1)} %param.25, s32[1024]{0:T(1024)S(1)} %pad_clamp_fusion.2), kind=kCustom, calls=%fused_computation.6 | custom fusion | bytes 8388736 | tf_op jit(solution)/shard_map/gather | solution.py:164
  15.4 8.8 %all-to-all-start.1 = ((bf16[16,2,512,128]{3,2,1,0:T(8,128)(2,1)}), bf16[16,2,512,128]{3,2,1,0:T(8,128)(2,1)}, u32[]{:S(2)}, u32[]{:S(2)}) async-start(bf16[16,2,512,128]{3,2,1,0:T(8,128)(2,1)} %bitcast.166), calls=%async_computation.1 | async-start | bytes 8388608 | tf_op jit(solution)/shard_map/all_to_all | solution.py:167
  26.6 2.9 %multiply_reduce_fusion = (f32[256,2]{0,1:T(2,128)S(1)}, f32[256,256]{0,1:T(8,128)}) fusion(bf16[2048,256]{1,0:T(8,128)(2,1)} %param.28, bf16[256,2048]{1,0:T(8,128)(2,1)} %param.20, f32[2048]{0:T(1024)S(1)} %copy-done.13, f32[256]{0:T(256)S(1)} %add_rsqrt_fusion.2), kind=kOutput, calls=%fused_computation.70 | convolution fusion | flops 270663168 | bytes 2370560 | tf_op jit(solution)/shard_map/dot_general | solution.py:135
  38.2 5.3 %gather_fusion.2 = bf16[32,512,128]{2,1,0:T(8,128)(2,1)} fusion(bf16[32,512,128]{2,1,0:T(8,128)(2,1)} %param.26, s32[1024]{0:T(1024)S(1)} %pad_clamp_fusion.2), kind=kCustom, calls=%fused_computation.4 | custom fusion | bytes 8388736 | tf_op jit(solution)/shard_map/gather | solution.py:165
  46.7 2.9 %convolution_bitcast_fusion = f32[1,256,2,128]{1,3,2,0:T(8,128)} fusion(bf16[2048,128]{1,0:T(8,128)(2,1)} %param.30, f32[1,2,256,256]{2,3,1,0:T(8,128)} %copy-done.1, f32[2,256]{1,0:T(2,128)} %copy-done.7, pred[256,256]{0,1:T(8,128)(4,1)S(1)} %compare_and_fusion, bf16[256,2048]{1,0:T(8,128)(2,1)} %param.20, f32[2048]{0:T(1024)} %param.27, f32[256]{0:T(256)} %copy-done.11), kind=kOutput, calls=%fused_computation.41 | convolution fusion | flops 170295296 | bytes 2436096 | tf_op jit(solution)/shard_map/hgmk,khd->mhgd/dot_general | solution.py:59
  49.6 10.0 %fusion.8 = pred[256,16384]{0,1:T(8,128)(4,1)} fusion(s32[256]{0:T(256)} %bitcast.180, pred[16384]{0:T(1024)(128)(4,1)S(1)} %copy-done.6), kind=kLoop, calls=%fused_computation.18 | loop fusion | flops 8388608 | bytes 4211712 | tf_op jit(solution)/shard_map/while/body/eval_jaxpr/and | solution.py:196
  59.6 24.8 %all-to-all-done.1 = bf16[16,2,512,128]{3,2,1,0:T(8,128)(2,1)} async-done(((bf16[16,2,512,128]{3,2,1,0:T(8,128)(2,1)}), bf16[16,2,512,128]{3,2,1,0:T(8,128)(2,1)}, u32[]{:S(2)}, u32[]{:S(2)}) %all-to-all-start.1) | async-done | bytes 4194336 | tf_op jit(solution)/shard_map/all_to_all | solution.py:167
  84.5 11.4 %all-to-all-start = ((bf16[16,2,512,128]{3,2,1,0:T(8,128)(2,1)}), bf16[16,2,512,128]{3,2,1,0:T(8,128)(2,1)}, u32[]{:S(2)}, u32[]{:S(2)}) async-start(bf16[16,2,512,128]{3,2,1,0:T(8,128)(2,1)} %bitcast.167), calls=%async_computation | async-start | bytes 8388608 | tf_op jit(solution)/shard_map/all_to_all | solution.py:168
  95.9 5.4 %gather_fusion.5 = bf16[32,512,128]{2,1,0:T(8,128)(2,1)} fusion(bf16[32,512,128]{2,1,0:T(8,128)(2,1)} %bitcast.11, s32[1024]{0:T(1024)} %pad_clamp_fusion.1), kind=kCustom, calls=%fused_computation.7 | custom fusion | bytes 8388736 | tf_op jit(solution)/shard_map/gather | solution.py:176
  101.3 3.2 %bitcast_convert_fusion = f32[1,32,512,1,128]{4,2,1,3,0:T(8,128)S(1)} fusion(bf16[32,512,128]{2,1,0:T(8,128)(2,1)} %gather_fusion.5), kind=kLoop, calls=%fused_computation.26 | loop fusion | flops 2097152 | bytes 12582912 | tf_op jit(solution)/shard_map/convert_element_type | solution.py:181
  104.5 5.1 %subtract_convert_fusion = (bf16[1,32,512,1,64]{4,2,1,3,0:T(8,128)(2,1)}, bf16[1,32,512,1,64]{4,2,1,3,0:T(8,128)(2,1)}) fusion(f32[1,32,512,1,128]{4,2,1,3,0:T(8,128)S(1)} %bitcast_convert_fusion, f32[32,64]{1,0:T(8,128)S(1)} %copy-done.5, f32[32,64]{1,0:T(8,128)S(1)} %copy-done.4), kind=kLoop, calls=%fused_computation.21 | loop fusion | flops 8388608 | bytes 12599296 | tf_op jit(solution)/shard_map/convert.10
  109.6 19.4 %fusion = (f32[2,256]{1,0:T(2,128)S(1)}, f32[16384,256,2]{1,0,2:T(8,128)}) fusion(pred[256,16384]{0,1:T(8,128)(4,1)} %fusion.8, bf16[256,2,64]{2,0,1:T(8,128)(2,1)S(1)} %get-tuple-element.49, bf16[256,2,64]{2,0,1:T(8,128)(2,1)S(1)} %get-tuple-element.48, bf16[16384,64]{1,0:T(8,128)(2,1)} %bitcast.171, bf16[16384,64]{1,0:T(8,128)(2,1)} %bitcast.170), kind=kOutput, calls=%fused_computation.10 | convolution fusion | flops 2181299712 | bytes 42076160 | tf_op jit(solution)/shard_map/while/body/eval_jaxpr/mhgd,khd->hgmk/dot_general | solution.py:53
  129.0 15.1 %fusion.3 = f32[2,256]{1,0:T(2,128)S(1)} fusion(f32[16384,256,2]{1,0,2:T(8,128)} %get-tuple-element.65, f32[2,256]{1,0:T(2,128)S(1)} %get-tuple-element.64, pred[256,16384]{0,1:T(8,128)(4,1)} %fusion.8), kind=kLoop, calls=%fused_computation.13 | loop fusion | flops 33553920 | bytes 37752832 | tf_op jit(solution)/shard_map/while/body/eval_jaxpr/reduce_sum | solution.py:58
  144.1 3.2 %all-to-all-done = bf16[16,2,512,128]{3,2,1,0:T(8,128)(2,1)} async-done(((bf16[16,2,512,128]{3,2,1,0:T(8,128)(2,1)}), bf16[16,2,512,128]{3,2,1,0:T(8,128)(2,1)}, u32[]{:S(2)}, u32[]{:S(2)}) %all-to-all-start) | async-done | bytes 4194336 | tf_op jit(solution)/shard_map/all_to_all | solution.py:168
  147.3 5.4 %gather_fusion.3 = bf16[32,512,128]{2,1,0:T(8,128)(2,1)} fusion(bf16[32,512,128]{2,1,0:T(8,128)(2,1)} %bitcast.4, s32[1024]{0:T(1024)} %pad_clamp_fusion.1), kind=kCustom, calls=%fused_computation.5 | custom fusion | bytes 8388736 | tf_op jit(solution)/shard_map/gather | solution.py:186
  152.8 16.8 %fusion.18 = f32[1,256,2,128]{1,3,2,0:T(8,128)} fusion(bf16[16384,128,1]{1,0,2:T(8,128)(2,1)} %bitcast.168, f32[16384,256,2]{1,0,2:T(8,128)} %get-tuple-element.65, f32[2,256]{1,0:T(2,128)S(1)} %get-tuple-element.64, pred[256,16384]{0,1:T(8,128)(4,1)} %fusion.8), kind=kOutput, calls=%fused_computation.42 | convolution fusion | flops 2181038080 | bytes 42207232 | tf_op jit(solution)/shard_map/while/body/eval_jaxpr/hgmk,khd->mhgd/dot_general | solution.py:59
  170.7 2.7 convolution_convert_fusion
  173.4 9.6 %all-to-all-start.2 = ((bf16[8,32,2048]{2,1,0:T(8,128)(2,1)}), bf16[8,32,2048]{2,1,0:T(8,128)(2,1)}, u32[]{:S(2)}, u32[]{:S(2)}) async-start(bf16[8,32,2048]{2,1,0:T(8,128)(2,1)} %bitcast.169), calls=%async_computation.2 | async-start | bytes 2097152 | tf_op jit(solution)/shard_map/all_to_all | solution.py:87
  184.0 14.0 %all-to-all-done.2 = bf16[8,32,2048]{2,1,0:T(8,128)(2,1)} async-done(((bf16[8,32,2048]{2,1,0:T(8,128)(2,1)}), bf16[8,32,2048]{2,1,0:T(8,128)(2,1)}, u32[]{:S(2)}, u32[]{:S(2)}) %all-to-all-start.2) | async-done | bytes 1048608 | tf_op jit(solution)/shard_map/all_to_all | solution.py:87
  206.1 2.6 collective-permute-start.4
  212.2 4.7 %collective-permute-done.2 = bf16[32,2048]{1,0:T(8,128)(2,1)S(1)} collective-permute-done((bf16[32,2048]{1,0:T(8,128)(2,1)S(1)}, bf16[32,2048]{1,0:T(8,128)(2,1)S(1)}, u32[]{:S(2)}, u32[]{:S(2)}) %collective-permute-start.2) | collective-permute-done | bytes 131104 | tf_op jit(solution)/shard_map/ppermute | solution.py:96
  220.3 2.8 %gather_fusion.6 = bf16[8,32,2048]{2,1,0:T(8,128)(2,1)} fusion(bf16[8,32,2048]{2,1,0:T(8,128)(2,1)} %bitcast_dynamic-update-slice_fusion.8, s32[1024]{0:T(1024)S(1)} %pad_clamp_fusion), kind=kCustom, calls=%fused_computation.clone | custom fusion | bytes 2097184 | tf_op jit(solution)/shard_map/jit(_take)/gather | solution.py:99
  225.5 3.8 %fusion.77 = f32[256,768]{1,0:T(8,128)} fusion(bf16[256,2048]{1,0:T(8,128)(2,1)S(1)} %bitcast.172, bf16[2048,768]{1,0:T(8,128)(2,1)} %param.35), kind=kOutput, calls=%fused_computation.168 | convolution fusion | flops 805306368 | bytes 4980736 | tf_op jit(solution)/shard_map/dot_general | solution.py:80
  229.3 5.5 %convolution_convert_fusion.1 = bf16[256,2048]{1,0:T(8,128)(2,1)} fusion(bf16[768,2048]{1,0:T(8,128)(2,1)S(1)} %copy-done, bf16[256,2048]{1,0:T(8,128)(2,1)} %bitcast.173, bf16[2048,768]{1,0:T(8,128)(2,1)} %param.36, f32[256,768]{1,0:T(8,128)} %fusion.77), kind=kOutput, calls=%fused_computation.30 | convolution fusion | flops 1612316672 | bytes 9175040 | tf_op jit(solution)/shard_map/dot_general | solution.py:225
  234.8 17.9 %all_to_all.20 = bf16[8,32,2048]{2,1,0:T(8,128)(2,1)S(1)} all-to-all(bf16[8,32,2048]{2,1,0:T(8,128)(2,1)} %bitcast.174), channel_id=1, replica_groups=mesh['req'=16,'tp'=8] {'tp'}, dimensions={0} | all-to-all | bytes 2097152 | tf_op jit(solution)/shard_map/all_to_all | solution.py:87
  258.3 2.6 collective-permute-start.11
  261.6 2.4 collective-permute-done.8
  264.7 4.6 %collective-permute-done.9 = bf16[32,2048]{1,0:T(8,128)(2,1)S(1)} collective-permute-done((bf16[32,2048]{1,0:T(8,128)(2,1)S(1)}, bf16[32,2048]{1,0:T(8,128)(2,1)S(1)}, u32[]{:S(2)}, u32[]{:S(2)}) %collective-permute-start.9) | collective-permute-done | bytes 131104 | tf_op jit(solution)/shard_map/ppermute | solution.py:96
  272.6 2.8 %gather_fusion.7 = bf16[8,32,2048]{2,1,0:T(8,128)(2,1)} fusion(bf16[8,32,2048]{2,1,0:T(8,128)(2,1)} %bitcast_dynamic-update-slice_fusion, s32[1024]{0:T(1024)S(1)} %pad_clamp_fusion), kind=kCustom, calls=%fused_computation.1.clone | custom fusion | bytes 2097184 | tf_op jit(solution)/shard_map/jit(_take)/gather | solution.py:99
  275.5 2.4 broadcast_select_fusion.1
  (124 shorter events, 46.9 us)
Async XLA Ops:
  0.0 229.3 %copy-start = (bf16[768,2048]{1,0:T(8,128)(2,1)S(1)}, bf16[768,2048]{1,0:T(8,128)(2,1)}, u32[]{:S(2)}) copy-start(bf16[768,2048]{1,0:T(8,128)(2,1)} %param.37) | copy-start | bytes 9437188
  15.3 11.3 %copy-start.13 = (f32[2048]{0:T(1024)S(1)}, f32[2048]{0:T(1024)}, u32[]{:S(2)}) copy-start(f32[2048]{0:T(1024)} %param.27) | copy-start | bytes 24580
  15.4 69.1 %all-to-all-start.1 = ((bf16[16,2,512,128]{3,2,1,0:T(8,128)(2,1)}), bf16[16,2,512,128]{3,2,1,0:T(8,128)(2,1)}, u32[]{:S(2)}, u32[]{:S(2)}) async-start(bf16[16,2,512,128]{3,2,1,0:T(8,128)(2,1)} %bitcast.166), calls=%async_computation.1 | async-start | bytes 8388608 | tf_op jit(solution)/shard_map/all_to_all | solution.py:167
  24.1 9.6 %copy-start.14 = (s32[16]{0:T(128)S(1)}, s32[16]{0:T(128)}, u32[]{:S(2)}) copy-start(s32[16]{0:T(128)} %param.22) | copy-start | bytes 196
  24.1 13.4 %copy-start.12 = (f32[128]{0:T(128)S(1)}, f32[128]{0:T(128)}, u32[]{:S(2)}) copy-start(f32[128]{0:T(128)} %param.32) | copy-start | bytes 1540
  25.1 13.1 %copy-start.9 = (s32[1,256]{1,0:T(1,128)}, s32[1,256]{1,0:T(1,128)S(1)}, u32[]{:S(2)}) copy-start(s32[1,256]{1,0:T(1,128)S(1)} %constant_dynamic-slice_fusion) | copy-start | bytes 3076
  26.6 11.1 %copy-start.11 = (f32[256]{0:T(256)}, f32[256]{0:T(256)S(1)}, u32[]{:S(2)}) copy-start(f32[256]{0:T(256)S(1)} %add_rsqrt_fusion.2) | copy-start | bytes 3076
  43.5 6.1 %copy-start.6 = (pred[16384]{0:T(1024)(128)(4,1)S(1)}, pred[16384]{0:T(1024)(128)(4,1)}, u32[]{:S(2)}) copy-start(pred[16384]{0:T(1024)(128)(4,1)} %fusion.46) | copy-start | bytes 49156
  45.8 0.8 copy-start.1
  45.8 0.8 copy-start.7
  84.5 62.9 %all-to-all-start = ((bf16[16,2,512,128]{3,2,1,0:T(8,128)(2,1)}), bf16[16,2,512,128]{3,2,1,0:T(8,128)(2,1)}, u32[]{:S(2)}, u32[]{:S(2)}) async-start(bf16[16,2,512,128]{3,2,1,0:T(8,128)(2,1)} %bitcast.167), calls=%async_computation | async-start | bytes 8388608 | tf_op jit(solution)/shard_map/all_to_all | solution.py:168
  101.3 3.2 %copy-start.4 = (f32[32,64]{1,0:T(8,128)S(1)}, f32[32,64]{1,0:T(8,128)}, u32[]{:S(2)}) copy-start(f32[32,64]{1,0:T(8,128)} %get-tuple-element.56) | copy-start | bytes 24580
  101.3 3.2 %copy-start.5 = (f32[32,64]{1,0:T(8,128)S(1)}, f32[32,64]{1,0:T(8,128)}, u32[]{:S(2)}) copy-start(f32[32,64]{1,0:T(8,128)} %get-tuple-element.57) | copy-start | bytes 24580
  109.6 19.4 %copy-start.8 = (f32[2,256]{1,0:T(2,128)S(1)}, f32[2,256]{1,0:T(2,128)}, u32[]{:S(2)}) copy-start(f32[2,256]{1,0:T(2,128)} %copy-done.7) | copy-start | bytes 6148
  152.8 16.9 %copy-start.3 = (f32[1,256,2,128]{1,3,2,0:T(8,128)S(1)}, f32[1,256,2,128]{1,3,2,0:T(8,128)}, u32[]{:S(2)}) copy-start(f32[1,256,2,128]{1,3,2,0:T(8,128)} %convolution_bitcast_fusion) | copy-start | bytes 786436
  169.6 30.9 %copy-start.10 = (f32[2048]{0:T(1024)S(1)}, f32[2048]{0:T(1024)}, u32[]{:S(2)}) copy-start(f32[2048]{0:T(1024)} %param.34) | copy-start | bytes 24580
  173.4 24.7 %all-to-all-start.2 = ((bf16[8,32,2048]{2,1,0:T(8,128)(2,1)}), bf16[8,32,2048]{2,1,0:T(8,128)(2,1)}, u32[]{:S(2)}, u32[]{:S(2)}) async-start(bf16[8,32,2048]{2,1,0:T(8,128)(2,1)} %bitcast.169), calls=%async_computation.2 | async-start | bytes 2097152 | tf_op jit(solution)/shard_map/all_to_all | solution.py:87
  201.3 7.4 %collective-permute-start = (bf16[32,2048]{1,0:T(8,128)(2,1)S(1)}, bf16[32,2048]{1,0:T(8,128)(2,1)S(1)}, u32[]{:S(2)}, u32[]{:S(2)}) collective-permute-start(bf16[32,2048]{1,0:T(8,128)(2,1)S(1)} %get-tuple-element.29), channel_id=1, source_target_pairs={{0,1},{1,2},{2,3},{3,4},{4,5},{5,6},{6,7},{7,0},{8,9},{9,10},{10,1... | collective-permute-start | bytes 393224 | tf_op jit(solution)/shard_map/ppermute | solution.py:96
  202.4 9.2 %collective-permute-start.1 = (bf16[32,2048]{1,0:T(8,128)(2,1)S(1)}, bf16[32,2048]{1,0:T(8,128)(2,1)S(1)}, u32[]{:S(2)}, u32[]{:S(2)}) collective-permute-start(bf16[32,2048]{1,0:T(8,128)(2,1)S(1)} %get-tuple-element.29), channel_id=1, source_target_pairs={{0,2},{1,3},{2,4},{3,5},{4,6},{5,7},{6,0},{7,1},{8,10},{9,11},{10,... | collective-permute-start | bytes 393224 | tf_op jit(solution)/shard_map/ppermute | solution.py:96
  202.5 14.5 %collective-permute-start.2 = (bf16[32,2048]{1,0:T(8,128)(2,1)S(1)}, bf16[32,2048]{1,0:T(8,128)(2,1)S(1)}, u32[]{:S(2)}, u32[]{:S(2)}) collective-permute-start(bf16[32,2048]{1,0:T(8,128)(2,1)S(1)} %get-tuple-element.29), channel_id=1, source_target_pairs={{0,3},{1,4},{2,5},{3,6},{4,7},{5,0},{6,1},{7,2},{8,11},{9,12},{10,... | collective-permute-start | bytes 393224 | tf_op jit(solution)/shard_map/ppermute | solution.py:96
  204.6 13.1 %collective-permute-start.3 = (bf16[32,2048]{1,0:T(8,128)(2,1)S(1)}, bf16[32,2048]{1,0:T(8,128)(2,1)S(1)}, u32[]{:S(2)}, u32[]{:S(2)}) collective-permute-start(bf16[32,2048]{1,0:T(8,128)(2,1)S(1)} %get-tuple-element.29), channel_id=1, source_target_pairs={{0,4},{1,5},{2,6},{3,7},{4,0},{5,1},{6,2},{7,3},{8,12},{9,13},{10,... | collective-permute-start | bytes 393224 | tf_op jit(solution)/shard_map/ppermute | solution.py:96
  206.1 12.2 %collective-permute-start.4 = (bf16[32,2048]{1,0:T(8,128)(2,1)S(1)}, bf16[32,2048]{1,0:T(8,128)(2,1)S(1)}, u32[]{:S(2)}, u32[]{:S(2)}) collective-permute-start(bf16[32,2048]{1,0:T(8,128)(2,1)S(1)} %get-tuple-element.29), channel_id=1, source_target_pairs={{0,5},{1,6},{2,7},{3,0},{4,1},{5,2},{6,3},{7,4},{8,13},{9,14},{10,... | collective-permute-start | bytes 393224 | tf_op jit(solution)/shard_map/ppermute | solution.py:96
  208.7 10.3 %collective-permute-start.5 = (bf16[32,2048]{1,0:T(8,128)(2,1)S(1)}, bf16[32,2048]{1,0:T(8,128)(2,1)S(1)}, u32[]{:S(2)}, u32[]{:S(2)}) collective-permute-start(bf16[32,2048]{1,0:T(8,128)(2,1)S(1)} %get-tuple-element.29), channel_id=1, source_target_pairs={{0,6},{1,7},{2,0},{3,1},{4,2},{5,3},{6,4},{7,5},{8,14},{9,15},{10,... | collective-permute-start | bytes 393224 | tf_op jit(solution)/shard_map/ppermute | solution.py:96
  211.6 8.1 %collective-permute-start.6 = (bf16[32,2048]{1,0:T(8,128)(2,1)S(1)}, bf16[32,2048]{1,0:T(8,128)(2,1)S(1)}, u32[]{:S(2)}, u32[]{:S(2)}) collective-permute-start(bf16[32,2048]{1,0:T(8,128)(2,1)S(1)} %get-tuple-element.29), channel_id=1, source_target_pairs={{0,7},{1,0},{2,1},{3,2},{4,3},{5,4},{6,5},{7,6},{8,15},{9,8},{10,9... | collective-permute-start | bytes 393224 | tf_op jit(solution)/shard_map/ppermute | solution.py:96
  224.5 1.0 copy-start.2
  253.5 7.4 %collective-permute-start.7 = (bf16[32,2048]{1,0:T(8,128)(2,1)S(1)}, bf16[32,2048]{1,0:T(8,128)(2,1)S(1)}, u32[]{:S(2)}, u32[]{:S(2)}) collective-permute-start(bf16[32,2048]{1,0:T(8,128)(2,1)S(1)} %get-tuple-element.27), channel_id=1, source_target_pairs={{0,1},{1,2},{2,3},{3,4},{4,5},{5,6},{6,7},{7,0},{8,9},{9,10},{10,1... | collective-permute-start | bytes 393224 | tf_op jit(solution)/shard_map/ppermute | solution.py:96
  254.8 9.2 %collective-permute-start.8 = (bf16[32,2048]{1,0:T(8,128)(2,1)S(1)}, bf16[32,2048]{1,0:T(8,128)(2,1)S(1)}, u32[]{:S(2)}, u32[]{:S(2)}) collective-permute-start(bf16[32,2048]{1,0:T(8,128)(2,1)S(1)} %get-tuple-element.27), channel_id=1, source_target_pairs={{0,2},{1,3},{2,4},{3,5},{4,6},{5,7},{6,0},{7,1},{8,10},{9,11},{10,... | collective-permute-start | bytes 393224 | tf_op jit(solution)/shard_map/ppermute | solution.py:96
  254.8 14.5 %collective-permute-start.9 = (bf16[32,2048]{1,0:T(8,128)(2,1)S(1)}, bf16[32,2048]{1,0:T(8,128)(2,1)S(1)}, u32[]{:S(2)}, u32[]{:S(2)}) collective-permute-start(bf16[32,2048]{1,0:T(8,128)(2,1)S(1)} %get-tuple-element.27), channel_id=1, source_target_pairs={{0,3},{1,4},{2,5},{3,6},{4,7},{5,0},{6,1},{7,2},{8,11},{9,12},{10,... | collective-permute-start | bytes 393224 | tf_op jit(solution)/shard_map/ppermute | solution.py:96
  256.8 13.2 %collective-permute-start.10 = (bf16[32,2048]{1,0:T(8,128)(2,1)S(1)}, bf16[32,2048]{1,0:T(8,128)(2,1)S(1)}, u32[]{:S(2)}, u32[]{:S(2)}) collective-permute-start(bf16[32,2048]{1,0:T(8,128)(2,1)S(1)} %get-tuple-element.27), channel_id=1, source_target_pairs={{0,4},{1,5},{2,6},{3,7},{4,0},{5,1},{6,2},{7,3},{8,12},{9,13},{10,... | collective-permute-start | bytes 393224 | tf_op jit(solution)/shard_map/ppermute | solution.py:96
  258.3 12.3 %collective-permute-start.11 = (bf16[32,2048]{1,0:T(8,128)(2,1)S(1)}, bf16[32,2048]{1,0:T(8,128)(2,1)S(1)}, u32[]{:S(2)}, u32[]{:S(2)}) collective-permute-start(bf16[32,2048]{1,0:T(8,128)(2,1)S(1)} %get-tuple-element.27), channel_id=1, source_target_pairs={{0,5},{1,6},{2,7},{3,0},{4,1},{5,2},{6,3},{7,4},{8,13},{9,14},{10,... | collective-permute-start | bytes 393224 | tf_op jit(solution)/shard_map/ppermute | solution.py:96
  260.9 10.4 %collective-permute-start.12 = (bf16[32,2048]{1,0:T(8,128)(2,1)S(1)}, bf16[32,2048]{1,0:T(8,128)(2,1)S(1)}, u32[]{:S(2)}, u32[]{:S(2)}) collective-permute-start(bf16[32,2048]{1,0:T(8,128)(2,1)S(1)} %get-tuple-element.27), channel_id=1, source_target_pairs={{0,6},{1,7},{2,0},{3,1},{4,2},{5,3},{6,4},{7,5},{8,14},{9,15},{10,... | collective-permute-start | bytes 393224 | tf_op jit(solution)/shard_map/ppermute | solution.py:96
  264.0 8.0 %collective-permute-start.13 = (bf16[32,2048]{1,0:T(8,128)(2,1)S(1)}, bf16[32,2048]{1,0:T(8,128)(2,1)S(1)}, u32[]{:S(2)}, u32[]{:S(2)}) collective-permute-start(bf16[32,2048]{1,0:T(8,128)(2,1)S(1)} %get-tuple-element.27), channel_id=1, source_target_pairs={{0,7},{1,0},{2,1},{3,2},{4,3},{5,4},{6,5},{7,6},{8,15},{9,8},{10,9... | collective-permute-start | bytes 393224 | tf_op jit(solution)/shard_map/ppermute | solution.py:96

commit v2 on v1

--- a/solution.py
+++ b/solution.py
@@ -161,57 +161,42 @@
         pair_rank[:, :, None] == jnp.arange(pair_cap)[None, None, :]
     )
     send_slot = jnp.sum(jnp.where(my_sends, slot_table[:, :, None], 0), axis=1)
-    send_keys = cached_key_pool[send_slot]
-    send_values = cached_value_pool[send_slot]
-    got_keys, got_values = (
-        lax.all_to_all(send_keys, "req", split_axis=0, concat_axis=0, tiled=True),
-        lax.all_to_all(send_values, "req", split_axis=0, concat_axis=0, tiled=True),
-    )
-    my_holder = lax.dynamic_index_in_dim(holder_table, my_index, 0, keepdims=False)
-    my_rank = lax.dynamic_index_in_dim(pair_rank, my_index, 0, keepdims=False)
-    buffer = my_holder * pair_cap + my_rank
-    position_shift_angle = angles(jnp.arange(MOST_STRETCHES) * STRETCH_TOKENS, head_size)[
-        None, :, None, None, :
-    ]
-    gathered_stretch_keys = got_keys.reshape((req_count * pair_cap,) + got_keys.shape[2:])[buffer]
-    gathered_stretch_keys = gathered_stretch_keys.reshape(
-        local_reqs, MOST_STRETCHES, STRETCH_TOKENS, key_heads, head_size
-    )
-    gathered_stretch_keys = rotate_halves(
-        gathered_stretch_keys.astype(jnp.float32), position_shift_angle
-    ).astype(jnp.bfloat16)
-    gathered_stretch_keys = gathered_stretch_keys.reshape(
-        local_reqs, MOST_STRETCHES * STRETCH_TOKENS, key_heads, head_size
-    )
-    gathered_stretch_values = got_values.reshape((req_count * pair_cap,) + got_values.shape[2:])[
-        buffer
-    ]
-    gathered_stretch_values = gathered_stretch_values.reshape(
-        local_reqs, MOST_STRETCHES * STRETCH_TOKENS, key_heads, head_size
-    )
-    key_place = jnp.arange(MOST_STRETCHES * STRETCH_TOKENS)
-
-    def cached_stats(packed):
-        group_query, position, length, key_block, value_block = packed
-        live_mask = (key_place[None, :] < position[:, None]) & (
-            key_place[None, :] // STRETCH_TOKENS < length
-        )
-        return block_stats(group_query, key_block, value_block, live_mask)
-
-    held_sum, held_peak, held_total = lax.map(
-        cached_stats,
-        (
-            grouped_heads.reshape(local_reqs, req_rows, key_heads, groups, head_size),
-            my_positions,
-            my_lengths,
-            gathered_stretch_keys,
-            gathered_stretch_values,
-        ),
-    )
+    send_place = jnp.sum(jnp.where(my_sends, jnp.arange(MOST_STRETCHES)[None, :, None], 0), axis=1)
+    request_count = holder_table.shape[0]
+    held_count = pair_cap * STRETCH_TOKENS
+    held_keys = cached_key_pool[send_slot].reshape(
+        request_count, pair_cap, STRETCH_TOKENS, key_heads, head_size
+    )
+    held_angle = angles(send_place * STRETCH_TOKENS, head_size)[:, :, None, None, :]
+    held_keys = rotate_halves(held_keys.astype(jnp.float32), held_angle).astype(jnp.bfloat16)
+    held_keys = held_keys.reshape(request_count, held_count, key_heads, head_size)
+    held_values = cached_value_pool[send_slot].reshape(request_count, held_count, key_heads, head_size)
+    query_copies = jnp.broadcast_to(queries[None], (req_count,) + queries.shape)
+    all_queries = lax.all_to_all(query_copies, "req", 0, 0, tiled=False)
+    all_queries = all_queries.reshape(request_count, req_rows, key_heads, groups, head_size)
+    key_pos = (
+        send_place[:, :, None] * STRETCH_TOKENS + jnp.arange(STRETCH_TOKENS)[None, None, :]
+    ).reshape(request_count, held_count)
+    key_ok = jnp.repeat(send_place < req_lengths[:, None], STRETCH_TOKENS, axis=1)
+    live = key_ok[:, None, :] & (key_pos[:, None, :] < recompute_pos[:, :, None])
+    scores = jnp.einsum(
+        "rmhgd,rkhd->rhgmk", all_queries, held_keys, preferred_element_type=jnp.float32
+    ) * head_size ** (-0.5)
+    live = live[:, None, None]
+    held_peak = jnp.max(jnp.where(live, scores, floor_score), axis=-1)
+    weights = jnp.where(live, jnp.exp(scores - held_peak[..., None]), 0.0)
+    held_total = jnp.sum(weights, axis=-1)
+    held_sum = jnp.einsum(
+        "rhgmk,rkhd->rmhgd", weights.astype(jnp.bfloat16), held_values, preferred_element_type=jnp.float32
+    )
+    got_sum = lax.all_to_all(held_sum, "req", 0, 0, tiled=False)
+    got_stats = lax.all_to_all(jnp.stack([held_peak, held_total], axis=1), "req", 0, 0, tiled=False)
+    head_total = key_heads * groups
+    got_stats = got_stats.transpose(0, 1, 4, 2, 3).reshape(req_count, 2, count_of_rows, head_total)
     attended = merge_stats(
-        jnp.stack([held_sum.reshape(fresh_sum.shape), fresh_sum]),
-        jnp.stack([held_peak.reshape(fresh_peak.shape), fresh_peak]),
-        jnp.stack([held_total.reshape(fresh_total.shape), fresh_total]),
+        jnp.concatenate([got_sum.reshape(req_count, count_of_rows, head_total, head_size), fresh_sum[None]]),
+        jnp.concatenate([got_stats[:, 0], fresh_peak[None]]),
+        jnp.concatenate([got_stats[:, 1], fresh_total[None]]),
     )
     tp_count = lax.axis_size("tp")
     tp_index = lax.axis_index("tp")

time: 279 us -> 287 us (1.029)
  waiting for transfers between devices: 56 us -> 73.1 us
  local copies, waits for them, and re-layouts: 48.8 us -> 39.1 us
    dot_general x0 -> x2, matrix products: none -> 35.8 us  [the longest x1 18 us: on_device(): jnp.einsum('rhgmk,rkhd->rmhgd', weights.astype(jnp.bfloat16), held_values...]
    dot_general x2 -> x1, matrix products: 19.8 us -> 0.27 us  [block_stats(): jnp.einsum('mhgd,khd->hgmk', grouped_heads, gathered_stretch_keys, prefer...]
    all_to_all x2 -> x3, waiting for transfers between devices: 28 us -> 45.1 us  [the longest x1 45.1 us: on_device(): got_sum = lax.all_to_all(held_sum, 'req', 0, 0, tiled=False)]
    dot_general x2 -> x1, matrix products: 19.8 us -> 2.9 us  [block_stats(): jnp.einsum('hgmk,khd->mhgd', weights.astype(jnp.bfloat16), values, prefer...]
    reduce_sum x2 -> x1, other arithmetic: 15.2 us -> 0.13 us  [block_stats(): weight_sum = jnp.sum(weights, axis=-1)]
    reduce_sum x1 -> x2, other arithmetic: 0.12 us -> 14.8 us  [the longest x1 14.6 us: on_device(): held_total = jnp.sum(weights, axis=-1)]
    gather x4 -> x2, local copies, waits for them, and re-layouts: 21.4 us -> 10.6 us  [the longest x1 5.32 us: on_device(): cached_value_pool[send_slot]]
    another operation x2 -> x3, other arithmetic: 6.2 us -> 11.3 us
  transfers between devices with their start and end apart: 17 -> 18, of which waited for: 7 -> 6; matrix products, arithmetic and copies ran while one was open for 33% -> 27% of each run, Pallas kernels for 0% -> 0%
where the time goes in v2:
time: 287 us; the launch traced here: 286 us
  waiting for transfers between devices  73.1 us (25%)
  other arithmetic  55 us (19%)
  matrix products  54.6 us (19%)
  starting transfers between devices  46.1 us (16%)
  local copies, waits for them, and re-layouts  39.1 us (14%)
  blocking collectives  17.9 us (6%)
    all_to_all x1, waiting for transfers between devices, on_device(): got_sum = lax.all_to_all(held_sum, 'req', 0, 0, tiled=False)  45.1 us
    dot_general x1, matrix products, on_device(): jnp.einsum('rhgmk,rkhd->rmhgd', weights.astype(jnp.bfloat16), held_values...  18 us
    all_to_all x1, blocking collectives, reduce_rows(): got = lax.all_to_all(blocks, 'tp', 0, 0, tiled=False)  17.9 us
    dot_general x1, matrix products, on_device(): jnp.einsum('rmhgd,rkhd->rhgmk', all_queries, held_keys, preferred_element...  17.8 us
    ppermute x14, starting transfers between devices, gather_rows(): parts.append(lax.ppermute(rows, 'tp', pairs))  14.8 us
    reduce_sum x1, other arithmetic, on_device(): held_total = jnp.sum(weights, axis=-1)  14.6 us
    all_to_all x1, waiting for transfers between devices, reduce_rows(): got = lax.all_to_all(blocks, 'tp', 0, 0, tiled=False)  14 us
    ppermute x14, waiting for transfers between devices, gather_rows(): parts.append(lax.ppermute(rows, 'tp', pairs))  14 us
  transfers between devices with their start and end apart: 18, of which 6 were waited for; matrix products, arithmetic and copies ran while one was open for 27% of the time, Pallas kernels for 0%

profile of v2, /device:TPU:1, one launch (start us, length us, event | category | flops | bytes accessed | tf_op | source)
XLA Modules:
  0.0 286.2 jit_solution(1795118041963914507)
XLA Ops:
  2.5 2.9 %multiply_reduce_fusion = (f32[256,2]{0,1:T(2,128)S(1)}, f32[256,256]{0,1:T(8,128)}) fusion(bf16[2048,256]{1,0:T(8,128)(2,1)} %param.28, bf16[256,2048]{1,0:T(8,128)(2,1)} %param.20, f32[2048]{0:T(1024)} %param.27, f32[256]{0:T(256)S(1)} %add_rsqrt_fusion.2), kind=kOutput, calls=%fused_computation.66 | convolution fusion | flops 270663168 | bytes 2370560 | tf_op jit(solution)/shard_map/dot_general | solution.py:135
  9.3 8.6 %all-to-all-start = ((bf16[16,256,2,128]{3,1,2,0:T(8,128)(2,1)}), bf16[16,256,2,128]{3,1,2,0:T(8,128)(2,1)}, u32[]{:S(2)}, u32[]{:S(2)}) async-start(bf16[16,256,2,128]{3,1,2,0:T(8,128)(2,1)} %broadcast_in_dim.75), calls=%async_computation | async-start | bytes 4194304 | tf_op jit(solution)/shard_map/all_to_all | solution.py:175
  18.1 3.5 %gather_fusion = s32[512]{0:T(512)S(1)} fusion(s32[512]{0:T(512)S(1)} %bitcast.168, s32[1024]{0:T(1024)S(1)} %pad_clamp_fusion.2), kind=kCustom, calls=%fused_computation.2 | custom fusion | bytes 6144 | tf_op jit(solution)/shard_map/gather | solution.py:155
  22.6 3.5 %gather_fusion.1 = s32[512]{0:T(512)S(1)} fusion(s32[512]{0:T(512)S(1)} %bitcast.167, s32[1024]{0:T(1024)S(1)} %pad_clamp_fusion.2), kind=kCustom, calls=%fused_computation.3 | custom fusion | bytes 6144 | tf_op jit(solution)/shard_map/gather | solution.py:156
  26.9 5.2 %gather_fusion.3 = bf16[32,512,128]{2,1,0:T(8,128)(2,1)} fusion(bf16[32,512,128]{2,1,0:T(8,128)(2,1)} %param.25, s32[1024]{0:T(1024)S(1)} %pad_clamp_fusion.1), kind=kCustom, calls=%fused_computation.5 | custom fusion | bytes 8388736 | tf_op jit(solution)/shard_map/gather | solution.py:167
  32.2 6.4 %convert.29 = f32[16,2,512,1,128]{4,2,1,0,3:T(8,128)} convert(bf16[16,2,512,1,128]{4,2,1,0,3:T(8,128)(2,1)} %bitcast.169) | non-fusion elementwise | flops 2097152 | bytes 12582912 | tf_op jit(solution)/shard_map/convert_element_type | solution.py:171
  39.1 5.3 %gather_fusion.2 = bf16[32,512,128]{2,1,0:T(8,128)(2,1)} fusion(bf16[32,512,128]{2,1,0:T(8,128)(2,1)} %param.26, s32[1024]{0:T(1024)S(1)} %pad_clamp_fusion.1), kind=kCustom, calls=%fused_computation.4 | custom fusion | bytes 8388736 | tf_op jit(solution)/shard_map/gather | solution.py:173
  44.4 10.4 %subtract_convert_fusion = (bf16[16,2,512,1,64]{4,2,1,0,3:T(8,128)(2,1)}, bf16[16,2,512,1,64]{4,2,1,0,3:T(8,128)(2,1)}) fusion(f32[16,2,512,1,128]{4,2,1,0,3:T(8,128)} %convert.29, f32[16,2,64]{2,1,0:T(2,128)S(1)} %get-tuple-element.27, f32[16,2,64]{2,1,0:T(2,128)S(1)} %get-tuple-element.26), kind=kLoop, calls=%fused_computation.18 | loop fusion | flops 8388608 | bytes 12599296 | tf_op jit(solution)/shard_map/convert.10
  54.8 6.5 %compare_and_fusion = pred[16,256,1024]{1,2,0:T(8,128)(4,1)} fusion(s32[16,256]{1,0:T(8,128)S(1)} %copy-done.5, s32[16,1024]{1,0:T(8,128)S(1)} %broadcast_add_fusion, pred[16,1024]{1,0:T(8,128)(4,1)S(1)} %bitcast.186), kind=kLoop, calls=%fused_computation.16 | loop fusion | flops 8388608 | bytes 4292608 | tf_op jit(solution)/shard_map/and | solution.py:181
  61.4 17.8 %fusion = (f32[16,2,256]{2,1,0:T(2,128)S(1)}, f32[16,1024,256,2]{2,1,3,0:T(8,128)}) fusion(pred[16,256,1024]{1,2,0:T(8,128)(4,1)} %compare_and_fusion, bf16[16,256,2,128]{3,1,2,0:T(8,128)(2,1)} %all-to-all-done, bf16[16,1024,64]{2,1,0:T(8,128)(2,1)} %bitcast.173, bf16[16,1024,64]{2,1,0:T(8,128)(2,1)} %bitcast.172), kind=kOutput, calls=%fused_computation.8 | convolution fusion | flops 2181029888 | bytes 44072960 | tf_op jit(solution)/shard_map/rmhgd,rkhd->rhgmk/dot_general | solution.py:182
  79.2 14.6 %fusion.3 = f32[16,2,256]{2,1,0:T(2,128)S(1)} fusion(f32[16,1024,256,2]{2,1,3,0:T(8,128)} %get-tuple-element.41, f32[16,2,256]{2,1,0:T(2,128)S(1)} %get-tuple-element.40, pred[16,256,1024]{1,2,0:T(8,128)(4,1)S(1)} %copy-done.1), kind=kLoop, calls=%fused_computation.11 | loop fusion | flops 33546240 | bytes 37814272 | tf_op jit(solution)/shard_map/reduce_sum | solution.py:188
  94.5 6.6 %all-to-all-start.2 = ((f32[16,2,1,2,256]{4,3,2,1,0:T(2,128)}), f32[16,2,1,2,256]{4,3,2,1,0:T(2,128)S(1)}, u32[]{:S(2)}, u32[]{:S(2)}) async-start(f32[16,2,1,2,256]{4,3,2,1,0:T(2,128)} %pad_maximum_fusion.1), calls=%async_computation.2 | async-start | bytes 131072 | tf_op jit(solution)/shard_map/all_to_all | solution.py:193
  101.1 18.0 %fusion.13 = f32[16,256,1,2,128]{1,4,3,2,0:T(8,128)} fusion(bf16[16,1024,128,1]{2,1,3,0:T(8,128)(2,1)} %bitcast.170, f32[16,1024,256,2]{2,1,3,0:T(8,128)} %get-tuple-element.41, f32[16,2,256]{2,1,0:T(2,128)S(1)} %get-tuple-element.40, pred[16,256,1024]{1,2,0:T(8,128)(4,1)} %compare_and_fusion), kind=kOutput, calls=%fused_computation.29 | convolution fusion | flops 2181038080 | bytes 46170112 | tf_op jit(solution)/shard_map/rhgmk,rkhd->rmhgd/dot_general | solution.py:189
  119.1 6.8 %all-to-all-start.1 = ((f32[16,256,1,2,128]{1,4,3,2,0:T(8,128)}), f32[16,256,1,2,128]{1,4,3,2,0:T(8,128)}, u32[]{:S(2)}, u32[]{:S(2)}) async-start(f32[16,256,1,2,128]{1,4,3,2,0:T(8,128)} %fusion.13), calls=%async_computation.1 | async-start | bytes 8388608 | tf_op jit(solution)/shard_map/all_to_all | solution.py:192
  129.7 2.9 %convolution_bitcast_fusion = f32[1,256,2,128]{1,3,2,0:T(8,128)} fusion(bf16[2048,128]{1,0:T(8,128)(2,1)} %param.30, f32[1,2,256,256]{2,3,1,0:T(8,128)} %copy-done.4, f32[2,256]{1,0:T(2,128)S(1)} %get-tuple-element.38, pred[256,256]{0,1:T(8,128)(4,1)S(1)} %compare_and_fusion.1, bf16[256,2048]{1,0:T(8,128)(2,1)} %param.20, f32[2048]{0:T(1024)S(1)} %copy-done.12, ...), kind=kOutput, calls=%fused_computation.40 | convolution fusion | flops 170295296 | bytes 2436096 | tf_op jit(solution)/shard_map/hgmk,khd->mhgd/dot_general | solution.py:59
  132.8 45.1 %all-to-all-done.1 = f32[16,256,1,2,128]{1,4,3,2,0:T(8,128)} async-done(((f32[16,256,1,2,128]{1,4,3,2,0:T(8,128)}), f32[16,256,1,2,128]{1,4,3,2,0:T(8,128)}, u32[]{:S(2)}, u32[]{:S(2)}) %all-to-all-start.1) | async-done | bytes 4194336 | tf_op jit(solution)/shard_map/all_to_all | solution.py:192
  177.8 2.8 fusion.9
  182.1 9.2 %all-to-all-start.3 = ((bf16[8,32,2048]{2,1,0:T(8,128)(2,1)}), bf16[8,32,2048]{2,1,0:T(8,128)(2,1)}, u32[]{:S(2)}, u32[]{:S(2)}) async-start(bf16[8,32,2048]{2,1,0:T(8,128)(2,1)} %bitcast.171), calls=%async_computation.3 | async-start | bytes 2097152 | tf_op jit(solution)/shard_map/all_to_all | solution.py:87
  192.4 14.0 %all-to-all-done.3 = bf16[8,32,2048]{2,1,0:T(8,128)(2,1)} async-done(((bf16[8,32,2048]{2,1,0:T(8,128)(2,1)}), bf16[8,32,2048]{2,1,0:T(8,128)(2,1)}, u32[]{:S(2)}, u32[]{:S(2)}) %all-to-all-start.3) | async-done | bytes 1048608 | tf_op jit(solution)/shard_map/all_to_all | solution.py:87
  210.9 2.1 collective-permute-start.2
  214.5 2.6 collective-permute-start.4
  217.8 2.2 collective-permute-done.1
  220.6 4.7 %collective-permute-done.2 = bf16[32,2048]{1,0:T(8,128)(2,1)S(1)} collective-permute-done((bf16[32,2048]{1,0:T(8,128)(2,1)S(1)}, bf16[32,2048]{1,0:T(8,128)(2,1)S(1)}, u32[]{:S(2)}, u32[]{:S(2)}) %collective-permute-start.2) | collective-permute-done | bytes 131104 | tf_op jit(solution)/shard_map/ppermute | solution.py:96
  228.7 2.8 gather_fusion.4
  233.9 3.8 %fusion.71 = f32[256,768]{1,0:T(8,128)} fusion(bf16[256,2048]{1,0:T(8,128)(2,1)S(1)} %bitcast.174, bf16[2048,768]{1,0:T(8,128)(2,1)} %param.35), kind=kOutput, calls=%fused_computation.160 | convolution fusion | flops 805306368 | bytes 4980736 | tf_op jit(solution)/shard_map/dot_general | solution.py:80
  237.7 5.5 %convolution_convert_fusion.1 = bf16[256,2048]{1,0:T(8,128)(2,1)} fusion(bf16[768,2048]{1,0:T(8,128)(2,1)S(1)} %copy-done, bf16[256,2048]{1,0:T(8,128)(2,1)} %bitcast.175, bf16[2048,768]{1,0:T(8,128)(2,1)} %param.36, f32[256,768]{1,0:T(8,128)} %fusion.71), kind=kOutput, calls=%fused_computation.28 | convolution fusion | flops 1612316672 | bytes 9175040 | tf_op jit(solution)/shard_map/dot_general | solution.py:210
  243.2 17.9 %all_to_all.25 = bf16[8,32,2048]{2,1,0:T(8,128)(2,1)S(1)} all-to-all(bf16[8,32,2048]{2,1,0:T(8,128)(2,1)} %bitcast.176), channel_id=1, replica_groups=mesh['req'=16,'tp'=8] {'tp'}, dimensions={0} | all-to-all | bytes 2097152 | tf_op jit(solution)/shard_map/all_to_all | solution.py:87
  266.7 2.6 collective-permute-start.11
  270.0 2.4 collective-permute-done.8
  273.1 4.6 %collective-permute-done.9 = bf16[32,2048]{1,0:T(8,128)(2,1)S(1)} collective-permute-done((bf16[32,2048]{1,0:T(8,128)(2,1)S(1)}, bf16[32,2048]{1,0:T(8,128)(2,1)S(1)}, u32[]{:S(2)}, u32[]{:S(2)}) %collective-permute-start.9) | collective-permute-done | bytes 131104 | tf_op jit(solution)/shard_map/ppermute | solution.py:96
  281.0 2.8 gather_fusion.5
  283.9 2.4 broadcast_select_fusion.1
  (131 shorter events, 38.9 us)
Async XLA Ops:
  0.0 237.7 %copy-start = (bf16[768,2048]{1,0:T(8,128)(2,1)S(1)}, bf16[768,2048]{1,0:T(8,128)(2,1)}, u32[]{:S(2)}) copy-start(bf16[768,2048]{1,0:T(8,128)(2,1)} %param.37) | copy-start | bytes 9437188
  0.0 7.0 %copy-start.9 = (f32[128]{0:T(128)S(1)}, f32[128]{0:T(128)}, u32[]{:S(2)}) copy-start(f32[128]{0:T(128)} %param.31) | copy-start | bytes 1540
  7.1 10.9 %copy-start.7 = (s32[16,32]{1,0:T(8,128)S(1)}, s32[16,32]{1,0:T(8,128)}, u32[]{:S(2)}) copy-start(s32[16,32]{1,0:T(8,128)} %param.23) | copy-start | bytes 6148
  7.1 11.0 %copy-start.8 = (s32[2,512]{1,0:T(2,128)S(1)}, s32[2,512]{1,0:T(2,128)}, u32[]{:S(2)}) copy-start(s32[2,512]{1,0:T(2,128)} %param.24) | copy-start | bytes 12292
  9.3 52.0 %all-to-all-start = ((bf16[16,256,2,128]{3,1,2,0:T(8,128)(2,1)}), bf16[16,256,2,128]{3,1,2,0:T(8,128)(2,1)}, u32[]{:S(2)}, u32[]{:S(2)}) async-start(bf16[16,256,2,128]{3,1,2,0:T(8,128)(2,1)} %broadcast_in_dim.75), calls=%async_computation | async-start | bytes 4194304 | tf_op jit(solution)/shard_map/all_to_all | solution.py:175
  32.2 6.6 %copy-start.11 = (s32[16]{0:T(128)S(1)}, s32[16]{0:T(128)}, u32[]{:S(2)}) copy-start(s32[16]{0:T(128)} %param.22) | copy-start | bytes 196
  44.4 10.4 %copy-start.5 = (s32[16,256]{1,0:T(8,128)S(1)}, s32[16,256]{1,0:T(8,128)}, u32[]{:S(2)}) copy-start(s32[16,256]{1,0:T(8,128)} %param.21) | copy-start | bytes 49156
  61.4 17.8 %copy-start.1 = (pred[16,256,1024]{1,2,0:T(8,128)(4,1)S(1)}, pred[16,256,1024]{1,2,0:T(8,128)(4,1)}, u32[]{:S(2)}) copy-start(pred[16,256,1024]{1,2,0:T(8,128)(4,1)} %compare_and_fusion) | copy-start | bytes 12582916
  94.5 24.6 %all-to-all-start.2 = ((f32[16,2,1,2,256]{4,3,2,1,0:T(2,128)}), f32[16,2,1,2,256]{4,3,2,1,0:T(2,128)S(1)}, u32[]{:S(2)}, u32[]{:S(2)}) async-start(f32[16,2,1,2,256]{4,3,2,1,0:T(2,128)} %pad_maximum_fusion.1), calls=%async_computation.2 | async-start | bytes 131072 | tf_op jit(solution)/shard_map/all_to_all | solution.py:193
  119.1 6.9 %copy-start.12 = (f32[2048]{0:T(1024)S(1)}, f32[2048]{0:T(1024)}, u32[]{:S(2)}) copy-start(f32[2048]{0:T(1024)} %param.27) | copy-start | bytes 24580
  119.1 9.0 %copy-start.10 = (f32[128]{0:T(128)S(1)}, f32[128]{0:T(128)}, u32[]{:S(2)}) copy-start(f32[128]{0:T(128)} %param.32) | copy-start | bytes 1540
  119.1 58.7 %all-to-all-start.1 = ((f32[16,256,1,2,128]{1,4,3,2,0:T(8,128)}), f32[16,256,1,2,128]{1,4,3,2,0:T(8,128)}, u32[]{:S(2)}, u32[]{:S(2)}) async-start(f32[16,256,1,2,128]{1,4,3,2,0:T(8,128)} %fusion.13), calls=%async_computation.1 | async-start | bytes 8388608 | tf_op jit(solution)/shard_map/all_to_all | solution.py:192
  128.8 0.8 copy-start.4
  177.8 2.9 copy-start.3
  180.6 28.2 %copy-start.6 = (f32[2048]{0:T(1024)S(1)}, f32[2048]{0:T(1024)}, u32[]{:S(2)}) copy-start(f32[2048]{0:T(1024)} %param.34) | copy-start | bytes 24580
  182.1 24.3 %all-to-all-start.3 = ((bf16[8,32,2048]{2,1,0:T(8,128)(2,1)}), bf16[8,32,2048]{2,1,0:T(8,128)(2,1)}, u32[]{:S(2)}, u32[]{:S(2)}) async-start(bf16[8,32,2048]{2,1,0:T(8,128)(2,1)} %bitcast.171), calls=%async_computation.3 | async-start | bytes 2097152 | tf_op jit(solution)/shard_map/all_to_all | solution.py:87
  209.7 7.4 %collective-permute-start = (bf16[32,2048]{1,0:T(8,128)(2,1)S(1)}, bf16[32,2048]{1,0:T(8,128)(2,1)S(1)}, u32[]{:S(2)}, u32[]{:S(2)}) collective-permute-start(bf16[32,2048]{1,0:T(8,128)(2,1)S(1)} %get-tuple-element.13), channel_id=1, source_target_pairs={{0,1},{1,2},{2,3},{3,4},{4,5},{5,6},{6,7},{7,0},{8,9},{9,10},{10,1... | collective-permute-start | bytes 393224 | tf_op jit(solution)/shard_map/ppermute | solution.py:96
  210.8 9.2 %collective-permute-start.1 = (bf16[32,2048]{1,0:T(8,128)(2,1)S(1)}, bf16[32,2048]{1,0:T(8,128)(2,1)S(1)}, u32[]{:S(2)}, u32[]{:S(2)}) collective-permute-start(bf16[32,2048]{1,0:T(8,128)(2,1)S(1)} %get-tuple-element.13), channel_id=1, source_target_pairs={{0,2},{1,3},{2,4},{3,5},{4,6},{5,7},{6,0},{7,1},{8,10},{9,11},{10,... | collective-permute-start | bytes 393224 | tf_op jit(solution)/shard_map/ppermute | solution.py:96
  210.9 14.5 %collective-permute-start.2 = (bf16[32,2048]{1,0:T(8,128)(2,1)S(1)}, bf16[32,2048]{1,0:T(8,128)(2,1)S(1)}, u32[]{:S(2)}, u32[]{:S(2)}) collective-permute-start(bf16[32,2048]{1,0:T(8,128)(2,1)S(1)} %get-tuple-element.13), channel_id=1, source_target_pairs={{0,3},{1,4},{2,5},{3,6},{4,7},{5,0},{6,1},{7,2},{8,11},{9,12},{10,... | collective-permute-start | bytes 393224 | tf_op jit(solution)/shard_map/ppermute | solution.py:96
  213.0 13.1 %collective-permute-start.3 = (bf16[32,2048]{1,0:T(8,128)(2,1)S(1)}, bf16[32,2048]{1,0:T(8,128)(2,1)S(1)}, u32[]{:S(2)}, u32[]{:S(2)}) collective-permute-start(bf16[32,2048]{1,0:T(8,128)(2,1)S(1)} %get-tuple-element.13), channel_id=1, source_target_pairs={{0,4},{1,5},{2,6},{3,7},{4,0},{5,1},{6,2},{7,3},{8,12},{9,13},{10,... | collective-permute-start | bytes 393224 | tf_op jit(solution)/shard_map/ppermute | solution.py:96
  214.5 12.2 %collective-permute-start.4 = (bf16[32,2048]{1,0:T(8,128)(2,1)S(1)}, bf16[32,2048]{1,0:T(8,128)(2,1)S(1)}, u32[]{:S(2)}, u32[]{:S(2)}) collective-permute-start(bf16[32,2048]{1,0:T(8,128)(2,1)S(1)} %get-tuple-element.13), channel_id=1, source_target_pairs={{0,5},{1,6},{2,7},{3,0},{4,1},{5,2},{6,3},{7,4},{8,13},{9,14},{10,... | collective-permute-start | bytes 393224 | tf_op jit(solution)/shard_map/ppermute | solution.py:96
  217.1 10.3 %collective-permute-start.5 = (bf16[32,2048]{1,0:T(8,128)(2,1)S(1)}, bf16[32,2048]{1,0:T(8,128)(2,1)S(1)}, u32[]{:S(2)}, u32[]{:S(2)}) collective-permute-start(bf16[32,2048]{1,0:T(8,128)(2,1)S(1)} %get-tuple-element.13), channel_id=1, source_target_pairs={{0,6},{1,7},{2,0},{3,1},{4,2},{5,3},{6,4},{7,5},{8,14},{9,15},{10,... | collective-permute-start | bytes 393224 | tf_op jit(solution)/shard_map/ppermute | solution.py:96
  220.0 8.1 %collective-permute-start.6 = (bf16[32,2048]{1,0:T(8,128)(2,1)S(1)}, bf16[32,2048]{1,0:T(8,128)(2,1)S(1)}, u32[]{:S(2)}, u32[]{:S(2)}) collective-permute-start(bf16[32,2048]{1,0:T(8,128)(2,1)S(1)} %get-tuple-element.13), channel_id=1, source_target_pairs={{0,7},{1,0},{2,1},{3,2},{4,3},{5,4},{6,5},{7,6},{8,15},{9,8},{10,9... | collective-permute-start | bytes 393224 | tf_op jit(solution)/shard_map/ppermute | solution.py:96
  232.9 1.0 copy-start.2
  261.9 7.4 %collective-permute-start.7 = (bf16[32,2048]{1,0:T(8,128)(2,1)S(1)}, bf16[32,2048]{1,0:T(8,128)(2,1)S(1)}, u32[]{:S(2)}, u32[]{:S(2)}) collective-permute-start(bf16[32,2048]{1,0:T(8,128)(2,1)S(1)} %get-tuple-element.11), channel_id=1, source_target_pairs={{0,1},{1,2},{2,3},{3,4},{4,5},{5,6},{6,7},{7,0},{8,9},{9,10},{10,1... | collective-permute-start | bytes 393224 | tf_op jit(solution)/shard_map/ppermute | solution.py:96
  263.2 9.2 %collective-permute-start.8 = (bf16[32,2048]{1,0:T(8,128)(2,1)S(1)}, bf16[32,2048]{1,0:T(8,128)(2,1)S(1)}, u32[]{:S(2)}, u32[]{:S(2)}) collective-permute-start(bf16[32,2048]{1,0:T(8,128)(2,1)S(1)} %get-tuple-element.11), channel_id=1, source_target_pairs={{0,2},{1,3},{2,4},{3,5},{4,6},{5,7},{6,0},{7,1},{8,10},{9,11},{10,... | collective-permute-start | bytes 393224 | tf_op jit(solution)/shard_map/ppermute | solution.py:96
  263.2 14.5 %collective-permute-start.9 = (bf16[32,2048]{1,0:T(8,128)(2,1)S(1)}, bf16[32,2048]{1,0:T(8,128)(2,1)S(1)}, u32[]{:S(2)}, u32[]{:S(2)}) collective-permute-start(bf16[32,2048]{1,0:T(8,128)(2,1)S(1)} %get-tuple-element.11), channel_id=1, source_target_pairs={{0,3},{1,4},{2,5},{3,6},{4,7},{5,0},{6,1},{7,2},{8,11},{9,12},{10,... | collective-permute-start | bytes 393224 | tf_op jit(solution)/shard_map/ppermute | solution.py:96
  265.2 13.2 %collective-permute-start.10 = (bf16[32,2048]{1,0:T(8,128)(2,1)S(1)}, bf16[32,2048]{1,0:T(8,128)(2,1)S(1)}, u32[]{:S(2)}, u32[]{:S(2)}) collective-permute-start(bf16[32,2048]{1,0:T(8,128)(2,1)S(1)} %get-tuple-element.11), channel_id=1, source_target_pairs={{0,4},{1,5},{2,6},{3,7},{4,0},{5,1},{6,2},{7,3},{8,12},{9,13},{10,... | collective-permute-start | bytes 393224 | tf_op jit(solution)/shard_map/ppermute | solution.py:96
  266.7 12.3 %collective-permute-start.11 = (bf16[32,2048]{1,0:T(8,128)(2,1)S(1)}, bf16[32,2048]{1,0:T(8,128)(2,1)S(1)}, u32[]{:S(2)}, u32[]{:S(2)}) collective-permute-start(bf16[32,2048]{1,0:T(8,128)(2,1)S(1)} %get-tuple-element.11), channel_id=1, source_target_pairs={{0,5},{1,6},{2,7},{3,0},{4,1},{5,2},{6,3},{7,4},{8,13},{9,14},{10,... | collective-permute-start | bytes 393224 | tf_op jit(solution)/shard_map/ppermute | solution.py:96
  269.3 10.4 %collective-permute-start.12 = (bf16[32,2048]{1,0:T(8,128)(2,1)S(1)}, bf16[32,2048]{1,0:T(8,128)(2,1)S(1)}, u32[]{:S(2)}, u32[]{:S(2)}) collective-permute-start(bf16[32,2048]{1,0:T(8,128)(2,1)S(1)} %get-tuple-element.11), channel_id=1, source_target_pairs={{0,6},{1,7},{2,0},{3,1},{4,2},{5,3},{6,4},{7,5},{8,14},{9,15},{10,... | collective-permute-start | bytes 393224 | tf_op jit(solution)/shard_map/ppermute | solution.py:96
  272.4 8.0 %collective-permute-start.13 = (bf16[32,2048]{1,0:T(8,128)(2,1)S(1)}, bf16[32,2048]{1,0:T(8,128)(2,1)S(1)}, u32[]{:S(2)}, u32[]{:S(2)}) collective-permute-start(bf16[32,2048]{1,0:T(8,128)(2,1)S(1)} %get-tuple-element.11), channel_id=1, source_target_pairs={{0,7},{1,0},{2,1},{3,2},{4,3},{5,4},{6,5},{7,6},{8,15},{9,8},{10,9... | collective-permute-start | bytes 393224 | tf_op jit(solution)/shard_map/ppermute | solution.py:96

commit v3 on v2

--- a/solution.py
+++ b/solution.py
@@ -2,6 +2,8 @@
 import jax.numpy as jnp
 from jax import lax
 from jax.sharding import PartitionSpec as P
+from jax.experimental import pallas as pl
+from jax.experimental.pallas import tpu as pltpu
 
 STRETCH_TOKENS = 512
 MOST_STRETCHES = 32
@@ -80,6 +82,73 @@
     gate_proj = jnp.dot(rows_in, w_gate, preferred_element_type=jnp.float32)
     up_proj = jnp.dot(rows_in, w_up, preferred_element_type=jnp.float32)
     return (jax.nn.silu(gate_proj) * up_proj).astype(jnp.bfloat16)
+
+
+far_position = 1 << 30
+
+
+def held_block_kernel(slot_ref, q_ref, k0_ref, k1_ref, v0_ref, v1_ref, cos_ref, sin_ref, qpos_ref, kpos_ref, sum_ref, stat_ref):
+    query = q_ref[0]
+    query_pos = qpos_ref[0]
+    scale = (query.shape[-1]) ** (-0.5)
+
+    def scores_of(k_ref, j):
+        key = k_ref[0].astype(jnp.float32)
+        half = key.shape[-1] // 2
+        rotated = (key * cos_ref[0, j] + pltpu.roll(key, half, 1) * sin_ref[0, j]).astype(jnp.bfloat16)
+        raw = lax.dot_general(query, rotated, (((1,), (1,)), ((), ())), preferred_element_type=jnp.float32)
+        return raw * scale, kpos_ref[0, j] < query_pos
+
+    s0, l0 = scores_of(k0_ref, 0)
+    s1, l1 = scores_of(k1_ref, 1)
+    peak = jnp.maximum(
+        jnp.max(jnp.where(l0, s0, floor_score), axis=1, keepdims=True),
+        jnp.max(jnp.where(l1, s1, floor_score), axis=1, keepdims=True),
+    )
+    w0 = jnp.where(l0, jnp.exp(s0 - peak), 0.0)
+    w1 = jnp.where(l1, jnp.exp(s1 - peak), 0.0)
+    total = jnp.sum(w0, axis=1, keepdims=True) + jnp.sum(w1, axis=1, keepdims=True)
+    sum_ref[0] = jnp.dot(w0.astype(jnp.bfloat16), v0_ref[0], preferred_element_type=jnp.float32) + jnp.dot(
+        w1.astype(jnp.bfloat16), v1_ref[0], preferred_element_type=jnp.float32
+    )
+    stat_ref[0] = jnp.concatenate([peak, total], axis=1)
+
+
+def held_blocks(slots, queries, key_pool, value_pool, cos_table, sin_table, query_pos, key_pos):
+    requests, rows, head_size = queries.shape
+    stretch = key_pool.shape[1]
+
+    def pool_spec(j):
+        return pl.BlockSpec((1, stretch, head_size), lambda r, slot: (slot[2 * r + j], 0, 0))
+
+    grid_spec = pltpu.PrefetchScalarGridSpec(
+        num_scalar_prefetch=1,
+        grid=(requests,),
+        in_specs=[
+            pl.BlockSpec((1, rows, head_size), lambda r, slot: (r, 0, 0)),
+            pool_spec(0),
+            pool_spec(1),
+            pool_spec(0),
+            pool_spec(1),
+            pl.BlockSpec((1, 2, 1, head_size), lambda r, slot: (r, 0, 0, 0)),
+            pl.BlockSpec((1, 2, 1, head_size), lambda r, slot: (r, 0, 0, 0)),
+            pl.BlockSpec((1, rows, 1), lambda r, slot: (r, 0, 0)),
+            pl.BlockSpec((1, 2, 1, stretch), lambda r, slot: (r, 0, 0, 0)),
+        ],
+        out_specs=[
+            pl.BlockSpec((1, rows, head_size), lambda r, slot: (r, 0, 0)),
+            pl.BlockSpec((1, rows, 2), lambda r, slot: (r, 0, 0)),
+        ],
+    )
+    return pl.pallas_call(
+        held_block_kernel,
+        grid_spec=grid_spec,
+        out_shape=[
+            jax.ShapeDtypeStruct((requests, rows, head_size), jnp.float32),
+            jax.ShapeDtypeStruct((requests, rows, 2), jnp.float32),
+        ],
+        compiler_params=pltpu.CompilerParams(dimension_semantics=("arbitrary",)),
+    )(slots, queries, key_pool, key_pool, value_pool, value_pool, cos_table, sin_table, query_pos, key_pos)
 
 
 def reduce_rows(terms, tp_count):
@@ -163,40 +232,33 @@
     send_slot = jnp.sum(jnp.where(my_sends, slot_table[:, :, None], 0), axis=1)
     send_place = jnp.sum(jnp.where(my_sends, jnp.arange(MOST_STRETCHES)[None, :, None], 0), axis=1)
     request_count = holder_table.shape[0]
-    held_count = pair_cap * STRETCH_TOKENS
-    held_keys = cached_key_pool[send_slot].reshape(
-        request_count, pair_cap, STRETCH_TOKENS, key_heads, head_size
-    )
-    held_angle = angles(send_place * STRETCH_TOKENS, head_size)[:, :, None, None, :]
-    held_keys = rotate_halves(held_keys.astype(jnp.float32), held_angle).astype(jnp.bfloat16)
-    held_keys = held_keys.reshape(request_count, held_count, key_heads, head_size)
-    held_values = cached_value_pool[send_slot].reshape(request_count, held_count, key_heads, head_size)
+    pool_slots = cached_key_pool.shape[0]
+    slots = jnp.clip(send_slot, 0, pool_slots - 1).reshape(request_count * pair_cap).astype(jnp.int32)
+    held_angle = angles(send_place * STRETCH_TOKENS, head_size)
+    cos_table = jnp.cos(held_angle)
+    sin_table = jnp.sin(held_angle)
+    cos_table = jnp.concatenate([cos_table, cos_table], axis=-1)[:, :, None, :]
+    sin_table = jnp.concatenate([-sin_table, sin_table], axis=-1)[:, :, None, :]
     query_copies = jnp.broadcast_to(queries[None], (req_count,) + queries.shape)
     all_queries = lax.all_to_all(query_copies, "req", 0, 0, tiled=False)
-    all_queries = all_queries.reshape(request_count, req_rows, key_heads, groups, head_size)
-    key_pos = (
-        send_place[:, :, None] * STRETCH_TOKENS + jnp.arange(STRETCH_TOKENS)[None, None, :]
-    ).reshape(request_count, held_count)
-    key_ok = jnp.repeat(send_place < req_lengths[:, None], STRETCH_TOKENS, axis=1)
-    live = key_ok[:, None, :] & (key_pos[:, None, :] < recompute_pos[:, :, None])
-    scores = jnp.einsum(
-        "rmhgd,rkhd->rhgmk", all_queries, held_keys, preferred_element_type=jnp.float32
-    ) * head_size ** (-0.5)
-    live = live[:, None, None]
-    held_peak = jnp.max(jnp.where(live, scores, floor_score), axis=-1)
-    weights = jnp.where(live, jnp.exp(scores - held_peak[..., None]), 0.0)
-    held_total = jnp.sum(weights, axis=-1)
-    held_sum = jnp.einsum(
-        "rhgmk,rkhd->rmhgd", weights.astype(jnp.bfloat16), held_values, preferred_element_type=jnp.float32
+    all_queries = all_queries.reshape(request_count, req_rows * groups, head_size)
+    query_pos = jnp.repeat(recompute_pos, groups, axis=1)[:, :, None]
+    key_pos = jnp.where(
+        (send_place < req_lengths[:, None])[:, :, None],
+        send_place[:, :, None] * STRETCH_TOKENS + jnp.arange(STRETCH_TOKENS)[None, None, :],
+        far_position,
+    )[:, :, None, :]
+    held_sum, held_stats = held_blocks(
+        slots, all_queries, cached_key_pool, cached_value_pool, cos_table, sin_table, query_pos, key_pos
     )
     got_sum = lax.all_to_all(held_sum, "req", 0, 0, tiled=False)
-    got_stats = lax.all_to_all(jnp.stack([held_peak, held_total], axis=1), "req", 0, 0, tiled=False)
+    got_stats = lax.all_to_all(held_stats, "req", 0, 0, tiled=False)
     head_total = key_heads * groups
-    got_stats = got_stats.transpose(0, 1, 4, 2, 3).reshape(req_count, 2, count_of_rows, head_total)
+    got_stats = got_stats.reshape(req_count, count_of_rows, head_total, 2)
     attended = merge_stats(
         jnp.concatenate([got_sum.reshape(req_count, count_of_rows, head_total, head_size), fresh_sum[None]]),
-        jnp.concatenate([got_stats[:, 0], fresh_peak[None]]),
-        jnp.concatenate([got_stats[:, 1], fresh_total[None]]),
+        jnp.concatenate([got_stats[..., 0], fresh_peak[None]]),
+        jnp.concatenate([got_stats[..., 1], fresh_total[None]]),
     )
     tp_count = lax.axis_size("tp")
     tp_index = lax.axis_index("tp")

time: 287 us -> 261 us (0.909)
  matrix products: 54.6 us -> 18.8 us
  Pallas kernels: 0 us -> 32.7 us
  other arithmetic: 55 us -> 27.5 us
  blocking collectives: 17.9 us -> 27.9 us
  local copies, waits for them, and re-layouts: 39.1 us -> 45.3 us
  starting transfers between devices: 46.1 us -> 40 us
  waiting for transfers between devices: 73.1 us -> 67.8 us
    dot_general x2 -> x0, matrix products: 35.8 us -> none  [the longest x1 18 us: on_device(): jnp.einsum('rhgmk,rkhd->rmhgd', weights.astype(jnp.bfloat16), held_values...]
    pallas_call x0 -> x1, Pallas kernels: none -> 32.7 us  [held_blocks(): pl.pallas_call(held_block_kernel, grid_spec=grid_spec, out_shape=[jax.Sha...]
    reduce_sum x1 -> x0, other arithmetic: 14.6 us -> none  [on_device(): held_total = jnp.sum(weights, axis=-1)]
    all_to_all x1, waiting for transfers between devices: 45.1 us -> 31.9 us  [on_device(): got_sum = lax.all_to_all(held_sum, 'req', 0, 0, tiled=False)]
    another operation x3 -> x1, other arithmetic: 11.3 us -> 0.16 us
    gather x2 -> x0, local copies, waits for them, and re-layouts: 10.6 us -> none  [the longest x1 5.32 us: on_device(): cached_value_pool[send_slot]]
    all_to_all x0 -> x1, blocking collectives: none -> 9.98 us  [on_device(): got_stats = lax.all_to_all(held_stats, 'req', 0, 0, tiled=False)]
    all_to_all x1, waiting for transfers between devices: 0.01 us -> 7.85 us  [on_device(): all_queries = lax.all_to_all(query_copies, 'req', 0, 0, tiled=False)]
  transfers between devices with their start and end apart: 18 -> 17, of which waited for: 6 -> 7; matrix products, arithmetic and copies ran while one was open for 27% -> 17% of each run, Pallas kernels for 0% -> 0%
where the time goes in v3:
time: 261 us; the launch traced here: 260 us
  waiting for transfers between devices  67.8 us (26%)
  local copies, waits for them, and re-layouts  45.3 us (17%)
  starting transfers between devices  40 us (15%)
  Pallas kernels  32.7 us (13%)
  blocking collectives  27.9 us (11%)
  other arithmetic  27.5 us (11%)
  matrix products  18.8 us (7%)
    pallas_call x1, Pallas kernels, held_blocks(): pl.pallas_call(held_block_kernel, grid_spec=grid_spec, out_shape=[jax.Sha...  32.7 us
    all_to_all x1, waiting for transfers between devices, on_device(): got_sum = lax.all_to_all(held_sum, 'req', 0, 0, tiled=False)  31.9 us
    all_to_all x1, blocking collectives, reduce_rows(): got = lax.all_to_all(blocks, 'tp', 0, 0, tiled=False)  17.9 us
    ppermute x14, starting transfers between devices, gather_rows(): parts.append(lax.ppermute(rows, 'tp', pairs))  14.8 us
    all_to_all x1, waiting for transfers between devices, reduce_rows(): got = lax.all_to_all(blocks, 'tp', 0, 0, tiled=False)  14.1 us
    ppermute x14, waiting for transfers between devices, gather_rows(): parts.append(lax.ppermute(rows, 'tp', pairs))  14 us
    all_to_all x1, starting transfers between devices, reduce_rows(): got = lax.all_to_all(blocks, 'tp', 0, 0, tiled=False)  11.8 us
    unnamed x49, local copies, waits for them, and re-layouts  10.4 us
  transfers between devices with their start and end apart: 17, of which 7 were waited for; matrix products, arithmetic and copies ran while one was open for 17% of the time, Pallas kernels for 0%

profile of v3, /device:TPU:1, one launch (start us, length us, event | category | flops | bytes accessed | tf_op | source)
XLA Modules:
  0.0 260.5 jit_solution(4655085508296780431)
XLA Ops:
  3.0 2.9 %multiply_reduce_fusion = (f32[256,2]{0,1:T(2,128)S(1)}, f32[256,256]{0,1:T(8,128)}) fusion(bf16[2048,256]{1,0:T(8,128)(2,1)} %param.28, bf16[256,2048]{1,0:T(8,128)(2,1)} %param.20, f32[2048]{0:T(1024)} %param.27, f32[256]{0:T(256)S(1)} %add_rsqrt_fusion.2), kind=kOutput, calls=%fused_computation.46 | convolution fusion | flops 270663168 | bytes 2370560 | tf_op jit(solution)/shard_map/dot_general | solution.py:204
  8.2 3.0 %broadcast_in_dim.70 = bf16[16,256,2,128]{3,2,1,0:T(2,128)(2,1)} broadcast(bf16[256,2,128]{2,1,0:T(2,128)(2,1)S(1)} %copy.140), dimensions={1,2,3} | broadcast | bytes 2228224 | tf_op jit(solution)/shard_map/broadcast_in_dim | solution.py:242
  11.1 8.6 %all-to-all-start = ((bf16[16,256,2,128]{3,2,1,0:T(2,128)(2,1)}), bf16[16,256,2,128]{3,2,1,0:T(2,128)(2,1)}, u32[]{:S(2)}, u32[]{:S(2)}) async-start(bf16[16,256,2,128]{3,2,1,0:T(2,128)(2,1)} %broadcast_in_dim.70), calls=%async_computation | async-start | bytes 4194304 | tf_op jit(solution)/shard_map/all_to_all | solution.py:243
  20.7 3.5 %gather_fusion = s32[512]{0:T(512)S(1)} fusion(s32[512]{0:T(512)S(1)} %bitcast.109, s32[1024]{0:T(1024)S(1)} %pad_clamp_fusion.1), kind=kCustom, calls=%fused_computation.2 | custom fusion | bytes 6144 | tf_op jit(solution)/shard_map/gather | solution.py:224
  25.2 3.5 %gather_fusion.1 = s32[512]{0:T(512)S(1)} fusion(s32[512]{0:T(512)S(1)} %bitcast.108, s32[1024]{0:T(1024)S(1)} %pad_clamp_fusion.1), kind=kCustom, calls=%fused_computation.3 | custom fusion | bytes 6144 | tf_op jit(solution)/shard_map/gather | solution.py:225
  31.5 4.9 %copy.146.qpos_ref = s32[16,512,1]{2,1,0:T(8,128)} copy(s32[16,512,1]{0,1,2:T(8,128)S(1)} %bitcast.114) | data formatting | bytes 65536 | tf_op jit(solution)/shard_map/broadcast_in_dim;reshape | solution.py:245
  40.2 7.8 %all-to-all-done = bf16[16,256,2,128]{3,2,1,0:T(2,128)(2,1)} async-done(((bf16[16,256,2,128]{3,2,1,0:T(2,128)(2,1)}), bf16[16,256,2,128]{3,2,1,0:T(2,128)(2,1)}, u32[]{:S(2)}, u32[]{:S(2)}) %all-to-all-start) | async-done | bytes 2097184 | tf_op jit(solution)/shard_map/all_to_all | solution.py:243
  48.0 32.7 %shard_map.172 = (f32[16,512,128]{2,1,0:T(8,128)}, f32[16,512,2]{2,1,0:T(8,128)}) custom-call(s32[32]{0:T(128)} %min.12.slot_ref, bf16[16,512,128]{2,1,0:T(8,128)(2,1)} %bitcast.4.q_ref, bf16[32,512,128]{2,1,0:T(8,128)(2,1)} %k1_ref.1, bf16[32,512,128]{2,1,0:T(8,128)(2,1)} %k1_ref.1, bf16[32,512,128]{2,1,0:T(8,128)(2,1)} %v1_ref.1, ...), custom_call_target="tpu_custom_call" | custom-call | tf_op jit(solution)/shard_map/pallas_call | solution.py:143
  80.7 2.8 %copy.151 = f32[16,512,2]{1,2,0:T(2,128)S(1)} copy(f32[16,512,2]{2,1,0:T(8,128)} %get-tuple-element.10) | data formatting | bytes 131072 | tf_op jit(solution)/shard_map/pallas_call | solution.py:143
  83.6 10.0 %all_to_all.25 = f32[16,512,2]{1,2,0:T(2,128)S(1)} all-to-all(f32[16,512,2]{1,2,0:T(2,128)S(1)} %copy.151), channel_id=1, replica_groups=mesh['req'=16,'tp'=8] {'req'}, dimensions={0} | all-to-all | bytes 131072 | tf_op jit(solution)/shard_map/all_to_all | solution.py:255
  93.6 4.7 %all-to-all-start.1 = ((f32[16,512,128]{2,1,0:T(8,128)}), f32[16,512,128]{2,1,0:T(8,128)}, u32[]{:S(2)}, u32[]{:S(2)}) async-start(f32[16,512,128]{2,1,0:T(8,128)} %get-tuple-element.9), calls=%async_computation.1 | async-start | bytes 8388608 | tf_op jit(solution)/shard_map/all_to_all | solution.py:254
  102.6 2.2 convolution_bitcast_fusion
  107.8 2.0 slice_bitcast_fusion.1
  111.1 2.1 copy.155
  113.4 31.9 %all-to-all-done.1 = f32[16,512,128]{2,1,0:T(8,128)} async-done(((f32[16,512,128]{2,1,0:T(8,128)}), f32[16,512,128]{2,1,0:T(8,128)}, u32[]{:S(2)}, u32[]{:S(2)}) %all-to-all-start.1) | async-done | bytes 4194336 | tf_op jit(solution)/shard_map/all_to_all | solution.py:254
  145.2 6.8 %fusion = f32[256,2,128]{2,1,0:T(2,128)S(1)} fusion(f32[1,256,2,128]{3,2,1,0:T(2,128)} %copy.150, f32[16,256,2,128]{3,2,1,0:T(2,128)} %bitcast.9, f32[17,256,2]{2,1,0:T(8,128)} %copy.155), kind=kLoop, calls=%fused_computation.5 | loop fusion | flops 3276800 | bytes 4753408 | tf_op jit(solution)/shard_map/reduce_sum | solution.py:75
  153.8 11.8 %all-to-all-start.3 = ((bf16[8,32,2048]{2,1,0:T(8,128)(2,1)}), bf16[8,32,2048]{2,1,0:T(8,128)(2,1)}, u32[]{:S(2)}, u32[]{:S(2)}) async-start(bf16[8,32,2048]{2,1,0:T(8,128)(2,1)} %bitcast.110), calls=%async_computation.3 | async-start | bytes 2097152 | tf_op jit(solution)/shard_map/all_to_all | solution.py:156
  166.7 14.1 %all-to-all-done.3 = bf16[8,32,2048]{2,1,0:T(8,128)(2,1)} async-done(((bf16[8,32,2048]{2,1,0:T(8,128)(2,1)}), bf16[8,32,2048]{2,1,0:T(8,128)(2,1)}, u32[]{:S(2)}, u32[]{:S(2)}) %all-to-all-start.3) | async-done | bytes 1048608 | tf_op jit(solution)/shard_map/all_to_all | solution.py:156
  185.2 2.1 collective-permute-start.2
  188.8 2.6 %collective-permute-start.4 = (bf16[32,2048]{1,0:T(8,128)(2,1)S(1)}, bf16[32,2048]{1,0:T(8,128)(2,1)S(1)}, u32[]{:S(2)}, u32[]{:S(2)}) collective-permute-start(bf16[32,2048]{1,0:T(8,128)(2,1)S(1)} %get-tuple-element.17), channel_id=1, source_target_pairs={{0,5},{1,6},{2,7},{3,0},{4,1},{5,2},{6,3},{7,4},{8,13},{9,14},{10,... | collective-permute-start | bytes 393224 | tf_op jit(solution)/shard_map/ppermute | solution.py:165
  192.1 2.2 collective-permute-done.1
  195.0 4.7 %collective-permute-done.2 = bf16[32,2048]{1,0:T(8,128)(2,1)S(1)} collective-permute-done((bf16[32,2048]{1,0:T(8,128)(2,1)S(1)}, bf16[32,2048]{1,0:T(8,128)(2,1)S(1)}, u32[]{:S(2)}, u32[]{:S(2)}) %collective-permute-start.2) | collective-permute-done | bytes 131104 | tf_op jit(solution)/shard_map/ppermute | solution.py:165
  203.0 2.8 %gather_fusion.2 = bf16[8,32,2048]{2,1,0:T(8,128)(2,1)} fusion(bf16[8,32,2048]{2,1,0:T(8,128)(2,1)} %bitcast_dynamic-update-slice_fusion.8, s32[1024]{0:T(1024)S(1)} %pad_clamp_fusion), kind=kCustom, calls=%fused_computation.clone | custom fusion | bytes 2097184 | tf_op jit(solution)/shard_map/jit(_take)/gather | solution.py:168
  208.2 3.8 %fusion.56 = f32[256,768]{1,0:T(8,128)} fusion(bf16[256,2048]{1,0:T(8,128)(2,1)S(1)} %bitcast.112, bf16[2048,768]{1,0:T(8,128)(2,1)} %param.35), kind=kOutput, calls=%fused_computation.139 | convolution fusion | flops 805306368 | bytes 4980736 | tf_op jit(solution)/shard_map/dot_general | solution.py:82
  212.0 5.5 %convolution_convert_fusion.1 = bf16[256,2048]{1,0:T(8,128)(2,1)} fusion(bf16[768,2048]{1,0:T(8,128)(2,1)S(1)} %copy-done, bf16[256,2048]{1,0:T(8,128)(2,1)} %bitcast.113, bf16[2048,768]{1,0:T(8,128)(2,1)} %param.36, f32[256,768]{1,0:T(8,128)} %fusion.56), kind=kOutput, calls=%fused_computation.9 | convolution fusion | flops 1612316672 | bytes 9175040 | tf_op jit(solution)/shard_map/dot_general | solution.py:272
  217.5 17.9 %all_to_all.26 = bf16[8,32,2048]{2,1,0:T(8,128)(2,1)S(1)} all-to-all(bf16[8,32,2048]{2,1,0:T(8,128)(2,1)} %bitcast.115), channel_id=1, replica_groups=mesh['req'=16,'tp'=8] {'tp'}, dimensions={0} | all-to-all | bytes 2097152 | tf_op jit(solution)/shard_map/all_to_all | solution.py:156
  237.5 2.0 collective-permute-start.9
  241.0 2.6 %collective-permute-start.11 = (bf16[32,2048]{1,0:T(8,128)(2,1)S(1)}, bf16[32,2048]{1,0:T(8,128)(2,1)S(1)}, u32[]{:S(2)}, u32[]{:S(2)}) collective-permute-start(bf16[32,2048]{1,0:T(8,128)(2,1)S(1)} %get-tuple-element.15), channel_id=1, source_target_pairs={{0,5},{1,6},{2,7},{3,0},{4,1},{5,2},{6,3},{7,4},{8,13},{9,14},{10,... | collective-permute-start | bytes 393224 | tf_op jit(solution)/shard_map/ppermute | solution.py:165
  244.3 2.4 collective-permute-done.8
  247.3 4.6 %collective-permute-done.9 = bf16[32,2048]{1,0:T(8,128)(2,1)S(1)} collective-permute-done((bf16[32,2048]{1,0:T(8,128)(2,1)S(1)}, bf16[32,2048]{1,0:T(8,128)(2,1)S(1)}, u32[]{:S(2)}, u32[]{:S(2)}) %collective-permute-start.9) | collective-permute-done | bytes 131104 | tf_op jit(solution)/shard_map/ppermute | solution.py:165
  255.3 2.8 %gather_fusion.3 = bf16[8,32,2048]{2,1,0:T(8,128)(2,1)} fusion(bf16[8,32,2048]{2,1,0:T(8,128)(2,1)} %bitcast_dynamic-update-slice_fusion, s32[1024]{0:T(1024)S(1)} %pad_clamp_fusion), kind=kCustom, calls=%fused_computation.1.clone | custom fusion | bytes 2097184 | tf_op jit(solution)/shard_map/jit(_take)/gather | solution.py:168
  258.1 2.4 broadcast_select_fusion.1
  (137 shorter events, 46.3 us)
Async XLA Ops:
  0.0 212.0 %copy-start = (bf16[768,2048]{1,0:T(8,128)(2,1)S(1)}, bf16[768,2048]{1,0:T(8,128)(2,1)}, u32[]{:S(2)}) copy-start(bf16[768,2048]{1,0:T(8,128)(2,1)} %param.37) | copy-start | bytes 9437188
  0.0 7.6 %copy-start.15 = (f32[128]{0:T(128)S(1)}, f32[128]{0:T(128)}, u32[]{:S(2)}) copy-start(f32[128]{0:T(128)} %param.31) | copy-start | bytes 1540
  0.0 7.9 %copy-start.10 = (f32[64]{0:T(128)}, f32[64]{0:T(128)S(1)}, u32[]{:S(2)}) copy-start(f32[64]{0:T(128)S(1)} %multiply_power_fusion) | copy-start | bytes 772
  1.5 6.4 %copy-start.6 = (f32[256]{0:T(256)}, f32[256]{0:T(256)S(1)}, u32[]{:S(2)}) copy-start(f32[256]{0:T(256)S(1)} %convert_element_type.83) | copy-start | bytes 3076
  8.1 11.6 %copy-start.9 = (s32[16,32]{1,0:T(8,128)S(1)}, s32[16,32]{1,0:T(8,128)}, u32[]{:S(2)}) copy-start(s32[16,32]{1,0:T(8,128)} %param.23) | copy-start | bytes 6148
  8.2 11.7 %copy-start.3 = (s32[16,256]{1,0:T(8,128)S(1)}, s32[16,256]{1,0:T(8,128)}, u32[]{:S(2)}) copy-start(s32[16,256]{1,0:T(8,128)} %param.21) | copy-start | bytes 49156
  8.2 12.5 %copy-start.12 = (s32[2,512]{1,0:T(2,128)S(1)}, s32[2,512]{1,0:T(2,128)}, u32[]{:S(2)}) copy-start(s32[2,512]{1,0:T(2,128)} %param.24) | copy-start | bytes 12292
  11.1 36.9 %all-to-all-start = ((bf16[16,256,2,128]{3,2,1,0:T(2,128)(2,1)}), bf16[16,256,2,128]{3,2,1,0:T(2,128)(2,1)}, u32[]{:S(2)}, u32[]{:S(2)}) async-start(bf16[16,256,2,128]{3,2,1,0:T(2,128)(2,1)} %broadcast_in_dim.70), calls=%async_computation | async-start | bytes 4194304 | tf_op jit(solution)/shard_map/all_to_all | solution.py:243
  25.2 3.9 %copy-start.16 = (s32[16]{0:T(128)S(1)}, s32[16]{0:T(128)}, u32[]{:S(2)}) copy-start(s32[16]{0:T(128)} %param.22) | copy-start | bytes 196
  93.5 4.8 %copy-start.14 = (f32[256]{0:T(256)S(1)}, f32[256]{0:T(256)}, u32[]{:S(2)}) copy-start(f32[256]{0:T(256)} %copy-done.13) | copy-start | bytes 3076
  93.5 4.8 %copy-start.17 = (f32[2048]{0:T(1024)S(1)}, f32[2048]{0:T(1024)}, u32[]{:S(2)}) copy-start(f32[2048]{0:T(1024)} %param.27) | copy-start | bytes 24580
  93.5 6.7 %copy-start.5 = (s32[1,256]{1,0:T(1,128)S(1)}, s32[1,256]{1,0:T(1,128)}, u32[]{:S(2)}) copy-start(s32[1,256]{1,0:T(1,128)} %copy-done.4) | copy-start | bytes 3076
  93.5 7.6 %copy-start.7 = (f32[256]{0:T(256)S(1)}, f32[256]{0:T(256)}, u32[]{:S(2)}) copy-start(f32[256]{0:T(256)} %copy-done.6) | copy-start | bytes 3076
  93.6 7.7 %copy-start.11 = (f32[64]{0:T(128)S(1)}, f32[64]{0:T(128)}, u32[]{:S(2)}) copy-start(f32[64]{0:T(128)} %copy-done.10) | copy-start | bytes 772
  93.6 51.7 %all-to-all-start.1 = ((f32[16,512,128]{2,1,0:T(8,128)}), f32[16,512,128]{2,1,0:T(8,128)}, u32[]{:S(2)}, u32[]{:S(2)}) async-start(f32[16,512,128]{2,1,0:T(8,128)} %get-tuple-element.9), calls=%async_computation.1 | async-start | bytes 8388608 | tf_op jit(solution)/shard_map/all_to_all | solution.py:254
  145.2 7.2 %copy-start.2 = (bf16[256,2048]{1,0:T(8,128)(2,1)S(1)}, bf16[256,2048]{1,0:T(8,128)(2,1)}, u32[]{:S(2)}) copy-start(bf16[256,2048]{1,0:T(8,128)(2,1)} %param.33) | copy-start | bytes 3145732
  152.4 30.8 %copy-start.8 = (f32[2048]{0:T(1024)S(1)}, f32[2048]{0:T(1024)}, u32[]{:S(2)}) copy-start(f32[2048]{0:T(1024)} %param.34) | copy-start | bytes 24580
  153.8 26.9 %all-to-all-start.3 = ((bf16[8,32,2048]{2,1,0:T(8,128)(2,1)}), bf16[8,32,2048]{2,1,0:T(8,128)(2,1)}, u32[]{:S(2)}, u32[]{:S(2)}) async-start(bf16[8,32,2048]{2,1,0:T(8,128)(2,1)} %bitcast.110), calls=%async_computation.3 | async-start | bytes 2097152 | tf_op jit(solution)/shard_map/all_to_all | solution.py:156
  184.0 7.4 %collective-permute-start = (bf16[32,2048]{1,0:T(8,128)(2,1)S(1)}, bf16[32,2048]{1,0:T(8,128)(2,1)S(1)}, u32[]{:S(2)}, u32[]{:S(2)}) collective-permute-start(bf16[32,2048]{1,0:T(8,128)(2,1)S(1)} %get-tuple-element.17), channel_id=1, source_target_pairs={{0,1},{1,2},{2,3},{3,4},{4,5},{5,6},{6,7},{7,0},{8,9},{9,10},{10,1... | collective-permute-start | bytes 393224 | tf_op jit(solution)/shard_map/ppermute | solution.py:165
  185.1 9.2 %collective-permute-start.1 = (bf16[32,2048]{1,0:T(8,128)(2,1)S(1)}, bf16[32,2048]{1,0:T(8,128)(2,1)S(1)}, u32[]{:S(2)}, u32[]{:S(2)}) collective-permute-start(bf16[32,2048]{1,0:T(8,128)(2,1)S(1)} %get-tuple-element.17), channel_id=1, source_target_pairs={{0,2},{1,3},{2,4},{3,5},{4,6},{5,7},{6,0},{7,1},{8,10},{9,11},{10,... | collective-permute-start | bytes 393224 | tf_op jit(solution)/shard_map/ppermute | solution.py:165
  185.2 14.5 %collective-permute-start.2 = (bf16[32,2048]{1,0:T(8,128)(2,1)S(1)}, bf16[32,2048]{1,0:T(8,128)(2,1)S(1)}, u32[]{:S(2)}, u32[]{:S(2)}) collective-permute-start(bf16[32,2048]{1,0:T(8,128)(2,1)S(1)} %get-tuple-element.17), channel_id=1, source_target_pairs={{0,3},{1,4},{2,5},{3,6},{4,7},{5,0},{6,1},{7,2},{8,11},{9,12},{10,... | collective-permute-start | bytes 393224 | tf_op jit(solution)/shard_map/ppermute | solution.py:165
  187.3 13.1 %collective-permute-start.3 = (bf16[32,2048]{1,0:T(8,128)(2,1)S(1)}, bf16[32,2048]{1,0:T(8,128)(2,1)S(1)}, u32[]{:S(2)}, u32[]{:S(2)}) collective-permute-start(bf16[32,2048]{1,0:T(8,128)(2,1)S(1)} %get-tuple-element.17), channel_id=1, source_target_pairs={{0,4},{1,5},{2,6},{3,7},{4,0},{5,1},{6,2},{7,3},{8,12},{9,13},{10,... | collective-permute-start | bytes 393224 | tf_op jit(solution)/shard_map/ppermute | solution.py:165
  188.8 12.2 %collective-permute-start.4 = (bf16[32,2048]{1,0:T(8,128)(2,1)S(1)}, bf16[32,2048]{1,0:T(8,128)(2,1)S(1)}, u32[]{:S(2)}, u32[]{:S(2)}) collective-permute-start(bf16[32,2048]{1,0:T(8,128)(2,1)S(1)} %get-tuple-element.17), channel_id=1, source_target_pairs={{0,5},{1,6},{2,7},{3,0},{4,1},{5,2},{6,3},{7,4},{8,13},{9,14},{10,... | collective-permute-start | bytes 393224 | tf_op jit(solution)/shard_map/ppermute | solution.py:165
  191.4 10.3 %collective-permute-start.5 = (bf16[32,2048]{1,0:T(8,128)(2,1)S(1)}, bf16[32,2048]{1,0:T(8,128)(2,1)S(1)}, u32[]{:S(2)}, u32[]{:S(2)}) collective-permute-start(bf16[32,2048]{1,0:T(8,128)(2,1)S(1)} %get-tuple-element.17), channel_id=1, source_target_pairs={{0,6},{1,7},{2,0},{3,1},{4,2},{5,3},{6,4},{7,5},{8,14},{9,15},{10,... | collective-permute-start | bytes 393224 | tf_op jit(solution)/shard_map/ppermute | solution.py:165
  194.3 8.1 %collective-permute-start.6 = (bf16[32,2048]{1,0:T(8,128)(2,1)S(1)}, bf16[32,2048]{1,0:T(8,128)(2,1)S(1)}, u32[]{:S(2)}, u32[]{:S(2)}) collective-permute-start(bf16[32,2048]{1,0:T(8,128)(2,1)S(1)} %get-tuple-element.17), channel_id=1, source_target_pairs={{0,7},{1,0},{2,1},{3,2},{4,3},{5,4},{6,5},{7,6},{8,15},{9,8},{10,9... | collective-permute-start | bytes 393224 | tf_op jit(solution)/shard_map/ppermute | solution.py:165
  236.2 7.4 %collective-permute-start.7 = (bf16[32,2048]{1,0:T(8,128)(2,1)S(1)}, bf16[32,2048]{1,0:T(8,128)(2,1)S(1)}, u32[]{:S(2)}, u32[]{:S(2)}) collective-permute-start(bf16[32,2048]{1,0:T(8,128)(2,1)S(1)} %get-tuple-element.15), channel_id=1, source_target_pairs={{0,1},{1,2},{2,3},{3,4},{4,5},{5,6},{6,7},{7,0},{8,9},{9,10},{10,1... | collective-permute-start | bytes 393224 | tf_op jit(solution)/shard_map/ppermute | solution.py:165
  237.5 9.2 %collective-permute-start.8 = (bf16[32,2048]{1,0:T(8,128)(2,1)S(1)}, bf16[32,2048]{1,0:T(8,128)(2,1)S(1)}, u32[]{:S(2)}, u32[]{:S(2)}) collective-permute-start(bf16[32,2048]{1,0:T(8,128)(2,1)S(1)} %get-tuple-element.15), channel_id=1, source_target_pairs={{0,2},{1,3},{2,4},{3,5},{4,6},{5,7},{6,0},{7,1},{8,10},{9,11},{10,... | collective-permute-start | bytes 393224 | tf_op jit(solution)/shard_map/ppermute | solution.py:165
  237.5 14.5 %collective-permute-start.9 = (bf16[32,2048]{1,0:T(8,128)(2,1)S(1)}, bf16[32,2048]{1,0:T(8,128)(2,1)S(1)}, u32[]{:S(2)}, u32[]{:S(2)}) collective-permute-start(bf16[32,2048]{1,0:T(8,128)(2,1)S(1)} %get-tuple-element.15), channel_id=1, source_target_pairs={{0,3},{1,4},{2,5},{3,6},{4,7},{5,0},{6,1},{7,2},{8,11},{9,12},{10,... | collective-permute-start | bytes 393224 | tf_op jit(solution)/shard_map/ppermute | solution.py:165
  239.5 13.2 %collective-permute-start.10 = (bf16[32,2048]{1,0:T(8,128)(2,1)S(1)}, bf16[32,2048]{1,0:T(8,128)(2,1)S(1)}, u32[]{:S(2)}, u32[]{:S(2)}) collective-permute-start(bf16[32,2048]{1,0:T(8,128)(2,1)S(1)} %get-tuple-element.15), channel_id=1, source_target_pairs={{0,4},{1,5},{2,6},{3,7},{4,0},{5,1},{6,2},{7,3},{8,12},{9,13},{10,... | collective-permute-start | bytes 393224 | tf_op jit(solution)/shard_map/ppermute | solution.py:165
  241.0 12.3 %collective-permute-start.11 = (bf16[32,2048]{1,0:T(8,128)(2,1)S(1)}, bf16[32,2048]{1,0:T(8,128)(2,1)S(1)}, u32[]{:S(2)}, u32[]{:S(2)}) collective-permute-start(bf16[32,2048]{1,0:T(8,128)(2,1)S(1)} %get-tuple-element.15), channel_id=1, source_target_pairs={{0,5},{1,6},{2,7},{3,0},{4,1},{5,2},{6,3},{7,4},{8,13},{9,14},{10,... | collective-permute-start | bytes 393224 | tf_op jit(solution)/shard_map/ppermute | solution.py:165
  243.6 10.4 %collective-permute-start.12 = (bf16[32,2048]{1,0:T(8,128)(2,1)S(1)}, bf16[32,2048]{1,0:T(8,128)(2,1)S(1)}, u32[]{:S(2)}, u32[]{:S(2)}) collective-permute-start(bf16[32,2048]{1,0:T(8,128)(2,1)S(1)} %get-tuple-element.15), channel_id=1, source_target_pairs={{0,6},{1,7},{2,0},{3,1},{4,2},{5,3},{6,4},{7,5},{8,14},{9,15},{10,... | collective-permute-start | bytes 393224 | tf_op jit(solution)/shard_map/ppermute | solution.py:165
  246.7 8.0 %collective-permute-start.13 = (bf16[32,2048]{1,0:T(8,128)(2,1)S(1)}, bf16[32,2048]{1,0:T(8,128)(2,1)S(1)}, u32[]{:S(2)}, u32[]{:S(2)}) collective-permute-start(bf16[32,2048]{1,0:T(8,128)(2,1)S(1)} %get-tuple-element.15), channel_id=1, source_target_pairs={{0,7},{1,0},{2,1},{3,2},{4,3},{5,4},{6,5},{7,6},{8,15},{9,8},{10,9... | collective-permute-start | bytes 393224 | tf_op jit(solution)/shard_map/ppermute | solution.py:165
  (3 other events, 4.5 us)

commit v4 on v3

--- a/solution.py
+++ b/solution.py
@@ -87,57 +87,76 @@
 far_position = 1 << 30
 
 
-def held_block_kernel(slot_ref, q_ref, k0_ref, k1_ref, v0_ref, v1_ref, cos_ref, sin_ref, qpos_ref, kpos_ref, sum_ref, stat_ref):
-    query = q_ref[0]
-    query_pos = qpos_ref[0]
-    scale = (query.shape[-1]) ** (-0.5)
-
-    def scores_of(k_ref, j):
-        key = k_ref[0].astype(jnp.float32)
-        half = key.shape[-1] // 2
-        rotated = (key * cos_ref[0, j] + pltpu.roll(key, half, 1) * sin_ref[0, j]).astype(jnp.bfloat16)
-        raw = lax.dot_general(query, rotated, (((1,), (1,)), ((), ())), preferred_element_type=jnp.float32)
-        return raw * scale, kpos_ref[0, j] < query_pos
-
-    s0, l0 = scores_of(k0_ref, 0)
-    s1, l1 = scores_of(k1_ref, 1)
-    peak = jnp.maximum(
-        jnp.max(jnp.where(l0, s0, floor_score), axis=1, keepdims=True),
-        jnp.max(jnp.where(l1, s1, floor_score), axis=1, keepdims=True),
-    )
-    w0 = jnp.where(l0, jnp.exp(s0 - peak), 0.0)
-    w1 = jnp.where(l1, jnp.exp(s1 - peak), 0.0)
-    total = jnp.sum(w0, axis=1, keepdims=True) + jnp.sum(w1, axis=1, keepdims=True)
-    sum_ref[0] = jnp.dot(w0.astype(jnp.bfloat16), v0_ref[0], preferred_element_type=jnp.float32) + jnp.dot(
-        w1.astype(jnp.bfloat16), v1_ref[0], preferred_element_type=jnp.float32
-    )
-    stat_ref[0] = jnp.concatenate([peak, total], axis=1)
-
-
-def held_blocks(slots, queries, key_pool, value_pool, cos_table, sin_table, query_pos, key_pos):
+def held_block_kernel(slot_ref, alive_ref, q_ref, k0_ref, k1_ref, v0_ref, v1_ref, cos_ref, sin_ref, qpos_ref, kpos_ref, sum_ref, stat_ref):
+    step = pl.program_id(0)
+    key_refs = (k0_ref, k1_ref)
+    value_refs = (v0_ref, v1_ref)
+
+    def run(parts):
+        query = q_ref[0]
+        query_pos = qpos_ref[0]
+        scale = (query.shape[-1]) ** (-0.5)
+        masked = []
+        for j in parts:
+            key = key_refs[j][0].astype(jnp.float32)
+            half = key.shape[-1] // 2
+            rotated = (key * cos_ref[0, j] + pltpu.roll(key, half, 1) * sin_ref[0, j]).astype(jnp.bfloat16)
+            raw = lax.dot_general(query, rotated, (((1,), (1,)), ((), ())), preferred_element_type=jnp.float32)
+            masked.append(jnp.where(kpos_ref[0, j] < query_pos, raw * scale, floor_score))
+        peak = jnp.max(masked[0], axis=1, keepdims=True)
+        for extra in masked[1:]:
+            peak = jnp.maximum(peak, jnp.max(extra, axis=1, keepdims=True))
+        safe_peak = jnp.where(peak == floor_score, 0.0, peak)
+        total = None
+        weighted = None
+        for j, block in zip(parts, masked):
+            w = jnp.exp(block - safe_peak)
+            part_total = jnp.sum(w, axis=1, keepdims=True)
+            part_sum = jnp.dot(w.astype(jnp.bfloat16), value_refs[j][0], preferred_element_type=jnp.float32)
+            total = part_total if total is None else total + part_total
+            weighted = part_sum if weighted is None else weighted + part_sum
+        sum_ref[0] = weighted
+        stat_ref[0] = jnp.concatenate([peak, total], axis=1)
+
+    live0 = alive_ref[2 * step] > 0
+    live1 = alive_ref[2 * step + 1] > 0
+    pl.when(live0 & live1)(lambda: run((0, 1)))
+    pl.when(live0 & jnp.logical_not(live1))(lambda: run((0,)))
+    pl.when(jnp.logical_not(live0) & live1)(lambda: run((1,)))
+
+    @pl.when(jnp.logical_not(live0) & jnp.logical_not(live1))
+    def _():
+        sum_ref[0] = jnp.zeros(sum_ref.shape[1:], jnp.float32)
+        rows = stat_ref.shape[1]
+        stat_ref[0] = jnp.concatenate(
+            [jnp.full((rows, 1), floor_score, jnp.float32), jnp.zeros((rows, 1), jnp.float32)], axis=1
+        )
+
+
+def held_blocks(slots, alive, queries, key_pool, value_pool, cos_table, sin_table, query_pos, key_pos):
     requests, rows, head_size = queries.shape
     stretch = key_pool.shape[1]
 
     def pool_spec(j):
-        return pl.BlockSpec((1, stretch, head_size), lambda r, slot: (slot[2 * r + j], 0, 0))
+        return pl.BlockSpec((1, stretch, head_size), lambda r, slot, alive: (slot[2 * r + j], 0, 0))
 
     grid_spec = pltpu.PrefetchScalarGridSpec(
-        num_scalar_prefetch=1,
+        num_scalar_prefetch=2,
         grid=(requests,),
         in_specs=[
-            pl.BlockSpec((1, rows, head_size), lambda r, slot: (r, 0, 0)),
+            pl.BlockSpec((1, rows, head_size), lambda r, slot, alive: (r, 0, 0)),
             pool_spec(0),
             pool_spec(1),
             pool_spec(0),
             pool_spec(1),
-            pl.BlockSpec((1, 2, 1, head_size), lambda r, slot: (r, 0, 0, 0)),
-            pl.BlockSpec((1, 2, 1, head_size), lambda r, slot: (r, 0, 0, 0)),
-            pl.BlockSpec((1, rows, 1), lambda r, slot: (r, 0, 0)),
-            pl.BlockSpec((1, 2, 1, stretch), lambda r, slot: (r, 0, 0, 0)),
+            pl.BlockSpec((1, 2, 1, head_size), lambda r, slot, alive: (r, 0, 0, 0)),
+            pl.BlockSpec((1, 2, 1, head_size), lambda r, slot, alive: (r, 0, 0, 0)),
+            pl.BlockSpec((1, rows, 1), lambda r, slot, alive: (r, 0, 0)),
+            pl.BlockSpec((1, 2, 1, stretch), lambda r, slot, alive: (r, 0, 0, 0)),
         ],
         out_specs=[
-            pl.BlockSpec((1, rows, head_size), lambda r, slot: (r, 0, 0)),
-            pl.BlockSpec((1, rows, 2), lambda r, slot: (r, 0, 0)),
+            pl.BlockSpec((1, rows, head_size), lambda r, slot, alive: (r, 0, 0)),
+            pl.BlockSpec((1, rows, 2), lambda r, slot, alive: (r, 0, 0)),
         ],
     )
     return pl.pallas_call(
@@ -148,7 +167,7 @@
             jax.ShapeDtypeStruct((requests, rows, 2), jnp.float32),
         ],
         compiler_params=pltpu.CompilerParams(dimension_semantics=("arbitrary",)),
-    )(slots, queries, key_pool, key_pool, value_pool, value_pool, cos_table, sin_table, query_pos, key_pos)
+    )(slots, alive, queries, key_pool, key_pool, value_pool, value_pool, cos_table, sin_table, query_pos, key_pos)
 
 
 def reduce_rows(terms, tp_count):
@@ -248,13 +267,18 @@
         send_place[:, :, None] * STRETCH_TOKENS + jnp.arange(STRETCH_TOKENS)[None, None, :],
         far_position,
     )[:, :, None, :]
+    alive = (send_place < req_lengths[:, None]).reshape(request_count * pair_cap).astype(jnp.int32)
     held_sum, held_stats = held_blocks(
-        slots, all_queries, cached_key_pool, cached_value_pool, cos_table, sin_table, query_pos, key_pos
-    )
-    got_sum = lax.all_to_all(held_sum, "req", 0, 0, tiled=False)
-    got_stats = lax.all_to_all(held_stats, "req", 0, 0, tiled=False)
+        slots, alive, all_queries, cached_key_pool, cached_value_pool, cos_table, sin_table, query_pos, key_pos
+    )
+    sum_width = req_rows * groups * head_size
+    payload = jnp.concatenate(
+        [held_sum.reshape(request_count, sum_width), held_stats.reshape(request_count, req_rows * groups * 2)], axis=1
+    )
+    got = lax.all_to_all(payload, "req", 0, 0, tiled=False)
+    got_sum = got[:, :sum_width]
     head_total = key_heads * groups
-    got_stats = got_stats.reshape(req_count, count_of_rows, head_total, 2)
+    got_stats = got[:, sum_width:].reshape(req_count, count_of_rows, head_total, 2)
     attended = merge_stats(
         jnp.concatenate([got_sum.reshape(req_count, count_of_rows, head_total, head_size), fresh_sum[None]]),
         jnp.concatenate([got_stats[..., 0], fresh_peak[None]]),

time: 261 us -> 281 us (1.077)
  local copies, waits for them, and re-layouts: 45.3 us -> 73.8 us
  blocking collectives: 27.9 us -> 17.9 us
  Pallas kernels: 32.7 us -> 24.2 us
  waiting for transfers between devices: 67.8 us -> 75.8 us
    reshape x0 -> x3, local copies, waits for them, and re-layouts: none -> 10.4 us  [the longest x2 9.24 us: on_device(): got_sum.reshape(req_count, count_of_rows, head_total, head_size)]
    all_to_all x1 -> x0, blocking collectives: 9.98 us -> none  [on_device(): got_stats = lax.all_to_all(held_stats, 'req', 0, 0, tiled=False)]
    unnamed x49 -> x53, local copies, waits for them, and re-layouts: 10.4 us -> 19.9 us
    all_to_all x1, waiting for transfers between devices: 31.9 us -> 40.5 us  [on_device(): got = lax.all_to_all(payload, 'req', 0, 0, tiled=False)]
    pallas_call x1, Pallas kernels: 32.7 us -> 24.2 us  [held_blocks(): pl.pallas_call(held_block_kernel, grid_spec=grid_spec, out_shape=[jax.Sha...]
    reduce_sum x1, other arithmetic: 6.8 us -> 1.49 us  [merge_stats(): merged = jnp.sum(weighted * factor[..., None], axis=0)]
    slice x0 -> x3, local copies, waits for them, and re-layouts: none -> 3.22 us  [the longest x1 2.21 us: on_device(): got_sum = got[:, :sum_width]]
    slice x0 -> x1, other arithmetic: none -> 3.15 us  [on_device(): got_stats[..., 0]]
  transfers between devices with their start and end apart: 17 -> 17, of which waited for: 7 -> 7; matrix products, arithmetic and copies ran while one was open for 17% -> 14% of each run, Pallas kernels for 0% -> 0%
where the time goes in v4:
time: 281 us; the launch traced here: 280 us
  waiting for transfers between devices  75.8 us (27%)
  local copies, waits for them, and re-layouts  73.8 us (26%)
  starting transfers between devices  41.6 us (15%)
  other arithmetic  25 us (9%)
  Pallas kernels  24.2 us (9%)
  matrix products  20.8 us (7%)
  blocking collectives  17.9 us (6%)
    all_to_all x1, waiting for transfers between devices, on_device(): got = lax.all_to_all(payload, 'req', 0, 0, tiled=False)  40.5 us
    pallas_call x1, Pallas kernels, held_blocks(): pl.pallas_call(held_block_kernel, grid_spec=grid_spec, out_shape=[jax.Sha...  24.2 us
    unnamed x53, local copies, waits for them, and re-layouts  19.9 us
    all_to_all x1, blocking collectives, reduce_rows(): got = lax.all_to_all(blocks, 'tp', 0, 0, tiled=False)  17.9 us
    ppermute x14, starting transfers between devices, gather_rows(): parts.append(lax.ppermute(rows, 'tp', pairs))  14.8 us
    all_to_all x1, waiting for transfers between devices, reduce_rows(): got = lax.all_to_all(blocks, 'tp', 0, 0, tiled=False)  14.1 us
    ppermute x14, waiting for transfers between devices, gather_rows(): parts.append(lax.ppermute(rows, 'tp', pairs))  14 us
    all_to_all x1, starting transfers between devices, reduce_rows(): got = lax.all_to_all(blocks, 'tp', 0, 0, tiled=False)  11.8 us
  transfers between devices with their start and end apart: 17, of which 7 were waited for; matrix products, arithmetic and copies ran while one was open for 14% of the time, Pallas kernels for 0%

profile of v4, /device:TPU:1, one launch (start us, length us, event | category | flops | bytes accessed | tf_op | source)
XLA Modules:
  0.0 279.5 jit_solution(5135331456809359221)
XLA Ops:
  3.0 2.9 %multiply_reduce_fusion = (f32[256,2]{0,1:T(2,128)S(1)}, f32[256,256]{0,1:T(8,128)}) fusion(bf16[2048,256]{1,0:T(8,128)(2,1)} %param.28, bf16[256,2048]{1,0:T(8,128)(2,1)} %param.20, f32[2048]{0:T(1024)} %param.27, f32[256]{0:T(256)S(1)} %add_rsqrt_fusion.2), kind=kOutput, calls=%fused_computation.49 | convolution fusion | flops 270663168 | bytes 2370560 | tf_op jit(solution)/shard_map/dot_general | solution.py:223
  8.2 2.9 %broadcast_in_dim.71 = bf16[16,256,2,128]{3,2,1,0:T(2,128)(2,1)} broadcast(bf16[256,2,128]{2,1,0:T(2,128)(2,1)S(1)} %copy.125), dimensions={1,2,3} | broadcast | bytes 2228224 | tf_op jit(solution)/shard_map/broadcast_in_dim | solution.py:261
  11.1 8.6 %all-to-all-start = ((bf16[16,256,2,128]{3,2,1,0:T(2,128)(2,1)}), bf16[16,256,2,128]{3,2,1,0:T(2,128)(2,1)}, u32[]{:S(2)}, u32[]{:S(2)}) async-start(bf16[16,256,2,128]{3,2,1,0:T(2,128)(2,1)} %broadcast_in_dim.71), calls=%async_computation | async-start | bytes 4194304 | tf_op jit(solution)/shard_map/all_to_all | solution.py:262
  20.6 3.5 %gather_fusion = s32[512]{0:T(512)S(1)} fusion(s32[512]{0:T(512)S(1)} %bitcast.112, s32[1024]{0:T(1024)S(1)} %pad_clamp_fusion.1), kind=kCustom, calls=%fused_computation.2 | custom fusion | bytes 6144 | tf_op jit(solution)/shard_map/gather | solution.py:243
  25.1 3.5 %gather_fusion.1 = s32[512]{0:T(512)S(1)} fusion(s32[512]{0:T(512)S(1)} %bitcast.111, s32[1024]{0:T(1024)S(1)} %pad_clamp_fusion.1), kind=kCustom, calls=%fused_computation.3 | custom fusion | bytes 6144 | tf_op jit(solution)/shard_map/gather | solution.py:244
  32.2 4.8 %copy.131.qpos_ref = s32[16,512,1]{2,1,0:T(8,128)} copy(s32[16,512,1]{0,1,2:T(8,128)S(1)} %bitcast.122) | data formatting | bytes 65536 | tf_op jit(solution)/shard_map/broadcast_in_dim;reshape | solution.py:264
  40.8 7.1 %all-to-all-done = bf16[16,256,2,128]{3,2,1,0:T(2,128)(2,1)} async-done(((bf16[16,256,2,128]{3,2,1,0:T(2,128)(2,1)}), bf16[16,256,2,128]{3,2,1,0:T(2,128)(2,1)}, u32[]{:S(2)}, u32[]{:S(2)}) %all-to-all-start) | async-done | bytes 2097184 | tf_op jit(solution)/shard_map/all_to_all | solution.py:262
  47.9 24.2 %shard_map.172 = (f32[16,512,128]{2,1,0:T(8,128)}, f32[16,512,2]{2,1,0:T(8,128)}) custom-call(s32[32]{0:T(128)} %min.12.slot_ref, s32[32]{0:T(128)} %reshape.373.alive_ref, bf16[16,512,128]{2,1,0:T(8,128)(2,1)} %bitcast.4.q_ref, bf16[32,512,128]{2,1,0:T(8,128)(2,1)} %k1_ref.1, bf16[32,512,128]{2,1,0:T(8,128)(2,1)} %k1_ref.1, bf16[32,512,128]{2,1,0:T(8,128)(2,1)} %v1_ref.1, ...), custom_call_target="tpu_custom_call" | custom-call | tf_op jit(solution)/shard_map/pallas_call | solution.py:162
  72.1 6.6 %copy.157 = f32[2,8,512,128]{3,1,2,0:T(8,128)} copy(f32[2,8,512,128]{3,2,1,0:T(8,128)} %bitcast.116) | data formatting | bytes 8388608
  78.7 5.4 %copy.132 = f32[16,512,2]{0,2,1:T(2,128)} copy(f32[16,512,2]{2,1,0:T(8,128)} %get-tuple-element.10) | data formatting | bytes 131072 | tf_op jit(solution)/shard_map/pallas_call | solution.py:162
  85.3 2.5 pad_maximum_fusion
  87.8 4.0 %all_to_all.18 = f32[16,1,66560]{2,1,0:T(1,128)} reshape(f32[16,66560]{1,0:T(8,128)S(1)} %pad_maximum_fusion) | data formatting | bytes 8519680 | tf_op jit(solution)/shard_map/all_to_all | solution.py:278
  91.8 6.4 %all-to-all-start.1 = ((f32[16,1,66560]{2,1,0:T(1,128)}), f32[16,1,66560]{2,1,0:T(1,128)}, u32[]{:S(2)}, u32[]{:S(2)}) async-start(f32[16,1,66560]{2,1,0:T(1,128)} %all_to_all.18), calls=%async_computation.1 | async-start | bytes 8519680 | tf_op jit(solution)/shard_map/all_to_all | solution.py:278
  101.9 2.9 %convolution_bitcast_fusion = f32[1,256,2,128]{1,3,2,0:T(8,128)} fusion(bf16[2048,128]{1,0:T(8,128)(2,1)} %param.30, f32[1,2,256,256]{2,3,1,0:T(8,128)} %get-tuple-element.45, f32[2,256]{1,0:T(2,128)S(1)} %get-tuple-element.44, pred[256,256]{0,1:T(8,128)(4,1)S(1)} %compare_and_fusion, bf16[256,2048]{1,0:T(8,128)(2,1)} %param.20, f32[2048]{0:T(1024)S(1)} %copy-done.18, ...), kind=kOutput, calls=%fused_computation.23 | convolution fusion | flops 170295296 | bytes 2436096 | tf_op jit(solution)/shard_map/hgmk,khd->mhgd/dot_general | solution.py:61
  107.1 40.5 %all-to-all-done.1 = f32[16,1,66560]{2,1,0:T(1,128)} async-done(((f32[16,1,66560]{2,1,0:T(1,128)}), f32[16,1,66560]{2,1,0:T(1,128)}, u32[]{:S(2)}, u32[]{:S(2)}) %all-to-all-start.1) | async-done | bytes 4259872 | tf_op jit(solution)/shard_map/all_to_all | solution.py:278
  147.6 3.0 %copy.156 = f32[16,1,66560]{2,0,1:T(8,128)S(1)} copy(f32[16,1,66560]{2,1,0:T(1,128)} %all-to-all-done.1) | data formatting | bytes 8519680
  153.8 3.1 %fusion.53 = (f32[16,256,2,1]{0,3,2,1:T(1,128)}, f32[256,2]{1,0:T(8,128)S(1)}, f32[16,256,2,1]{0,3,2,1:T(1,128)}) fusion(f32[16,256,2,2]{0,3,2,1:T(2,128)} %bitcast.119), kind=kLoop, calls=%fused_computation.137 | loop fusion | flops 7680 | bytes 133120 | tf_op jit(solution)/shard_map/slice | solution.py:284
  159.2 6.5 %reshape.366 = f32[16,256,2,128]{3,2,1,0:T(2,128)} reshape(f32[16,65536]{1,0:T(8,128)} %slice.50) | data formatting | bytes 8388608 | tf_op jit(solution)/shard_map/reshape | solution.py:283
  165.7 2.7 copy.137
  170.3 2.7 convolution_convert_fusion
  172.9 11.8 %all-to-all-start.2 = ((bf16[8,32,2048]{2,1,0:T(8,128)(2,1)}), bf16[8,32,2048]{2,1,0:T(8,128)(2,1)}, u32[]{:S(2)}, u32[]{:S(2)}) async-start(bf16[8,32,2048]{2,1,0:T(8,128)(2,1)} %bitcast.117), calls=%async_computation.2 | async-start | bytes 2097152 | tf_op jit(solution)/shard_map/all_to_all | solution.py:175
  185.7 14.1 %all-to-all-done.2 = bf16[8,32,2048]{2,1,0:T(8,128)(2,1)} async-done(((bf16[8,32,2048]{2,1,0:T(8,128)(2,1)}), bf16[8,32,2048]{2,1,0:T(8,128)(2,1)}, u32[]{:S(2)}, u32[]{:S(2)}) %all-to-all-start.2) | async-done | bytes 1048608 | tf_op jit(solution)/shard_map/all_to_all | solution.py:175
  207.8 2.6 collective-permute-start.4
  214.0 4.7 %collective-permute-done.2 = bf16[32,2048]{1,0:T(8,128)(2,1)S(1)} collective-permute-done((bf16[32,2048]{1,0:T(8,128)(2,1)S(1)}, bf16[32,2048]{1,0:T(8,128)(2,1)S(1)}, u32[]{:S(2)}, u32[]{:S(2)}) %collective-permute-start.2) | collective-permute-done | bytes 131104 | tf_op jit(solution)/shard_map/ppermute | solution.py:184
  222.1 2.8 %gather_fusion.2 = bf16[8,32,2048]{2,1,0:T(8,128)(2,1)} fusion(bf16[8,32,2048]{2,1,0:T(8,128)(2,1)} %bitcast_dynamic-update-slice_fusion.8, s32[1024]{0:T(1024)S(1)} %pad_clamp_fusion), kind=kCustom, calls=%fused_computation.clone | custom fusion | bytes 2097184 | tf_op jit(solution)/shard_map/jit(_take)/gather | solution.py:187
  227.3 3.8 %fusion.56 = f32[256,768]{1,0:T(8,128)} fusion(bf16[256,2048]{1,0:T(8,128)(2,1)S(1)} %bitcast.120, bf16[2048,768]{1,0:T(8,128)(2,1)} %param.35), kind=kOutput, calls=%fused_computation.140 | convolution fusion | flops 805306368 | bytes 4980736 | tf_op jit(solution)/shard_map/dot_general | solution.py:82
  231.0 5.5 %convolution_convert_fusion.1 = bf16[256,2048]{1,0:T(8,128)(2,1)} fusion(bf16[768,2048]{1,0:T(8,128)(2,1)S(1)} %copy-done, bf16[256,2048]{1,0:T(8,128)(2,1)} %bitcast.121, bf16[2048,768]{1,0:T(8,128)(2,1)} %param.36, f32[256,768]{1,0:T(8,128)} %fusion.56), kind=kOutput, calls=%fused_computation.12 | convolution fusion | flops 1612316672 | bytes 9175040 | tf_op jit(solution)/shard_map/dot_general | solution.py:296
  236.5 17.9 %all_to_all.27 = bf16[8,32,2048]{2,1,0:T(8,128)(2,1)S(1)} all-to-all(bf16[8,32,2048]{2,1,0:T(8,128)(2,1)} %bitcast.123), channel_id=1, replica_groups=mesh['req'=16,'tp'=8] {'tp'}, dimensions={0} | all-to-all | bytes 2097152 | tf_op jit(solution)/shard_map/all_to_all | solution.py:175
  260.0 2.6 collective-permute-start.11
  263.3 2.4 collective-permute-done.8
  266.4 4.6 %collective-permute-done.9 = bf16[32,2048]{1,0:T(8,128)(2,1)S(1)} collective-permute-done((bf16[32,2048]{1,0:T(8,128)(2,1)S(1)}, bf16[32,2048]{1,0:T(8,128)(2,1)S(1)}, u32[]{:S(2)}, u32[]{:S(2)}) %collective-permute-start.9) | collective-permute-done | bytes 131104 | tf_op jit(solution)/shard_map/ppermute | solution.py:184
  274.4 2.8 %gather_fusion.3 = bf16[8,32,2048]{2,1,0:T(8,128)(2,1)} fusion(bf16[8,32,2048]{2,1,0:T(8,128)(2,1)} %bitcast_dynamic-update-slice_fusion, s32[1024]{0:T(1024)S(1)} %pad_clamp_fusion), kind=kCustom, calls=%fused_computation.1.clone | custom fusion | bytes 2097184 | tf_op jit(solution)/shard_map/jit(_take)/gather | solution.py:187
  (148 shorter events, 59.4 us)
Async XLA Ops:
  0.0 231.0 %copy-start = (bf16[768,2048]{1,0:T(8,128)(2,1)S(1)}, bf16[768,2048]{1,0:T(8,128)(2,1)}, u32[]{:S(2)}) copy-start(bf16[768,2048]{1,0:T(8,128)(2,1)} %param.37) | copy-start | bytes 9437188
  0.0 7.5 %copy-start.15 = (f32[128]{0:T(128)S(1)}, f32[128]{0:T(128)}, u32[]{:S(2)}) copy-start(f32[128]{0:T(128)} %param.31) | copy-start | bytes 1540
  0.0 7.8 %copy-start.10 = (f32[64]{0:T(128)}, f32[64]{0:T(128)S(1)}, u32[]{:S(2)}) copy-start(f32[64]{0:T(128)S(1)} %multiply_power_fusion) | copy-start | bytes 772
  1.5 6.4 %copy-start.6 = (f32[256]{0:T(256)}, f32[256]{0:T(256)S(1)}, u32[]{:S(2)}) copy-start(f32[256]{0:T(256)S(1)} %convert_element_type.90) | copy-start | bytes 3076
  8.1 11.6 %copy-start.9 = (s32[16,32]{1,0:T(8,128)S(1)}, s32[16,32]{1,0:T(8,128)}, u32[]{:S(2)}) copy-start(s32[16,32]{1,0:T(8,128)} %param.23) | copy-start | bytes 6148
  8.1 11.7 %copy-start.3 = (s32[16,256]{1,0:T(8,128)S(1)}, s32[16,256]{1,0:T(8,128)}, u32[]{:S(2)}) copy-start(s32[16,256]{1,0:T(8,128)} %param.21) | copy-start | bytes 49156
  8.2 12.5 %copy-start.12 = (s32[2,512]{1,0:T(2,128)S(1)}, s32[2,512]{1,0:T(2,128)}, u32[]{:S(2)}) copy-start(s32[2,512]{1,0:T(2,128)} %param.24) | copy-start | bytes 12292
  11.1 36.8 %all-to-all-start = ((bf16[16,256,2,128]{3,2,1,0:T(2,128)(2,1)}), bf16[16,256,2,128]{3,2,1,0:T(2,128)(2,1)}, u32[]{:S(2)}, u32[]{:S(2)}) async-start(bf16[16,256,2,128]{3,2,1,0:T(2,128)(2,1)} %broadcast_in_dim.71), calls=%async_computation | async-start | bytes 4194304 | tf_op jit(solution)/shard_map/all_to_all | solution.py:262
  25.1 3.9 %copy-start.17 = (s32[16]{0:T(128)S(1)}, s32[16]{0:T(128)}, u32[]{:S(2)}) copy-start(s32[16]{0:T(128)} %param.22) | copy-start | bytes 196
  91.8 6.4 %copy-start.14 = (f32[256]{0:T(256)S(1)}, f32[256]{0:T(256)}, u32[]{:S(2)}) copy-start(f32[256]{0:T(256)} %copy-done.13) | copy-start | bytes 3076
  91.8 6.4 %copy-start.18 = (f32[2048]{0:T(1024)S(1)}, f32[2048]{0:T(1024)}, u32[]{:S(2)}) copy-start(f32[2048]{0:T(1024)} %param.27) | copy-start | bytes 24580
  91.8 8.4 %copy-start.5 = (s32[1,256]{1,0:T(1,128)S(1)}, s32[1,256]{1,0:T(1,128)}, u32[]{:S(2)}) copy-start(s32[1,256]{1,0:T(1,128)} %copy-done.4) | copy-start | bytes 3076
  91.8 8.6 %copy-start.16 = (f32[128]{0:T(128)S(1)}, f32[128]{0:T(128)}, u32[]{:S(2)}) copy-start(f32[128]{0:T(128)} %param.32) | copy-start | bytes 1540
  91.8 8.6 %copy-start.7 = (f32[256]{0:T(256)S(1)}, f32[256]{0:T(256)}, u32[]{:S(2)}) copy-start(f32[256]{0:T(256)} %copy-done.6) | copy-start | bytes 3076
  91.8 8.6 %copy-start.11 = (f32[64]{0:T(128)S(1)}, f32[64]{0:T(128)}, u32[]{:S(2)}) copy-start(f32[64]{0:T(128)} %copy-done.10) | copy-start | bytes 772
  91.8 55.7 %all-to-all-start.1 = ((f32[16,1,66560]{2,1,0:T(1,128)}), f32[16,1,66560]{2,1,0:T(1,128)}, u32[]{:S(2)}, u32[]{:S(2)}) async-start(f32[16,1,66560]{2,1,0:T(1,128)} %all_to_all.18), calls=%async_computation.1 | async-start | bytes 8519680 | tf_op jit(solution)/shard_map/all_to_all | solution.py:278
  170.3 32.0 %copy-start.8 = (f32[2048]{0:T(1024)S(1)}, f32[2048]{0:T(1024)}, u32[]{:S(2)}) copy-start(f32[2048]{0:T(1024)} %param.34) | copy-start | bytes 24580
  172.9 26.9 %all-to-all-start.2 = ((bf16[8,32,2048]{2,1,0:T(8,128)(2,1)}), bf16[8,32,2048]{2,1,0:T(8,128)(2,1)}, u32[]{:S(2)}, u32[]{:S(2)}) async-start(bf16[8,32,2048]{2,1,0:T(8,128)(2,1)} %bitcast.117), calls=%async_computation.2 | async-start | bytes 2097152 | tf_op jit(solution)/shard_map/all_to_all | solution.py:175
  203.0 7.4 %collective-permute-start = (bf16[32,2048]{1,0:T(8,128)(2,1)S(1)}, bf16[32,2048]{1,0:T(8,128)(2,1)S(1)}, u32[]{:S(2)}, u32[]{:S(2)}) collective-permute-start(bf16[32,2048]{1,0:T(8,128)(2,1)S(1)} %get-tuple-element.17), channel_id=1, source_target_pairs={{0,1},{1,2},{2,3},{3,4},{4,5},{5,6},{6,7},{7,0},{8,9},{9,10},{10,1... | collective-permute-start | bytes 393224 | tf_op jit(solution)/shard_map/ppermute | solution.py:184
  204.2 9.2 %collective-permute-start.1 = (bf16[32,2048]{1,0:T(8,128)(2,1)S(1)}, bf16[32,2048]{1,0:T(8,128)(2,1)S(1)}, u32[]{:S(2)}, u32[]{:S(2)}) collective-permute-start(bf16[32,2048]{1,0:T(8,128)(2,1)S(1)} %get-tuple-element.17), channel_id=1, source_target_pairs={{0,2},{1,3},{2,4},{3,5},{4,6},{5,7},{6,0},{7,1},{8,10},{9,11},{10,... | collective-permute-start | bytes 393224 | tf_op jit(solution)/shard_map/ppermute | solution.py:184
  204.3 14.5 %collective-permute-start.2 = (bf16[32,2048]{1,0:T(8,128)(2,1)S(1)}, bf16[32,2048]{1,0:T(8,128)(2,1)S(1)}, u32[]{:S(2)}, u32[]{:S(2)}) collective-permute-start(bf16[32,2048]{1,0:T(8,128)(2,1)S(1)} %get-tuple-element.17), channel_id=1, source_target_pairs={{0,3},{1,4},{2,5},{3,6},{4,7},{5,0},{6,1},{7,2},{8,11},{9,12},{10,... | collective-permute-start | bytes 393224 | tf_op jit(solution)/shard_map/ppermute | solution.py:184
  206.3 13.1 %collective-permute-start.3 = (bf16[32,2048]{1,0:T(8,128)(2,1)S(1)}, bf16[32,2048]{1,0:T(8,128)(2,1)S(1)}, u32[]{:S(2)}, u32[]{:S(2)}) collective-permute-start(bf16[32,2048]{1,0:T(8,128)(2,1)S(1)} %get-tuple-element.17), channel_id=1, source_target_pairs={{0,4},{1,5},{2,6},{3,7},{4,0},{5,1},{6,2},{7,3},{8,12},{9,13},{10,... | collective-permute-start | bytes 393224 | tf_op jit(solution)/shard_map/ppermute | solution.py:184
  207.8 12.2 %collective-permute-start.4 = (bf16[32,2048]{1,0:T(8,128)(2,1)S(1)}, bf16[32,2048]{1,0:T(8,128)(2,1)S(1)}, u32[]{:S(2)}, u32[]{:S(2)}) collective-permute-start(bf16[32,2048]{1,0:T(8,128)(2,1)S(1)} %get-tuple-element.17), channel_id=1, source_target_pairs={{0,5},{1,6},{2,7},{3,0},{4,1},{5,2},{6,3},{7,4},{8,13},{9,14},{10,... | collective-permute-start | bytes 393224 | tf_op jit(solution)/shard_map/ppermute | solution.py:184
  210.5 10.3 %collective-permute-start.5 = (bf16[32,2048]{1,0:T(8,128)(2,1)S(1)}, bf16[32,2048]{1,0:T(8,128)(2,1)S(1)}, u32[]{:S(2)}, u32[]{:S(2)}) collective-permute-start(bf16[32,2048]{1,0:T(8,128)(2,1)S(1)} %get-tuple-element.17), channel_id=1, source_target_pairs={{0,6},{1,7},{2,0},{3,1},{4,2},{5,3},{6,4},{7,5},{8,14},{9,15},{10,... | collective-permute-start | bytes 393224 | tf_op jit(solution)/shard_map/ppermute | solution.py:184
  213.4 8.1 %collective-permute-start.6 = (bf16[32,2048]{1,0:T(8,128)(2,1)S(1)}, bf16[32,2048]{1,0:T(8,128)(2,1)S(1)}, u32[]{:S(2)}, u32[]{:S(2)}) collective-permute-start(bf16[32,2048]{1,0:T(8,128)(2,1)S(1)} %get-tuple-element.17), channel_id=1, source_target_pairs={{0,7},{1,0},{2,1},{3,2},{4,3},{5,4},{6,5},{7,6},{8,15},{9,8},{10,9... | collective-permute-start | bytes 393224 | tf_op jit(solution)/shard_map/ppermute | solution.py:184
  255.2 7.4 %collective-permute-start.7 = (bf16[32,2048]{1,0:T(8,128)(2,1)S(1)}, bf16[32,2048]{1,0:T(8,128)(2,1)S(1)}, u32[]{:S(2)}, u32[]{:S(2)}) collective-permute-start(bf16[32,2048]{1,0:T(8,128)(2,1)S(1)} %get-tuple-element.15), channel_id=1, source_target_pairs={{0,1},{1,2},{2,3},{3,4},{4,5},{5,6},{6,7},{7,0},{8,9},{9,10},{10,1... | collective-permute-start | bytes 393224 | tf_op jit(solution)/shard_map/ppermute | solution.py:184
  256.5 9.2 %collective-permute-start.8 = (bf16[32,2048]{1,0:T(8,128)(2,1)S(1)}, bf16[32,2048]{1,0:T(8,128)(2,1)S(1)}, u32[]{:S(2)}, u32[]{:S(2)}) collective-permute-start(bf16[32,2048]{1,0:T(8,128)(2,1)S(1)} %get-tuple-element.15), channel_id=1, source_target_pairs={{0,2},{1,3},{2,4},{3,5},{4,6},{5,7},{6,0},{7,1},{8,10},{9,11},{10,... | collective-permute-start | bytes 393224 | tf_op jit(solution)/shard_map/ppermute | solution.py:184
  256.5 14.5 %collective-permute-start.9 = (bf16[32,2048]{1,0:T(8,128)(2,1)S(1)}, bf16[32,2048]{1,0:T(8,128)(2,1)S(1)}, u32[]{:S(2)}, u32[]{:S(2)}) collective-permute-start(bf16[32,2048]{1,0:T(8,128)(2,1)S(1)} %get-tuple-element.15), channel_id=1, source_target_pairs={{0,3},{1,4},{2,5},{3,6},{4,7},{5,0},{6,1},{7,2},{8,11},{9,12},{10,... | collective-permute-start | bytes 393224 | tf_op jit(solution)/shard_map/ppermute | solution.py:184
  258.5 13.2 %collective-permute-start.10 = (bf16[32,2048]{1,0:T(8,128)(2,1)S(1)}, bf16[32,2048]{1,0:T(8,128)(2,1)S(1)}, u32[]{:S(2)}, u32[]{:S(2)}) collective-permute-start(bf16[32,2048]{1,0:T(8,128)(2,1)S(1)} %get-tuple-element.15), channel_id=1, source_target_pairs={{0,4},{1,5},{2,6},{3,7},{4,0},{5,1},{6,2},{7,3},{8,12},{9,13},{10,... | collective-permute-start | bytes 393224 | tf_op jit(solution)/shard_map/ppermute | solution.py:184
  260.0 12.3 %collective-permute-start.11 = (bf16[32,2048]{1,0:T(8,128)(2,1)S(1)}, bf16[32,2048]{1,0:T(8,128)(2,1)S(1)}, u32[]{:S(2)}, u32[]{:S(2)}) collective-permute-start(bf16[32,2048]{1,0:T(8,128)(2,1)S(1)} %get-tuple-element.15), channel_id=1, source_target_pairs={{0,5},{1,6},{2,7},{3,0},{4,1},{5,2},{6,3},{7,4},{8,13},{9,14},{10,... | collective-permute-start | bytes 393224 | tf_op jit(solution)/shard_map/ppermute | solution.py:184
  262.6 10.4 %collective-permute-start.12 = (bf16[32,2048]{1,0:T(8,128)(2,1)S(1)}, bf16[32,2048]{1,0:T(8,128)(2,1)S(1)}, u32[]{:S(2)}, u32[]{:S(2)}) collective-permute-start(bf16[32,2048]{1,0:T(8,128)(2,1)S(1)} %get-tuple-element.15), channel_id=1, source_target_pairs={{0,6},{1,7},{2,0},{3,1},{4,2},{5,3},{6,4},{7,5},{8,14},{9,15},{10,... | collective-permute-start | bytes 393224 | tf_op jit(solution)/shard_map/ppermute | solution.py:184
  265.7 8.0 %collective-permute-start.13 = (bf16[32,2048]{1,0:T(8,128)(2,1)S(1)}, bf16[32,2048]{1,0:T(8,128)(2,1)S(1)}, u32[]{:S(2)}, u32[]{:S(2)}) collective-permute-start(bf16[32,2048]{1,0:T(8,128)(2,1)S(1)} %get-tuple-element.15), channel_id=1, source_target_pairs={{0,7},{1,0},{2,1},{3,2},{4,3},{5,4},{6,5},{7,6},{8,15},{9,8},{10,9... | collective-permute-start | bytes 393224 | tf_op jit(solution)/shard_map/ppermute | solution.py:184
  (4 other events, 6.0 us)

commit v5 on v4

--- a/solution.py
+++ b/solution.py
@@ -87,9 +87,22 @@
 far_position = 1 << 30
 
 
-def held_block_kernel(slot_ref, alive_ref, q_ref, k0_ref, k1_ref, v0_ref, v1_ref, cos_ref, sin_ref, qpos_ref, kpos_ref, sum_ref, stat_ref):
+def held_block_kernel(slot_ref, alive_ref, q_ref, k0_ref, k1_ref, v0_ref, v1_ref, cos_ref, sin_ref, qpos_ref, kpos_ref, out_ref):
     step = pl.program_id(0)
     key_refs = (k0_ref, k1_ref)
+
+    def store(weighted, peak, total):
+        rows, lanes = weighted.shape
+        chunks = rows // lanes
+        lane = lax.broadcasted_iota(jnp.int32, (rows, lanes), 1)
+        packed = jnp.where(lane == 0, peak, jnp.where(lane == 1, total, 0.0)).T
+        out_ref[0, :rows] = weighted
+        out_ref[0, rows:rows + chunks] = jnp.concatenate(
+            [packed[0:1, c * lanes:(c + 1) * lanes] for c in range(chunks)], axis=0
+        )
+        out_ref[0, rows + chunks:rows + 2 * chunks] = jnp.concatenate(
+            [packed[1:2, c * lanes:(c + 1) * lanes] for c in range(chunks)], axis=0
+        )
     value_refs = (v0_ref, v1_ref)
 
     def run(parts):
@@ -115,8 +128,7 @@
             part_sum = jnp.dot(w.astype(jnp.bfloat16), value_refs[j][0], preferred_element_type=jnp.float32)
             total = part_total if total is None else total + part_total
             weighted = part_sum if weighted is None else weighted + part_sum
-        sum_ref[0] = weighted
-        stat_ref[0] = jnp.concatenate([peak, total], axis=1)
+        store(weighted, peak, total)
 
     live0 = alive_ref[2 * step] > 0
     live1 = alive_ref[2 * step + 1] > 0
@@ -126,11 +138,11 @@
 
     @pl.when(jnp.logical_not(live0) & jnp.logical_not(live1))
     def _():
-        sum_ref[0] = jnp.zeros(sum_ref.shape[1:], jnp.float32)
-        rows = stat_ref.shape[1]
-        stat_ref[0] = jnp.concatenate(
-            [jnp.full((rows, 1), floor_score, jnp.float32), jnp.zeros((rows, 1), jnp.float32)], axis=1
-        )
+        rows, lanes = q_ref.shape[1], q_ref.shape[2]
+        out_ref[0, :rows] = jnp.zeros((rows, lanes), jnp.float32)
+        chunks = rows // lanes
+        out_ref[0, rows:rows + chunks] = jnp.full((chunks, lanes), floor_score, jnp.float32)
+        out_ref[0, rows + chunks:rows + 2 * chunks] = jnp.zeros((chunks, lanes), jnp.float32)
 
 
 def held_blocks(slots, alive, queries, key_pool, value_pool, cos_table, sin_table, query_pos, key_pos):
@@ -154,18 +166,12 @@
             pl.BlockSpec((1, rows, 1), lambda r, slot, alive: (r, 0, 0)),
             pl.BlockSpec((1, 2, 1, stretch), lambda r, slot, alive: (r, 0, 0, 0)),
         ],
-        out_specs=[
-            pl.BlockSpec((1, rows, head_size), lambda r, slot, alive: (r, 0, 0)),
-            pl.BlockSpec((1, rows, 2), lambda r, slot, alive: (r, 0, 0)),
-        ],
+        out_specs=pl.BlockSpec((1, rows + 2 * rows // head_size, head_size), lambda r, slot, alive: (r, 0, 0)),
     )
     return pl.pallas_call(
         held_block_kernel,
         grid_spec=grid_spec,
-        out_shape=[
-            jax.ShapeDtypeStruct((requests, rows, head_size), jnp.float32),
-            jax.ShapeDtypeStruct((requests, rows, 2), jnp.float32),
-        ],
+        out_shape=jax.ShapeDtypeStruct((requests, rows + 2 * rows // head_size, head_size), jnp.float32),
         compiler_params=pltpu.CompilerParams(dimension_semantics=("arbitrary",)),
     )(slots, alive, queries, key_pool, key_pool, value_pool, value_pool, cos_table, sin_table, query_pos, key_pos)
 
@@ -268,21 +274,20 @@
         far_position,
     )[:, :, None, :]
     alive = (send_place < req_lengths[:, None]).reshape(request_count * pair_cap).astype(jnp.int32)
-    held_sum, held_stats = held_blocks(
+    held = held_blocks(
         slots, alive, all_queries, cached_key_pool, cached_value_pool, cos_table, sin_table, query_pos, key_pos
     )
-    sum_width = req_rows * groups * head_size
-    payload = jnp.concatenate(
-        [held_sum.reshape(request_count, sum_width), held_stats.reshape(request_count, req_rows * groups * 2)], axis=1
-    )
-    got = lax.all_to_all(payload, "req", 0, 0, tiled=False)
-    got_sum = got[:, :sum_width]
+    got = lax.all_to_all(held, "req", 0, 0, tiled=False)
+    sum_rows = req_rows * groups
+    chunks = sum_rows // head_size
     head_total = key_heads * groups
-    got_stats = got[:, sum_width:].reshape(req_count, count_of_rows, head_total, 2)
+    got_sum = got[:, :sum_rows]
+    got_peak = got[:, sum_rows:sum_rows + chunks].reshape(req_count, count_of_rows, head_total)
+    got_total = got[:, sum_rows + chunks:].reshape(req_count, count_of_rows, head_total)
     attended = merge_stats(
         jnp.concatenate([got_sum.reshape(req_count, count_of_rows, head_total, head_size), fresh_sum[None]]),
-        jnp.concatenate([got_stats[..., 0], fresh_peak[None]]),
-        jnp.concatenate([got_stats[..., 1], fresh_total[None]]),
+        jnp.concatenate([got_peak, fresh_peak[None]]),
+        jnp.concatenate([got_total, fresh_total[None]]),
     )
     tp_count = lax.axis_size("tp")
     tp_index = lax.axis_index("tp")

time: 281 us -> 255 us (0.907)
  local copies, waits for them, and re-layouts: 73.8 us -> 44.4 us
  starting transfers between devices: 41.6 us -> 44.8 us
    reshape x3 -> x1, local copies, waits for them, and re-layouts: 10.4 us -> 0.12 us  [on_device(): got[:, sum_rows + chunks:].reshape(req_count, count_of_rows, head_total)]
    unnamed x53 -> x55, local copies, waits for them, and re-layouts: 19.9 us -> 10.6 us
    pallas_call x1 -> x0, local copies, waits for them, and re-layouts: 5.45 us -> none  [held_blocks(): pl.pallas_call(held_block_kernel, grid_spec=grid_spec, out_shape=[jax.Sha...]
    ppermute x14, starting transfers between devices: 14.8 us -> 18.9 us  [gather_rows(): parts.append(lax.ppermute(rows, 'tp', pairs))]
    all_to_all x1 -> x0, local copies, waits for them, and re-layouts: 4 us -> none  [on_device(): got = lax.all_to_all(payload, 'req', 0, 0, tiled=False)]
    reduce_sum x1, other arithmetic: 1.49 us -> 5.34 us  [merge_stats(): merged = jnp.sum(weighted * factor[..., None], axis=0)]
  transfers between devices with their start and end apart: 17 -> 17, of which waited for: 7 -> 5; matrix products, arithmetic and copies ran while one was open for 14% -> 15% of each run, Pallas kernels for 0% -> 0%
where the time goes in v5:
time: 255 us; the launch traced here: 253 us
  waiting for transfers between devices  78.5 us (31%)
  starting transfers between devices  44.8 us (18%)
  local copies, waits for them, and re-layouts  44.4 us (17%)
  other arithmetic  24.4 us (10%)
  Pallas kernels  23 us (9%)
  matrix products  18.8 us (7%)
  blocking collectives  18.5 us (7%)
    all_to_all x1, waiting for transfers between devices, on_device(): got = lax.all_to_all(held, 'req', 0, 0, tiled=False)  41.4 us
    pallas_call x1, Pallas kernels, held_blocks(): pl.pallas_call(held_block_kernel, grid_spec=grid_spec, out_shape=jax.Shap...  23 us
    ppermute x14, starting transfers between devices, gather_rows(): parts.append(lax.ppermute(rows, 'tp', pairs))  18.9 us
    all_to_all x1, blocking collectives, reduce_rows(): got = lax.all_to_all(blocks, 'tp', 0, 0, tiled=False)  18.5 us
    ppermute x14, waiting for transfers between devices, gather_rows(): parts.append(lax.ppermute(rows, 'tp', pairs))  15.9 us
    all_to_all x1, waiting for transfers between devices, reduce_rows(): got = lax.all_to_all(blocks, 'tp', 0, 0, tiled=False)  14 us
    all_to_all x1, starting transfers between devices, reduce_rows(): got = lax.all_to_all(blocks, 'tp', 0, 0, tiled=False)  11.9 us
    unnamed x55, local copies, waits for them, and re-layouts  10.6 us
  transfers between devices with their start and end apart: 17, of which 5 were waited for; matrix products, arithmetic and copies ran while one was open for 15% of the time, Pallas kernels for 0%

profile of v5, /device:TPU:1, one launch (start us, length us, event | category | flops | bytes accessed | tf_op | source)
XLA Modules:
  0.0 252.9 jit_solution(11303933328125483126)
XLA Ops:
  1.4 1.5 fusion.1
  3.0 2.9 %multiply_reduce_fusion = (f32[256,2]{0,1:T(2,128)S(1)}, f32[256,256]{0,1:T(8,128)}) fusion(bf16[2048,256]{1,0:T(8,128)(2,1)} %param.28, bf16[256,2048]{1,0:T(8,128)(2,1)} %param.20, f32[2048]{0:T(1024)} %param.27, f32[256]{0:T(256)S(1)} %add_rsqrt_fusion.2), kind=kOutput, calls=%fused_computation.45 | convolution fusion | flops 270663168 | bytes 2370560 | tf_op jit(solution)/shard_map/dot_general | solution.py:229
  8.1 2.9 %broadcast_in_dim.71 = bf16[16,256,2,128]{3,2,1,0:T(2,128)(2,1)} broadcast(bf16[256,2,128]{2,1,0:T(2,128)(2,1)S(1)} %copy.97), dimensions={1,2,3} | broadcast | bytes 2228224 | tf_op jit(solution)/shard_map/broadcast_in_dim | solution.py:267
  11.1 8.6 %all-to-all-start = ((bf16[16,256,2,128]{3,2,1,0:T(2,128)(2,1)}), bf16[16,256,2,128]{3,2,1,0:T(2,128)(2,1)}, u32[]{:S(2)}, u32[]{:S(2)}) async-start(bf16[16,256,2,128]{3,2,1,0:T(2,128)(2,1)} %broadcast_in_dim.71), calls=%async_computation | async-start | bytes 4194304 | tf_op jit(solution)/shard_map/all_to_all | solution.py:268
  20.6 3.5 %gather_fusion.1 = s32[512]{0:T(512)S(1)} fusion(s32[512]{0:T(512)S(1)} %bitcast.106, s32[1024]{0:T(1024)S(1)} %pad_clamp_fusion.1), kind=kCustom, calls=%fused_computation.3 | custom fusion | bytes 6144 | tf_op jit(solution)/shard_map/gather | solution.py:250
  24.1 3.5 %gather_fusion = s32[512]{0:T(512)S(1)} fusion(s32[512]{0:T(512)S(1)} %bitcast.105, s32[1024]{0:T(1024)S(1)} %pad_clamp_fusion.1), kind=kCustom, calls=%fused_computation.2 | custom fusion | bytes 6144 | tf_op jit(solution)/shard_map/gather | solution.py:249
  32.1 4.8 %copy.103.qpos_ref = s32[16,512,1]{2,1,0:T(8,128)} copy(s32[16,512,1]{0,1,2:T(8,128)S(1)} %bitcast.111) | data formatting | bytes 65536 | tf_op jit(solution)/shard_map/broadcast_in_dim;reshape | solution.py:270
  40.7 7.3 %all-to-all-done = bf16[16,256,2,128]{3,2,1,0:T(2,128)(2,1)} async-done(((bf16[16,256,2,128]{3,2,1,0:T(2,128)(2,1)}), bf16[16,256,2,128]{3,2,1,0:T(2,128)(2,1)}, u32[]{:S(2)}, u32[]{:S(2)}) %all-to-all-start) | async-done | bytes 2097184 | tf_op jit(solution)/shard_map/all_to_all | solution.py:268
  47.9 23.0 %shard_map.172 = f32[16,520,128]{2,1,0:T(8,128)} custom-call(s32[32]{0:T(128)} %min.12.slot_ref, s32[32]{0:T(128)} %reshape.369.alive_ref, bf16[16,512,128]{2,1,0:T(8,128)(2,1)} %bitcast.4.q_ref, bf16[32,512,128]{2,1,0:T(8,128)(2,1)} %k1_ref.1, bf16[32,512,128]{2,1,0:T(8,128)(2,1)} %k1_ref.1, bf16[32,512,128]{2,1,0:T(8,128)(2,1)} %v1_ref.1, ...), custom_call_target="tpu_custom_call" | custom-call | tf_op jit(solution)/shard_map/pallas_call | solution.py:171
  71.0 5.4 %all-to-all-start.1 = ((f32[16,520,128]{2,1,0:T(8,128)}), f32[16,520,128]{2,1,0:T(8,128)}, u32[]{:S(2)}, u32[]{:S(2)}) async-start(f32[16,520,128]{2,1,0:T(8,128)} %shard_map.172), calls=%async_computation.1 | async-start | bytes 8519680 | tf_op jit(solution)/shard_map/all_to_all | solution.py:280
  76.4 1.9 multiply_reduce_fusion.1
  80.0 2.2 convolution_bitcast_fusion
  84.2 41.4 %all-to-all-done.1 = f32[16,520,128]{2,1,0:T(8,128)} async-done(((f32[16,520,128]{2,1,0:T(8,128)}), f32[16,520,128]{2,1,0:T(8,128)}, u32[]{:S(2)}, u32[]{:S(2)}) %all-to-all-start.1) | async-done | bytes 4259872 | tf_op jit(solution)/shard_map/all_to_all | solution.py:280
  127.5 2.1 copy.111
  129.6 2.6 %slice.46 = f32[16,512,128]{2,1,0:T(8,128)S(1)} slice(f32[16,520,128]{2,1,0:T(8,128)} %all-to-all-done.1), slice={[0:16], [0:512], [0:128]} | slice | bytes 8388608 | tf_op jit(solution)/shard_map/slice | solution.py:284
  132.5 5.3 %fusion = f32[256,2,128]{2,1,0:T(2,128)S(1)} fusion(f32[1,256,2,128]{3,2,1,0:T(2,128)S(1)} %copy-done.4, f32[16,256,2,128]{3,2,1,0:T(2,128)S(1)} %bitcast.107, f32[17,256,2]{2,1,0:T(8,128)S(1)} %copy-done.1), kind=kLoop, calls=%fused_computation.5 | loop fusion | flops 3276800 | bytes 4753408 | tf_op jit(solution)/shard_map/reduce_sum | solution.py:75
  139.6 11.9 %all-to-all-start.2 = ((bf16[8,32,2048]{2,1,0:T(8,128)(2,1)}), bf16[8,32,2048]{2,1,0:T(8,128)(2,1)}, u32[]{:S(2)}, u32[]{:S(2)}) async-start(bf16[8,32,2048]{2,1,0:T(8,128)(2,1)} %bitcast.108), calls=%async_computation.2 | async-start | bytes 2097152 | tf_op jit(solution)/shard_map/all_to_all | solution.py:181
  152.6 14.0 %all-to-all-done.2 = bf16[8,32,2048]{2,1,0:T(8,128)(2,1)} async-done(((bf16[8,32,2048]{2,1,0:T(8,128)(2,1)}), bf16[8,32,2048]{2,1,0:T(8,128)(2,1)}, u32[]{:S(2)}, u32[]{:S(2)}) %all-to-all-start.2) | async-done | bytes 1048608 | tf_op jit(solution)/shard_map/all_to_all | solution.py:181
  171.0 2.5 collective-permute-start.5
  174.3 2.4 collective-permute-start.2
  178.3 7.9 %collective-permute-done.1 = bf16[32,2048]{1,0:T(8,128)(2,1)S(1)} collective-permute-done((bf16[32,2048]{1,0:T(8,128)(2,1)S(1)}, bf16[32,2048]{1,0:T(8,128)(2,1)S(1)}, u32[]{:S(2)}, u32[]{:S(2)}) %collective-permute-start.1) | collective-permute-done | bytes 131104 | tf_op jit(solution)/shard_map/ppermute | solution.py:190
  186.2 1.7 collective-permute-start.6
  191.9 2.8 %gather_fusion.2 = bf16[8,32,2048]{2,1,0:T(8,128)(2,1)} fusion(bf16[8,32,2048]{2,1,0:T(8,128)(2,1)} %bitcast_dynamic-update-slice_fusion.8, s32[1024]{0:T(1024)S(1)} %pad_clamp_fusion), kind=kCustom, calls=%fused_computation.clone | custom fusion | bytes 2097184 | tf_op jit(solution)/shard_map/jit(_take)/gather | solution.py:193
  197.1 3.8 %fusion.58 = f32[256,768]{1,0:T(8,128)} fusion(bf16[256,2048]{1,0:T(8,128)(2,1)S(1)} %bitcast.109, bf16[2048,768]{1,0:T(8,128)(2,1)} %param.35), kind=kOutput, calls=%fused_computation.139 | convolution fusion | flops 805306368 | bytes 4980736 | tf_op jit(solution)/shard_map/dot_general | solution.py:82
  200.9 5.5 %convolution_convert_fusion.1 = bf16[256,2048]{1,0:T(8,128)(2,1)} fusion(bf16[768,2048]{1,0:T(8,128)(2,1)S(1)} %copy-done, bf16[256,2048]{1,0:T(8,128)(2,1)} %bitcast.110, bf16[2048,768]{1,0:T(8,128)(2,1)} %param.36, f32[256,768]{1,0:T(8,128)} %fusion.58), kind=kOutput, calls=%fused_computation.9 | convolution fusion | flops 1612316672 | bytes 9175040 | tf_op jit(solution)/shard_map/dot_general | solution.py:301
  206.3 18.5 %all_to_all.20 = bf16[8,32,2048]{2,1,0:T(8,128)(2,1)S(1)} all-to-all(bf16[8,32,2048]{2,1,0:T(8,128)(2,1)} %bitcast.114), channel_id=1, replica_groups=mesh['req'=16,'tp'=8] {'tp'}, dimensions={0} | all-to-all | bytes 2097152 | tf_op jit(solution)/shard_map/all_to_all | solution.py:181
  226.9 2.3 collective-permute-start.12
  230.1 2.4 collective-permute-start.9
  234.0 8.0 %collective-permute-done.8 = bf16[32,2048]{1,0:T(8,128)(2,1)S(1)} collective-permute-done((bf16[32,2048]{1,0:T(8,128)(2,1)S(1)}, bf16[32,2048]{1,0:T(8,128)(2,1)S(1)}, u32[]{:S(2)}, u32[]{:S(2)}) %collective-permute-start.8) | collective-permute-done | bytes 131104 | tf_op jit(solution)/shard_map/ppermute | solution.py:190
  242.0 1.7 collective-permute-start.13
  247.7 2.8 %gather_fusion.3 = bf16[8,32,2048]{2,1,0:T(8,128)(2,1)} fusion(bf16[8,32,2048]{2,1,0:T(8,128)(2,1)} %bitcast_dynamic-update-slice_fusion, s32[1024]{0:T(1024)S(1)} %pad_clamp_fusion), kind=kCustom, calls=%fused_computation.1.clone | custom fusion | bytes 2097184 | tf_op jit(solution)/shard_map/jit(_take)/gather | solution.py:193
  250.5 2.4 broadcast_select_fusion.1
  (146 shorter events, 42.9 us)
Async XLA Ops:
  0.0 200.9 %copy-start = (bf16[768,2048]{1,0:T(8,128)(2,1)S(1)}, bf16[768,2048]{1,0:T(8,128)(2,1)}, u32[]{:S(2)}) copy-start(bf16[768,2048]{1,0:T(8,128)(2,1)} %param.37) | copy-start | bytes 9437188
  0.0 7.5 %copy-start.17 = (f32[128]{0:T(128)S(1)}, f32[128]{0:T(128)}, u32[]{:S(2)}) copy-start(f32[128]{0:T(128)} %param.31) | copy-start | bytes 1540
  0.0 7.8 %copy-start.12 = (f32[64]{0:T(128)}, f32[64]{0:T(128)S(1)}, u32[]{:S(2)}) copy-start(f32[64]{0:T(128)S(1)} %multiply_power_fusion) | copy-start | bytes 772
  1.4 6.4 %copy-start.8 = (f32[256]{0:T(256)}, f32[256]{0:T(256)S(1)}, u32[]{:S(2)}) copy-start(f32[256]{0:T(256)S(1)} %convert_element_type.90) | copy-start | bytes 3076
  8.1 11.6 %copy-start.11 = (s32[16,32]{1,0:T(8,128)S(1)}, s32[16,32]{1,0:T(8,128)}, u32[]{:S(2)}) copy-start(s32[16,32]{1,0:T(8,128)} %param.23) | copy-start | bytes 6148
  8.1 11.7 %copy-start.5 = (s32[16,256]{1,0:T(8,128)S(1)}, s32[16,256]{1,0:T(8,128)}, u32[]{:S(2)}) copy-start(s32[16,256]{1,0:T(8,128)} %param.21) | copy-start | bytes 49156
  8.1 12.5 %copy-start.14 = (s32[2,512]{1,0:T(2,128)S(1)}, s32[2,512]{1,0:T(2,128)}, u32[]{:S(2)}) copy-start(s32[2,512]{1,0:T(2,128)} %param.24) | copy-start | bytes 12292
  11.1 36.9 %all-to-all-start = ((bf16[16,256,2,128]{3,2,1,0:T(2,128)(2,1)}), bf16[16,256,2,128]{3,2,1,0:T(2,128)(2,1)}, u32[]{:S(2)}, u32[]{:S(2)}) async-start(bf16[16,256,2,128]{3,2,1,0:T(2,128)(2,1)} %broadcast_in_dim.71), calls=%async_computation | async-start | bytes 4194304 | tf_op jit(solution)/shard_map/all_to_all | solution.py:268
  70.9 5.4 %copy-start.16 = (f32[256]{0:T(256)S(1)}, f32[256]{0:T(256)}, u32[]{:S(2)}) copy-start(f32[256]{0:T(256)} %copy-done.15) | copy-start | bytes 3076
  70.9 5.5 %copy-start.20 = (f32[2048]{0:T(1024)S(1)}, f32[2048]{0:T(1024)}, u32[]{:S(2)}) copy-start(f32[2048]{0:T(1024)} %param.27) | copy-start | bytes 24580
  70.9 7.4 %copy-start.7 = (s32[1,256]{1,0:T(1,128)S(1)}, s32[1,256]{1,0:T(1,128)}, u32[]{:S(2)}) copy-start(s32[1,256]{1,0:T(1,128)} %copy-done.6) | copy-start | bytes 3076
  70.9 7.6 %copy-start.18 = (f32[128]{0:T(128)S(1)}, f32[128]{0:T(128)}, u32[]{:S(2)}) copy-start(f32[128]{0:T(128)} %param.32) | copy-start | bytes 1540
  70.9 7.7 %copy-start.9 = (f32[256]{0:T(256)S(1)}, f32[256]{0:T(256)}, u32[]{:S(2)}) copy-start(f32[256]{0:T(256)} %copy-done.8) | copy-start | bytes 3076
  71.0 7.7 %copy-start.13 = (f32[64]{0:T(128)S(1)}, f32[64]{0:T(128)}, u32[]{:S(2)}) copy-start(f32[64]{0:T(128)} %copy-done.12) | copy-start | bytes 772
  71.0 54.6 %all-to-all-start.1 = ((f32[16,520,128]{2,1,0:T(8,128)}), f32[16,520,128]{2,1,0:T(8,128)}, u32[]{:S(2)}, u32[]{:S(2)}) async-start(f32[16,520,128]{2,1,0:T(8,128)} %shard_map.172), calls=%async_computation.1 | async-start | bytes 8519680 | tf_op jit(solution)/shard_map/all_to_all | solution.py:280
  132.5 5.7 %copy-start.3 = (bf16[256,2048]{1,0:T(8,128)(2,1)S(1)}, bf16[256,2048]{1,0:T(8,128)(2,1)}, u32[]{:S(2)}) copy-start(bf16[256,2048]{1,0:T(8,128)(2,1)} %param.33) | copy-start | bytes 3145732
  138.2 30.9 %copy-start.10 = (f32[2048]{0:T(1024)S(1)}, f32[2048]{0:T(1024)}, u32[]{:S(2)}) copy-start(f32[2048]{0:T(1024)} %param.34) | copy-start | bytes 24580
  139.6 27.0 %all-to-all-start.2 = ((bf16[8,32,2048]{2,1,0:T(8,128)(2,1)}), bf16[8,32,2048]{2,1,0:T(8,128)(2,1)}, u32[]{:S(2)}, u32[]{:S(2)}) async-start(bf16[8,32,2048]{2,1,0:T(8,128)(2,1)} %bitcast.108), calls=%async_computation.2 | async-start | bytes 2097152 | tf_op jit(solution)/shard_map/all_to_all | solution.py:181
  169.8 6.9 %collective-permute-start = (bf16[32,2048]{1,0:T(8,128)(2,1)S(1)}, bf16[32,2048]{1,0:T(8,128)(2,1)S(1)}, u32[]{:S(2)}, u32[]{:S(2)}) collective-permute-start(bf16[32,2048]{1,0:T(8,128)(2,1)S(1)} %get-tuple-element.13), channel_id=1, source_target_pairs={{0,1},{1,2},{2,3},{3,4},{4,5},{5,6},{6,7},{7,0},{8,9},{9,10},{10,1... | collective-permute-start | bytes 393224 | tf_op jit(solution)/shard_map/ppermute | solution.py:190
  171.0 19.6 %collective-permute-start.5 = (bf16[32,2048]{1,0:T(8,128)(2,1)S(1)}, bf16[32,2048]{1,0:T(8,128)(2,1)S(1)}, u32[]{:S(2)}, u32[]{:S(2)}) collective-permute-start(bf16[32,2048]{1,0:T(8,128)(2,1)S(1)} %get-tuple-element.13), channel_id=1, source_target_pairs={{0,6},{1,7},{2,0},{3,1},{4,2},{5,3},{6,4},{7,5},{8,14},{9,15},{10,... | collective-permute-start | bytes 393224 | tf_op jit(solution)/shard_map/ppermute | solution.py:190
  173.5 16.4 %collective-permute-start.4 = (bf16[32,2048]{1,0:T(8,128)(2,1)S(1)}, bf16[32,2048]{1,0:T(8,128)(2,1)S(1)}, u32[]{:S(2)}, u32[]{:S(2)}) collective-permute-start(bf16[32,2048]{1,0:T(8,128)(2,1)S(1)} %get-tuple-element.13), channel_id=1, source_target_pairs={{0,5},{1,6},{2,7},{3,0},{4,1},{5,2},{6,3},{7,4},{8,13},{9,14},{10,... | collective-permute-start | bytes 393224 | tf_op jit(solution)/shard_map/ppermute | solution.py:190
  173.5 15.8 %collective-permute-start.3 = (bf16[32,2048]{1,0:T(8,128)(2,1)S(1)}, bf16[32,2048]{1,0:T(8,128)(2,1)S(1)}, u32[]{:S(2)}, u32[]{:S(2)}) collective-permute-start(bf16[32,2048]{1,0:T(8,128)(2,1)S(1)} %get-tuple-element.13), channel_id=1, source_target_pairs={{0,4},{1,5},{2,6},{3,7},{4,0},{5,1},{6,2},{7,3},{8,12},{9,13},{10,... | collective-permute-start | bytes 393224 | tf_op jit(solution)/shard_map/ppermute | solution.py:190
  174.3 14.2 %collective-permute-start.2 = (bf16[32,2048]{1,0:T(8,128)(2,1)S(1)}, bf16[32,2048]{1,0:T(8,128)(2,1)S(1)}, u32[]{:S(2)}, u32[]{:S(2)}) collective-permute-start(bf16[32,2048]{1,0:T(8,128)(2,1)S(1)} %get-tuple-element.13), channel_id=1, source_target_pairs={{0,3},{1,4},{2,5},{3,6},{4,7},{5,0},{6,1},{7,2},{8,11},{9,12},{10,... | collective-permute-start | bytes 393224 | tf_op jit(solution)/shard_map/ppermute | solution.py:190
  176.7 9.5 %collective-permute-start.1 = (bf16[32,2048]{1,0:T(8,128)(2,1)S(1)}, bf16[32,2048]{1,0:T(8,128)(2,1)S(1)}, u32[]{:S(2)}, u32[]{:S(2)}) collective-permute-start(bf16[32,2048]{1,0:T(8,128)(2,1)S(1)} %get-tuple-element.13), channel_id=1, source_target_pairs={{0,2},{1,3},{2,4},{3,5},{4,6},{5,7},{6,0},{7,1},{8,10},{9,11},{10,... | collective-permute-start | bytes 393224 | tf_op jit(solution)/shard_map/ppermute | solution.py:190
  186.2 5.0 %collective-permute-start.6 = (bf16[32,2048]{1,0:T(8,128)(2,1)S(1)}, bf16[32,2048]{1,0:T(8,128)(2,1)S(1)}, u32[]{:S(2)}, u32[]{:S(2)}) collective-permute-start(bf16[32,2048]{1,0:T(8,128)(2,1)S(1)} %get-tuple-element.13), channel_id=1, source_target_pairs={{0,7},{1,0},{2,1},{3,2},{4,3},{5,4},{6,5},{7,6},{8,15},{9,8},{10,9... | collective-permute-start | bytes 393224 | tf_op jit(solution)/shard_map/ppermute | solution.py:190
  225.6 6.9 %collective-permute-start.7 = (bf16[32,2048]{1,0:T(8,128)(2,1)S(1)}, bf16[32,2048]{1,0:T(8,128)(2,1)S(1)}, u32[]{:S(2)}, u32[]{:S(2)}) collective-permute-start(bf16[32,2048]{1,0:T(8,128)(2,1)S(1)} %get-tuple-element.11), channel_id=1, source_target_pairs={{0,1},{1,2},{2,3},{3,4},{4,5},{5,6},{6,7},{7,0},{8,9},{9,10},{10,1... | collective-permute-start | bytes 393224 | tf_op jit(solution)/shard_map/ppermute | solution.py:190
  226.9 19.4 %collective-permute-start.12 = (bf16[32,2048]{1,0:T(8,128)(2,1)S(1)}, bf16[32,2048]{1,0:T(8,128)(2,1)S(1)}, u32[]{:S(2)}, u32[]{:S(2)}) collective-permute-start(bf16[32,2048]{1,0:T(8,128)(2,1)S(1)} %get-tuple-element.11), channel_id=1, source_target_pairs={{0,6},{1,7},{2,0},{3,1},{4,2},{5,3},{6,4},{7,5},{8,14},{9,15},{10,... | collective-permute-start | bytes 393224 | tf_op jit(solution)/shard_map/ppermute | solution.py:190
  229.2 16.4 %collective-permute-start.11 = (bf16[32,2048]{1,0:T(8,128)(2,1)S(1)}, bf16[32,2048]{1,0:T(8,128)(2,1)S(1)}, u32[]{:S(2)}, u32[]{:S(2)}) collective-permute-start(bf16[32,2048]{1,0:T(8,128)(2,1)S(1)} %get-tuple-element.11), channel_id=1, source_target_pairs={{0,5},{1,6},{2,7},{3,0},{4,1},{5,2},{6,3},{7,4},{8,13},{9,14},{10,... | collective-permute-start | bytes 393224 | tf_op jit(solution)/shard_map/ppermute | solution.py:190
  229.2 15.8 %collective-permute-start.10 = (bf16[32,2048]{1,0:T(8,128)(2,1)S(1)}, bf16[32,2048]{1,0:T(8,128)(2,1)S(1)}, u32[]{:S(2)}, u32[]{:S(2)}) collective-permute-start(bf16[32,2048]{1,0:T(8,128)(2,1)S(1)} %get-tuple-element.11), channel_id=1, source_target_pairs={{0,4},{1,5},{2,6},{3,7},{4,0},{5,1},{6,2},{7,3},{8,12},{9,13},{10,... | collective-permute-start | bytes 393224 | tf_op jit(solution)/shard_map/ppermute | solution.py:190
  230.1 14.2 %collective-permute-start.9 = (bf16[32,2048]{1,0:T(8,128)(2,1)S(1)}, bf16[32,2048]{1,0:T(8,128)(2,1)S(1)}, u32[]{:S(2)}, u32[]{:S(2)}) collective-permute-start(bf16[32,2048]{1,0:T(8,128)(2,1)S(1)} %get-tuple-element.11), channel_id=1, source_target_pairs={{0,3},{1,4},{2,5},{3,6},{4,7},{5,0},{6,1},{7,2},{8,11},{9,12},{10,... | collective-permute-start | bytes 393224 | tf_op jit(solution)/shard_map/ppermute | solution.py:190
  232.5 9.5 %collective-permute-start.8 = (bf16[32,2048]{1,0:T(8,128)(2,1)S(1)}, bf16[32,2048]{1,0:T(8,128)(2,1)S(1)}, u32[]{:S(2)}, u32[]{:S(2)}) collective-permute-start(bf16[32,2048]{1,0:T(8,128)(2,1)S(1)} %get-tuple-element.11), channel_id=1, source_target_pairs={{0,2},{1,3},{2,4},{3,5},{4,6},{5,7},{6,0},{7,1},{8,10},{9,11},{10,... | collective-permute-start | bytes 393224 | tf_op jit(solution)/shard_map/ppermute | solution.py:190
  242.0 5.0 %collective-permute-start.13 = (bf16[32,2048]{1,0:T(8,128)(2,1)S(1)}, bf16[32,2048]{1,0:T(8,128)(2,1)S(1)}, u32[]{:S(2)}, u32[]{:S(2)}) collective-permute-start(bf16[32,2048]{1,0:T(8,128)(2,1)S(1)} %get-tuple-element.11), channel_id=1, source_target_pairs={{0,7},{1,0},{2,1},{3,2},{4,3},{5,4},{6,5},{7,6},{8,15},{9,8},{10,9... | collective-permute-start | bytes 393224 | tf_op jit(solution)/shard_map/ppermute | solution.py:190
  (6 other events, 15.0 us)

commit v6 on v5

--- a/solution.py
+++ b/solution.py
@@ -87,7 +87,7 @@
 far_position = 1 << 30
 
 
-def held_block_kernel(slot_ref, alive_ref, q_ref, k0_ref, k1_ref, v0_ref, v1_ref, cos_ref, sin_ref, qpos_ref, kpos_ref, out_ref):
+def held_block_kernel(slot_ref, alive_ref, q_ref, k0_ref, k1_ref, v0_ref, v1_ref, cos_ref, sin_ref, qpos_ref, kpos_ref, out_ref, stat_ref):
     step = pl.program_id(0)
     key_refs = (k0_ref, k1_ref)
 
@@ -96,11 +96,11 @@
         chunks = rows // lanes
         lane = lax.broadcasted_iota(jnp.int32, (rows, lanes), 1)
         packed = jnp.where(lane == 0, peak, jnp.where(lane == 1, total, 0.0)).T
-        out_ref[0, :rows] = weighted
-        out_ref[0, rows:rows + chunks] = jnp.concatenate(
+        out_ref[0] = weighted.astype(out_ref.dtype)
+        stat_ref[0, 0:chunks] = jnp.concatenate(
             [packed[0:1, c * lanes:(c + 1) * lanes] for c in range(chunks)], axis=0
         )
-        out_ref[0, rows + chunks:rows + 2 * chunks] = jnp.concatenate(
+        stat_ref[0, chunks:2 * chunks] = jnp.concatenate(
             [packed[1:2, c * lanes:(c + 1) * lanes] for c in range(chunks)], axis=0
         )
     value_refs = (v0_ref, v1_ref)
@@ -139,10 +139,10 @@
     @pl.when(jnp.logical_not(live0) & jnp.logical_not(live1))
     def _():
         rows, lanes = q_ref.shape[1], q_ref.shape[2]
-        out_ref[0, :rows] = jnp.zeros((rows, lanes), jnp.float32)
+        out_ref[0] = jnp.zeros((rows, lanes), out_ref.dtype)
         chunks = rows // lanes
-        out_ref[0, rows:rows + chunks] = jnp.full((chunks, lanes), floor_score, jnp.float32)
-        out_ref[0, rows + chunks:rows + 2 * chunks] = jnp.zeros((chunks, lanes), jnp.float32)
+        stat_ref[0, 0:chunks] = jnp.full((chunks, lanes), floor_score, jnp.float32)
+        stat_ref[0, chunks:2 * chunks] = jnp.zeros((chunks, lanes), jnp.float32)
 
 
 def held_blocks(slots, alive, queries, key_pool, value_pool, cos_table, sin_table, query_pos, key_pos):
@@ -166,12 +166,18 @@
             pl.BlockSpec((1, rows, 1), lambda r, slot, alive: (r, 0, 0)),
             pl.BlockSpec((1, 2, 1, stretch), lambda r, slot, alive: (r, 0, 0, 0)),
         ],
-        out_specs=pl.BlockSpec((1, rows + 2 * rows // head_size, head_size), lambda r, slot, alive: (r, 0, 0)),
+        out_specs=[
+            pl.BlockSpec((1, rows, head_size), lambda r, slot, alive: (r, 0, 0)),
+            pl.BlockSpec((1, 2 * rows // head_size, head_size), lambda r, slot, alive: (r, 0, 0)),
+        ],
     )
     return pl.pallas_call(
         held_block_kernel,
         grid_spec=grid_spec,
-        out_shape=jax.ShapeDtypeStruct((requests, rows + 2 * rows // head_size, head_size), jnp.float32),
+        out_shape=[
+            jax.ShapeDtypeStruct((requests, rows, head_size), jnp.bfloat16),
+            jax.ShapeDtypeStruct((requests, 2 * rows // head_size, head_size), jnp.float32),
+        ],
         compiler_params=pltpu.CompilerParams(dimension_semantics=("arbitrary",)),
     )(slots, alive, queries, key_pool, key_pool, value_pool, value_pool, cos_table, sin_table, query_pos, key_pos)
 
@@ -274,16 +280,15 @@
         far_position,
     )[:, :, None, :]
     alive = (send_place < req_lengths[:, None]).reshape(request_count * pair_cap).astype(jnp.int32)
-    held = held_blocks(
+    held_sum, held_stats = held_blocks(
         slots, alive, all_queries, cached_key_pool, cached_value_pool, cos_table, sin_table, query_pos, key_pos
     )
-    got = lax.all_to_all(held, "req", 0, 0, tiled=False)
-    sum_rows = req_rows * groups
-    chunks = sum_rows // head_size
+    got_sum = lax.all_to_all(held_sum, "req", 0, 0, tiled=False).astype(jnp.float32)
+    got_stats = lax.all_to_all(held_stats, "req", 0, 0, tiled=False)
+    chunks = req_rows * groups // head_size
     head_total = key_heads * groups
-    got_sum = got[:, :sum_rows]
-    got_peak = got[:, sum_rows:sum_rows + chunks].reshape(req_count, count_of_rows, head_total)
-    got_total = got[:, sum_rows + chunks:].reshape(req_count, count_of_rows, head_total)
+    got_peak = got_stats[:, :chunks].reshape(req_count, count_of_rows, head_total)
+    got_total = got_stats[:, chunks:].reshape(req_count, count_of_rows, head_total)
     attended = merge_stats(
         jnp.concatenate([got_sum.reshape(req_count, count_of_rows, head_total, head_size), fresh_sum[None]]),
         jnp.concatenate([got_peak, fresh_peak[None]]),

time: 255 us -> 237 us (0.929)
  waiting for transfers between devices: 78.5 us -> 57.2 us
  starting transfers between devices: 44.8 us -> 48.6 us
  local copies, waits for them, and re-layouts: 44.4 us -> 41.6 us
    all_to_all x1 -> x2, waiting for transfers between devices: 41.4 us -> 22.1 us  [the longest x1 15.6 us: on_device(): lax.all_to_all(held_sum, 'req', 0, 0, tiled=False).astype(jnp.float32)]
    all_to_all x1 -> x2, starting transfers between devices: 5.37 us -> 10.1 us  [the longest x1 5.37 us: on_device(): got_stats = lax.all_to_all(held_stats, 'req', 0, 0, tiled=False)]
    reshape x0 -> x1, other arithmetic: none -> 3.48 us  [on_device(): got_sum.reshape(req_count, count_of_rows, head_total, head_size)]
    slice x3 -> x2, local copies, waits for them, and re-layouts: 2.91 us -> 0.28 us  [the longest x1 0.14 us: on_device(): got_stats[:, :chunks].reshape(req_count, count_of_rows, head_total)]
    unnamed x55 -> x59, local copies, waits for them, and re-layouts: 10.6 us -> 10.3 us
  transfers between devices with their start and end apart: 17 -> 18, of which waited for: 5 -> 6; matrix products, arithmetic and copies ran while one was open for 15% -> 17% of each run, Pallas kernels for 0% -> 0%
where the time goes in v6:
time: 237 us; the launch traced here: 235 us
  waiting for transfers between devices  57.2 us (24%)
  starting transfers between devices  48.6 us (21%)
  local copies, waits for them, and re-layouts  41.6 us (18%)
  other arithmetic  26.9 us (11%)
  Pallas kernels  23.3 us (10%)
  matrix products  18.9 us (8%)
  blocking collectives  18.5 us (8%)
    pallas_call x1, Pallas kernels, held_blocks(): pl.pallas_call(held_block_kernel, grid_spec=grid_spec, out_shape=[jax.Sha...  23.3 us
    ppermute x14, starting transfers between devices, gather_rows(): parts.append(lax.ppermute(rows, 'tp', pairs))  18.9 us
    all_to_all x1, blocking collectives, reduce_rows(): got = lax.all_to_all(blocks, 'tp', 0, 0, tiled=False)  18.5 us
    ppermute x14, waiting for transfers between devices, gather_rows(): parts.append(lax.ppermute(rows, 'tp', pairs))  15.9 us
    all_to_all x1, waiting for transfers between devices, on_device(): lax.all_to_all(held_sum, 'req', 0, 0, tiled=False).astype(jnp.float32)  15.6 us
    all_to_all x1, waiting for transfers between devices, reduce_rows(): got = lax.all_to_all(blocks, 'tp', 0, 0, tiled=False)  14.1 us
    all_to_all x1, starting transfers between devices, reduce_rows(): got = lax.all_to_all(blocks, 'tp', 0, 0, tiled=False)  10.8 us
    unnamed x59, local copies, waits for them, and re-layouts  10.3 us
  transfers between devices with their start and end apart: 18, of which 6 were waited for; matrix products, arithmetic and copies ran while one was open for 17% of the time, Pallas kernels for 0%

profile of v6, /device:TPU:1, one launch (start us, length us, event | category | flops | bytes accessed | tf_op | source)
XLA Modules:
  0.0 235.4 jit_solution(4922897100968308457)
XLA Ops:
  3.0 2.9 %multiply_reduce_fusion = (f32[256,2]{0,1:T(2,128)S(1)}, f32[256,256]{0,1:T(8,128)}) fusion(bf16[2048,256]{1,0:T(8,128)(2,1)} %param.28, bf16[256,2048]{1,0:T(8,128)(2,1)} %param.20, f32[2048]{0:T(1024)} %param.27, f32[256]{0:T(256)S(1)} %add_rsqrt_fusion.2), kind=kOutput, calls=%fused_computation.45 | convolution fusion | flops 270663168 | bytes 2370560 | tf_op jit(solution)/shard_map/dot_general | solution.py:235
  8.1 2.9 %broadcast_in_dim.71 = bf16[16,256,2,128]{3,2,1,0:T(2,128)(2,1)} broadcast(bf16[256,2,128]{2,1,0:T(2,128)(2,1)S(1)} %copy.97), dimensions={1,2,3} | broadcast | bytes 2228224 | tf_op jit(solution)/shard_map/broadcast_in_dim | solution.py:273
  11.1 8.8 %all-to-all-start = ((bf16[16,256,2,128]{3,2,1,0:T(2,128)(2,1)}), bf16[16,256,2,128]{3,2,1,0:T(2,128)(2,1)}, u32[]{:S(2)}, u32[]{:S(2)}) async-start(bf16[16,256,2,128]{3,2,1,0:T(2,128)(2,1)} %broadcast_in_dim.71), calls=%async_computation | async-start | bytes 4194304 | tf_op jit(solution)/shard_map/all_to_all | solution.py:274
  20.7 3.5 %gather_fusion.1 = s32[512]{0:T(512)S(1)} fusion(s32[512]{0:T(512)S(1)} %bitcast.107, s32[1024]{0:T(1024)S(1)} %pad_clamp_fusion.1), kind=kCustom, calls=%fused_computation.3 | custom fusion | bytes 6144 | tf_op jit(solution)/shard_map/gather | solution.py:256
  24.2 3.5 %gather_fusion = s32[512]{0:T(512)S(1)} fusion(s32[512]{0:T(512)S(1)} %bitcast.106, s32[1024]{0:T(1024)S(1)} %pad_clamp_fusion.1), kind=kCustom, calls=%fused_computation.2 | custom fusion | bytes 6144 | tf_op jit(solution)/shard_map/gather | solution.py:255
  32.3 4.9 %copy.103.qpos_ref = s32[16,512,1]{2,1,0:T(8,128)} copy(s32[16,512,1]{0,1,2:T(8,128)S(1)} %bitcast.111) | data formatting | bytes 65536 | tf_op jit(solution)/shard_map/broadcast_in_dim;reshape | solution.py:276
  40.8 2.0 multiply_reduce_fusion.1
  42.8 5.2 %all-to-all-done = bf16[16,256,2,128]{3,2,1,0:T(2,128)(2,1)} async-done(((bf16[16,256,2,128]{3,2,1,0:T(2,128)(2,1)}), bf16[16,256,2,128]{3,2,1,0:T(2,128)(2,1)}, u32[]{:S(2)}, u32[]{:S(2)}) %all-to-all-start) | async-done | bytes 2097184 | tf_op jit(solution)/shard_map/all_to_all | solution.py:274
  48.0 23.3 %shard_map.172 = (bf16[16,512,128]{2,1,0:T(8,128)(2,1)}, f32[16,8,128]{2,1,0:T(8,128)}) custom-call(s32[32]{0:T(128)} %min.12.slot_ref, s32[32]{0:T(128)} %reshape.373.alive_ref, bf16[16,512,128]{2,1,0:T(8,128)(2,1)} %bitcast.4.q_ref, bf16[32,512,128]{2,1,0:T(8,128)(2,1)} %k1_ref.1, bf16[32,512,128]{2,1,0:T(8,128)(2,1)} %k1_ref.1, ...), custom_call_target="tpu_custom_call" | custom-call | tf_op jit(solution)/shard_map/pallas_call | solution.py:174
  71.3 5.4 %all-to-all-start.2 = ((f32[16,8,128]{2,1,0:T(8,128)}), f32[16,8,128]{2,1,0:T(8,128)S(1)}, u32[]{:S(2)}, u32[]{:S(2)}) async-start(f32[16,8,128]{2,1,0:T(8,128)} %get-tuple-element.10), calls=%async_computation.2 | async-start | bytes 131072 | tf_op jit(solution)/shard_map/all_to_all | solution.py:287
  76.7 6.5 %all-to-all-done.2 = f32[16,8,128]{2,1,0:T(8,128)S(1)} async-done(((f32[16,8,128]{2,1,0:T(8,128)}), f32[16,8,128]{2,1,0:T(8,128)S(1)}, u32[]{:S(2)}, u32[]{:S(2)}) %all-to-all-start.2) | async-done | bytes 65568 | tf_op jit(solution)/shard_map/all_to_all | solution.py:287
  83.3 4.8 %all-to-all-start.1 = ((bf16[16,512,128]{2,1,0:T(8,128)(2,1)}), bf16[16,512,128]{2,1,0:T(8,128)(2,1)}, u32[]{:S(2)}, u32[]{:S(2)}) async-start(bf16[16,512,128]{2,1,0:T(8,128)(2,1)} %get-tuple-element.9), calls=%async_computation.1 | async-start | bytes 4194304 | tf_op jit(solution)/shard_map/all_to_all | solution.py:286
  89.7 2.2 convolution_bitcast_fusion
  95.0 2.1 copy.111
  97.1 15.6 %all-to-all-done.1 = bf16[16,512,128]{2,1,0:T(8,128)(2,1)} async-done(((bf16[16,512,128]{2,1,0:T(8,128)(2,1)}), bf16[16,512,128]{2,1,0:T(8,128)(2,1)}, u32[]{:S(2)}, u32[]{:S(2)}) %all-to-all-start.1) | async-done | bytes 2097184 | tf_op jit(solution)/shard_map/all_to_all | solution.py:286
  112.6 3.5 %convert.20 = f32[16,256,2,128]{3,2,1,0:T(2,128)S(1)} convert(bf16[16,256,2,128]{3,2,1,0:T(2,128)(2,1)} %bitcast.53) | non-fusion elementwise | flops 1048576 | bytes 6291456 | tf_op jit(solution)/shard_map/reshape | solution.py:293
  116.2 5.3 %fusion = f32[256,2,128]{2,1,0:T(2,128)S(1)} fusion(f32[1,256,2,128]{3,2,1,0:T(2,128)S(1)} %copy-done.4, f32[16,256,2,128]{3,2,1,0:T(2,128)S(1)} %convert.20, f32[17,256,2]{2,1,0:T(8,128)S(1)} %copy-done.1), kind=kLoop, calls=%fused_computation.5 | loop fusion | flops 3276800 | bytes 4753408 | tf_op jit(solution)/shard_map/reduce_sum | solution.py:75
  123.3 10.8 %all-to-all-start.3 = ((bf16[8,32,2048]{2,1,0:T(8,128)(2,1)}), bf16[8,32,2048]{2,1,0:T(8,128)(2,1)}, u32[]{:S(2)}, u32[]{:S(2)}) async-start(bf16[8,32,2048]{2,1,0:T(8,128)(2,1)} %bitcast.108), calls=%async_computation.3 | async-start | bytes 2097152 | tf_op jit(solution)/shard_map/all_to_all | solution.py:187
  135.1 14.1 %all-to-all-done.3 = bf16[8,32,2048]{2,1,0:T(8,128)(2,1)} async-done(((bf16[8,32,2048]{2,1,0:T(8,128)(2,1)}), bf16[8,32,2048]{2,1,0:T(8,128)(2,1)}, u32[]{:S(2)}, u32[]{:S(2)}) %all-to-all-start.3) | async-done | bytes 1048608 | tf_op jit(solution)/shard_map/all_to_all | solution.py:187
  153.6 2.5 %collective-permute-start.5 = (bf16[32,2048]{1,0:T(8,128)(2,1)S(1)}, bf16[32,2048]{1,0:T(8,128)(2,1)S(1)}, u32[]{:S(2)}, u32[]{:S(2)}) collective-permute-start(bf16[32,2048]{1,0:T(8,128)(2,1)S(1)} %get-tuple-element.17), channel_id=1, source_target_pairs={{0,6},{1,7},{2,0},{3,1},{4,2},{5,3},{6,4},{7,5},{8,14},{9,15},{10,... | collective-permute-start | bytes 393224 | tf_op jit(solution)/shard_map/ppermute | solution.py:196
  156.9 2.4 %collective-permute-start.2 = (bf16[32,2048]{1,0:T(8,128)(2,1)S(1)}, bf16[32,2048]{1,0:T(8,128)(2,1)S(1)}, u32[]{:S(2)}, u32[]{:S(2)}) collective-permute-start(bf16[32,2048]{1,0:T(8,128)(2,1)S(1)} %get-tuple-element.17), channel_id=1, source_target_pairs={{0,3},{1,4},{2,5},{3,6},{4,7},{5,0},{6,1},{7,2},{8,11},{9,12},{10,... | collective-permute-start | bytes 393224 | tf_op jit(solution)/shard_map/ppermute | solution.py:196
  160.9 7.9 %collective-permute-done.1 = bf16[32,2048]{1,0:T(8,128)(2,1)S(1)} collective-permute-done((bf16[32,2048]{1,0:T(8,128)(2,1)S(1)}, bf16[32,2048]{1,0:T(8,128)(2,1)S(1)}, u32[]{:S(2)}, u32[]{:S(2)}) %collective-permute-start.1) | collective-permute-done | bytes 131104 | tf_op jit(solution)/shard_map/ppermute | solution.py:196
  168.7 1.7 collective-permute-start.6
  174.5 2.8 %gather_fusion.2 = bf16[8,32,2048]{2,1,0:T(8,128)(2,1)} fusion(bf16[8,32,2048]{2,1,0:T(8,128)(2,1)} %bitcast_dynamic-update-slice_fusion.8, s32[1024]{0:T(1024)S(1)} %pad_clamp_fusion), kind=kCustom, calls=%fused_computation.clone | custom fusion | bytes 2097184 | tf_op jit(solution)/shard_map/jit(_take)/gather | solution.py:199
  179.6 3.8 %fusion.58 = f32[256,768]{1,0:T(8,128)} fusion(bf16[256,2048]{1,0:T(8,128)(2,1)S(1)} %bitcast.109, bf16[2048,768]{1,0:T(8,128)(2,1)} %param.35), kind=kOutput, calls=%fused_computation.139 | convolution fusion | flops 805306368 | bytes 4980736 | tf_op jit(solution)/shard_map/dot_general | solution.py:82
  183.4 5.5 %convolution_convert_fusion.1 = bf16[256,2048]{1,0:T(8,128)(2,1)} fusion(bf16[768,2048]{1,0:T(8,128)(2,1)S(1)} %copy-done, bf16[256,2048]{1,0:T(8,128)(2,1)} %bitcast.110, bf16[2048,768]{1,0:T(8,128)(2,1)} %param.36, f32[256,768]{1,0:T(8,128)} %fusion.58), kind=kOutput, calls=%fused_computation.9 | convolution fusion | flops 1612316672 | bytes 9175040 | tf_op jit(solution)/shard_map/dot_general | solution.py:306
  188.9 18.5 %all_to_all.25 = bf16[8,32,2048]{2,1,0:T(8,128)(2,1)S(1)} all-to-all(bf16[8,32,2048]{2,1,0:T(8,128)(2,1)} %bitcast.114), channel_id=1, replica_groups=mesh['req'=16,'tp'=8] {'tp'}, dimensions={0} | all-to-all | bytes 2097152 | tf_op jit(solution)/shard_map/all_to_all | solution.py:187
  209.5 2.3 collective-permute-start.12
  212.7 2.4 %collective-permute-start.9 = (bf16[32,2048]{1,0:T(8,128)(2,1)S(1)}, bf16[32,2048]{1,0:T(8,128)(2,1)S(1)}, u32[]{:S(2)}, u32[]{:S(2)}) collective-permute-start(bf16[32,2048]{1,0:T(8,128)(2,1)S(1)} %get-tuple-element.15), channel_id=1, source_target_pairs={{0,3},{1,4},{2,5},{3,6},{4,7},{5,0},{6,1},{7,2},{8,11},{9,12},{10,... | collective-permute-start | bytes 393224 | tf_op jit(solution)/shard_map/ppermute | solution.py:196
  216.6 8.0 %collective-permute-done.8 = bf16[32,2048]{1,0:T(8,128)(2,1)S(1)} collective-permute-done((bf16[32,2048]{1,0:T(8,128)(2,1)S(1)}, bf16[32,2048]{1,0:T(8,128)(2,1)S(1)}, u32[]{:S(2)}, u32[]{:S(2)}) %collective-permute-start.8) | collective-permute-done | bytes 131104 | tf_op jit(solution)/shard_map/ppermute | solution.py:196
  230.3 2.8 %gather_fusion.3 = bf16[8,32,2048]{2,1,0:T(8,128)(2,1)} fusion(bf16[8,32,2048]{2,1,0:T(8,128)(2,1)} %bitcast_dynamic-update-slice_fusion, s32[1024]{0:T(1024)S(1)} %pad_clamp_fusion), kind=kCustom, calls=%fused_computation.1.clone | custom fusion | bytes 2097184 | tf_op jit(solution)/shard_map/jit(_take)/gather | solution.py:199
  233.1 2.4 %broadcast_select_fusion.1 = bf16[8,32,2048]{2,1,0:T(8,128)(2,1)} fusion(bf16[8,32,2048]{2,1,0:T(8,128)(2,1)} %gather_fusion.3, pred[8]{0:T(512)(128)(4,1)S(1)} %compare_and_fusion.1), kind=kLoop, calls=%fused_computation.25 | loop fusion | flops 524288 | bytes 2097160 | tf_op jit(solution)/shard_map/jit(_take)/select_n | solution.py:199
  (152 shorter events, 45.0 us)
Async XLA Ops:
  0.0 183.4 %copy-start = (bf16[768,2048]{1,0:T(8,128)(2,1)S(1)}, bf16[768,2048]{1,0:T(8,128)(2,1)}, u32[]{:S(2)}) copy-start(bf16[768,2048]{1,0:T(8,128)(2,1)} %param.37) | copy-start | bytes 9437188
  0.0 7.0 %copy-start.14 = (f32[64]{0:T(128)}, f32[64]{0:T(128)S(1)}, u32[]{:S(2)}) copy-start(f32[64]{0:T(128)S(1)} %multiply_power_fusion) | copy-start | bytes 772
  1.4 5.6 %copy-start.10 = (f32[256]{0:T(256)}, f32[256]{0:T(256)S(1)}, u32[]{:S(2)}) copy-start(f32[256]{0:T(256)S(1)} %convert_element_type.91) | copy-start | bytes 3076
  1.4 6.1 %copy-start.19 = (f32[128]{0:T(128)S(1)}, f32[128]{0:T(128)}, u32[]{:S(2)}) copy-start(f32[128]{0:T(128)} %param.31) | copy-start | bytes 1540
  11.0 8.8 %copy-start.7 = (s32[16,256]{1,0:T(8,128)S(1)}, s32[16,256]{1,0:T(8,128)}, u32[]{:S(2)}) copy-start(s32[16,256]{1,0:T(8,128)} %param.21) | copy-start | bytes 49156
  11.0 9.5 %copy-start.16 = (s32[2,512]{1,0:T(2,128)S(1)}, s32[2,512]{1,0:T(2,128)}, u32[]{:S(2)}) copy-start(s32[2,512]{1,0:T(2,128)} %param.24) | copy-start | bytes 12292
  11.1 9.6 %copy-start.13 = (s32[16,32]{1,0:T(8,128)S(1)}, s32[16,32]{1,0:T(8,128)}, u32[]{:S(2)}) copy-start(s32[16,32]{1,0:T(8,128)} %param.23) | copy-start | bytes 6148
  11.1 37.0 %all-to-all-start = ((bf16[16,256,2,128]{3,2,1,0:T(2,128)(2,1)}), bf16[16,256,2,128]{3,2,1,0:T(2,128)(2,1)}, u32[]{:S(2)}, u32[]{:S(2)}) async-start(bf16[16,256,2,128]{3,2,1,0:T(2,128)(2,1)} %broadcast_in_dim.71), calls=%async_computation | async-start | bytes 4194304 | tf_op jit(solution)/shard_map/all_to_all | solution.py:274
  71.3 16.7 %copy-start.9 = (s32[1,256]{1,0:T(1,128)S(1)}, s32[1,256]{1,0:T(1,128)}, u32[]{:S(2)}) copy-start(s32[1,256]{1,0:T(1,128)} %copy-done.8) | copy-start | bytes 3076
  71.3 16.9 %copy-start.20 = (f32[128]{0:T(128)S(1)}, f32[128]{0:T(128)}, u32[]{:S(2)}) copy-start(f32[128]{0:T(128)} %param.32) | copy-start | bytes 1540
  71.3 11.9 %all-to-all-start.2 = ((f32[16,8,128]{2,1,0:T(8,128)}), f32[16,8,128]{2,1,0:T(8,128)S(1)}, u32[]{:S(2)}, u32[]{:S(2)}) async-start(f32[16,8,128]{2,1,0:T(8,128)} %get-tuple-element.10), calls=%async_computation.2 | async-start | bytes 131072 | tf_op jit(solution)/shard_map/all_to_all | solution.py:287
  83.3 5.1 %copy-start.15 = (f32[64]{0:T(128)S(1)}, f32[64]{0:T(128)}, u32[]{:S(2)}) copy-start(f32[64]{0:T(128)} %copy-done.14) | copy-start | bytes 772
  83.3 6.5 %copy-start.18 = (f32[256]{0:T(256)S(1)}, f32[256]{0:T(256)}, u32[]{:S(2)}) copy-start(f32[256]{0:T(256)} %copy-done.17) | copy-start | bytes 3076
  83.3 6.5 %copy-start.22 = (f32[2048]{0:T(1024)S(1)}, f32[2048]{0:T(1024)}, u32[]{:S(2)}) copy-start(f32[2048]{0:T(1024)} %param.27) | copy-start | bytes 24580
  83.3 29.4 %all-to-all-start.1 = ((bf16[16,512,128]{2,1,0:T(8,128)(2,1)}), bf16[16,512,128]{2,1,0:T(8,128)(2,1)}, u32[]{:S(2)}, u32[]{:S(2)}) async-start(bf16[16,512,128]{2,1,0:T(8,128)(2,1)} %get-tuple-element.9), calls=%async_computation.1 | async-start | bytes 4194304 | tf_op jit(solution)/shard_map/all_to_all | solution.py:286
  116.2 5.7 %copy-start.3 = (bf16[256,2048]{1,0:T(8,128)(2,1)S(1)}, bf16[256,2048]{1,0:T(8,128)(2,1)}, u32[]{:S(2)}) copy-start(bf16[256,2048]{1,0:T(8,128)(2,1)} %param.33) | copy-start | bytes 3145732
  123.3 28.3 %copy-start.12 = (f32[2048]{0:T(1024)S(1)}, f32[2048]{0:T(1024)}, u32[]{:S(2)}) copy-start(f32[2048]{0:T(1024)} %param.34) | copy-start | bytes 24580
  123.3 25.9 %all-to-all-start.3 = ((bf16[8,32,2048]{2,1,0:T(8,128)(2,1)}), bf16[8,32,2048]{2,1,0:T(8,128)(2,1)}, u32[]{:S(2)}, u32[]{:S(2)}) async-start(bf16[8,32,2048]{2,1,0:T(8,128)(2,1)} %bitcast.108), calls=%async_computation.3 | async-start | bytes 2097152 | tf_op jit(solution)/shard_map/all_to_all | solution.py:187
  152.4 6.9 %collective-permute-start = (bf16[32,2048]{1,0:T(8,128)(2,1)S(1)}, bf16[32,2048]{1,0:T(8,128)(2,1)S(1)}, u32[]{:S(2)}, u32[]{:S(2)}) collective-permute-start(bf16[32,2048]{1,0:T(8,128)(2,1)S(1)} %get-tuple-element.17), channel_id=1, source_target_pairs={{0,1},{1,2},{2,3},{3,4},{4,5},{5,6},{6,7},{7,0},{8,9},{9,10},{10,1... | collective-permute-start | bytes 393224 | tf_op jit(solution)/shard_map/ppermute | solution.py:196
  153.6 19.6 %collective-permute-start.5 = (bf16[32,2048]{1,0:T(8,128)(2,1)S(1)}, bf16[32,2048]{1,0:T(8,128)(2,1)S(1)}, u32[]{:S(2)}, u32[]{:S(2)}) collective-permute-start(bf16[32,2048]{1,0:T(8,128)(2,1)S(1)} %get-tuple-element.17), channel_id=1, source_target_pairs={{0,6},{1,7},{2,0},{3,1},{4,2},{5,3},{6,4},{7,5},{8,14},{9,15},{10,... | collective-permute-start | bytes 393224 | tf_op jit(solution)/shard_map/ppermute | solution.py:196
  156.0 16.4 %collective-permute-start.4 = (bf16[32,2048]{1,0:T(8,128)(2,1)S(1)}, bf16[32,2048]{1,0:T(8,128)(2,1)S(1)}, u32[]{:S(2)}, u32[]{:S(2)}) collective-permute-start(bf16[32,2048]{1,0:T(8,128)(2,1)S(1)} %get-tuple-element.17), channel_id=1, source_target_pairs={{0,5},{1,6},{2,7},{3,0},{4,1},{5,2},{6,3},{7,4},{8,13},{9,14},{10,... | collective-permute-start | bytes 393224 | tf_op jit(solution)/shard_map/ppermute | solution.py:196
  156.0 15.8 %collective-permute-start.3 = (bf16[32,2048]{1,0:T(8,128)(2,1)S(1)}, bf16[32,2048]{1,0:T(8,128)(2,1)S(1)}, u32[]{:S(2)}, u32[]{:S(2)}) collective-permute-start(bf16[32,2048]{1,0:T(8,128)(2,1)S(1)} %get-tuple-element.17), channel_id=1, source_target_pairs={{0,4},{1,5},{2,6},{3,7},{4,0},{5,1},{6,2},{7,3},{8,12},{9,13},{10,... | collective-permute-start | bytes 393224 | tf_op jit(solution)/shard_map/ppermute | solution.py:196
  156.9 14.2 %collective-permute-start.2 = (bf16[32,2048]{1,0:T(8,128)(2,1)S(1)}, bf16[32,2048]{1,0:T(8,128)(2,1)S(1)}, u32[]{:S(2)}, u32[]{:S(2)}) collective-permute-start(bf16[32,2048]{1,0:T(8,128)(2,1)S(1)} %get-tuple-element.17), channel_id=1, source_target_pairs={{0,3},{1,4},{2,5},{3,6},{4,7},{5,0},{6,1},{7,2},{8,11},{9,12},{10,... | collective-permute-start | bytes 393224 | tf_op jit(solution)/shard_map/ppermute | solution.py:196
  159.3 9.5 %collective-permute-start.1 = (bf16[32,2048]{1,0:T(8,128)(2,1)S(1)}, bf16[32,2048]{1,0:T(8,128)(2,1)S(1)}, u32[]{:S(2)}, u32[]{:S(2)}) collective-permute-start(bf16[32,2048]{1,0:T(8,128)(2,1)S(1)} %get-tuple-element.17), channel_id=1, source_target_pairs={{0,2},{1,3},{2,4},{3,5},{4,6},{5,7},{6,0},{7,1},{8,10},{9,11},{10,... | collective-permute-start | bytes 393224 | tf_op jit(solution)/shard_map/ppermute | solution.py:196
  168.7 5.0 %collective-permute-start.6 = (bf16[32,2048]{1,0:T(8,128)(2,1)S(1)}, bf16[32,2048]{1,0:T(8,128)(2,1)S(1)}, u32[]{:S(2)}, u32[]{:S(2)}) collective-permute-start(bf16[32,2048]{1,0:T(8,128)(2,1)S(1)} %get-tuple-element.17), channel_id=1, source_target_pairs={{0,7},{1,0},{2,1},{3,2},{4,3},{5,4},{6,5},{7,6},{8,15},{9,8},{10,9... | collective-permute-start | bytes 393224 | tf_op jit(solution)/shard_map/ppermute | solution.py:196
  208.2 6.9 %collective-permute-start.7 = (bf16[32,2048]{1,0:T(8,128)(2,1)S(1)}, bf16[32,2048]{1,0:T(8,128)(2,1)S(1)}, u32[]{:S(2)}, u32[]{:S(2)}) collective-permute-start(bf16[32,2048]{1,0:T(8,128)(2,1)S(1)} %get-tuple-element.15), channel_id=1, source_target_pairs={{0,1},{1,2},{2,3},{3,4},{4,5},{5,6},{6,7},{7,0},{8,9},{9,10},{10,1... | collective-permute-start | bytes 393224 | tf_op jit(solution)/shard_map/ppermute | solution.py:196
  209.5 19.4 %collective-permute-start.12 = (bf16[32,2048]{1,0:T(8,128)(2,1)S(1)}, bf16[32,2048]{1,0:T(8,128)(2,1)S(1)}, u32[]{:S(2)}, u32[]{:S(2)}) collective-permute-start(bf16[32,2048]{1,0:T(8,128)(2,1)S(1)} %get-tuple-element.15), channel_id=1, source_target_pairs={{0,6},{1,7},{2,0},{3,1},{4,2},{5,3},{6,4},{7,5},{8,14},{9,15},{10,... | collective-permute-start | bytes 393224 | tf_op jit(solution)/shard_map/ppermute | solution.py:196
  211.8 16.4 %collective-permute-start.11 = (bf16[32,2048]{1,0:T(8,128)(2,1)S(1)}, bf16[32,2048]{1,0:T(8,128)(2,1)S(1)}, u32[]{:S(2)}, u32[]{:S(2)}) collective-permute-start(bf16[32,2048]{1,0:T(8,128)(2,1)S(1)} %get-tuple-element.15), channel_id=1, source_target_pairs={{0,5},{1,6},{2,7},{3,0},{4,1},{5,2},{6,3},{7,4},{8,13},{9,14},{10,... | collective-permute-start | bytes 393224 | tf_op jit(solution)/shard_map/ppermute | solution.py:196
  211.8 15.8 %collective-permute-start.10 = (bf16[32,2048]{1,0:T(8,128)(2,1)S(1)}, bf16[32,2048]{1,0:T(8,128)(2,1)S(1)}, u32[]{:S(2)}, u32[]{:S(2)}) collective-permute-start(bf16[32,2048]{1,0:T(8,128)(2,1)S(1)} %get-tuple-element.15), channel_id=1, source_target_pairs={{0,4},{1,5},{2,6},{3,7},{4,0},{5,1},{6,2},{7,3},{8,12},{9,13},{10,... | collective-permute-start | bytes 393224 | tf_op jit(solution)/shard_map/ppermute | solution.py:196
  212.7 14.2 %collective-permute-start.9 = (bf16[32,2048]{1,0:T(8,128)(2,1)S(1)}, bf16[32,2048]{1,0:T(8,128)(2,1)S(1)}, u32[]{:S(2)}, u32[]{:S(2)}) collective-permute-start(bf16[32,2048]{1,0:T(8,128)(2,1)S(1)} %get-tuple-element.15), channel_id=1, source_target_pairs={{0,3},{1,4},{2,5},{3,6},{4,7},{5,0},{6,1},{7,2},{8,11},{9,12},{10,... | collective-permute-start | bytes 393224 | tf_op jit(solution)/shard_map/ppermute | solution.py:196
  215.1 9.5 %collective-permute-start.8 = (bf16[32,2048]{1,0:T(8,128)(2,1)S(1)}, bf16[32,2048]{1,0:T(8,128)(2,1)S(1)}, u32[]{:S(2)}, u32[]{:S(2)}) collective-permute-start(bf16[32,2048]{1,0:T(8,128)(2,1)S(1)} %get-tuple-element.15), channel_id=1, source_target_pairs={{0,2},{1,3},{2,4},{3,5},{4,6},{5,7},{6,0},{7,1},{8,10},{9,11},{10,... | collective-permute-start | bytes 393224 | tf_op jit(solution)/shard_map/ppermute | solution.py:196
  224.5 5.0 %collective-permute-start.13 = (bf16[32,2048]{1,0:T(8,128)(2,1)S(1)}, bf16[32,2048]{1,0:T(8,128)(2,1)S(1)}, u32[]{:S(2)}, u32[]{:S(2)}) collective-permute-start(bf16[32,2048]{1,0:T(8,128)(2,1)S(1)} %get-tuple-element.15), channel_id=1, source_target_pairs={{0,7},{1,0},{2,1},{3,2},{4,3},{5,4},{6,5},{7,6},{8,15},{9,8},{10,9... | collective-permute-start | bytes 393224 | tf_op jit(solution)/shard_map/ppermute | solution.py:196
  (9 other events, 30.3 us)

commit v7 on v5

--- a/solution.py
+++ b/solution.py
@@ -91,18 +91,28 @@
     step = pl.program_id(0)
     key_refs = (k0_ref, k1_ref)
 
+    def store_stats(peak_rows, total_rows):
+        pieces = []
+        for value in (peak_rows, total_rows):
+            rest = value
+            for _ in range(3):
+                piece = rest.astype(jnp.bfloat16).astype(jnp.float32)
+                pieces.append(piece)
+                rest = rest - piece
+        rows = q_ref.shape[1]
+        spare = out_ref.shape[1] - rows - 6 * peak_rows.shape[0]
+        pieces.append(jnp.zeros((spare, peak_rows.shape[1]), jnp.float32))
+        out_ref[0, rows:] = jnp.concatenate(pieces, axis=0).astype(out_ref.dtype)
+
     def store(weighted, peak, total):
         rows, lanes = weighted.shape
         chunks = rows // lanes
         lane = lax.broadcasted_iota(jnp.int32, (rows, lanes), 1)
         packed = jnp.where(lane == 0, peak, jnp.where(lane == 1, total, 0.0)).T
-        out_ref[0, :rows] = weighted
-        out_ref[0, rows:rows + chunks] = jnp.concatenate(
-            [packed[0:1, c * lanes:(c + 1) * lanes] for c in range(chunks)], axis=0
-        )
-        out_ref[0, rows + chunks:rows + 2 * chunks] = jnp.concatenate(
-            [packed[1:2, c * lanes:(c + 1) * lanes] for c in range(chunks)], axis=0
-        )
+        out_ref[0, :rows] = weighted.astype(out_ref.dtype)
+        peak_rows = jnp.concatenate([packed[0:1, c * lanes:(c + 1) * lanes] for c in range(chunks)], axis=0)
+        total_rows = jnp.concatenate([packed[1:2, c * lanes:(c + 1) * lanes] for c in range(chunks)], axis=0)
+        store_stats(peak_rows, total_rows)
     value_refs = (v0_ref, v1_ref)
 
     def run(parts):
@@ -139,15 +149,15 @@
     @pl.when(jnp.logical_not(live0) & jnp.logical_not(live1))
     def _():
         rows, lanes = q_ref.shape[1], q_ref.shape[2]
-        out_ref[0, :rows] = jnp.zeros((rows, lanes), jnp.float32)
+        out_ref[0, :rows] = jnp.zeros((rows, lanes), out_ref.dtype)
         chunks = rows // lanes
-        out_ref[0, rows:rows + chunks] = jnp.full((chunks, lanes), floor_score, jnp.float32)
-        out_ref[0, rows + chunks:rows + 2 * chunks] = jnp.zeros((chunks, lanes), jnp.float32)
+        store_stats(jnp.full((chunks, lanes), floor_score, jnp.float32), jnp.zeros((chunks, lanes), jnp.float32))
 
 
 def held_blocks(slots, alive, queries, key_pool, value_pool, cos_table, sin_table, query_pos, key_pos):
     requests, rows, head_size = queries.shape
     stretch = key_pool.shape[1]
+    stat_rows = -(-6 * rows // head_size // 16) * 16
 
     def pool_spec(j):
         return pl.BlockSpec((1, stretch, head_size), lambda r, slot, alive: (slot[2 * r + j], 0, 0))
@@ -166,12 +176,12 @@
             pl.BlockSpec((1, rows, 1), lambda r, slot, alive: (r, 0, 0)),
             pl.BlockSpec((1, 2, 1, stretch), lambda r, slot, alive: (r, 0, 0, 0)),
         ],
-        out_specs=pl.BlockSpec((1, rows + 2 * rows // head_size, head_size), lambda r, slot, alive: (r, 0, 0)),
+        out_specs=pl.BlockSpec((1, rows + stat_rows, head_size), lambda r, slot, alive: (r, 0, 0)),
     )
     return pl.pallas_call(
         held_block_kernel,
         grid_spec=grid_spec,
-        out_shape=jax.ShapeDtypeStruct((requests, rows + 2 * rows // head_size, head_size), jnp.float32),
+        out_shape=jax.ShapeDtypeStruct((requests, rows + stat_rows, head_size), jnp.bfloat16),
         compiler_params=pltpu.CompilerParams(dimension_semantics=("arbitrary",)),
     )(slots, alive, queries, key_pool, key_pool, value_pool, value_pool, cos_table, sin_table, query_pos, key_pos)
 
@@ -281,9 +291,15 @@
     sum_rows = req_rows * groups
     chunks = sum_rows // head_size
     head_total = key_heads * groups
-    got_sum = got[:, :sum_rows]
-    got_peak = got[:, sum_rows:sum_rows + chunks].reshape(req_count, count_of_rows, head_total)
-    got_total = got[:, sum_rows + chunks:].reshape(req_count, count_of_rows, head_total)
+    got_sum = got[:, :sum_rows].astype(jnp.float32)
+
+    def stat_of(k):
+        base = sum_rows + 3 * k * chunks
+        hi, mid, lo = (got[:, base + i * chunks:base + (i + 1) * chunks].astype(jnp.float32) for i in range(3))
+        return ((hi + mid) + lo).reshape(req_count, count_of_rows, head_total)
+
+    got_peak = stat_of(0)
+    got_total = stat_of(1)
     attended = merge_stats(
         jnp.concatenate([got_sum.reshape(req_count, count_of_rows, head_total, head_size), fresh_sum[None]]),
         jnp.concatenate([got_peak, fresh_peak[None]]),

time: 255 us -> 235 us (0.922)
  waiting for transfers between devices: 78.5 us -> 56.1 us
  other arithmetic: 24.4 us -> 30 us
    all_to_all x1, waiting for transfers between devices: 41.4 us -> 18.8 us  [on_device(): got = lax.all_to_all(held, 'req', 0, 0, tiled=False)]
    reshape x0 -> x1, other arithmetic: none -> 3.69 us  [on_device(): got_sum.reshape(req_count, count_of_rows, head_total, head_size)]
    unnamed x55 -> x53, local copies, waits for them, and re-layouts: 10.6 us -> 10.3 us
  transfers between devices with their start and end apart: 17 -> 17, of which waited for: 5 -> 5; matrix products, arithmetic and copies ran while one was open for 15% -> 16% of each run, Pallas kernels for 0% -> 0%
where the time goes in v7:
time: 235 us
  waiting for transfers between devices  56.1 us (24%)
  local copies, waits for them, and re-layouts  44 us (19%)
  starting transfers between devices  43 us (18%)
  other arithmetic  30 us (13%)
  Pallas kernels  24 us (10%)
  matrix products  18.8 us (8%)
  blocking collectives  18.5 us (8%)
    pallas_call x1, Pallas kernels, held_blocks(): pl.pallas_call(held_block_kernel, grid_spec=grid_spec, out_shape=jax.Shap...  24 us
    ppermute x14, starting transfers between devices, gather_rows(): parts.append(lax.ppermute(rows, 'tp', pairs))  18.9 us
    all_to_all x1, waiting for transfers between devices, on_device(): got = lax.all_to_all(held, 'req', 0, 0, tiled=False)  18.8 us
    all_to_all x1, blocking collectives, reduce_rows(): got = lax.all_to_all(blocks, 'tp', 0, 0, tiled=False)  18.5 us
    ppermute x14, waiting for transfers between devices, gather_rows(): parts.append(lax.ppermute(rows, 'tp', pairs))  15.9 us
    all_to_all x1, waiting for transfers between devices, reduce_rows(): got = lax.all_to_all(blocks, 'tp', 0, 0, tiled=False)  14.1 us
    unnamed x53, local copies, waits for them, and re-layouts  10.3 us
    all_to_all x1, starting transfers between devices, reduce_rows(): got = lax.all_to_all(blocks, 'tp', 0, 0, tiled=False)  10.1 us
  transfers between devices with their start and end apart: 17, of which 5 were waited for; matrix products, arithmetic and copies ran while one was open for 16% of the time, Pallas kernels for 0%

profile of v7, /device:TPU:1, one launch (start us, length us, event | category | flops | bytes accessed | tf_op | source)
XLA Modules:
  0.0 234.9 jit_solution(16707988945431449089)
XLA Ops:
  3.0 2.9 %multiply_reduce_fusion = (f32[256,2]{0,1:T(2,128)S(1)}, f32[256,256]{0,1:T(8,128)}) fusion(bf16[2048,256]{1,0:T(8,128)(2,1)} %param.28, bf16[256,2048]{1,0:T(8,128)(2,1)} %param.20, f32[2048]{0:T(1024)} %param.27, f32[256]{0:T(256)S(1)} %add_rsqrt_fusion.2), kind=kOutput, calls=%fused_computation.45 | convolution fusion | flops 270663168 | bytes 2370560 | tf_op jit(solution)/shard_map/dot_general | solution.py:239
  8.1 2.9 %broadcast_in_dim.71 = bf16[16,256,2,128]{3,2,1,0:T(2,128)(2,1)} broadcast(bf16[256,2,128]{2,1,0:T(2,128)(2,1)S(1)} %copy.97), dimensions={1,2,3} | broadcast | bytes 2228224 | tf_op jit(solution)/shard_map/broadcast_in_dim | solution.py:277
  11.1 8.8 %all-to-all-start = ((bf16[16,256,2,128]{3,2,1,0:T(2,128)(2,1)}), bf16[16,256,2,128]{3,2,1,0:T(2,128)(2,1)}, u32[]{:S(2)}, u32[]{:S(2)}) async-start(bf16[16,256,2,128]{3,2,1,0:T(2,128)(2,1)} %broadcast_in_dim.71), calls=%async_computation | async-start | bytes 4194304 | tf_op jit(solution)/shard_map/all_to_all | solution.py:278
  20.7 3.5 %gather_fusion.1 = s32[512]{0:T(512)S(1)} fusion(s32[512]{0:T(512)S(1)} %bitcast.107, s32[1024]{0:T(1024)S(1)} %pad_clamp_fusion.1), kind=kCustom, calls=%fused_computation.3 | custom fusion | bytes 6144 | tf_op jit(solution)/shard_map/gather | solution.py:260
  24.2 3.5 %gather_fusion = s32[512]{0:T(512)S(1)} fusion(s32[512]{0:T(512)S(1)} %bitcast.106, s32[1024]{0:T(1024)S(1)} %pad_clamp_fusion.1), kind=kCustom, calls=%fused_computation.2 | custom fusion | bytes 6144 | tf_op jit(solution)/shard_map/gather | solution.py:259
  32.2 4.8 %copy.103.qpos_ref = s32[16,512,1]{2,1,0:T(8,128)} copy(s32[16,512,1]{0,1,2:T(8,128)S(1)} %bitcast.112) | data formatting | bytes 65536 | tf_op jit(solution)/shard_map/broadcast_in_dim;reshape | solution.py:280
  40.8 7.3 %all-to-all-done = bf16[16,256,2,128]{3,2,1,0:T(2,128)(2,1)} async-done(((bf16[16,256,2,128]{3,2,1,0:T(2,128)(2,1)}), bf16[16,256,2,128]{3,2,1,0:T(2,128)(2,1)}, u32[]{:S(2)}, u32[]{:S(2)}) %all-to-all-start) | async-done | bytes 2097184 | tf_op jit(solution)/shard_map/all_to_all | solution.py:278
  48.1 24.0 %shard_map.172 = bf16[16,544,128]{2,1,0:T(8,128)(2,1)} custom-call(s32[32]{0:T(128)} %min.12.slot_ref, s32[32]{0:T(128)} %reshape.373.alive_ref, bf16[16,512,128]{2,1,0:T(8,128)(2,1)} %bitcast.4.q_ref, bf16[32,512,128]{2,1,0:T(8,128)(2,1)} %k1_ref.1, bf16[32,512,128]{2,1,0:T(8,128)(2,1)} %k1_ref.1, bf16[32,512,128]{2,1,0:T(8,128)(2,1)} %v1_ref.1, ...), custom_call_target="tpu_custom_call" | custom-call | tf_op jit(solution)/shard_map/pallas_call | solution.py:181
  72.1 5.3 %all-to-all-start.1 = ((bf16[16,544,128]{2,1,0:T(8,128)(2,1)}), bf16[16,544,128]{2,1,0:T(8,128)(2,1)}, u32[]{:S(2)}, u32[]{:S(2)}) async-start(bf16[16,544,128]{2,1,0:T(8,128)(2,1)} %shard_map.172), calls=%async_computation.1 | async-start | bytes 4456448 | tf_op jit(solution)/shard_map/all_to_all | solution.py:290
  77.5 1.9 multiply_reduce_fusion.1
  81.1 2.2 convolution_bitcast_fusion
  85.3 18.8 %all-to-all-done.1 = bf16[16,544,128]{2,1,0:T(8,128)(2,1)} async-done(((bf16[16,544,128]{2,1,0:T(8,128)(2,1)}), bf16[16,544,128]{2,1,0:T(8,128)(2,1)}, u32[]{:S(2)}, u32[]{:S(2)}) %all-to-all-start.1) | async-done | bytes 2228256 | tf_op jit(solution)/shard_map/all_to_all | solution.py:290
  106.6 1.8 slice.62
  108.4 3.7 %convert.20 = f32[16,256,2,128]{3,2,1,0:T(2,128)} convert(bf16[16,256,2,128]{3,2,1,0:T(2,128)(2,1)S(1)} %bitcast.108) | non-fusion elementwise | flops 1048576 | bytes 6291456 | tf_op jit(solution)/shard_map/reshape | solution.py:304
  112.1 2.8 %copy.111 = f32[17,256,2]{2,1,0:T(8,128)} copy(f32[17,256,2]{1,2,0:T(2,128)} %get-tuple-element.17) | data formatting | bytes 69632 | tf_op jit(solution)/shard_map/exp | solution.py:74
  114.9 6.8 %fusion = f32[256,2,128]{2,1,0:T(2,128)S(1)} fusion(f32[1,256,2,128]{3,2,1,0:T(2,128)S(1)} %copy-done.3, f32[16,256,2,128]{3,2,1,0:T(2,128)} %convert.20, f32[17,256,2]{2,1,0:T(8,128)} %copy.111), kind=kLoop, calls=%fused_computation.5 | loop fusion | flops 3276800 | bytes 4753408 | tf_op jit(solution)/shard_map/reduce_sum | solution.py:75
  123.5 10.1 %all-to-all-start.2 = ((bf16[8,32,2048]{2,1,0:T(8,128)(2,1)}), bf16[8,32,2048]{2,1,0:T(8,128)(2,1)}, u32[]{:S(2)}, u32[]{:S(2)}) async-start(bf16[8,32,2048]{2,1,0:T(8,128)(2,1)} %bitcast.109), calls=%async_computation.2 | async-start | bytes 2097152 | tf_op jit(solution)/shard_map/all_to_all | solution.py:191
  134.5 14.1 %all-to-all-done.2 = bf16[8,32,2048]{2,1,0:T(8,128)(2,1)} async-done(((bf16[8,32,2048]{2,1,0:T(8,128)(2,1)}), bf16[8,32,2048]{2,1,0:T(8,128)(2,1)}, u32[]{:S(2)}, u32[]{:S(2)}) %all-to-all-start.2) | async-done | bytes 1048608 | tf_op jit(solution)/shard_map/all_to_all | solution.py:191
  153.0 2.5 %collective-permute-start.5 = (bf16[32,2048]{1,0:T(8,128)(2,1)S(1)}, bf16[32,2048]{1,0:T(8,128)(2,1)S(1)}, u32[]{:S(2)}, u32[]{:S(2)}) collective-permute-start(bf16[32,2048]{1,0:T(8,128)(2,1)S(1)} %get-tuple-element.13), channel_id=1, source_target_pairs={{0,6},{1,7},{2,0},{3,1},{4,2},{5,3},{6,4},{7,5},{8,14},{9,15},{10,... | collective-permute-start | bytes 393224 | tf_op jit(solution)/shard_map/ppermute | solution.py:200
  156.3 2.4 %collective-permute-start.2 = (bf16[32,2048]{1,0:T(8,128)(2,1)S(1)}, bf16[32,2048]{1,0:T(8,128)(2,1)S(1)}, u32[]{:S(2)}, u32[]{:S(2)}) collective-permute-start(bf16[32,2048]{1,0:T(8,128)(2,1)S(1)} %get-tuple-element.13), channel_id=1, source_target_pairs={{0,3},{1,4},{2,5},{3,6},{4,7},{5,0},{6,1},{7,2},{8,11},{9,12},{10,... | collective-permute-start | bytes 393224 | tf_op jit(solution)/shard_map/ppermute | solution.py:200
  160.3 7.9 %collective-permute-done.1 = bf16[32,2048]{1,0:T(8,128)(2,1)S(1)} collective-permute-done((bf16[32,2048]{1,0:T(8,128)(2,1)S(1)}, bf16[32,2048]{1,0:T(8,128)(2,1)S(1)}, u32[]{:S(2)}, u32[]{:S(2)}) %collective-permute-start.1) | collective-permute-done | bytes 131104 | tf_op jit(solution)/shard_map/ppermute | solution.py:200
  168.2 1.7 collective-permute-start.6
  173.9 2.8 %gather_fusion.2 = bf16[8,32,2048]{2,1,0:T(8,128)(2,1)} fusion(bf16[8,32,2048]{2,1,0:T(8,128)(2,1)} %bitcast_dynamic-update-slice_fusion.8, s32[1024]{0:T(1024)S(1)} %pad_clamp_fusion), kind=kCustom, calls=%fused_computation.clone | custom fusion | bytes 2097184 | tf_op jit(solution)/shard_map/jit(_take)/gather | solution.py:203
  179.1 3.8 %fusion.58 = f32[256,768]{1,0:T(8,128)} fusion(bf16[256,2048]{1,0:T(8,128)(2,1)S(1)} %bitcast.110, bf16[2048,768]{1,0:T(8,128)(2,1)} %param.35), kind=kOutput, calls=%fused_computation.140 | convolution fusion | flops 805306368 | bytes 4980736 | tf_op jit(solution)/shard_map/dot_general | solution.py:82
  182.9 5.5 %convolution_convert_fusion.1 = bf16[256,2048]{1,0:T(8,128)(2,1)} fusion(bf16[768,2048]{1,0:T(8,128)(2,1)S(1)} %copy-done, bf16[256,2048]{1,0:T(8,128)(2,1)} %bitcast.111, bf16[2048,768]{1,0:T(8,128)(2,1)} %param.36, f32[256,768]{1,0:T(8,128)} %fusion.58), kind=kOutput, calls=%fused_computation.9 | convolution fusion | flops 1612316672 | bytes 9175040 | tf_op jit(solution)/shard_map/dot_general | solution.py:317
  188.3 18.5 %all_to_all.20 = bf16[8,32,2048]{2,1,0:T(8,128)(2,1)S(1)} all-to-all(bf16[8,32,2048]{2,1,0:T(8,128)(2,1)} %bitcast.115), channel_id=1, replica_groups=mesh['req'=16,'tp'=8] {'tp'}, dimensions={0} | all-to-all | bytes 2097152 | tf_op jit(solution)/shard_map/all_to_all | solution.py:191
  208.9 2.3 collective-permute-start.12
  212.1 2.4 %collective-permute-start.9 = (bf16[32,2048]{1,0:T(8,128)(2,1)S(1)}, bf16[32,2048]{1,0:T(8,128)(2,1)S(1)}, u32[]{:S(2)}, u32[]{:S(2)}) collective-permute-start(bf16[32,2048]{1,0:T(8,128)(2,1)S(1)} %get-tuple-element.11), channel_id=1, source_target_pairs={{0,3},{1,4},{2,5},{3,6},{4,7},{5,0},{6,1},{7,2},{8,11},{9,12},{10,... | collective-permute-start | bytes 393224 | tf_op jit(solution)/shard_map/ppermute | solution.py:200
  216.0 8.0 %collective-permute-done.8 = bf16[32,2048]{1,0:T(8,128)(2,1)S(1)} collective-permute-done((bf16[32,2048]{1,0:T(8,128)(2,1)S(1)}, bf16[32,2048]{1,0:T(8,128)(2,1)S(1)}, u32[]{:S(2)}, u32[]{:S(2)}) %collective-permute-start.8) | collective-permute-done | bytes 131104 | tf_op jit(solution)/shard_map/ppermute | solution.py:200
  224.0 1.7 collective-permute-start.13
  229.7 2.8 %gather_fusion.3 = bf16[8,32,2048]{2,1,0:T(8,128)(2,1)} fusion(bf16[8,32,2048]{2,1,0:T(8,128)(2,1)} %bitcast_dynamic-update-slice_fusion, s32[1024]{0:T(1024)S(1)} %pad_clamp_fusion), kind=kCustom, calls=%fused_computation.1.clone | custom fusion | bytes 2097184 | tf_op jit(solution)/shard_map/jit(_take)/gather | solution.py:203
  232.5 2.4 %broadcast_select_fusion.1 = bf16[8,32,2048]{2,1,0:T(8,128)(2,1)} fusion(bf16[8,32,2048]{2,1,0:T(8,128)(2,1)} %gather_fusion.3, pred[8]{0:T(512)(128)(4,1)S(1)} %compare_and_fusion.1), kind=kLoop, calls=%fused_computation.25 | loop fusion | flops 524288 | bytes 2097160 | tf_op jit(solution)/shard_map/jit(_take)/select_n | solution.py:203
  (145 shorter events, 44.6 us)
Async XLA Ops:
  0.0 182.9 %copy-start = (bf16[768,2048]{1,0:T(8,128)(2,1)S(1)}, bf16[768,2048]{1,0:T(8,128)(2,1)}, u32[]{:S(2)}) copy-start(bf16[768,2048]{1,0:T(8,128)(2,1)} %param.37) | copy-start | bytes 9437188
  0.0 7.0 %copy-start.11 = (f32[64]{0:T(128)}, f32[64]{0:T(128)S(1)}, u32[]{:S(2)}) copy-start(f32[64]{0:T(128)S(1)} %multiply_power_fusion) | copy-start | bytes 772
  1.5 5.6 %copy-start.7 = (f32[256]{0:T(256)}, f32[256]{0:T(256)S(1)}, u32[]{:S(2)}) copy-start(f32[256]{0:T(256)S(1)} %convert_element_type.109) | copy-start | bytes 3076
  1.5 6.1 %copy-start.16 = (f32[128]{0:T(128)S(1)}, f32[128]{0:T(128)}, u32[]{:S(2)}) copy-start(f32[128]{0:T(128)} %param.31) | copy-start | bytes 1540
  3.0 2.9 %copy-start.14 = (f32[256]{0:T(256)}, f32[256]{0:T(256)S(1)}, u32[]{:S(2)}) copy-start(f32[256]{0:T(256)S(1)} %add_rsqrt_fusion.2) | copy-start | bytes 3076
  11.1 8.8 %copy-start.10 = (s32[16,32]{1,0:T(8,128)S(1)}, s32[16,32]{1,0:T(8,128)}, u32[]{:S(2)}) copy-start(s32[16,32]{1,0:T(8,128)} %param.23) | copy-start | bytes 6148
  11.1 8.9 %copy-start.4 = (s32[16,256]{1,0:T(8,128)S(1)}, s32[16,256]{1,0:T(8,128)}, u32[]{:S(2)}) copy-start(s32[16,256]{1,0:T(8,128)} %param.21) | copy-start | bytes 49156
  11.1 9.7 %copy-start.13 = (s32[2,512]{1,0:T(2,128)S(1)}, s32[2,512]{1,0:T(2,128)}, u32[]{:S(2)}) copy-start(s32[2,512]{1,0:T(2,128)} %param.24) | copy-start | bytes 12292
  11.1 37.0 %all-to-all-start = ((bf16[16,256,2,128]{3,2,1,0:T(2,128)(2,1)}), bf16[16,256,2,128]{3,2,1,0:T(2,128)(2,1)}, u32[]{:S(2)}, u32[]{:S(2)}) async-start(bf16[16,256,2,128]{3,2,1,0:T(2,128)(2,1)} %broadcast_in_dim.71), calls=%async_computation | async-start | bytes 4194304 | tf_op jit(solution)/shard_map/all_to_all | solution.py:278
  24.2 4.7 %copy-start.18 = (s32[16]{0:T(128)S(1)}, s32[16]{0:T(128)}, u32[]{:S(2)}) copy-start(s32[16]{0:T(128)} %param.22) | copy-start | bytes 196
  72.1 5.4 %copy-start.15 = (f32[256]{0:T(256)S(1)}, f32[256]{0:T(256)}, u32[]{:S(2)}) copy-start(f32[256]{0:T(256)} %copy-done.14) | copy-start | bytes 3076
  72.1 5.4 %copy-start.19 = (f32[2048]{0:T(1024)S(1)}, f32[2048]{0:T(1024)}, u32[]{:S(2)}) copy-start(f32[2048]{0:T(1024)} %param.27) | copy-start | bytes 24580
  72.1 32.0 %all-to-all-start.1 = ((bf16[16,544,128]{2,1,0:T(8,128)(2,1)}), bf16[16,544,128]{2,1,0:T(8,128)(2,1)}, u32[]{:S(2)}, u32[]{:S(2)}) async-start(bf16[16,544,128]{2,1,0:T(8,128)(2,1)} %shard_map.172), calls=%async_computation.1 | async-start | bytes 4456448 | tf_op jit(solution)/shard_map/all_to_all | solution.py:290
  77.4 2.3 copy-start.8
  112.1 2.9 %copy-start.3 = (f32[1,256,2,128]{3,2,1,0:T(2,128)S(1)}, f32[1,256,2,128]{3,2,1,0:T(2,128)}, u32[]{:S(2)}) copy-start(f32[1,256,2,128]{3,2,1,0:T(2,128)} %copy.107) | copy-start | bytes 786436
  114.9 7.1 %copy-start.2 = (bf16[256,2048]{1,0:T(8,128)(2,1)S(1)}, bf16[256,2048]{1,0:T(8,128)(2,1)}, u32[]{:S(2)}) copy-start(bf16[256,2048]{1,0:T(8,128)(2,1)} %param.33) | copy-start | bytes 3145732
  123.5 27.6 %copy-start.9 = (f32[2048]{0:T(1024)S(1)}, f32[2048]{0:T(1024)}, u32[]{:S(2)}) copy-start(f32[2048]{0:T(1024)} %param.34) | copy-start | bytes 24580
  123.5 25.1 %all-to-all-start.2 = ((bf16[8,32,2048]{2,1,0:T(8,128)(2,1)}), bf16[8,32,2048]{2,1,0:T(8,128)(2,1)}, u32[]{:S(2)}, u32[]{:S(2)}) async-start(bf16[8,32,2048]{2,1,0:T(8,128)(2,1)} %bitcast.109), calls=%async_computation.2 | async-start | bytes 2097152 | tf_op jit(solution)/shard_map/all_to_all | solution.py:191
  151.9 6.9 %collective-permute-start = (bf16[32,2048]{1,0:T(8,128)(2,1)S(1)}, bf16[32,2048]{1,0:T(8,128)(2,1)S(1)}, u32[]{:S(2)}, u32[]{:S(2)}) collective-permute-start(bf16[32,2048]{1,0:T(8,128)(2,1)S(1)} %get-tuple-element.13), channel_id=1, source_target_pairs={{0,1},{1,2},{2,3},{3,4},{4,5},{5,6},{6,7},{7,0},{8,9},{9,10},{10,1... | collective-permute-start | bytes 393224 | tf_op jit(solution)/shard_map/ppermute | solution.py:200
  153.0 19.6 %collective-permute-start.5 = (bf16[32,2048]{1,0:T(8,128)(2,1)S(1)}, bf16[32,2048]{1,0:T(8,128)(2,1)S(1)}, u32[]{:S(2)}, u32[]{:S(2)}) collective-permute-start(bf16[32,2048]{1,0:T(8,128)(2,1)S(1)} %get-tuple-element.13), channel_id=1, source_target_pairs={{0,6},{1,7},{2,0},{3,1},{4,2},{5,3},{6,4},{7,5},{8,14},{9,15},{10,... | collective-permute-start | bytes 393224 | tf_op jit(solution)/shard_map/ppermute | solution.py:200
  155.5 16.4 %collective-permute-start.4 = (bf16[32,2048]{1,0:T(8,128)(2,1)S(1)}, bf16[32,2048]{1,0:T(8,128)(2,1)S(1)}, u32[]{:S(2)}, u32[]{:S(2)}) collective-permute-start(bf16[32,2048]{1,0:T(8,128)(2,1)S(1)} %get-tuple-element.13), channel_id=1, source_target_pairs={{0,5},{1,6},{2,7},{3,0},{4,1},{5,2},{6,3},{7,4},{8,13},{9,14},{10,... | collective-permute-start | bytes 393224 | tf_op jit(solution)/shard_map/ppermute | solution.py:200
  155.5 15.8 %collective-permute-start.3 = (bf16[32,2048]{1,0:T(8,128)(2,1)S(1)}, bf16[32,2048]{1,0:T(8,128)(2,1)S(1)}, u32[]{:S(2)}, u32[]{:S(2)}) collective-permute-start(bf16[32,2048]{1,0:T(8,128)(2,1)S(1)} %get-tuple-element.13), channel_id=1, source_target_pairs={{0,4},{1,5},{2,6},{3,7},{4,0},{5,1},{6,2},{7,3},{8,12},{9,13},{10,... | collective-permute-start | bytes 393224 | tf_op jit(solution)/shard_map/ppermute | solution.py:200
  156.3 14.2 %collective-permute-start.2 = (bf16[32,2048]{1,0:T(8,128)(2,1)S(1)}, bf16[32,2048]{1,0:T(8,128)(2,1)S(1)}, u32[]{:S(2)}, u32[]{:S(2)}) collective-permute-start(bf16[32,2048]{1,0:T(8,128)(2,1)S(1)} %get-tuple-element.13), channel_id=1, source_target_pairs={{0,3},{1,4},{2,5},{3,6},{4,7},{5,0},{6,1},{7,2},{8,11},{9,12},{10,... | collective-permute-start | bytes 393224 | tf_op jit(solution)/shard_map/ppermute | solution.py:200
  158.7 9.5 %collective-permute-start.1 = (bf16[32,2048]{1,0:T(8,128)(2,1)S(1)}, bf16[32,2048]{1,0:T(8,128)(2,1)S(1)}, u32[]{:S(2)}, u32[]{:S(2)}) collective-permute-start(bf16[32,2048]{1,0:T(8,128)(2,1)S(1)} %get-tuple-element.13), channel_id=1, source_target_pairs={{0,2},{1,3},{2,4},{3,5},{4,6},{5,7},{6,0},{7,1},{8,10},{9,11},{10,... | collective-permute-start | bytes 393224 | tf_op jit(solution)/shard_map/ppermute | solution.py:200
  168.2 5.0 %collective-permute-start.6 = (bf16[32,2048]{1,0:T(8,128)(2,1)S(1)}, bf16[32,2048]{1,0:T(8,128)(2,1)S(1)}, u32[]{:S(2)}, u32[]{:S(2)}) collective-permute-start(bf16[32,2048]{1,0:T(8,128)(2,1)S(1)} %get-tuple-element.13), channel_id=1, source_target_pairs={{0,7},{1,0},{2,1},{3,2},{4,3},{5,4},{6,5},{7,6},{8,15},{9,8},{10,9... | collective-permute-start | bytes 393224 | tf_op jit(solution)/shard_map/ppermute | solution.py:200
  207.6 6.9 %collective-permute-start.7 = (bf16[32,2048]{1,0:T(8,128)(2,1)S(1)}, bf16[32,2048]{1,0:T(8,128)(2,1)S(1)}, u32[]{:S(2)}, u32[]{:S(2)}) collective-permute-start(bf16[32,2048]{1,0:T(8,128)(2,1)S(1)} %get-tuple-element.11), channel_id=1, source_target_pairs={{0,1},{1,2},{2,3},{3,4},{4,5},{5,6},{6,7},{7,0},{8,9},{9,10},{10,1... | collective-permute-start | bytes 393224 | tf_op jit(solution)/shard_map/ppermute | solution.py:200
  208.9 19.4 %collective-permute-start.12 = (bf16[32,2048]{1,0:T(8,128)(2,1)S(1)}, bf16[32,2048]{1,0:T(8,128)(2,1)S(1)}, u32[]{:S(2)}, u32[]{:S(2)}) collective-permute-start(bf16[32,2048]{1,0:T(8,128)(2,1)S(1)} %get-tuple-element.11), channel_id=1, source_target_pairs={{0,6},{1,7},{2,0},{3,1},{4,2},{5,3},{6,4},{7,5},{8,14},{9,15},{10,... | collective-permute-start | bytes 393224 | tf_op jit(solution)/shard_map/ppermute | solution.py:200
  211.2 16.4 %collective-permute-start.11 = (bf16[32,2048]{1,0:T(8,128)(2,1)S(1)}, bf16[32,2048]{1,0:T(8,128)(2,1)S(1)}, u32[]{:S(2)}, u32[]{:S(2)}) collective-permute-start(bf16[32,2048]{1,0:T(8,128)(2,1)S(1)} %get-tuple-element.11), channel_id=1, source_target_pairs={{0,5},{1,6},{2,7},{3,0},{4,1},{5,2},{6,3},{7,4},{8,13},{9,14},{10,... | collective-permute-start | bytes 393224 | tf_op jit(solution)/shard_map/ppermute | solution.py:200
  211.3 15.8 %collective-permute-start.10 = (bf16[32,2048]{1,0:T(8,128)(2,1)S(1)}, bf16[32,2048]{1,0:T(8,128)(2,1)S(1)}, u32[]{:S(2)}, u32[]{:S(2)}) collective-permute-start(bf16[32,2048]{1,0:T(8,128)(2,1)S(1)} %get-tuple-element.11), channel_id=1, source_target_pairs={{0,4},{1,5},{2,6},{3,7},{4,0},{5,1},{6,2},{7,3},{8,12},{9,13},{10,... | collective-permute-start | bytes 393224 | tf_op jit(solution)/shard_map/ppermute | solution.py:200
  212.1 14.2 %collective-permute-start.9 = (bf16[32,2048]{1,0:T(8,128)(2,1)S(1)}, bf16[32,2048]{1,0:T(8,128)(2,1)S(1)}, u32[]{:S(2)}, u32[]{:S(2)}) collective-permute-start(bf16[32,2048]{1,0:T(8,128)(2,1)S(1)} %get-tuple-element.11), channel_id=1, source_target_pairs={{0,3},{1,4},{2,5},{3,6},{4,7},{5,0},{6,1},{7,2},{8,11},{9,12},{10,... | collective-permute-start | bytes 393224 | tf_op jit(solution)/shard_map/ppermute | solution.py:200
  214.5 9.5 %collective-permute-start.8 = (bf16[32,2048]{1,0:T(8,128)(2,1)S(1)}, bf16[32,2048]{1,0:T(8,128)(2,1)S(1)}, u32[]{:S(2)}, u32[]{:S(2)}) collective-permute-start(bf16[32,2048]{1,0:T(8,128)(2,1)S(1)} %get-tuple-element.11), channel_id=1, source_target_pairs={{0,2},{1,3},{2,4},{3,5},{4,6},{5,7},{6,0},{7,1},{8,10},{9,11},{10,... | collective-permute-start | bytes 393224 | tf_op jit(solution)/shard_map/ppermute | solution.py:200
  224.0 5.0 %collective-permute-start.13 = (bf16[32,2048]{1,0:T(8,128)(2,1)S(1)}, bf16[32,2048]{1,0:T(8,128)(2,1)S(1)}, u32[]{:S(2)}, u32[]{:S(2)}) collective-permute-start(bf16[32,2048]{1,0:T(8,128)(2,1)S(1)} %get-tuple-element.11), channel_id=1, source_target_pairs={{0,7},{1,0},{2,1},{3,2},{4,3},{5,4},{6,5},{7,6},{8,15},{9,8},{10,9... | collective-permute-start | bytes 393224 | tf_op jit(solution)/shard_map/ppermute | solution.py:200
  (5 other events, 8.0 us)

commit v8 on v7

--- a/solution.py
+++ b/solution.py
@@ -274,9 +274,6 @@
     sin_table = jnp.sin(held_angle)
     cos_table = jnp.concatenate([cos_table, cos_table], axis=-1)[:, :, None, :]
     sin_table = jnp.concatenate([-sin_table, sin_table], axis=-1)[:, :, None, :]
-    query_copies = jnp.broadcast_to(queries[None], (req_count,) + queries.shape)
-    all_queries = lax.all_to_all(query_copies, "req", 0, 0, tiled=False)
-    all_queries = all_queries.reshape(request_count, req_rows * groups, head_size)
     query_pos = jnp.repeat(recompute_pos, groups, axis=1)[:, :, None]
     key_pos = jnp.where(
         (send_place < req_lengths[:, None])[:, :, None],
@@ -284,22 +281,41 @@
         far_position,
     )[:, :, None, :]
     alive = (send_place < req_lengths[:, None]).reshape(request_count * pair_cap).astype(jnp.int32)
-    held = held_blocks(
-        slots, alive, all_queries, cached_key_pool, cached_value_pool, cos_table, sin_table, query_pos, key_pos
-    )
-    got = lax.all_to_all(held, "req", 0, 0, tiled=False)
-    sum_rows = req_rows * groups
+    halves = 2
+    part_rows = req_rows // halves
+    sum_rows = part_rows * groups
     chunks = sum_rows // head_size
     head_total = key_heads * groups
-    got_sum = got[:, :sum_rows].astype(jnp.float32)
-
-    def stat_of(k):
-        base = sum_rows + 3 * k * chunks
-        hi, mid, lo = (got[:, base + i * chunks:base + (i + 1) * chunks].astype(jnp.float32) for i in range(3))
-        return ((hi + mid) + lo).reshape(req_count, count_of_rows, head_total)
-
-    got_peak = stat_of(0)
-    got_total = stat_of(1)
+    got_sums, got_peaks, got_totals = [], [], []
+    for part in range(halves):
+        part_queries = queries[part * part_rows:(part + 1) * part_rows]
+        query_copies = jnp.broadcast_to(part_queries[None], (req_count,) + part_queries.shape)
+        all_queries = lax.all_to_all(query_copies, "req", 0, 0, tiled=False)
+        all_queries = all_queries.reshape(request_count, sum_rows, head_size)
+        held = held_blocks(
+            slots,
+            alive,
+            all_queries,
+            cached_key_pool,
+            cached_value_pool,
+            cos_table,
+            sin_table,
+            query_pos[:, part * sum_rows:(part + 1) * sum_rows],
+            key_pos,
+        )
+        got = lax.all_to_all(held, "req", 0, 0, tiled=False)
+        got_sums.append(got[:, :sum_rows].astype(jnp.float32).reshape(req_count, part_rows, head_total, head_size))
+
+        def stat_of(k):
+            base = sum_rows + 3 * k * chunks
+            hi, mid, lo = (got[:, base + i * chunks:base + (i + 1) * chunks].astype(jnp.float32) for i in range(3))
+            return ((hi + mid) + lo).reshape(req_count, part_rows, head_total)
+
+        got_peaks.append(stat_of(0))
+        got_totals.append(stat_of(1))
+    got_sum = jnp.concatenate(got_sums, axis=1)
+    got_peak = jnp.concatenate(got_peaks, axis=1)
+    got_total = jnp.concatenate(got_totals, axis=1)
     attended = merge_stats(
         jnp.concatenate([got_sum.reshape(req_count, count_of_rows, head_total, head_size), fresh_sum[None]]),
         jnp.concatenate([got_peak, fresh_peak[None]]),

time: 235 us -> 261 us (1.11)
  waiting for transfers between devices: 56.1 us -> 38.9 us
  starting transfers between devices: 43 us -> 55.5 us
  Pallas kernels: 24 us -> 35.8 us
  local copies, waits for them, and re-layouts: 44 us -> 54.9 us
  other arithmetic: 30 us -> 35.6 us
    all_to_all x1 -> x2, waiting for transfers between devices: 18.8 us -> 4.3 us  [on_device(): got = lax.all_to_all(held, 'req', 0, 0, tiled=False)]
    pallas_call x1 -> x2, Pallas kernels: 24 us -> 35.8 us  [held_blocks(): pl.pallas_call(held_block_kernel, grid_spec=grid_spec, out_shape=jax.Shap...]
    all_to_all x1 -> x2, starting transfers between devices: 5.29 us -> 13.2 us  [on_device(): got = lax.all_to_all(held, 'req', 0, 0, tiled=False)]
    unnamed x53 -> x51, local copies, waits for them, and re-layouts: 10.3 us -> 17.5 us
    concatenate x0 -> x3, other arithmetic: none -> 5.3 us  [the longest x1 2.27 us: on_device(): got_sum = jnp.concatenate(got_sums, axis=1)]
    another operation x1 -> x0, local copies, waits for them, and re-layouts: 4.82 us -> none  [on_device(): query_pos = jnp.repeat(recompute_pos, groups, axis=1)[:, :, None]]
    all_to_all x1 -> x2, starting transfers between devices: 8.77 us -> 13 us  [on_device(): all_queries = lax.all_to_all(query_copies, 'req', 0, 0, tiled=False)]
    reshape x1 -> x0, other arithmetic: 3.69 us -> none  [on_device(): got_sum.reshape(req_count, count_of_rows, head_total, head_size)]
  transfers between devices with their start and end apart: 17 -> 19, of which waited for: 5 -> 5; matrix products, arithmetic and copies ran while one was open for 16% -> 20% of each run, Pallas kernels for 0% -> 14%
where the time goes in v8:
time: 261 us; the launch traced here: 259 us
  starting transfers between devices  55.5 us (21%)
  local copies, waits for them, and re-layouts  54.9 us (21%)
  waiting for transfers between devices  38.9 us (15%)
  Pallas kernels  35.8 us (14%)
  other arithmetic  35.6 us (14%)
  matrix products  18.9 us (7%)
  blocking collectives  18.5 us (7%)
    pallas_call x2, Pallas kernels, held_blocks(): pl.pallas_call(held_block_kernel, grid_spec=grid_spec, out_shape=jax.Shap...  35.8 us
    ppermute x14, starting transfers between devices, gather_rows(): parts.append(lax.ppermute(rows, 'tp', pairs))  18.9 us
    all_to_all x1, blocking collectives, reduce_rows(): got = lax.all_to_all(blocks, 'tp', 0, 0, tiled=False)  18.5 us
    unnamed x51, local copies, waits for them, and re-layouts  17.5 us
    ppermute x14, waiting for transfers between devices, gather_rows(): parts.append(lax.ppermute(rows, 'tp', pairs))  15.9 us
    all_to_all x1, waiting for transfers between devices, reduce_rows(): got = lax.all_to_all(blocks, 'tp', 0, 0, tiled=False)  14.1 us
    all_to_all x2, starting transfers between devices, on_device(): got = lax.all_to_all(held, 'req', 0, 0, tiled=False)  13.2 us
    all_to_all x2, starting transfers between devices, on_device(): all_queries = lax.all_to_all(query_copies, 'req', 0, 0, tiled=False)  13 us
  transfers between devices with their start and end apart: 19, of which 5 were waited for; matrix products, arithmetic and copies ran while one was open for 20% of the time, Pallas kernels for 14%

profile of v8, /device:TPU:1, one launch (start us, length us, event | category | flops | bytes accessed | tf_op | source)
XLA Modules:
  0.0 258.6 jit_solution(15907249926554854717)
XLA Ops:
  3.0 2.9 %multiply_reduce_fusion = (f32[256,2]{0,1:T(2,128)S(1)}, f32[256,256]{0,1:T(8,128)}) fusion(bf16[2048,256]{1,0:T(8,128)(2,1)} %param.28, bf16[256,2048]{1,0:T(8,128)(2,1)} %param.20, f32[2048]{0:T(1024)} %param.27, f32[256]{0:T(256)S(1)} %add_rsqrt_fusion.2), kind=kOutput, calls=%fused_computation.48 | convolution fusion | flops 270663168 | bytes 2370560 | tf_op jit(solution)/shard_map/dot_general | solution.py:239
  9.8 8.6 %all-to-all-start = ((bf16[16,128,2,128]{3,2,1,0:T(2,128)(2,1)}), bf16[16,128,2,128]{3,2,1,0:T(2,128)(2,1)}, u32[]{:S(2)}, u32[]{:S(2)}) async-start(bf16[16,128,2,128]{3,2,1,0:T(2,128)(2,1)} %broadcast_in_dim.73), calls=%async_computation | async-start | bytes 2097152 | tf_op jit(solution)/shard_map/all_to_all | solution.py:293
  19.4 3.5 %gather_fusion.1 = s32[512]{0:T(512)S(1)} fusion(s32[512]{0:T(512)S(1)} %bitcast.110, s32[1024]{0:T(1024)S(1)} %pad_clamp_fusion.1), kind=kCustom, calls=%fused_computation.3 | custom fusion | bytes 6144 | tf_op jit(solution)/shard_map/gather | solution.py:260
  22.9 3.5 %gather_fusion = s32[512]{0:T(512)S(1)} fusion(s32[512]{0:T(512)S(1)} %bitcast.109, s32[1024]{0:T(1024)S(1)} %pad_clamp_fusion.1), kind=kCustom, calls=%fused_computation.2 | custom fusion | bytes 6144 | tf_op jit(solution)/shard_map/gather | solution.py:259
  29.6 4.6 %all-to-all-done = bf16[16,128,2,128]{3,2,1,0:T(2,128)(2,1)} async-done(((bf16[16,128,2,128]{3,2,1,0:T(2,128)(2,1)}), bf16[16,128,2,128]{3,2,1,0:T(2,128)(2,1)}, u32[]{:S(2)}, u32[]{:S(2)}) %all-to-all-start) | async-done | bytes 1048608 | tf_op jit(solution)/shard_map/all_to_all | solution.py:293
  36.0 4.3 %all-to-all-start.2 = ((bf16[16,128,2,128]{3,2,1,0:T(2,128)(2,1)}), bf16[16,128,2,128]{3,2,1,0:T(2,128)(2,1)}, u32[]{:S(2)}, u32[]{:S(2)}) async-start(bf16[16,128,2,128]{3,2,1,0:T(2,128)(2,1)} %broadcast_in_dim.79), calls=%async_computation.2 | async-start | bytes 2097152 | tf_op jit(solution)/shard_map/all_to_all | solution.py:293
  48.6 4.0 %copy.186.qpos_ref = s32[16,256,1]{2,1,0:T(8,128)} copy(s32[16,256,1]{0,1,2:T(8,128)} %get-tuple-element.28) | data formatting | bytes 32768
  56.4 17.9 %shard_map.172 = bf16[16,272,128]{2,1,0:T(8,128)(2,1)} custom-call(s32[32]{0:T(128)} %min.12.slot_ref, s32[32]{0:T(128)} %reshape.372.alive_ref, bf16[16,256,128]{2,1,0:T(8,128)(2,1)} %bitcast.4.q_ref, bf16[32,512,128]{2,1,0:T(8,128)(2,1)} %k1_ref.3, bf16[32,512,128]{2,1,0:T(8,128)(2,1)} %k1_ref.3, bf16[32,512,128]{2,1,0:T(8,128)(2,1)} %v1_ref.3, ...), custom_call_target="tpu_custom_call" | custom-call | tf_op jit(solution)/shard_map/pallas_call | solution.py:181
  74.3 6.6 %all-to-all-start.1 = ((bf16[16,272,128]{2,1,0:T(8,128)(2,1)}), bf16[16,272,128]{2,1,0:T(8,128)(2,1)}, u32[]{:S(2)}, u32[]{:S(2)}) async-start(bf16[16,272,128]{2,1,0:T(8,128)(2,1)} %shard_map.172), calls=%async_computation.1 | async-start | bytes 2228224 | tf_op jit(solution)/shard_map/all_to_all | solution.py:306
  80.9 3.1 %copy.187.qpos_ref = s32[16,256,1]{2,1,0:T(8,128)} copy(s32[16,256,1]{0,1,2:T(8,128)S(1)} %get-tuple-element.29) | data formatting | bytes 32768
  84.1 2.0 multiply_reduce_fusion.1
  86.8 17.9 %shard_map.173 = bf16[16,272,128]{2,1,0:T(8,128)(2,1)} custom-call(s32[32]{0:T(128)} %min.12.slot_ref, s32[32]{0:T(128)} %reshape.372.alive_ref, bf16[16,256,128]{2,1,0:T(8,128)(2,1)} %bitcast.10.q_ref, bf16[32,512,128]{2,1,0:T(8,128)(2,1)} %k1_ref.3, bf16[32,512,128]{2,1,0:T(8,128)(2,1)} %k1_ref.3, bf16[32,512,128]{2,1,0:T(8,128)(2,1)} %v1_ref.3, ...), custom_call_target="tpu_custom_call" | custom-call | tf_op jit(solution)/shard_map/pallas_call | solution.py:181
  104.7 6.7 %all-to-all-start.3 = ((bf16[16,272,128]{2,1,0:T(8,128)(2,1)}), bf16[16,272,128]{2,1,0:T(8,128)(2,1)}, u32[]{:S(2)}, u32[]{:S(2)}) async-start(bf16[16,272,128]{2,1,0:T(8,128)(2,1)} %shard_map.173), calls=%async_computation.3 | async-start | bytes 2228224 | tf_op jit(solution)/shard_map/all_to_all | solution.py:306
  113.9 2.2 convolution_bitcast_fusion
  120.1 4.3 %all-to-all-done.3 = bf16[16,272,128]{2,1,0:T(8,128)(2,1)} async-done(((bf16[16,272,128]{2,1,0:T(8,128)(2,1)}), bf16[16,272,128]{2,1,0:T(8,128)(2,1)}, u32[]{:S(2)}, u32[]{:S(2)}) %all-to-all-start.3) | async-done | bytes 1114144 | tf_op jit(solution)/shard_map/all_to_all | solution.py:306
  132.7 2.1 copy.176
  137.4 2.3 maximum_convert_fusion
  139.7 5.3 %fusion = f32[256,2,128]{2,1,0:T(2,128)S(1)} fusion(f32[1,256,2,128]{3,2,1,0:T(2,128)S(1)} %copy-done.4, f32[16,256,2,128]{3,2,1,0:T(2,128)S(1)} %maximum_convert_fusion, f32[17,256,2]{2,1,0:T(8,128)S(1)} %copy-done.1), kind=kLoop, calls=%fused_computation.5 | loop fusion | flops 3276800 | bytes 4753408 | tf_op jit(solution)/shard_map/reduce_sum | solution.py:75
  146.9 10.4 %all-to-all-start.4 = ((bf16[8,32,2048]{2,1,0:T(8,128)(2,1)}), bf16[8,32,2048]{2,1,0:T(8,128)(2,1)}, u32[]{:S(2)}, u32[]{:S(2)}) async-start(bf16[8,32,2048]{2,1,0:T(8,128)(2,1)} %bitcast.111), calls=%async_computation.4 | async-start | bytes 2097152 | tf_op jit(solution)/shard_map/all_to_all | solution.py:191
  158.3 14.1 %all-to-all-done.4 = bf16[8,32,2048]{2,1,0:T(8,128)(2,1)} async-done(((bf16[8,32,2048]{2,1,0:T(8,128)(2,1)}), bf16[8,32,2048]{2,1,0:T(8,128)(2,1)}, u32[]{:S(2)}, u32[]{:S(2)}) %all-to-all-start.4) | async-done | bytes 1048608 | tf_op jit(solution)/shard_map/all_to_all | solution.py:191
  176.7 2.5 collective-permute-start.5
  180.0 2.4 collective-permute-start.2
  184.0 7.9 %collective-permute-done.1 = bf16[32,2048]{1,0:T(8,128)(2,1)S(1)} collective-permute-done((bf16[32,2048]{1,0:T(8,128)(2,1)S(1)}, bf16[32,2048]{1,0:T(8,128)(2,1)S(1)}, u32[]{:S(2)}, u32[]{:S(2)}) %collective-permute-start.1) | collective-permute-done | bytes 131104 | tf_op jit(solution)/shard_map/ppermute | solution.py:200
  197.6 2.8 %gather_fusion.2 = bf16[8,32,2048]{2,1,0:T(8,128)(2,1)} fusion(bf16[8,32,2048]{2,1,0:T(8,128)(2,1)} %bitcast_dynamic-update-slice_fusion.8, s32[1024]{0:T(1024)S(1)} %pad_clamp_fusion), kind=kCustom, calls=%fused_computation.clone | custom fusion | bytes 2097184 | tf_op jit(solution)/shard_map/jit(_take)/gather | solution.py:203
  202.8 3.8 %fusion.64 = f32[256,768]{1,0:T(8,128)} fusion(bf16[256,2048]{1,0:T(8,128)(2,1)S(1)} %bitcast.114, bf16[2048,768]{1,0:T(8,128)(2,1)} %param.35), kind=kOutput, calls=%fused_computation.154 | convolution fusion | flops 805306368 | bytes 4980736 | tf_op jit(solution)/shard_map/dot_general | solution.py:82
  206.6 5.5 %convolution_convert_fusion.1 = bf16[256,2048]{1,0:T(8,128)(2,1)} fusion(bf16[768,2048]{1,0:T(8,128)(2,1)S(1)} %copy-done, bf16[256,2048]{1,0:T(8,128)(2,1)} %bitcast.115, bf16[2048,768]{1,0:T(8,128)(2,1)} %param.36, f32[256,768]{1,0:T(8,128)} %fusion.64), kind=kOutput, calls=%fused_computation.9 | convolution fusion | flops 1612316672 | bytes 9175040 | tf_op jit(solution)/shard_map/dot_general | solution.py:333
  212.1 18.5 %all_to_all.30 = bf16[8,32,2048]{2,1,0:T(8,128)(2,1)S(1)} all-to-all(bf16[8,32,2048]{2,1,0:T(8,128)(2,1)} %bitcast.116), channel_id=1, replica_groups=mesh['req'=16,'tp'=8] {'tp'}, dimensions={0} | all-to-all | bytes 2097152 | tf_op jit(solution)/shard_map/all_to_all | solution.py:191
  232.6 2.3 collective-permute-start.12
  235.8 2.4 collective-permute-start.9
  239.7 8.0 %collective-permute-done.8 = bf16[32,2048]{1,0:T(8,128)(2,1)S(1)} collective-permute-done((bf16[32,2048]{1,0:T(8,128)(2,1)S(1)}, bf16[32,2048]{1,0:T(8,128)(2,1)S(1)}, u32[]{:S(2)}, u32[]{:S(2)}) %collective-permute-start.8) | collective-permute-done | bytes 131104 | tf_op jit(solution)/shard_map/ppermute | solution.py:200
  253.4 2.8 %gather_fusion.3 = bf16[8,32,2048]{2,1,0:T(8,128)(2,1)} fusion(bf16[8,32,2048]{2,1,0:T(8,128)(2,1)} %bitcast_dynamic-update-slice_fusion, s32[1024]{0:T(1024)S(1)} %pad_clamp_fusion), kind=kCustom, calls=%fused_computation.1.clone | custom fusion | bytes 2097184 | tf_op jit(solution)/shard_map/jit(_take)/gather | solution.py:203
  256.2 2.4 broadcast_select_fusion.1
  (155 shorter events, 70.6 us)
Async XLA Ops:
  0.0 206.6 %copy-start = (bf16[768,2048]{1,0:T(8,128)(2,1)S(1)}, bf16[768,2048]{1,0:T(8,128)(2,1)}, u32[]{:S(2)}) copy-start(bf16[768,2048]{1,0:T(8,128)(2,1)} %param.37) | copy-start | bytes 9437188
  0.0 7.0 %copy-start.11 = (f32[64]{0:T(128)}, f32[64]{0:T(128)S(1)}, u32[]{:S(2)}) copy-start(f32[64]{0:T(128)S(1)} %multiply_power_fusion) | copy-start | bytes 772
  1.4 5.6 %copy-start.7 = (f32[256]{0:T(256)}, f32[256]{0:T(256)S(1)}, u32[]{:S(2)}) copy-start(f32[256]{0:T(256)S(1)} %convert_element_type.124) | copy-start | bytes 3076
  2.9 4.6 %copy-start.15 = (f32[128]{0:T(128)S(1)}, f32[128]{0:T(128)}, u32[]{:S(2)}) copy-start(f32[128]{0:T(128)} %param.31) | copy-start | bytes 1540
  7.9 10.6 %copy-start.10 = (s32[16,32]{1,0:T(8,128)S(1)}, s32[16,32]{1,0:T(8,128)}, u32[]{:S(2)}) copy-start(s32[16,32]{1,0:T(8,128)} %param.23) | copy-start | bytes 6148
  9.8 24.4 %all-to-all-start = ((bf16[16,128,2,128]{3,2,1,0:T(2,128)(2,1)}), bf16[16,128,2,128]{3,2,1,0:T(2,128)(2,1)}, u32[]{:S(2)}, u32[]{:S(2)}) async-start(bf16[16,128,2,128]{3,2,1,0:T(2,128)(2,1)} %broadcast_in_dim.73), calls=%async_computation | async-start | bytes 2097152 | tf_op jit(solution)/shard_map/all_to_all | solution.py:293
  36.0 38.3 %all-to-all-start.2 = ((bf16[16,128,2,128]{3,2,1,0:T(2,128)(2,1)}), bf16[16,128,2,128]{3,2,1,0:T(2,128)(2,1)}, u32[]{:S(2)}, u32[]{:S(2)}) async-start(bf16[16,128,2,128]{3,2,1,0:T(2,128)(2,1)} %broadcast_in_dim.79), calls=%async_computation.2 | async-start | bytes 2097152 | tf_op jit(solution)/shard_map/all_to_all | solution.py:293
  74.3 9.8 %copy-start.14 = (f32[256]{0:T(256)S(1)}, f32[256]{0:T(256)}, u32[]{:S(2)}) copy-start(f32[256]{0:T(256)} %copy-done.13) | copy-start | bytes 3076
  74.3 30.4 %all-to-all-start.1 = ((bf16[16,272,128]{2,1,0:T(8,128)(2,1)}), bf16[16,272,128]{2,1,0:T(8,128)(2,1)}, u32[]{:S(2)}, u32[]{:S(2)}) async-start(bf16[16,272,128]{2,1,0:T(8,128)(2,1)} %shard_map.172), calls=%async_computation.1 | async-start | bytes 2228224 | tf_op jit(solution)/shard_map/all_to_all | solution.py:306
  80.9 5.1 %copy-start.16 = (f32[128]{0:T(128)S(1)}, f32[128]{0:T(128)}, u32[]{:S(2)}) copy-start(f32[128]{0:T(128)} %param.32) | copy-start | bytes 1540
  104.7 6.7 %copy-start.6 = (s32[1,256]{1,0:T(1,128)S(1)}, s32[1,256]{1,0:T(1,128)}, u32[]{:S(2)}) copy-start(s32[1,256]{1,0:T(1,128)} %copy-done.5) | copy-start | bytes 3076
  104.7 6.9 %copy-start.8 = (f32[256]{0:T(256)S(1)}, f32[256]{0:T(256)}, u32[]{:S(2)}) copy-start(f32[256]{0:T(256)} %copy-done.7) | copy-start | bytes 3076
  104.7 6.9 %copy-start.12 = (f32[64]{0:T(128)S(1)}, f32[64]{0:T(128)}, u32[]{:S(2)}) copy-start(f32[64]{0:T(128)} %copy-done.11) | copy-start | bytes 772
  104.7 9.2 %copy-start.17 = (f32[2048]{0:T(1024)S(1)}, f32[2048]{0:T(1024)}, u32[]{:S(2)}) copy-start(f32[2048]{0:T(1024)} %param.27) | copy-start | bytes 24580
  104.7 19.6 %all-to-all-start.3 = ((bf16[16,272,128]{2,1,0:T(8,128)(2,1)}), bf16[16,272,128]{2,1,0:T(8,128)(2,1)}, u32[]{:S(2)}, u32[]{:S(2)}) async-start(bf16[16,272,128]{2,1,0:T(8,128)(2,1)} %shard_map.173), calls=%async_computation.3 | async-start | bytes 2228224 | tf_op jit(solution)/shard_map/all_to_all | solution.py:306
  139.7 5.7 %copy-start.3 = (bf16[256,2048]{1,0:T(8,128)(2,1)S(1)}, bf16[256,2048]{1,0:T(8,128)(2,1)}, u32[]{:S(2)}) copy-start(bf16[256,2048]{1,0:T(8,128)(2,1)} %param.33) | copy-start | bytes 3145732
  146.9 27.9 %copy-start.9 = (f32[2048]{0:T(1024)S(1)}, f32[2048]{0:T(1024)}, u32[]{:S(2)}) copy-start(f32[2048]{0:T(1024)} %param.34) | copy-start | bytes 24580
  146.9 25.4 %all-to-all-start.4 = ((bf16[8,32,2048]{2,1,0:T(8,128)(2,1)}), bf16[8,32,2048]{2,1,0:T(8,128)(2,1)}, u32[]{:S(2)}, u32[]{:S(2)}) async-start(bf16[8,32,2048]{2,1,0:T(8,128)(2,1)} %bitcast.111), calls=%async_computation.4 | async-start | bytes 2097152 | tf_op jit(solution)/shard_map/all_to_all | solution.py:191
  175.5 6.9 %collective-permute-start = (bf16[32,2048]{1,0:T(8,128)(2,1)S(1)}, bf16[32,2048]{1,0:T(8,128)(2,1)S(1)}, u32[]{:S(2)}, u32[]{:S(2)}) collective-permute-start(bf16[32,2048]{1,0:T(8,128)(2,1)S(1)} %get-tuple-element.13), channel_id=1, source_target_pairs={{0,1},{1,2},{2,3},{3,4},{4,5},{5,6},{6,7},{7,0},{8,9},{9,10},{10,1... | collective-permute-start | bytes 393224 | tf_op jit(solution)/shard_map/ppermute | solution.py:200
  176.7 19.6 %collective-permute-start.5 = (bf16[32,2048]{1,0:T(8,128)(2,1)S(1)}, bf16[32,2048]{1,0:T(8,128)(2,1)S(1)}, u32[]{:S(2)}, u32[]{:S(2)}) collective-permute-start(bf16[32,2048]{1,0:T(8,128)(2,1)S(1)} %get-tuple-element.13), channel_id=1, source_target_pairs={{0,6},{1,7},{2,0},{3,1},{4,2},{5,3},{6,4},{7,5},{8,14},{9,15},{10,... | collective-permute-start | bytes 393224 | tf_op jit(solution)/shard_map/ppermute | solution.py:200
  179.2 16.4 %collective-permute-start.4 = (bf16[32,2048]{1,0:T(8,128)(2,1)S(1)}, bf16[32,2048]{1,0:T(8,128)(2,1)S(1)}, u32[]{:S(2)}, u32[]{:S(2)}) collective-permute-start(bf16[32,2048]{1,0:T(8,128)(2,1)S(1)} %get-tuple-element.13), channel_id=1, source_target_pairs={{0,5},{1,6},{2,7},{3,0},{4,1},{5,2},{6,3},{7,4},{8,13},{9,14},{10,... | collective-permute-start | bytes 393224 | tf_op jit(solution)/shard_map/ppermute | solution.py:200
  179.2 15.8 %collective-permute-start.3 = (bf16[32,2048]{1,0:T(8,128)(2,1)S(1)}, bf16[32,2048]{1,0:T(8,128)(2,1)S(1)}, u32[]{:S(2)}, u32[]{:S(2)}) collective-permute-start(bf16[32,2048]{1,0:T(8,128)(2,1)S(1)} %get-tuple-element.13), channel_id=1, source_target_pairs={{0,4},{1,5},{2,6},{3,7},{4,0},{5,1},{6,2},{7,3},{8,12},{9,13},{10,... | collective-permute-start | bytes 393224 | tf_op jit(solution)/shard_map/ppermute | solution.py:200
  180.0 14.2 %collective-permute-start.2 = (bf16[32,2048]{1,0:T(8,128)(2,1)S(1)}, bf16[32,2048]{1,0:T(8,128)(2,1)S(1)}, u32[]{:S(2)}, u32[]{:S(2)}) collective-permute-start(bf16[32,2048]{1,0:T(8,128)(2,1)S(1)} %get-tuple-element.13), channel_id=1, source_target_pairs={{0,3},{1,4},{2,5},{3,6},{4,7},{5,0},{6,1},{7,2},{8,11},{9,12},{10,... | collective-permute-start | bytes 393224 | tf_op jit(solution)/shard_map/ppermute | solution.py:200
  182.4 9.5 %collective-permute-start.1 = (bf16[32,2048]{1,0:T(8,128)(2,1)S(1)}, bf16[32,2048]{1,0:T(8,128)(2,1)S(1)}, u32[]{:S(2)}, u32[]{:S(2)}) collective-permute-start(bf16[32,2048]{1,0:T(8,128)(2,1)S(1)} %get-tuple-element.13), channel_id=1, source_target_pairs={{0,2},{1,3},{2,4},{3,5},{4,6},{5,7},{6,0},{7,1},{8,10},{9,11},{10,... | collective-permute-start | bytes 393224 | tf_op jit(solution)/shard_map/ppermute | solution.py:200
  191.9 5.0 %collective-permute-start.6 = (bf16[32,2048]{1,0:T(8,128)(2,1)S(1)}, bf16[32,2048]{1,0:T(8,128)(2,1)S(1)}, u32[]{:S(2)}, u32[]{:S(2)}) collective-permute-start(bf16[32,2048]{1,0:T(8,128)(2,1)S(1)} %get-tuple-element.13), channel_id=1, source_target_pairs={{0,7},{1,0},{2,1},{3,2},{4,3},{5,4},{6,5},{7,6},{8,15},{9,8},{10,9... | collective-permute-start | bytes 393224 | tf_op jit(solution)/shard_map/ppermute | solution.py:200
  231.4 6.9 %collective-permute-start.7 = (bf16[32,2048]{1,0:T(8,128)(2,1)S(1)}, bf16[32,2048]{1,0:T(8,128)(2,1)S(1)}, u32[]{:S(2)}, u32[]{:S(2)}) collective-permute-start(bf16[32,2048]{1,0:T(8,128)(2,1)S(1)} %get-tuple-element.11), channel_id=1, source_target_pairs={{0,1},{1,2},{2,3},{3,4},{4,5},{5,6},{6,7},{7,0},{8,9},{9,10},{10,1... | collective-permute-start | bytes 393224 | tf_op jit(solution)/shard_map/ppermute | solution.py:200
  232.6 19.4 %collective-permute-start.12 = (bf16[32,2048]{1,0:T(8,128)(2,1)S(1)}, bf16[32,2048]{1,0:T(8,128)(2,1)S(1)}, u32[]{:S(2)}, u32[]{:S(2)}) collective-permute-start(bf16[32,2048]{1,0:T(8,128)(2,1)S(1)} %get-tuple-element.11), channel_id=1, source_target_pairs={{0,6},{1,7},{2,0},{3,1},{4,2},{5,3},{6,4},{7,5},{8,14},{9,15},{10,... | collective-permute-start | bytes 393224 | tf_op jit(solution)/shard_map/ppermute | solution.py:200
  235.0 16.4 %collective-permute-start.11 = (bf16[32,2048]{1,0:T(8,128)(2,1)S(1)}, bf16[32,2048]{1,0:T(8,128)(2,1)S(1)}, u32[]{:S(2)}, u32[]{:S(2)}) collective-permute-start(bf16[32,2048]{1,0:T(8,128)(2,1)S(1)} %get-tuple-element.11), channel_id=1, source_target_pairs={{0,5},{1,6},{2,7},{3,0},{4,1},{5,2},{6,3},{7,4},{8,13},{9,14},{10,... | collective-permute-start | bytes 393224 | tf_op jit(solution)/shard_map/ppermute | solution.py:200
  235.0 15.8 %collective-permute-start.10 = (bf16[32,2048]{1,0:T(8,128)(2,1)S(1)}, bf16[32,2048]{1,0:T(8,128)(2,1)S(1)}, u32[]{:S(2)}, u32[]{:S(2)}) collective-permute-start(bf16[32,2048]{1,0:T(8,128)(2,1)S(1)} %get-tuple-element.11), channel_id=1, source_target_pairs={{0,4},{1,5},{2,6},{3,7},{4,0},{5,1},{6,2},{7,3},{8,12},{9,13},{10,... | collective-permute-start | bytes 393224 | tf_op jit(solution)/shard_map/ppermute | solution.py:200
  235.8 14.2 %collective-permute-start.9 = (bf16[32,2048]{1,0:T(8,128)(2,1)S(1)}, bf16[32,2048]{1,0:T(8,128)(2,1)S(1)}, u32[]{:S(2)}, u32[]{:S(2)}) collective-permute-start(bf16[32,2048]{1,0:T(8,128)(2,1)S(1)} %get-tuple-element.11), channel_id=1, source_target_pairs={{0,3},{1,4},{2,5},{3,6},{4,7},{5,0},{6,1},{7,2},{8,11},{9,12},{10,... | collective-permute-start | bytes 393224 | tf_op jit(solution)/shard_map/ppermute | solution.py:200
  238.2 9.5 %collective-permute-start.8 = (bf16[32,2048]{1,0:T(8,128)(2,1)S(1)}, bf16[32,2048]{1,0:T(8,128)(2,1)S(1)}, u32[]{:S(2)}, u32[]{:S(2)}) collective-permute-start(bf16[32,2048]{1,0:T(8,128)(2,1)S(1)} %get-tuple-element.11), channel_id=1, source_target_pairs={{0,2},{1,3},{2,4},{3,5},{4,6},{5,7},{6,0},{7,1},{8,10},{9,11},{10,... | collective-permute-start | bytes 393224 | tf_op jit(solution)/shard_map/ppermute | solution.py:200
  247.7 5.0 %collective-permute-start.13 = (bf16[32,2048]{1,0:T(8,128)(2,1)S(1)}, bf16[32,2048]{1,0:T(8,128)(2,1)S(1)}, u32[]{:S(2)}, u32[]{:S(2)}) collective-permute-start(bf16[32,2048]{1,0:T(8,128)(2,1)S(1)} %get-tuple-element.11), channel_id=1, source_target_pairs={{0,7},{1,0},{2,1},{3,2},{4,3},{5,4},{6,5},{7,6},{8,15},{9,8},{10,9... | collective-permute-start | bytes 393224 | tf_op jit(solution)/shard_map/ppermute | solution.py:200
  (5 other events, 9.0 us)

commit v9 on v7

--- a/solution.py
+++ b/solution.py
@@ -117,7 +117,9 @@
 
     def run(parts):
         query = q_ref[0]
-        query_pos = qpos_ref[0]
+        rows, lanes = query.shape
+        pos_t = qpos_ref[0].T
+        query_pos = jnp.concatenate([pos_t[:, c:c + 1] for c in range(rows // lanes)], axis=0)
         scale = (query.shape[-1]) ** (-0.5)
         masked = []
         for j in parts:
@@ -162,6 +164,8 @@
     def pool_spec(j):
         return pl.BlockSpec((1, stretch, head_size), lambda r, slot, alive: (slot[2 * r + j], 0, 0))
 
+    pos_rows = query_pos.shape[1]
+
     grid_spec = pltpu.PrefetchScalarGridSpec(
         num_scalar_prefetch=2,
         grid=(requests,),
@@ -173,7 +177,7 @@
             pool_spec(1),
             pl.BlockSpec((1, 2, 1, head_size), lambda r, slot, alive: (r, 0, 0, 0)),
             pl.BlockSpec((1, 2, 1, head_size), lambda r, slot, alive: (r, 0, 0, 0)),
-            pl.BlockSpec((1, rows, 1), lambda r, slot, alive: (r, 0, 0)),
+            pl.BlockSpec((1, pos_rows, head_size), lambda r, slot, alive: (r, 0, 0)),
             pl.BlockSpec((1, 2, 1, stretch), lambda r, slot, alive: (r, 0, 0, 0)),
         ],
         out_specs=pl.BlockSpec((1, rows + stat_rows, head_size), lambda r, slot, alive: (r, 0, 0)),
@@ -268,7 +272,10 @@
     send_place = jnp.sum(jnp.where(my_sends, jnp.arange(MOST_STRETCHES)[None, :, None], 0), axis=1)
     request_count = holder_table.shape[0]
     pool_slots = cached_key_pool.shape[0]
-    slots = jnp.clip(send_slot, 0, pool_slots - 1).reshape(request_count * pair_cap).astype(jnp.int32)
+    slot_live = send_place < req_lengths[:, None]
+    last_live = lax.cummax(jnp.where(slot_live, jnp.arange(request_count)[:, None], -1), axis=0)
+    fetch_slot = jnp.take_along_axis(send_slot, jnp.maximum(last_live, 0), axis=0)
+    slots = jnp.clip(fetch_slot, 0, pool_slots - 1).reshape(request_count * pair_cap).astype(jnp.int32)
     held_angle = angles(send_place * STRETCH_TOKENS, head_size)
     cos_table = jnp.cos(held_angle)
     sin_table = jnp.sin(held_angle)
@@ -277,12 +284,14 @@
     query_copies = jnp.broadcast_to(queries[None], (req_count,) + queries.shape)
     all_queries = lax.all_to_all(query_copies, "req", 0, 0, tiled=False)
     all_queries = all_queries.reshape(request_count, req_rows * groups, head_size)
-    query_pos = jnp.repeat(recompute_pos, groups, axis=1)[:, :, None]
+    pos_lanes = jnp.repeat(recompute_pos, groups, axis=1).astype(jnp.float32).reshape(request_count, -1, head_size)
+    pos_pad = -pos_lanes.shape[1] % 8
+    query_pos = jnp.pad(pos_lanes, ((0, 0), (0, pos_pad), (0, 0)))
     key_pos = jnp.where(
         (send_place < req_lengths[:, None])[:, :, None],
         send_place[:, :, None] * STRETCH_TOKENS + jnp.arange(STRETCH_TOKENS)[None, None, :],
         far_position,
-    )[:, :, None, :]
+    ).astype(jnp.float32)[:, :, None, :]
     alive = (send_place < req_lengths[:, None]).reshape(request_count * pair_cap).astype(jnp.int32)
     held = held_blocks(
         slots, alive, all_queries, cached_key_pool, cached_value_pool, cos_table, sin_table, query_pos, key_pos

time: 235 us -> 239 us (1.017)
  starting transfers between devices: 43 us -> 49.1 us
  Pallas kernels: 24 us -> 20.7 us
    all_to_all x1, starting transfers between devices: 5.29 us -> 11.7 us  [on_device(): got = lax.all_to_all(held, 'req', 0, 0, tiled=False)]
    another operation x1 -> x0, local copies, waits for them, and re-layouts: 4.82 us -> none  [on_device(): query_pos = jnp.repeat(recompute_pos, groups, axis=1)[:, :, None]]
    pallas_call x1, Pallas kernels: 24 us -> 20.7 us  [held_blocks(): pl.pallas_call(held_block_kernel, grid_spec=grid_spec, out_shape=jax.Shap...]
    unnamed x53 -> x52, local copies, waits for them, and re-layouts: 10.3 us -> 9.55 us
  transfers between devices with their start and end apart: 17 -> 17, of which waited for: 5 -> 5; matrix products, arithmetic and copies ran while one was open for 16% -> 15% of each run, Pallas kernels for 0% -> 0%
where the time goes in v9:
time: 239 us; the launch traced here: 238 us
  waiting for transfers between devices  58.4 us (24%)
  starting transfers between devices  49.1 us (21%)
  local copies, waits for them, and re-layouts  42.5 us (18%)
  other arithmetic  29.5 us (12%)
  Pallas kernels  20.7 us (9%)
  matrix products  18.8 us (8%)
  blocking collectives  18.5 us (8%)
    pallas_call x1, Pallas kernels, held_blocks(): pl.pallas_call(held_block_kernel, grid_spec=grid_spec, out_shape=jax.Shap...  20.7 us
    all_to_all x1, waiting for transfers between devices, on_device(): got = lax.all_to_all(held, 'req', 0, 0, tiled=False)  19.2 us
    ppermute x14, starting transfers between devices, gather_rows(): parts.append(lax.ppermute(rows, 'tp', pairs))  18.9 us
    all_to_all x1, blocking collectives, reduce_rows(): got = lax.all_to_all(blocks, 'tp', 0, 0, tiled=False)  18.5 us
    ppermute x14, waiting for transfers between devices, gather_rows(): parts.append(lax.ppermute(rows, 'tp', pairs))  15.9 us
    all_to_all x1, waiting for transfers between devices, reduce_rows(): got = lax.all_to_all(blocks, 'tp', 0, 0, tiled=False)  14.1 us
    all_to_all x1, starting transfers between devices, on_device(): got = lax.all_to_all(held, 'req', 0, 0, tiled=False)  11.7 us
    all_to_all x1, starting transfers between devices, reduce_rows(): got = lax.all_to_all(blocks, 'tp', 0, 0, tiled=False)  9.74 us
  transfers between devices with their start and end apart: 17, of which 5 were waited for; matrix products, arithmetic and copies ran while one was open for 15% of the time, Pallas kernels for 0%

profile of v9, /device:TPU:1, one launch (start us, length us, event | category | flops | bytes accessed | tf_op | source)
XLA Modules:
  0.0 238.0 jit_solution(15592718573786024054)
XLA Ops:
  1.4 1.5 fusion.1
  3.0 2.9 %multiply_reduce_fusion = (f32[256,2]{0,1:T(2,128)S(1)}, f32[256,256]{0,1:T(8,128)}) fusion(bf16[2048,256]{1,0:T(8,128)(2,1)} %param.28, bf16[256,2048]{1,0:T(8,128)(2,1)} %param.20, f32[2048]{0:T(1024)} %param.27, f32[256]{0:T(256)S(1)} %add_rsqrt_fusion.2), kind=kOutput, calls=%fused_computation.46 | convolution fusion | flops 270663168 | bytes 2370560 | tf_op jit(solution)/shard_map/dot_general | solution.py:243
  8.1 3.0 %broadcast_in_dim.139 = bf16[16,256,2,128]{3,2,1,0:T(2,128)(2,1)} broadcast(bf16[256,2,128]{2,1,0:T(2,128)(2,1)S(1)} %copy.135), dimensions={1,2,3} | broadcast | bytes 2228224 | tf_op jit(solution)/shard_map/broadcast_in_dim | solution.py:284
  11.1 8.8 %all-to-all-start = ((bf16[16,256,2,128]{3,2,1,0:T(2,128)(2,1)}), bf16[16,256,2,128]{3,2,1,0:T(2,128)(2,1)}, u32[]{:S(2)}, u32[]{:S(2)}) async-start(bf16[16,256,2,128]{3,2,1,0:T(2,128)(2,1)} %broadcast_in_dim.139), calls=%async_computation | async-start | bytes 4194304 | tf_op jit(solution)/shard_map/all_to_all | solution.py:285
  20.0 3.5 %gather_fusion = s32[512]{0:T(512)S(1)} fusion(s32[512]{0:T(512)S(1)} %bitcast.111, s32[1024]{0:T(1024)S(1)} %pad_clamp_fusion.1), kind=kCustom, calls=%fused_computation.2 | custom fusion | bytes 6144 | tf_op jit(solution)/shard_map/gather | solution.py:263
  23.6 3.5 %gather_fusion.1 = s32[512]{0:T(512)S(1)} fusion(s32[512]{0:T(512)S(1)} %bitcast.110, s32[1024]{0:T(1024)S(1)} %pad_clamp_fusion.1), kind=kCustom, calls=%fused_computation.3 | custom fusion | bytes 6144 | tf_op jit(solution)/shard_map/gather | solution.py:264
  38.7 9.3 %all-to-all-done = bf16[16,256,2,128]{3,2,1,0:T(2,128)(2,1)} async-done(((bf16[16,256,2,128]{3,2,1,0:T(2,128)(2,1)}), bf16[16,256,2,128]{3,2,1,0:T(2,128)(2,1)}, u32[]{:S(2)}, u32[]{:S(2)}) %all-to-all-start) | async-done | bytes 2097184 | tf_op jit(solution)/shard_map/all_to_all | solution.py:285
  48.1 20.7 %shard_map.172 = bf16[16,544,128]{2,1,0:T(8,128)(2,1)} custom-call(s32[32]{0:T(128)} %min.12.slot_ref, s32[32]{0:T(128)} %reshape.403.alive_ref, bf16[16,512,128]{2,1,0:T(8,128)(2,1)} %bitcast.5.q_ref, bf16[32,512,128]{2,1,0:T(8,128)(2,1)} %k1_ref.1, bf16[32,512,128]{2,1,0:T(8,128)(2,1)} %k1_ref.1, bf16[32,512,128]{2,1,0:T(8,128)(2,1)} %v1_ref.1, ...), custom_call_target="tpu_custom_call" | custom-call | tf_op jit(solution)/shard_map/pallas_call | solution.py:185
  68.8 11.7 %all-to-all-start.1 = ((bf16[16,544,128]{2,1,0:T(8,128)(2,1)}), bf16[16,544,128]{2,1,0:T(8,128)(2,1)}, u32[]{:S(2)}, u32[]{:S(2)}) async-start(bf16[16,544,128]{2,1,0:T(8,128)(2,1)} %shard_map.172), calls=%async_computation.1 | async-start | bytes 4456448 | tf_op jit(solution)/shard_map/all_to_all | solution.py:299
  80.6 1.9 multiply_reduce_fusion.1
  84.2 2.2 convolution_bitcast_fusion
  88.4 19.2 %all-to-all-done.1 = bf16[16,544,128]{2,1,0:T(8,128)(2,1)} async-done(((bf16[16,544,128]{2,1,0:T(8,128)(2,1)}), bf16[16,544,128]{2,1,0:T(8,128)(2,1)}, u32[]{:S(2)}, u32[]{:S(2)}) %all-to-all-start.1) | async-done | bytes 2228256 | tf_op jit(solution)/shard_map/all_to_all | solution.py:299
  110.0 1.8 slice.64
  111.8 3.7 %convert.20 = f32[16,256,2,128]{3,2,1,0:T(2,128)} convert(bf16[16,256,2,128]{3,2,1,0:T(2,128)(2,1)S(1)} %bitcast.112) | non-fusion elementwise | flops 1048576 | bytes 6291456 | tf_op jit(solution)/shard_map/reshape | solution.py:313
  115.5 2.8 %copy.149 = f32[17,256,2]{2,1,0:T(8,128)} copy(f32[17,256,2]{1,2,0:T(2,128)} %get-tuple-element.17) | data formatting | bytes 69632 | tf_op jit(solution)/shard_map/exp | solution.py:74
  118.4 6.8 %fusion = f32[256,2,128]{2,1,0:T(2,128)S(1)} fusion(f32[1,256,2,128]{3,2,1,0:T(2,128)S(1)} %copy-done.3, f32[16,256,2,128]{3,2,1,0:T(2,128)} %convert.20, f32[17,256,2]{2,1,0:T(8,128)} %copy.149), kind=kLoop, calls=%fused_computation.6 | loop fusion | flops 3276800 | bytes 4753408 | tf_op jit(solution)/shard_map/reduce_sum | solution.py:75
  126.9 9.7 %all-to-all-start.2 = ((bf16[8,32,2048]{2,1,0:T(8,128)(2,1)}), bf16[8,32,2048]{2,1,0:T(8,128)(2,1)}, u32[]{:S(2)}, u32[]{:S(2)}) async-start(bf16[8,32,2048]{2,1,0:T(8,128)(2,1)} %bitcast.113), calls=%async_computation.2 | async-start | bytes 2097152 | tf_op jit(solution)/shard_map/all_to_all | solution.py:195
  137.7 14.1 %all-to-all-done.2 = bf16[8,32,2048]{2,1,0:T(8,128)(2,1)} async-done(((bf16[8,32,2048]{2,1,0:T(8,128)(2,1)}), bf16[8,32,2048]{2,1,0:T(8,128)(2,1)}, u32[]{:S(2)}, u32[]{:S(2)}) %all-to-all-start.2) | async-done | bytes 1048608 | tf_op jit(solution)/shard_map/all_to_all | solution.py:195
  156.1 2.5 %collective-permute-start.5 = (bf16[32,2048]{1,0:T(8,128)(2,1)S(1)}, bf16[32,2048]{1,0:T(8,128)(2,1)S(1)}, u32[]{:S(2)}, u32[]{:S(2)}) collective-permute-start(bf16[32,2048]{1,0:T(8,128)(2,1)S(1)} %get-tuple-element.13), channel_id=1, source_target_pairs={{0,6},{1,7},{2,0},{3,1},{4,2},{5,3},{6,4},{7,5},{8,14},{9,15},{10,... | collective-permute-start | bytes 393224 | tf_op jit(solution)/shard_map/ppermute | solution.py:204
  159.4 2.4 %collective-permute-start.2 = (bf16[32,2048]{1,0:T(8,128)(2,1)S(1)}, bf16[32,2048]{1,0:T(8,128)(2,1)S(1)}, u32[]{:S(2)}, u32[]{:S(2)}) collective-permute-start(bf16[32,2048]{1,0:T(8,128)(2,1)S(1)} %get-tuple-element.13), channel_id=1, source_target_pairs={{0,3},{1,4},{2,5},{3,6},{4,7},{5,0},{6,1},{7,2},{8,11},{9,12},{10,... | collective-permute-start | bytes 393224 | tf_op jit(solution)/shard_map/ppermute | solution.py:204
  163.4 7.9 %collective-permute-done.1 = bf16[32,2048]{1,0:T(8,128)(2,1)S(1)} collective-permute-done((bf16[32,2048]{1,0:T(8,128)(2,1)S(1)}, bf16[32,2048]{1,0:T(8,128)(2,1)S(1)}, u32[]{:S(2)}, u32[]{:S(2)}) %collective-permute-start.1) | collective-permute-done | bytes 131104 | tf_op jit(solution)/shard_map/ppermute | solution.py:204
  171.3 1.7 collective-permute-start.6
  177.0 2.8 %gather_fusion.3 = bf16[8,32,2048]{2,1,0:T(8,128)(2,1)} fusion(bf16[8,32,2048]{2,1,0:T(8,128)(2,1)} %bitcast_dynamic-update-slice_fusion.8, s32[1024]{0:T(1024)S(1)} %pad_clamp_fusion), kind=kCustom, calls=%fused_computation.clone | custom fusion | bytes 2097184 | tf_op jit(solution)/shard_map/jit(_take)/gather | solution.py:207
  182.2 3.8 %fusion.59 = f32[256,768]{1,0:T(8,128)} fusion(bf16[256,2048]{1,0:T(8,128)(2,1)S(1)} %bitcast.114, bf16[2048,768]{1,0:T(8,128)(2,1)} %param.35), kind=kOutput, calls=%fused_computation.145 | convolution fusion | flops 805306368 | bytes 4980736 | tf_op jit(solution)/shard_map/dot_general | solution.py:82
  186.0 5.5 %convolution_convert_fusion.1 = bf16[256,2048]{1,0:T(8,128)(2,1)} fusion(bf16[768,2048]{1,0:T(8,128)(2,1)S(1)} %copy-done, bf16[256,2048]{1,0:T(8,128)(2,1)} %bitcast.115, bf16[2048,768]{1,0:T(8,128)(2,1)} %param.36, f32[256,768]{1,0:T(8,128)} %fusion.59), kind=kOutput, calls=%fused_computation.10 | convolution fusion | flops 1612316672 | bytes 9175040 | tf_op jit(solution)/shard_map/dot_general | solution.py:326
  191.5 18.5 %all_to_all.20 = bf16[8,32,2048]{2,1,0:T(8,128)(2,1)S(1)} all-to-all(bf16[8,32,2048]{2,1,0:T(8,128)(2,1)} %bitcast.119), channel_id=1, replica_groups=mesh['req'=16,'tp'=8] {'tp'}, dimensions={0} | all-to-all | bytes 2097152 | tf_op jit(solution)/shard_map/all_to_all | solution.py:195
  212.1 2.3 collective-permute-start.12
  215.2 2.4 %collective-permute-start.9 = (bf16[32,2048]{1,0:T(8,128)(2,1)S(1)}, bf16[32,2048]{1,0:T(8,128)(2,1)S(1)}, u32[]{:S(2)}, u32[]{:S(2)}) collective-permute-start(bf16[32,2048]{1,0:T(8,128)(2,1)S(1)} %get-tuple-element.11), channel_id=1, source_target_pairs={{0,3},{1,4},{2,5},{3,6},{4,7},{5,0},{6,1},{7,2},{8,11},{9,12},{10,... | collective-permute-start | bytes 393224 | tf_op jit(solution)/shard_map/ppermute | solution.py:204
  219.1 8.0 %collective-permute-done.8 = bf16[32,2048]{1,0:T(8,128)(2,1)S(1)} collective-permute-done((bf16[32,2048]{1,0:T(8,128)(2,1)S(1)}, bf16[32,2048]{1,0:T(8,128)(2,1)S(1)}, u32[]{:S(2)}, u32[]{:S(2)}) %collective-permute-start.8) | collective-permute-done | bytes 131104 | tf_op jit(solution)/shard_map/ppermute | solution.py:204
  227.1 1.7 collective-permute-start.13
  232.8 2.8 %gather_fusion.4 = bf16[8,32,2048]{2,1,0:T(8,128)(2,1)} fusion(bf16[8,32,2048]{2,1,0:T(8,128)(2,1)} %bitcast_dynamic-update-slice_fusion, s32[1024]{0:T(1024)S(1)} %pad_clamp_fusion), kind=kCustom, calls=%fused_computation.1.clone | custom fusion | bytes 2097184 | tf_op jit(solution)/shard_map/jit(_take)/gather | solution.py:207
  235.6 2.4 broadcast_select_fusion.1
  (156 shorter events, 45.9 us)
Async XLA Ops:
  0.0 186.0 %copy-start = (bf16[768,2048]{1,0:T(8,128)(2,1)S(1)}, bf16[768,2048]{1,0:T(8,128)(2,1)}, u32[]{:S(2)}) copy-start(bf16[768,2048]{1,0:T(8,128)(2,1)} %param.37) | copy-start | bytes 9437188
  0.0 7.0 %copy-start.11 = (f32[64]{0:T(128)}, f32[64]{0:T(128)S(1)}, u32[]{:S(2)}) copy-start(f32[64]{0:T(128)S(1)} %multiply_power_fusion) | copy-start | bytes 772
  1.4 5.6 %copy-start.7 = (f32[256]{0:T(256)}, f32[256]{0:T(256)S(1)}, u32[]{:S(2)}) copy-start(f32[256]{0:T(256)S(1)} %convert_element_type.129) | copy-start | bytes 3076
  1.4 6.1 %copy-start.16 = (f32[128]{0:T(128)S(1)}, f32[128]{0:T(128)}, u32[]{:S(2)}) copy-start(f32[128]{0:T(128)} %param.31) | copy-start | bytes 1540
  3.0 2.9 %copy-start.14 = (f32[256]{0:T(256)}, f32[256]{0:T(256)S(1)}, u32[]{:S(2)}) copy-start(f32[256]{0:T(256)S(1)} %add_rsqrt_fusion.2) | copy-start | bytes 3076
  11.1 8.8 %copy-start.13 = (s32[2,512]{1,0:T(2,128)S(1)}, s32[2,512]{1,0:T(2,128)}, u32[]{:S(2)}) copy-start(s32[2,512]{1,0:T(2,128)} %param.24) | copy-start | bytes 12292
  11.1 8.8 %copy-start.10 = (s32[16,32]{1,0:T(8,128)S(1)}, s32[16,32]{1,0:T(8,128)}, u32[]{:S(2)}) copy-start(s32[16,32]{1,0:T(8,128)} %param.23) | copy-start | bytes 6148
  11.1 37.0 %all-to-all-start = ((bf16[16,256,2,128]{3,2,1,0:T(2,128)(2,1)}), bf16[16,256,2,128]{3,2,1,0:T(2,128)(2,1)}, u32[]{:S(2)}, u32[]{:S(2)}) async-start(bf16[16,256,2,128]{3,2,1,0:T(2,128)(2,1)} %broadcast_in_dim.139), calls=%async_computation | async-start | bytes 4194304 | tf_op jit(solution)/shard_map/all_to_all | solution.py:285
  23.6 4.6 %copy-start.4 = (s32[16,256]{1,0:T(8,128)S(1)}, s32[16,256]{1,0:T(8,128)}, u32[]{:S(2)}) copy-start(s32[16,256]{1,0:T(8,128)} %param.21) | copy-start | bytes 49156
  23.6 4.6 %copy-start.18 = (s32[16]{0:T(128)S(1)}, s32[16]{0:T(128)}, u32[]{:S(2)}) copy-start(s32[16]{0:T(128)} %param.22) | copy-start | bytes 196
  68.8 11.8 %copy-start.15 = (f32[256]{0:T(256)S(1)}, f32[256]{0:T(256)}, u32[]{:S(2)}) copy-start(f32[256]{0:T(256)} %copy-done.14) | copy-start | bytes 3076
  68.8 11.8 %copy-start.19 = (f32[2048]{0:T(1024)S(1)}, f32[2048]{0:T(1024)}, u32[]{:S(2)}) copy-start(f32[2048]{0:T(1024)} %param.27) | copy-start | bytes 24580
  68.8 38.8 %all-to-all-start.1 = ((bf16[16,544,128]{2,1,0:T(8,128)(2,1)}), bf16[16,544,128]{2,1,0:T(8,128)(2,1)}, u32[]{:S(2)}, u32[]{:S(2)}) async-start(bf16[16,544,128]{2,1,0:T(8,128)(2,1)} %shard_map.172), calls=%async_computation.1 | async-start | bytes 4456448 | tf_op jit(solution)/shard_map/all_to_all | solution.py:299
  80.5 2.3 copy-start.8
  115.5 2.8 %copy-start.3 = (f32[1,256,2,128]{3,2,1,0:T(2,128)S(1)}, f32[1,256,2,128]{3,2,1,0:T(2,128)}, u32[]{:S(2)}) copy-start(f32[1,256,2,128]{3,2,1,0:T(2,128)} %copy.145) | copy-start | bytes 786436
  118.4 7.1 %copy-start.2 = (bf16[256,2048]{1,0:T(8,128)(2,1)S(1)}, bf16[256,2048]{1,0:T(8,128)(2,1)}, u32[]{:S(2)}) copy-start(bf16[256,2048]{1,0:T(8,128)(2,1)} %param.33) | copy-start | bytes 3145732
  126.9 27.3 %copy-start.9 = (f32[2048]{0:T(1024)S(1)}, f32[2048]{0:T(1024)}, u32[]{:S(2)}) copy-start(f32[2048]{0:T(1024)} %param.34) | copy-start | bytes 24580
  126.9 24.8 %all-to-all-start.2 = ((bf16[8,32,2048]{2,1,0:T(8,128)(2,1)}), bf16[8,32,2048]{2,1,0:T(8,128)(2,1)}, u32[]{:S(2)}, u32[]{:S(2)}) async-start(bf16[8,32,2048]{2,1,0:T(8,128)(2,1)} %bitcast.113), calls=%async_computation.2 | async-start | bytes 2097152 | tf_op jit(solution)/shard_map/all_to_all | solution.py:195
  155.0 6.9 %collective-permute-start = (bf16[32,2048]{1,0:T(8,128)(2,1)S(1)}, bf16[32,2048]{1,0:T(8,128)(2,1)S(1)}, u32[]{:S(2)}, u32[]{:S(2)}) collective-permute-start(bf16[32,2048]{1,0:T(8,128)(2,1)S(1)} %get-tuple-element.13), channel_id=1, source_target_pairs={{0,1},{1,2},{2,3},{3,4},{4,5},{5,6},{6,7},{7,0},{8,9},{9,10},{10,1... | collective-permute-start | bytes 393224 | tf_op jit(solution)/shard_map/ppermute | solution.py:204
  156.1 19.6 %collective-permute-start.5 = (bf16[32,2048]{1,0:T(8,128)(2,1)S(1)}, bf16[32,2048]{1,0:T(8,128)(2,1)S(1)}, u32[]{:S(2)}, u32[]{:S(2)}) collective-permute-start(bf16[32,2048]{1,0:T(8,128)(2,1)S(1)} %get-tuple-element.13), channel_id=1, source_target_pairs={{0,6},{1,7},{2,0},{3,1},{4,2},{5,3},{6,4},{7,5},{8,14},{9,15},{10,... | collective-permute-start | bytes 393224 | tf_op jit(solution)/shard_map/ppermute | solution.py:204
  158.6 16.4 %collective-permute-start.4 = (bf16[32,2048]{1,0:T(8,128)(2,1)S(1)}, bf16[32,2048]{1,0:T(8,128)(2,1)S(1)}, u32[]{:S(2)}, u32[]{:S(2)}) collective-permute-start(bf16[32,2048]{1,0:T(8,128)(2,1)S(1)} %get-tuple-element.13), channel_id=1, source_target_pairs={{0,5},{1,6},{2,7},{3,0},{4,1},{5,2},{6,3},{7,4},{8,13},{9,14},{10,... | collective-permute-start | bytes 393224 | tf_op jit(solution)/shard_map/ppermute | solution.py:204
  158.6 15.8 %collective-permute-start.3 = (bf16[32,2048]{1,0:T(8,128)(2,1)S(1)}, bf16[32,2048]{1,0:T(8,128)(2,1)S(1)}, u32[]{:S(2)}, u32[]{:S(2)}) collective-permute-start(bf16[32,2048]{1,0:T(8,128)(2,1)S(1)} %get-tuple-element.13), channel_id=1, source_target_pairs={{0,4},{1,5},{2,6},{3,7},{4,0},{5,1},{6,2},{7,3},{8,12},{9,13},{10,... | collective-permute-start | bytes 393224 | tf_op jit(solution)/shard_map/ppermute | solution.py:204
  159.4 14.2 %collective-permute-start.2 = (bf16[32,2048]{1,0:T(8,128)(2,1)S(1)}, bf16[32,2048]{1,0:T(8,128)(2,1)S(1)}, u32[]{:S(2)}, u32[]{:S(2)}) collective-permute-start(bf16[32,2048]{1,0:T(8,128)(2,1)S(1)} %get-tuple-element.13), channel_id=1, source_target_pairs={{0,3},{1,4},{2,5},{3,6},{4,7},{5,0},{6,1},{7,2},{8,11},{9,12},{10,... | collective-permute-start | bytes 393224 | tf_op jit(solution)/shard_map/ppermute | solution.py:204
  161.8 9.5 %collective-permute-start.1 = (bf16[32,2048]{1,0:T(8,128)(2,1)S(1)}, bf16[32,2048]{1,0:T(8,128)(2,1)S(1)}, u32[]{:S(2)}, u32[]{:S(2)}) collective-permute-start(bf16[32,2048]{1,0:T(8,128)(2,1)S(1)} %get-tuple-element.13), channel_id=1, source_target_pairs={{0,2},{1,3},{2,4},{3,5},{4,6},{5,7},{6,0},{7,1},{8,10},{9,11},{10,... | collective-permute-start | bytes 393224 | tf_op jit(solution)/shard_map/ppermute | solution.py:204
  171.3 5.0 %collective-permute-start.6 = (bf16[32,2048]{1,0:T(8,128)(2,1)S(1)}, bf16[32,2048]{1,0:T(8,128)(2,1)S(1)}, u32[]{:S(2)}, u32[]{:S(2)}) collective-permute-start(bf16[32,2048]{1,0:T(8,128)(2,1)S(1)} %get-tuple-element.13), channel_id=1, source_target_pairs={{0,7},{1,0},{2,1},{3,2},{4,3},{5,4},{6,5},{7,6},{8,15},{9,8},{10,9... | collective-permute-start | bytes 393224 | tf_op jit(solution)/shard_map/ppermute | solution.py:204
  210.8 6.9 %collective-permute-start.7 = (bf16[32,2048]{1,0:T(8,128)(2,1)S(1)}, bf16[32,2048]{1,0:T(8,128)(2,1)S(1)}, u32[]{:S(2)}, u32[]{:S(2)}) collective-permute-start(bf16[32,2048]{1,0:T(8,128)(2,1)S(1)} %get-tuple-element.11), channel_id=1, source_target_pairs={{0,1},{1,2},{2,3},{3,4},{4,5},{5,6},{6,7},{7,0},{8,9},{9,10},{10,1... | collective-permute-start | bytes 393224 | tf_op jit(solution)/shard_map/ppermute | solution.py:204
  212.1 19.4 %collective-permute-start.12 = (bf16[32,2048]{1,0:T(8,128)(2,1)S(1)}, bf16[32,2048]{1,0:T(8,128)(2,1)S(1)}, u32[]{:S(2)}, u32[]{:S(2)}) collective-permute-start(bf16[32,2048]{1,0:T(8,128)(2,1)S(1)} %get-tuple-element.11), channel_id=1, source_target_pairs={{0,6},{1,7},{2,0},{3,1},{4,2},{5,3},{6,4},{7,5},{8,14},{9,15},{10,... | collective-permute-start | bytes 393224 | tf_op jit(solution)/shard_map/ppermute | solution.py:204
  214.4 16.4 %collective-permute-start.11 = (bf16[32,2048]{1,0:T(8,128)(2,1)S(1)}, bf16[32,2048]{1,0:T(8,128)(2,1)S(1)}, u32[]{:S(2)}, u32[]{:S(2)}) collective-permute-start(bf16[32,2048]{1,0:T(8,128)(2,1)S(1)} %get-tuple-element.11), channel_id=1, source_target_pairs={{0,5},{1,6},{2,7},{3,0},{4,1},{5,2},{6,3},{7,4},{8,13},{9,14},{10,... | collective-permute-start | bytes 393224 | tf_op jit(solution)/shard_map/ppermute | solution.py:204
  214.4 15.8 %collective-permute-start.10 = (bf16[32,2048]{1,0:T(8,128)(2,1)S(1)}, bf16[32,2048]{1,0:T(8,128)(2,1)S(1)}, u32[]{:S(2)}, u32[]{:S(2)}) collective-permute-start(bf16[32,2048]{1,0:T(8,128)(2,1)S(1)} %get-tuple-element.11), channel_id=1, source_target_pairs={{0,4},{1,5},{2,6},{3,7},{4,0},{5,1},{6,2},{7,3},{8,12},{9,13},{10,... | collective-permute-start | bytes 393224 | tf_op jit(solution)/shard_map/ppermute | solution.py:204
  215.2 14.2 %collective-permute-start.9 = (bf16[32,2048]{1,0:T(8,128)(2,1)S(1)}, bf16[32,2048]{1,0:T(8,128)(2,1)S(1)}, u32[]{:S(2)}, u32[]{:S(2)}) collective-permute-start(bf16[32,2048]{1,0:T(8,128)(2,1)S(1)} %get-tuple-element.11), channel_id=1, source_target_pairs={{0,3},{1,4},{2,5},{3,6},{4,7},{5,0},{6,1},{7,2},{8,11},{9,12},{10,... | collective-permute-start | bytes 393224 | tf_op jit(solution)/shard_map/ppermute | solution.py:204
  217.6 9.5 %collective-permute-start.8 = (bf16[32,2048]{1,0:T(8,128)(2,1)S(1)}, bf16[32,2048]{1,0:T(8,128)(2,1)S(1)}, u32[]{:S(2)}, u32[]{:S(2)}) collective-permute-start(bf16[32,2048]{1,0:T(8,128)(2,1)S(1)} %get-tuple-element.11), channel_id=1, source_target_pairs={{0,2},{1,3},{2,4},{3,5},{4,6},{5,7},{6,0},{7,1},{8,10},{9,11},{10,... | collective-permute-start | bytes 393224 | tf_op jit(solution)/shard_map/ppermute | solution.py:204
  227.1 5.0 %collective-permute-start.13 = (bf16[32,2048]{1,0:T(8,128)(2,1)S(1)}, bf16[32,2048]{1,0:T(8,128)(2,1)S(1)}, u32[]{:S(2)}, u32[]{:S(2)}) collective-permute-start(bf16[32,2048]{1,0:T(8,128)(2,1)S(1)} %get-tuple-element.11), channel_id=1, source_target_pairs={{0,7},{1,0},{2,1},{3,2},{4,3},{5,4},{6,5},{7,6},{8,15},{9,8},{10,9... | collective-permute-start | bytes 393224 | tf_op jit(solution)/shard_map/ppermute | solution.py:204
  (5 other events, 8.0 us)

commit v10 on v7

--- a/solution.py
+++ b/solution.py
@@ -193,15 +193,9 @@
 
 
 def gather_rows(rows, tp_count):
-    tp_index = lax.axis_index("tp")
-    parts = [rows]
-    for shift in range(1, tp_count):
-        pairs = [(i, (i + shift) % tp_count) for i in range(tp_count)]
-        parts.append(lax.ppermute(rows, "tp", pairs))
-    stacked = jnp.stack(parts)
-    source = (tp_index - jnp.arange(tp_count)) % tp_count
-    ordered = jnp.take(stacked, jnp.argsort(source), axis=0)
-    return ordered.reshape(tp_count * rows.shape[0], rows.shape[1])
+    copies = jnp.broadcast_to(rows[None], (tp_count,) + rows.shape)
+    got = lax.all_to_all(copies, "tp", 0, 0, tiled=False)
+    return got.reshape(tp_count * rows.shape[0], rows.shape[1])
 
 
 def on_device(

time: 235 us -> 219 us (0.932)
  blocking collectives: 18.5 us -> 56.2 us
  starting transfers between devices: 43 us -> 23.4 us
  waiting for transfers between devices: 56.1 us -> 41 us
  local copies, waits for them, and re-layouts: 44 us -> 30.4 us
  other arithmetic: 30 us -> 24.2 us
    all_to_all x0 -> x2, blocking collectives: none -> 36.7 us  [gather_rows(): got = lax.all_to_all(copies, 'tp', 0, 0, tiled=False)]
    ppermute x14 -> x0, starting transfers between devices: 18.9 us -> none  [gather_rows(): parts.append(lax.ppermute(rows, 'tp', pairs))]
    ppermute x14 -> x0, waiting for transfers between devices: 15.9 us -> none  [gather_rows(): parts.append(lax.ppermute(rows, 'tp', pairs))]
    unnamed x53 -> x44, local copies, waits for them, and re-layouts: 10.3 us -> 3.35 us
    gather x2 -> x0, local copies, waits for them, and re-layouts: 5.61 us -> none  [gather_rows(): ordered = jnp.take(stacked, jnp.argsort(source), axis=0)]
    select_n x4 -> x0, other arithmetic: 3.76 us -> none  [the longest x3 3.75 us: gather_rows(): ordered = jnp.take(stacked, jnp.argsort(source), axis=0)]
  transfers between devices with their start and end apart: 17 -> 3, of which waited for: 5 -> 3; matrix products, arithmetic and copies ran while one was open for 16% -> 13% of each run, Pallas kernels for 0% -> 0%
where the time goes in v10:
time: 219 us; the launch traced here: 218 us
  blocking collectives  56.2 us (26%)
  waiting for transfers between devices  41 us (19%)
  local copies, waits for them, and re-layouts  30.4 us (14%)
  Pallas kernels  25.8 us (12%)
  other arithmetic  24.2 us (11%)
  starting transfers between devices  23.4 us (11%)
  matrix products  17 us (8%)
    all_to_all x2, blocking collectives, gather_rows(): got = lax.all_to_all(copies, 'tp', 0, 0, tiled=False)  36.7 us
    pallas_call x1, Pallas kernels, held_blocks(): pl.pallas_call(held_block_kernel, grid_spec=grid_spec, out_shape=jax.Shap...  25.8 us
    all_to_all x1, blocking collectives, reduce_rows(): got = lax.all_to_all(blocks, 'tp', 0, 0, tiled=False)  19.4 us
    all_to_all x1, waiting for transfers between devices, on_device(): got = lax.all_to_all(held, 'req', 0, 0, tiled=False)  18.8 us
    all_to_all x1, waiting for transfers between devices, reduce_rows(): got = lax.all_to_all(blocks, 'tp', 0, 0, tiled=False)  15.1 us
    all_to_all x1, starting transfers between devices, reduce_rows(): got = lax.all_to_all(blocks, 'tp', 0, 0, tiled=False)  9.96 us
    all_to_all x1, starting transfers between devices, on_device(): all_queries = lax.all_to_all(query_copies, 'req', 0, 0, tiled=False)  8.77 us
    all_to_all x1, waiting for transfers between devices, on_device(): all_queries = lax.all_to_all(query_copies, 'req', 0, 0, tiled=False)  7.12 us
  transfers between devices with their start and end apart: 3, of which 3 were waited for; matrix products, arithmetic and copies ran while one was open for 13% of the time, Pallas kernels for 0%

profile of v10, /device:TPU:1, one launch (start us, length us, event | category | flops | bytes accessed | tf_op | source)
XLA Modules:
  0.0 218.3 jit_solution(1769915372725580942)
XLA Ops:
  1.5 1.5 fusion.1
  3.0 2.9 %multiply_reduce_fusion = (f32[256,2]{0,1:T(2,128)S(1)}, f32[256,256]{0,1:T(8,128)}) fusion(bf16[2048,256]{1,0:T(8,128)(2,1)} %param.26, bf16[256,2048]{1,0:T(8,128)(2,1)} %param.18, f32[2048]{0:T(1024)} %param.25, f32[256]{0:T(256)S(1)} %add_rsqrt_fusion.2), kind=kOutput, calls=%fused_computation.41 | convolution fusion | flops 270663168 | bytes 2370560 | tf_op jit(solution)/shard_map/dot_general | solution.py:233
  5.9 1.1 copy.96
  8.1 3.0 %broadcast_in_dim.69 = bf16[16,256,2,128]{3,2,1,0:T(2,128)(2,1)} broadcast(bf16[256,2,128]{2,1,0:T(2,128)(2,1)S(1)} %copy.97), dimensions={1,2,3} | broadcast | bytes 2228224 | tf_op jit(solution)/shard_map/broadcast_in_dim | solution.py:271
  11.1 8.8 %all-to-all-start = ((bf16[16,256,2,128]{3,2,1,0:T(2,128)(2,1)}), bf16[16,256,2,128]{3,2,1,0:T(2,128)(2,1)}, u32[]{:S(2)}, u32[]{:S(2)}) async-start(bf16[16,256,2,128]{3,2,1,0:T(2,128)(2,1)} %broadcast_in_dim.69), calls=%async_computation | async-start | bytes 4194304 | tf_op jit(solution)/shard_map/all_to_all | solution.py:272
  20.8 3.5 %gather_fusion.1 = s32[512]{0:T(512)S(1)} fusion(s32[512]{0:T(512)S(1)} %bitcast.75, s32[1024]{0:T(1024)S(1)} %pad_clamp_fusion), kind=kCustom, calls=%fused_computation.1 | custom fusion | bytes 6144 | tf_op jit(solution)/shard_map/gather | solution.py:254
  24.3 3.5 %gather_fusion = s32[512]{0:T(512)S(1)} fusion(s32[512]{0:T(512)S(1)} %bitcast.74, s32[1024]{0:T(1024)S(1)} %pad_clamp_fusion), kind=kCustom, calls=%fused_computation | custom fusion | bytes 6144 | tf_op jit(solution)/shard_map/gather | solution.py:253
  31.3 1.0 broadcast_in_dim.72
  32.3 4.8 %copy.103.qpos_ref = s32[16,512,1]{2,1,0:T(8,128)} copy(s32[16,512,1]{0,1,2:T(8,128)S(1)} %bitcast.79) | data formatting | bytes 65536 | tf_op jit(solution)/shard_map/broadcast_in_dim;reshape | solution.py:274
  39.5 1.4 broadcast_select_fusion.kpos_ref
  41.0 7.1 %all-to-all-done = bf16[16,256,2,128]{3,2,1,0:T(2,128)(2,1)} async-done(((bf16[16,256,2,128]{3,2,1,0:T(2,128)(2,1)}), bf16[16,256,2,128]{3,2,1,0:T(2,128)(2,1)}, u32[]{:S(2)}, u32[]{:S(2)}) %all-to-all-start) | async-done | bytes 2097184 | tf_op jit(solution)/shard_map/all_to_all | solution.py:272
  48.1 25.8 %shard_map.172 = bf16[16,544,128]{2,1,0:T(8,128)(2,1)} custom-call(s32[32]{0:T(128)} %min.12.slot_ref, s32[32]{0:T(128)} %reshape.370.alive_ref, bf16[16,512,128]{2,1,0:T(8,128)(2,1)} %bitcast.4.q_ref, bf16[32,512,128]{2,1,0:T(8,128)(2,1)} %k1_ref.1, bf16[32,512,128]{2,1,0:T(8,128)(2,1)} %k1_ref.1, bf16[32,512,128]{2,1,0:T(8,128)(2,1)} %v1_ref.1, ...), custom_call_target="tpu_custom_call" | custom-call | tf_op jit(solution)/shard_map/pallas_call | solution.py:181
  73.9 4.6 %all-to-all-start.1 = ((bf16[16,544,128]{2,1,0:T(8,128)(2,1)}), bf16[16,544,128]{2,1,0:T(8,128)(2,1)}, u32[]{:S(2)}, u32[]{:S(2)}) async-start(bf16[16,544,128]{2,1,0:T(8,128)(2,1)} %shard_map.172), calls=%async_computation.1 | async-start | bytes 4456448 | tf_op jit(solution)/shard_map/all_to_all | solution.py:284
  78.6 1.9 multiply_reduce_fusion.1
  81.1 1.1 select_reduce_fusion
  82.2 2.2 %convolution_bitcast_fusion = f32[1,256,2,128]{1,3,2,0:T(8,128)S(1)} fusion(bf16[2048,128]{1,0:T(8,128)(2,1)} %param.28, f32[1,2,256,256]{2,3,1,0:T(8,128)} %get-tuple-element.34, f32[2,256]{1,0:T(2,128)S(1)} %get-tuple-element.33, pred[256,256]{0,1:T(8,128)(4,1)S(1)} %compare_and_fusion, bf16[256,2048]{1,0:T(8,128)(2,1)} %param.18, ...), kind=kOutput, calls=%fused_computation.18 | convolution fusion | flops 170295296 | bytes 2436096 | tf_op jit(solution)/shard_map/hgmk,khd->mhgd/dot_general | solution.py:61
  85.2 1.2 fusion.8
  86.4 18.8 %all-to-all-done.1 = bf16[16,544,128]{2,1,0:T(8,128)(2,1)} async-done(((bf16[16,544,128]{2,1,0:T(8,128)(2,1)}), bf16[16,544,128]{2,1,0:T(8,128)(2,1)}, u32[]{:S(2)}, u32[]{:S(2)}) %all-to-all-start.1) | async-done | bytes 2228256 | tf_op jit(solution)/shard_map/all_to_all | solution.py:284
  107.7 1.8 slice.58
  109.5 3.7 %convert.20 = f32[16,256,2,128]{3,2,1,0:T(2,128)} convert(bf16[16,256,2,128]{3,2,1,0:T(2,128)(2,1)S(1)} %bitcast.76) | non-fusion elementwise | flops 1048576 | bytes 6291456 | tf_op jit(solution)/shard_map/reshape | solution.py:298
  113.2 2.8 %copy.111 = f32[17,256,2]{2,1,0:T(8,128)} copy(f32[17,256,2]{1,2,0:T(2,128)} %get-tuple-element.10) | data formatting | bytes 69632 | tf_op jit(solution)/shard_map/exp | solution.py:74
  116.0 6.8 %fusion = f32[256,2,128]{2,1,0:T(2,128)S(1)} fusion(f32[1,256,2,128]{3,2,1,0:T(2,128)S(1)} %copy-done.3, f32[16,256,2,128]{3,2,1,0:T(2,128)} %convert.20, f32[17,256,2]{2,1,0:T(8,128)} %copy.111), kind=kLoop, calls=%fused_computation.3 | loop fusion | flops 3276800 | bytes 4753408 | tf_op jit(solution)/shard_map/reduce_sum | solution.py:75
  123.2 1.4 convolution_convert_fusion
  124.6 10.0 %all-to-all-start.2 = ((bf16[8,32,2048]{2,1,0:T(8,128)(2,1)}), bf16[8,32,2048]{2,1,0:T(8,128)(2,1)}, u32[]{:S(2)}, u32[]{:S(2)}) async-start(bf16[8,32,2048]{2,1,0:T(8,128)(2,1)} %bitcast.77), calls=%async_computation.2 | async-start | bytes 2097152 | tf_op jit(solution)/shard_map/all_to_all | solution.py:191
  134.5 15.1 %all-to-all-done.2 = bf16[8,32,2048]{2,1,0:T(8,128)(2,1)} async-done(((bf16[8,32,2048]{2,1,0:T(8,128)(2,1)}), bf16[8,32,2048]{2,1,0:T(8,128)(2,1)}, u32[]{:S(2)}, u32[]{:S(2)}) %all-to-all-start.2) | async-done | bytes 1048608 | tf_op jit(solution)/shard_map/all_to_all | solution.py:191
  149.6 1.4 convert_reduce_fusion.1
  151.0 1.2 fusion.11
  152.5 18.3 %all_to_all.30 = bf16[8,32,2048]{2,1,0:T(8,128)(2,1)S(1)} all-to-all(bf16[8,32,2048]{2,1,0:T(8,128)(2,1)S(1)} %broadcast_in_dim.78), channel_id=1, replica_groups=mesh['req'=16,'tp'=8] {'tp'}, dimensions={0} | all-to-all | bytes 2097152 | tf_op jit(solution)/shard_map/all_to_all | solution.py:197
  171.8 1.9 fusion.55
  173.7 5.5 %convolution_convert_fusion.1 = bf16[256,2048]{1,0:T(8,128)(2,1)} fusion(bf16[768,2048]{1,0:T(8,128)(2,1)S(1)} %copy-done, bf16[256,2048]{1,0:T(8,128)(2,1)} %bitcast.83, bf16[2048,768]{1,0:T(8,128)(2,1)} %param.34, f32[256,768]{1,0:T(8,128)} %fusion.55), kind=kOutput, calls=%fused_computation.7 | convolution fusion | flops 1612316672 | bytes 9175040 | tf_op jit(solution)/shard_map/dot_general | solution.py:311
  179.2 19.4 %all_to_all.31 = bf16[8,32,2048]{2,1,0:T(8,128)(2,1)S(1)} all-to-all(bf16[8,32,2048]{2,1,0:T(8,128)(2,1)} %bitcast.84), channel_id=1, replica_groups=mesh['req'=16,'tp'=8] {'tp'}, dimensions={0} | all-to-all | bytes 2097152 | tf_op jit(solution)/shard_map/all_to_all | solution.py:191
  198.9 18.4 %all_to_all.32 = bf16[8,32,2048]{2,1,0:T(8,128)(2,1)S(1)} all-to-all(bf16[8,32,2048]{2,1,0:T(8,128)(2,1)S(1)} %broadcast_in_dim.79), channel_id=1, replica_groups=mesh['req'=16,'tp'=8] {'tp'}, dimensions={0} | all-to-all | bytes 2097152 | tf_op jit(solution)/shard_map/all_to_all | solution.py:197
  (100 shorter events, 15.9 us)
Async XLA Ops:
  0.0 173.7 %copy-start = (bf16[768,2048]{1,0:T(8,128)(2,1)S(1)}, bf16[768,2048]{1,0:T(8,128)(2,1)}, u32[]{:S(2)}) copy-start(bf16[768,2048]{1,0:T(8,128)(2,1)} %param.35) | copy-start | bytes 9437188
  0.0 7.0 %copy-start.11 = (f32[64]{0:T(128)}, f32[64]{0:T(128)S(1)}, u32[]{:S(2)}) copy-start(f32[64]{0:T(128)S(1)} %multiply_power_fusion) | copy-start | bytes 772
  0.9 0.6 copy-start.5
  1.5 5.6 %copy-start.7 = (f32[256]{0:T(256)}, f32[256]{0:T(256)S(1)}, u32[]{:S(2)}) copy-start(f32[256]{0:T(256)S(1)} %convert_element_type.109) | copy-start | bytes 3076
  1.5 6.1 %copy-start.16 = (f32[128]{0:T(128)S(1)}, f32[128]{0:T(128)}, u32[]{:S(2)}) copy-start(f32[128]{0:T(128)} %param.29) | copy-start | bytes 1540
  3.0 2.9 %copy-start.14 = (f32[256]{0:T(256)}, f32[256]{0:T(256)S(1)}, u32[]{:S(2)}) copy-start(f32[256]{0:T(256)S(1)} %add_rsqrt_fusion.2) | copy-start | bytes 3076
  11.1 8.8 %copy-start.10 = (s32[16,32]{1,0:T(8,128)S(1)}, s32[16,32]{1,0:T(8,128)}, u32[]{:S(2)}) copy-start(s32[16,32]{1,0:T(8,128)} %param.21) | copy-start | bytes 6148
  11.1 8.9 %copy-start.4 = (s32[16,256]{1,0:T(8,128)S(1)}, s32[16,256]{1,0:T(8,128)}, u32[]{:S(2)}) copy-start(s32[16,256]{1,0:T(8,128)} %param.19) | copy-start | bytes 49156
  11.1 9.7 %copy-start.13 = (s32[2,512]{1,0:T(2,128)S(1)}, s32[2,512]{1,0:T(2,128)}, u32[]{:S(2)}) copy-start(s32[2,512]{1,0:T(2,128)} %param.22) | copy-start | bytes 12292
  11.1 37.0 %all-to-all-start = ((bf16[16,256,2,128]{3,2,1,0:T(2,128)(2,1)}), bf16[16,256,2,128]{3,2,1,0:T(2,128)(2,1)}, u32[]{:S(2)}, u32[]{:S(2)}) async-start(bf16[16,256,2,128]{3,2,1,0:T(2,128)(2,1)} %broadcast_in_dim.69), calls=%async_computation | async-start | bytes 4194304 | tf_op jit(solution)/shard_map/all_to_all | solution.py:272
  24.3 4.7 %copy-start.18 = (s32[16]{0:T(128)S(1)}, s32[16]{0:T(128)}, u32[]{:S(2)}) copy-start(s32[16]{0:T(128)} %param.20) | copy-start | bytes 196
  73.9 4.7 %copy-start.15 = (f32[256]{0:T(256)S(1)}, f32[256]{0:T(256)}, u32[]{:S(2)}) copy-start(f32[256]{0:T(256)} %copy-done.14) | copy-start | bytes 3076
  73.9 4.7 %copy-start.20 = (f32[2048]{0:T(1024)S(1)}, f32[2048]{0:T(1024)}, u32[]{:S(2)}) copy-start(f32[2048]{0:T(1024)} %param.25) | copy-start | bytes 24580
  73.9 31.3 %all-to-all-start.1 = ((bf16[16,544,128]{2,1,0:T(8,128)(2,1)}), bf16[16,544,128]{2,1,0:T(8,128)(2,1)}, u32[]{:S(2)}, u32[]{:S(2)}) async-start(bf16[16,544,128]{2,1,0:T(8,128)(2,1)} %shard_map.172), calls=%async_computation.1 | async-start | bytes 4456448 | tf_op jit(solution)/shard_map/all_to_all | solution.py:284
  78.5 2.0 copy-start.6
  78.5 2.2 %copy-start.17 = (f32[128]{0:T(128)S(1)}, f32[128]{0:T(128)}, u32[]{:S(2)}) copy-start(f32[128]{0:T(128)} %param.30) | copy-start | bytes 1540
  78.5 2.3 %copy-start.8 = (f32[256]{0:T(256)S(1)}, f32[256]{0:T(256)}, u32[]{:S(2)}) copy-start(f32[256]{0:T(256)} %copy-done.7) | copy-start | bytes 3076
  78.5 2.3 %copy-start.12 = (f32[64]{0:T(128)S(1)}, f32[64]{0:T(128)}, u32[]{:S(2)}) copy-start(f32[64]{0:T(128)} %copy-done.11) | copy-start | bytes 772
  113.2 2.9 %copy-start.3 = (f32[1,256,2,128]{3,2,1,0:T(2,128)S(1)}, f32[1,256,2,128]{3,2,1,0:T(2,128)}, u32[]{:S(2)}) copy-start(f32[1,256,2,128]{3,2,1,0:T(2,128)} %copy.107) | copy-start | bytes 786436
  116.0 7.1 %copy-start.1 = (bf16[256,2048]{1,0:T(8,128)(2,1)S(1)}, bf16[256,2048]{1,0:T(8,128)(2,1)}, u32[]{:S(2)}) copy-start(bf16[256,2048]{1,0:T(8,128)(2,1)} %param.31) | copy-start | bytes 3145732
  124.6 27.7 %copy-start.9 = (f32[2048]{0:T(1024)S(1)}, f32[2048]{0:T(1024)}, u32[]{:S(2)}) copy-start(f32[2048]{0:T(1024)} %param.32) | copy-start | bytes 24580
  124.6 25.0 %all-to-all-start.2 = ((bf16[8,32,2048]{2,1,0:T(8,128)(2,1)}), bf16[8,32,2048]{2,1,0:T(8,128)(2,1)}, u32[]{:S(2)}, u32[]{:S(2)}) async-start(bf16[8,32,2048]{2,1,0:T(8,128)(2,1)} %bitcast.77), calls=%async_computation.2 | async-start | bytes 2097152 | tf_op jit(solution)/shard_map/all_to_all | solution.py:191
  151.0 20.8 %copy-start.19 = (bf16[2048,768]{1,0:T(8,128)(2,1)S(1)}, bf16[2048,768]{1,0:T(8,128)(2,1)}, u32[]{:S(2)}) copy-start(bf16[2048,768]{1,0:T(8,128)(2,1)} %param.33) | copy-start | bytes 9437188
  170.8 1.0 copy-start.2

commit v11 on v10

--- a/solution.py
+++ b/solution.py
@@ -294,11 +294,13 @@
 
     got_peak = stat_of(0)
     got_total = stat_of(1)
-    attended = merge_stats(
-        jnp.concatenate([got_sum.reshape(req_count, count_of_rows, head_total, head_size), fresh_sum[None]]),
-        jnp.concatenate([got_peak, fresh_peak[None]]),
-        jnp.concatenate([got_total, fresh_total[None]]),
-    )
+    got_sum = got_sum.reshape(req_count, count_of_rows, head_total, head_size)
+    row_top = jnp.maximum(jnp.max(got_peak, axis=0), fresh_peak)
+    held_factor = jnp.exp(got_peak - row_top[None])
+    fresh_factor = jnp.exp(fresh_peak - row_top)
+    merged = jnp.sum(got_sum * held_factor[..., None], axis=0) + fresh_sum * fresh_factor[..., None]
+    merged_total = jnp.sum(got_total * held_factor, axis=0) + fresh_total * fresh_factor
+    attended = (merged / merged_total[..., None]).astype(jnp.bfloat16).reshape(count_of_rows, -1)
     tp_count = lax.axis_size("tp")
     tp_index = lax.axis_index("tp")
     block_rows = count_of_rows // tp_count

time: 219 us -> 218 us (level)
  other arithmetic: 24.2 us -> 20.7 us
  local copies, waits for them, and re-layouts: 30.4 us -> 33 us
  Pallas kernels: 25.8 us -> 23.6 us
    reshape x1 -> x0, other arithmetic: 3.68 us -> none  [on_device(): got_sum.reshape(req_count, count_of_rows, head_total, head_size)]
    reduce_sum x1 -> x3, local copies, waits for them, and re-layouts: 0.14 us -> 3.49 us  [the longest x2 1.77 us: on_device(): jnp.sum(got_total * held_factor, axis=0) + fresh_total * fresh_factor]
    reduce_sum x2, other arithmetic: 7.43 us -> 4.75 us  [the longest x1 3.87 us: on_device(): jnp.sum(got_sum * held_factor[..., None], axis=0)]
  transfers between devices with their start and end apart: 3 -> 3, of which waited for: 3 -> 3; matrix products, arithmetic and copies ran while one was open for 13% -> 14% of each run, Pallas kernels for 0% -> 0%
where the time goes in v11:
time: 218 us; the launch traced here: 215 us
  blocking collectives  56.2 us (26%)
  waiting for transfers between devices  39 us (18%)
  local copies, waits for them, and re-layouts  33 us (15%)
  Pallas kernels  23.6 us (11%)
  starting transfers between devices  23.4 us (11%)
  other arithmetic  20.7 us (9%)
  matrix products  19 us (9%)
    all_to_all x2, blocking collectives, gather_rows(): got = lax.all_to_all(copies, 'tp', 0, 0, tiled=False)  36.7 us
    pallas_call x1, Pallas kernels, held_blocks(): pl.pallas_call(held_block_kernel, grid_spec=grid_spec, out_shape=jax.Shap...  23.6 us
    all_to_all x1, blocking collectives, reduce_rows(): got = lax.all_to_all(blocks, 'tp', 0, 0, tiled=False)  19.4 us
    all_to_all x1, waiting for transfers between devices, on_device(): got = lax.all_to_all(held, 'req', 0, 0, tiled=False)  16.8 us
    all_to_all x1, waiting for transfers between devices, reduce_rows(): got = lax.all_to_all(blocks, 'tp', 0, 0, tiled=False)  15.1 us
    all_to_all x1, starting transfers between devices, reduce_rows(): got = lax.all_to_all(blocks, 'tp', 0, 0, tiled=False)  9.99 us
    all_to_all x1, starting transfers between devices, on_device(): all_queries = lax.all_to_all(query_copies, 'req', 0, 0, tiled=False)  8.77 us
    all_to_all x1, waiting for transfers between devices, on_device(): all_queries = lax.all_to_all(query_copies, 'req', 0, 0, tiled=False)  7.14 us
  transfers between devices with their start and end apart: 3, of which 3 were waited for; matrix products, arithmetic and copies ran while one was open for 14% of the time, Pallas kernels for 0%

profile of v11, /device:TPU:1, one launch (start us, length us, event | category | flops | bytes accessed | tf_op | source)
XLA Modules:
  0.0 215.3 jit_solution(8485799183793798108)
XLA Ops:
  1.5 1.5 fusion
  3.0 2.9 %multiply_reduce_fusion.1 = (f32[256,2]{0,1:T(2,128)S(1)}, f32[256,256]{0,1:T(8,128)}) fusion(bf16[2048,256]{1,0:T(8,128)(2,1)} %param.26, bf16[256,2048]{1,0:T(8,128)(2,1)} %param.18, f32[2048]{0:T(1024)} %param.25, f32[256]{0:T(256)S(1)} %add_rsqrt_fusion.2), kind=kOutput, calls=%fused_computation.44 | convolution fusion | flops 270663168 | bytes 2370560 | tf_op jit(solution)/shard_map/dot_general | solution.py:233
  5.9 1.1 copy.58
  8.2 3.0 %broadcast_in_dim.69 = bf16[16,256,2,128]{3,2,1,0:T(2,128)(2,1)} broadcast(bf16[256,2,128]{2,1,0:T(2,128)(2,1)S(1)} %copy.59), dimensions={1,2,3} | broadcast | bytes 2228224 | tf_op jit(solution)/shard_map/broadcast_in_dim | solution.py:271
  11.1 8.8 %all-to-all-start = ((bf16[16,256,2,128]{3,2,1,0:T(2,128)(2,1)}), bf16[16,256,2,128]{3,2,1,0:T(2,128)(2,1)}, u32[]{:S(2)}, u32[]{:S(2)}) async-start(bf16[16,256,2,128]{3,2,1,0:T(2,128)(2,1)} %broadcast_in_dim.69), calls=%async_computation | async-start | bytes 4194304 | tf_op jit(solution)/shard_map/all_to_all | solution.py:272
  20.8 3.5 %gather_fusion = s32[512]{0:T(512)S(1)} fusion(s32[512]{0:T(512)S(1)} %bitcast.93, s32[1024]{0:T(1024)S(1)} %pad_clamp_fusion), kind=kCustom, calls=%fused_computation | custom fusion | bytes 6144 | tf_op jit(solution)/shard_map/gather | solution.py:253
  25.3 3.5 %gather_fusion.1 = s32[512]{0:T(512)S(1)} fusion(s32[512]{0:T(512)S(1)} %bitcast.92, s32[1024]{0:T(1024)S(1)} %pad_clamp_fusion), kind=kCustom, calls=%fused_computation.1 | custom fusion | bytes 6144 | tf_op jit(solution)/shard_map/gather | solution.py:254
  32.3 4.8 %copy.65.qpos_ref = s32[16,512,1]{2,1,0:T(8,128)} copy(s32[16,512,1]{0,1,2:T(8,128)S(1)} %bitcast.98) | data formatting | bytes 65536 | tf_op jit(solution)/shard_map/broadcast_in_dim;reshape | solution.py:274
  39.5 1.4 broadcast_select_fusion.kpos_ref
  41.0 7.1 %all-to-all-done = bf16[16,256,2,128]{3,2,1,0:T(2,128)(2,1)} async-done(((bf16[16,256,2,128]{3,2,1,0:T(2,128)(2,1)}), bf16[16,256,2,128]{3,2,1,0:T(2,128)(2,1)}, u32[]{:S(2)}, u32[]{:S(2)}) %all-to-all-start) | async-done | bytes 2097184 | tf_op jit(solution)/shard_map/all_to_all | solution.py:272
  48.1 23.6 %shard_map.172 = bf16[16,544,128]{2,1,0:T(8,128)(2,1)} custom-call(s32[32]{0:T(128)} %min.12.slot_ref, s32[32]{0:T(128)} %reshape.412.alive_ref, bf16[16,512,128]{2,1,0:T(8,128)(2,1)} %bitcast.4.q_ref, bf16[32,512,128]{2,1,0:T(8,128)(2,1)} %k1_ref.1, bf16[32,512,128]{2,1,0:T(8,128)(2,1)} %k1_ref.1, bf16[32,512,128]{2,1,0:T(8,128)(2,1)} %v1_ref.1, ...), custom_call_target="tpu_custom_call" | custom-call | tf_op jit(solution)/shard_map/pallas_call | solution.py:181
  71.7 4.7 %all-to-all-start.1 = ((bf16[16,544,128]{2,1,0:T(8,128)(2,1)}), bf16[16,544,128]{2,1,0:T(8,128)(2,1)}, u32[]{:S(2)}, u32[]{:S(2)}) async-start(bf16[16,544,128]{2,1,0:T(8,128)(2,1)} %shard_map.172), calls=%async_computation.1 | async-start | bytes 4456448 | tf_op jit(solution)/shard_map/all_to_all | solution.py:284
  76.5 1.9 multiply_reduce_fusion.2
  80.5 2.9 %fusion.7 = f32[128,2,256]{2,0,1:T(8,128)} fusion(bf16[2048,128]{1,0:T(8,128)(2,1)} %param.28, f32[1,2,256,256]{2,3,1,0:T(8,128)} %get-tuple-element.33, f32[2,256]{1,0:T(2,128)S(1)} %get-tuple-element.32, pred[256,256]{0,1:T(8,128)(4,1)S(1)} %compare_and_fusion, bf16[256,2048]{1,0:T(8,128)(2,1)} %param.18, f32[2048]{0:T(1024)} %param.25, f32[256]{0:T(256)S(1)} %copy-done.15), kind=kOutput, calls=%fused_computation.20 | convolution fusion | flops 170295296 | bytes 2436096 | tf_op jit(solution)/shard_map/hgmk,khd->mhgd/dot_general | solution.py:61
  83.5 1.1 copy.72
  84.6 1.7 fusion.8
  86.3 16.8 %all-to-all-done.1 = bf16[16,544,128]{2,1,0:T(8,128)(2,1)} async-done(((bf16[16,544,128]{2,1,0:T(8,128)(2,1)}), bf16[16,544,128]{2,1,0:T(8,128)(2,1)}, u32[]{:S(2)}, u32[]{:S(2)}) %all-to-all-start.1) | async-done | bytes 2228256 | tf_op jit(solution)/shard_map/all_to_all | solution.py:284
  103.1 1.5 fusion.53
  105.5 3.9 %multiply_reduce_fusion = f32[512,128]{1,0:T(8,128)} fusion(bf16[16,544,128]{2,1,0:T(8,128)(2,1)} %all-to-all-done.1, f32[16,512]{1,0:T(8,128)S(1)} %fusion.35), kind=kLoop, calls=%fused_computation.2 | loop fusion | flops 3080192 | bytes 2392064 | tf_op jit(solution)/shard_map/reduce_sum | solution.py:301
  109.4 1.7 reduce_sum.121
  114.4 1.3 fusion.40
  117.6 1.2 div.65
  118.9 2.7 %convolution_convert_fusion = bf16[256,2048]{1,0:T(8,128)(2,1)} fusion(bf16[256,2048]{1,0:T(8,128)(2,1)} %param.31, f32[32,8,2,128]{3,2,1,0:T(2,128)S(1)} %bitcast.97, f32[256,256]{1,0:T(8,128)} %reduce_sum.121, f32[256,256]{1,0:T(8,128)S(1)} %copy.72, f32[32,8,2,128]{3,2,1,0:T(2,128)S(1)} %bitcast.96), kind=kOutput, calls=%fused_computation.5 | convolution fusion | flops 269221888 | bytes 3145728 | tf_op jit(solution)/shard_map/dot_general | solution.py:307
  121.6 10.0 %all-to-all-start.2 = ((bf16[8,32,2048]{2,1,0:T(8,128)(2,1)}), bf16[8,32,2048]{2,1,0:T(8,128)(2,1)}, u32[]{:S(2)}, u32[]{:S(2)}) async-start(bf16[8,32,2048]{2,1,0:T(8,128)(2,1)} %bitcast.94), calls=%async_computation.2 | async-start | bytes 2097152 | tf_op jit(solution)/shard_map/all_to_all | solution.py:191
  131.6 15.1 %all-to-all-done.2 = bf16[8,32,2048]{2,1,0:T(8,128)(2,1)} async-done(((bf16[8,32,2048]{2,1,0:T(8,128)(2,1)}), bf16[8,32,2048]{2,1,0:T(8,128)(2,1)}, u32[]{:S(2)}, u32[]{:S(2)}) %all-to-all-start.2) | async-done | bytes 1048608 | tf_op jit(solution)/shard_map/all_to_all | solution.py:191
  146.7 1.4 convert_reduce_fusion.1
  148.1 1.2 fusion.11
  149.5 18.3 %all_to_all.30 = bf16[8,32,2048]{2,1,0:T(8,128)(2,1)S(1)} all-to-all(bf16[8,32,2048]{2,1,0:T(8,128)(2,1)S(1)} %broadcast_in_dim.78), channel_id=1, replica_groups=mesh['req'=16,'tp'=8] {'tp'}, dimensions={0} | all-to-all | bytes 2097152 | tf_op jit(solution)/shard_map/all_to_all | solution.py:197
  168.8 1.9 fusion.57
  170.7 5.5 %convolution_convert_fusion.1 = bf16[256,2048]{1,0:T(8,128)(2,1)} fusion(bf16[768,2048]{1,0:T(8,128)(2,1)S(1)} %copy-done, bf16[256,2048]{1,0:T(8,128)(2,1)} %bitcast.100, bf16[2048,768]{1,0:T(8,128)(2,1)} %param.34, f32[256,768]{1,0:T(8,128)} %fusion.57), kind=kOutput, calls=%fused_computation.6 | convolution fusion | flops 1612316672 | bytes 9175040 | tf_op jit(solution)/shard_map/dot_general | solution.py:313
  176.2 19.4 %all_to_all.31 = bf16[8,32,2048]{2,1,0:T(8,128)(2,1)S(1)} all-to-all(bf16[8,32,2048]{2,1,0:T(8,128)(2,1)} %bitcast.101), channel_id=1, replica_groups=mesh['req'=16,'tp'=8] {'tp'}, dimensions={0} | all-to-all | bytes 2097152 | tf_op jit(solution)/shard_map/all_to_all | solution.py:191
  196.0 18.4 %all_to_all.32 = bf16[8,32,2048]{2,1,0:T(8,128)(2,1)S(1)} all-to-all(bf16[8,32,2048]{2,1,0:T(8,128)(2,1)S(1)} %broadcast_in_dim.79), channel_id=1, replica_groups=mesh['req'=16,'tp'=8] {'tp'}, dimensions={0} | all-to-all | bytes 2097152 | tf_op jit(solution)/shard_map/all_to_all | solution.py:197
  (104 shorter events, 21.0 us)
Async XLA Ops:
  0.0 170.7 %copy-start = (bf16[768,2048]{1,0:T(8,128)(2,1)S(1)}, bf16[768,2048]{1,0:T(8,128)(2,1)}, u32[]{:S(2)}) copy-start(bf16[768,2048]{1,0:T(8,128)(2,1)} %param.35) | copy-start | bytes 9437188
  0.0 7.0 %copy-start.11 = (f32[64]{0:T(128)}, f32[64]{0:T(128)S(1)}, u32[]{:S(2)}) copy-start(f32[64]{0:T(128)S(1)} %multiply_power_fusion) | copy-start | bytes 772
  0.9 0.6 copy-start.4
  1.5 5.6 %copy-start.6 = (f32[256]{0:T(256)}, f32[256]{0:T(256)S(1)}, u32[]{:S(2)}) copy-start(f32[256]{0:T(256)S(1)} %convert_element_type.108) | copy-start | bytes 3076
  1.5 6.1 %copy-start.16 = (f32[128]{0:T(128)S(1)}, f32[128]{0:T(128)}, u32[]{:S(2)}) copy-start(f32[128]{0:T(128)} %param.29) | copy-start | bytes 1540
  3.0 2.9 %copy-start.14 = (f32[256]{0:T(256)}, f32[256]{0:T(256)S(1)}, u32[]{:S(2)}) copy-start(f32[256]{0:T(256)S(1)} %add_rsqrt_fusion.2) | copy-start | bytes 3076
  11.1 8.8 %copy-start.10 = (s32[16,32]{1,0:T(8,128)S(1)}, s32[16,32]{1,0:T(8,128)}, u32[]{:S(2)}) copy-start(s32[16,32]{1,0:T(8,128)} %param.21) | copy-start | bytes 6148
  11.1 8.9 %copy-start.3 = (s32[16,256]{1,0:T(8,128)S(1)}, s32[16,256]{1,0:T(8,128)}, u32[]{:S(2)}) copy-start(s32[16,256]{1,0:T(8,128)} %param.19) | copy-start | bytes 49156
  11.1 9.7 %copy-start.13 = (s32[2,512]{1,0:T(2,128)S(1)}, s32[2,512]{1,0:T(2,128)}, u32[]{:S(2)}) copy-start(s32[2,512]{1,0:T(2,128)} %param.22) | copy-start | bytes 12292
  11.1 37.0 %all-to-all-start = ((bf16[16,256,2,128]{3,2,1,0:T(2,128)(2,1)}), bf16[16,256,2,128]{3,2,1,0:T(2,128)(2,1)}, u32[]{:S(2)}, u32[]{:S(2)}) async-start(bf16[16,256,2,128]{3,2,1,0:T(2,128)(2,1)} %broadcast_in_dim.69), calls=%async_computation | async-start | bytes 4194304 | tf_op jit(solution)/shard_map/all_to_all | solution.py:272
  25.3 3.9 %copy-start.18 = (s32[16]{0:T(128)S(1)}, s32[16]{0:T(128)}, u32[]{:S(2)}) copy-start(s32[16]{0:T(128)} %param.20) | copy-start | bytes 196
  71.7 4.7 %copy-start.15 = (f32[256]{0:T(256)S(1)}, f32[256]{0:T(256)}, u32[]{:S(2)}) copy-start(f32[256]{0:T(256)} %copy-done.14) | copy-start | bytes 3076
  71.7 4.7 %copy-start.20 = (f32[2048]{0:T(1024)S(1)}, f32[2048]{0:T(1024)}, u32[]{:S(2)}) copy-start(f32[2048]{0:T(1024)} %param.25) | copy-start | bytes 24580
  71.7 31.3 %all-to-all-start.1 = ((bf16[16,544,128]{2,1,0:T(8,128)(2,1)}), bf16[16,544,128]{2,1,0:T(8,128)(2,1)}, u32[]{:S(2)}, u32[]{:S(2)}) async-start(bf16[16,544,128]{2,1,0:T(8,128)(2,1)} %shard_map.172), calls=%async_computation.1 | async-start | bytes 4456448 | tf_op jit(solution)/shard_map/all_to_all | solution.py:284
  76.4 2.0 copy-start.5
  76.4 2.2 %copy-start.17 = (f32[128]{0:T(128)S(1)}, f32[128]{0:T(128)}, u32[]{:S(2)}) copy-start(f32[128]{0:T(128)} %param.30) | copy-start | bytes 1540
  76.4 2.3 %copy-start.7 = (f32[256]{0:T(256)S(1)}, f32[256]{0:T(256)}, u32[]{:S(2)}) copy-start(f32[256]{0:T(256)} %copy-done.6) | copy-start | bytes 3076
  76.5 2.3 %copy-start.12 = (f32[64]{0:T(128)S(1)}, f32[64]{0:T(128)}, u32[]{:S(2)}) copy-start(f32[64]{0:T(128)} %copy-done.11) | copy-start | bytes 772
  78.6 4.9 %copy-start.2 = (pred[256,256]{0,1:T(8,128)(4,1)}, pred[256,256]{0,1:T(8,128)(4,1)S(1)}, u32[]{:S(2)}) copy-start(pred[256,256]{0,1:T(8,128)(4,1)S(1)} %compare_and_fusion) | copy-start | bytes 196612
  104.7 9.7 %copy-start.8 = (f32[2,256]{1,0:T(2,128)S(1)}, f32[2,256]{1,0:T(2,128)}, u32[]{:S(2)}) copy-start(f32[2,256]{1,0:T(2,128)} %fusion.8) | copy-start | bytes 6148
  121.6 27.7 %copy-start.9 = (f32[2048]{0:T(1024)S(1)}, f32[2048]{0:T(1024)}, u32[]{:S(2)}) copy-start(f32[2048]{0:T(1024)} %param.32) | copy-start | bytes 24580
  121.6 25.1 %all-to-all-start.2 = ((bf16[8,32,2048]{2,1,0:T(8,128)(2,1)}), bf16[8,32,2048]{2,1,0:T(8,128)(2,1)}, u32[]{:S(2)}, u32[]{:S(2)}) async-start(bf16[8,32,2048]{2,1,0:T(8,128)(2,1)} %bitcast.94), calls=%async_computation.2 | async-start | bytes 2097152 | tf_op jit(solution)/shard_map/all_to_all | solution.py:191
  148.1 20.8 %copy-start.19 = (bf16[2048,768]{1,0:T(8,128)(2,1)S(1)}, bf16[2048,768]{1,0:T(8,128)(2,1)}, u32[]{:S(2)}) copy-start(bf16[2048,768]{1,0:T(8,128)(2,1)} %param.33) | copy-start | bytes 9437188
  167.9 1.0 copy-start.1

commit v12 on v11

--- a/solution.py
+++ b/solution.py
@@ -262,7 +262,10 @@
     send_place = jnp.sum(jnp.where(my_sends, jnp.arange(MOST_STRETCHES)[None, :, None], 0), axis=1)
     request_count = holder_table.shape[0]
     pool_slots = cached_key_pool.shape[0]
-    slots = jnp.clip(send_slot, 0, pool_slots - 1).reshape(request_count * pair_cap).astype(jnp.int32)
+    slot_live = send_place < req_lengths[:, None]
+    last_live = lax.cummax(jnp.where(slot_live, jnp.arange(request_count)[:, None], -1), axis=0)
+    fetch_slot = jnp.take_along_axis(send_slot, jnp.maximum(last_live, 0), axis=0)
+    slots = jnp.clip(fetch_slot, 0, pool_slots - 1).reshape(request_count * pair_cap).astype(jnp.int32)
     held_angle = angles(send_place * STRETCH_TOKENS, head_size)
     cos_table = jnp.cos(held_angle)
     sin_table = jnp.sin(held_angle)

time: 218 us -> 216 us (level)
  no operation moved by 1% of the time
where the time goes in v12:
time: 216 us; the launch traced here: 215 us
  blocking collectives  56.2 us (26%)
  waiting for transfers between devices  38.5 us (18%)
  local copies, waits for them, and re-layouts  34.1 us (16%)
  starting transfers between devices  24 us (11%)
  Pallas kernels  22.8 us (11%)
  other arithmetic  20.1 us (9%)
  matrix products  19 us (9%)
    all_to_all x2, blocking collectives, gather_rows(): got = lax.all_to_all(copies, 'tp', 0, 0, tiled=False)  36.7 us
    pallas_call x1, Pallas kernels, held_blocks(): pl.pallas_call(held_block_kernel, grid_spec=grid_spec, out_shape=jax.Shap...  22.8 us
    all_to_all x1, blocking collectives, reduce_rows(): got = lax.all_to_all(blocks, 'tp', 0, 0, tiled=False)  19.4 us
    all_to_all x1, waiting for transfers between devices, on_device(): got = lax.all_to_all(held, 'req', 0, 0, tiled=False)  16.8 us
    all_to_all x1, waiting for transfers between devices, reduce_rows(): got = lax.all_to_all(blocks, 'tp', 0, 0, tiled=False)  15.1 us
    all_to_all x1, starting transfers between devices, reduce_rows(): got = lax.all_to_all(blocks, 'tp', 0, 0, tiled=False)  10.1 us
    all_to_all x1, starting transfers between devices, on_device(): all_queries = lax.all_to_all(query_copies, 'req', 0, 0, tiled=False)  8.77 us
    all_to_all x1, waiting for transfers between devices, on_device(): all_queries = lax.all_to_all(query_copies, 'req', 0, 0, tiled=False)  6.61 us
  transfers between devices with their start and end apart: 3, of which 3 were waited for; matrix products, arithmetic and copies ran while one was open for 14% of the time, Pallas kernels for 0%

profile of v12, /device:TPU:1, one launch (start us, length us, event | category | flops | bytes accessed | tf_op | source)
XLA Modules:
  0.0 215.2 jit_solution(16816644786898875681)
XLA Ops:
  1.5 1.5 fusion
  3.0 2.9 %multiply_reduce_fusion.1 = (f32[256,2]{0,1:T(2,128)S(1)}, f32[256,256]{0,1:T(8,128)}) fusion(bf16[2048,256]{1,0:T(8,128)(2,1)} %param.26, bf16[256,2048]{1,0:T(8,128)(2,1)} %param.18, f32[2048]{0:T(1024)} %param.25, f32[256]{0:T(256)S(1)} %add_rsqrt_fusion.2), kind=kOutput, calls=%fused_computation.45 | convolution fusion | flops 270663168 | bytes 2370560 | tf_op jit(solution)/shard_map/dot_general | solution.py:233
  5.9 1.1 copy.91
  8.2 3.0 %broadcast_in_dim.88 = bf16[16,256,2,128]{3,2,1,0:T(2,128)(2,1)} broadcast(bf16[256,2,128]{2,1,0:T(2,128)(2,1)S(1)} %copy.92), dimensions={1,2,3} | broadcast | bytes 2228224 | tf_op jit(solution)/shard_map/broadcast_in_dim | solution.py:274
  11.1 8.8 %all-to-all-start = ((bf16[16,256,2,128]{3,2,1,0:T(2,128)(2,1)}), bf16[16,256,2,128]{3,2,1,0:T(2,128)(2,1)}, u32[]{:S(2)}, u32[]{:S(2)}) async-start(bf16[16,256,2,128]{3,2,1,0:T(2,128)(2,1)} %broadcast_in_dim.88), calls=%async_computation | async-start | bytes 4194304 | tf_op jit(solution)/shard_map/all_to_all | solution.py:275
  20.0 3.5 %gather_fusion = s32[512]{0:T(512)S(1)} fusion(s32[512]{0:T(512)S(1)} %bitcast.97, s32[1024]{0:T(1024)S(1)} %pad_clamp_fusion), kind=kCustom, calls=%fused_computation | custom fusion | bytes 6144 | tf_op jit(solution)/shard_map/gather | solution.py:253
  24.5 3.5 %gather_fusion.1 = s32[512]{0:T(512)S(1)} fusion(s32[512]{0:T(512)S(1)} %bitcast.96, s32[1024]{0:T(1024)S(1)} %pad_clamp_fusion), kind=kCustom, calls=%fused_computation.1 | custom fusion | bytes 6144 | tf_op jit(solution)/shard_map/gather | solution.py:254
  33.5 4.8 %copy.98.qpos_ref = s32[16,512,1]{2,1,0:T(8,128)} copy(s32[16,512,1]{0,1,2:T(8,128)S(1)} %bitcast.102) | data formatting | bytes 65536 | tf_op jit(solution)/shard_map/broadcast_in_dim;reshape | solution.py:277
  40.0 1.4 broadcast_select_fusion.kpos_ref
  41.5 6.6 %all-to-all-done = bf16[16,256,2,128]{3,2,1,0:T(2,128)(2,1)} async-done(((bf16[16,256,2,128]{3,2,1,0:T(2,128)(2,1)}), bf16[16,256,2,128]{3,2,1,0:T(2,128)(2,1)}, u32[]{:S(2)}, u32[]{:S(2)}) %all-to-all-start) | async-done | bytes 2097184 | tf_op jit(solution)/shard_map/all_to_all | solution.py:275
  48.1 22.8 %shard_map.172 = bf16[16,544,128]{2,1,0:T(8,128)(2,1)} custom-call(s32[32]{0:T(128)} %min.12.slot_ref, s32[32]{0:T(128)} %reshape.435.alive_ref, bf16[16,512,128]{2,1,0:T(8,128)(2,1)} %bitcast.5.q_ref, bf16[32,512,128]{2,1,0:T(8,128)(2,1)} %k1_ref.1, bf16[32,512,128]{2,1,0:T(8,128)(2,1)} %k1_ref.1, bf16[32,512,128]{2,1,0:T(8,128)(2,1)} %v1_ref.1, ...), custom_call_target="tpu_custom_call" | custom-call | tf_op jit(solution)/shard_map/pallas_call | solution.py:181
  70.9 5.2 %all-to-all-start.1 = ((bf16[16,544,128]{2,1,0:T(8,128)(2,1)}), bf16[16,544,128]{2,1,0:T(8,128)(2,1)}, u32[]{:S(2)}, u32[]{:S(2)}) async-start(bf16[16,544,128]{2,1,0:T(8,128)(2,1)} %shard_map.172), calls=%async_computation.1 | async-start | bytes 4456448 | tf_op jit(solution)/shard_map/all_to_all | solution.py:287
  76.2 1.9 multiply_reduce_fusion.2
  80.3 2.9 %fusion.7 = f32[128,2,256]{2,0,1:T(8,128)} fusion(bf16[2048,128]{1,0:T(8,128)(2,1)} %param.28, f32[1,2,256,256]{2,3,1,0:T(8,128)} %get-tuple-element.33, f32[2,256]{1,0:T(2,128)S(1)} %get-tuple-element.32, pred[256,256]{0,1:T(8,128)(4,1)S(1)} %compare_and_fusion, bf16[256,2048]{1,0:T(8,128)(2,1)} %param.18, f32[2048]{0:T(1024)} %param.25, f32[256]{0:T(256)S(1)} %copy-done.15), kind=kOutput, calls=%fused_computation.21 | convolution fusion | flops 170295296 | bytes 2436096 | tf_op jit(solution)/shard_map/hgmk,khd->mhgd/dot_general | solution.py:61
  83.2 1.1 copy.105
  84.3 1.7 fusion.8
  86.0 16.8 %all-to-all-done.1 = bf16[16,544,128]{2,1,0:T(8,128)(2,1)} async-done(((bf16[16,544,128]{2,1,0:T(8,128)(2,1)}), bf16[16,544,128]{2,1,0:T(8,128)(2,1)}, u32[]{:S(2)}, u32[]{:S(2)}) %all-to-all-start.1) | async-done | bytes 2228256 | tf_op jit(solution)/shard_map/all_to_all | solution.py:287
  102.9 1.5 fusion.53
  105.3 3.9 %multiply_reduce_fusion = f32[512,128]{1,0:T(8,128)} fusion(bf16[16,544,128]{2,1,0:T(8,128)(2,1)} %all-to-all-done.1, f32[16,512]{1,0:T(8,128)S(1)} %fusion.35), kind=kLoop, calls=%fused_computation.3 | loop fusion | flops 3080192 | bytes 2392064 | tf_op jit(solution)/shard_map/reduce_sum | solution.py:304
  109.1 1.7 reduce_sum.121
  114.2 1.3 fusion.40
  117.4 1.2 div.65
  118.6 2.7 %convolution_convert_fusion = bf16[256,2048]{1,0:T(8,128)(2,1)} fusion(bf16[256,2048]{1,0:T(8,128)(2,1)} %param.31, f32[32,8,2,128]{3,2,1,0:T(2,128)S(1)} %bitcast.101, f32[256,256]{1,0:T(8,128)} %reduce_sum.121, f32[256,256]{1,0:T(8,128)S(1)} %copy.105, f32[32,8,2,128]{3,2,1,0:T(2,128)S(1)} %bitcast.100), kind=kOutput, calls=%fused_computation.6 | convolution fusion | flops 269221888 | bytes 3145728 | tf_op jit(solution)/shard_map/dot_general | solution.py:310
  121.4 10.1 %all-to-all-start.2 = ((bf16[8,32,2048]{2,1,0:T(8,128)(2,1)}), bf16[8,32,2048]{2,1,0:T(8,128)(2,1)}, u32[]{:S(2)}, u32[]{:S(2)}) async-start(bf16[8,32,2048]{2,1,0:T(8,128)(2,1)} %bitcast.98), calls=%async_computation.2 | async-start | bytes 2097152 | tf_op jit(solution)/shard_map/all_to_all | solution.py:191
  131.4 15.1 %all-to-all-done.2 = bf16[8,32,2048]{2,1,0:T(8,128)(2,1)} async-done(((bf16[8,32,2048]{2,1,0:T(8,128)(2,1)}), bf16[8,32,2048]{2,1,0:T(8,128)(2,1)}, u32[]{:S(2)}, u32[]{:S(2)}) %all-to-all-start.2) | async-done | bytes 1048608 | tf_op jit(solution)/shard_map/all_to_all | solution.py:191
  146.5 1.4 convert_reduce_fusion.1
  147.9 1.2 fusion.11
  149.4 18.3 %all_to_all.30 = bf16[8,32,2048]{2,1,0:T(8,128)(2,1)S(1)} all-to-all(bf16[8,32,2048]{2,1,0:T(8,128)(2,1)S(1)} %broadcast_in_dim.152), channel_id=1, replica_groups=mesh['req'=16,'tp'=8] {'tp'}, dimensions={0} | all-to-all | bytes 2097152 | tf_op jit(solution)/shard_map/all_to_all | solution.py:197
  168.7 1.9 fusion.57
  170.6 5.5 %convolution_convert_fusion.1 = bf16[256,2048]{1,0:T(8,128)(2,1)} fusion(bf16[768,2048]{1,0:T(8,128)(2,1)S(1)} %copy-done, bf16[256,2048]{1,0:T(8,128)(2,1)} %bitcast.104, bf16[2048,768]{1,0:T(8,128)(2,1)} %param.34, f32[256,768]{1,0:T(8,128)} %fusion.57), kind=kOutput, calls=%fused_computation.7 | convolution fusion | flops 1612316672 | bytes 9175040 | tf_op jit(solution)/shard_map/dot_general | solution.py:316
  176.1 19.4 %all_to_all.31 = bf16[8,32,2048]{2,1,0:T(8,128)(2,1)S(1)} all-to-all(bf16[8,32,2048]{2,1,0:T(8,128)(2,1)} %bitcast.105), channel_id=1, replica_groups=mesh['req'=16,'tp'=8] {'tp'}, dimensions={0} | all-to-all | bytes 2097152 | tf_op jit(solution)/shard_map/all_to_all | solution.py:191
  195.8 18.4 %all_to_all.32 = bf16[8,32,2048]{2,1,0:T(8,128)(2,1)S(1)} all-to-all(bf16[8,32,2048]{2,1,0:T(8,128)(2,1)S(1)} %broadcast_in_dim.153), channel_id=1, replica_groups=mesh['req'=16,'tp'=8] {'tp'}, dimensions={0} | all-to-all | bytes 2097152 | tf_op jit(solution)/shard_map/all_to_all | solution.py:197
  (113 shorter events, 21.5 us)
Async XLA Ops:
  0.0 170.6 %copy-start = (bf16[768,2048]{1,0:T(8,128)(2,1)S(1)}, bf16[768,2048]{1,0:T(8,128)(2,1)}, u32[]{:S(2)}) copy-start(bf16[768,2048]{1,0:T(8,128)(2,1)} %param.35) | copy-start | bytes 9437188
  0.0 7.0 %copy-start.11 = (f32[64]{0:T(128)}, f32[64]{0:T(128)S(1)}, u32[]{:S(2)}) copy-start(f32[64]{0:T(128)S(1)} %multiply_power_fusion) | copy-start | bytes 772
  0.9 0.6 copy-start.4
  1.5 5.6 %copy-start.6 = (f32[256]{0:T(256)}, f32[256]{0:T(256)S(1)}, u32[]{:S(2)}) copy-start(f32[256]{0:T(256)S(1)} %convert_element_type.108) | copy-start | bytes 3076
  1.5 6.1 %copy-start.16 = (f32[128]{0:T(128)S(1)}, f32[128]{0:T(128)}, u32[]{:S(2)}) copy-start(f32[128]{0:T(128)} %param.29) | copy-start | bytes 1540
  3.0 2.9 %copy-start.14 = (f32[256]{0:T(256)}, f32[256]{0:T(256)S(1)}, u32[]{:S(2)}) copy-start(f32[256]{0:T(256)S(1)} %add_rsqrt_fusion.2) | copy-start | bytes 3076
  11.1 8.8 %copy-start.10 = (s32[16,32]{1,0:T(8,128)S(1)}, s32[16,32]{1,0:T(8,128)}, u32[]{:S(2)}) copy-start(s32[16,32]{1,0:T(8,128)} %param.21) | copy-start | bytes 6148
  11.1 8.9 %copy-start.13 = (s32[2,512]{1,0:T(2,128)S(1)}, s32[2,512]{1,0:T(2,128)}, u32[]{:S(2)}) copy-start(s32[2,512]{1,0:T(2,128)} %param.22) | copy-start | bytes 12292
  11.1 37.0 %all-to-all-start = ((bf16[16,256,2,128]{3,2,1,0:T(2,128)(2,1)}), bf16[16,256,2,128]{3,2,1,0:T(2,128)(2,1)}, u32[]{:S(2)}, u32[]{:S(2)}) async-start(bf16[16,256,2,128]{3,2,1,0:T(2,128)(2,1)} %broadcast_in_dim.88), calls=%async_computation | async-start | bytes 4194304 | tf_op jit(solution)/shard_map/all_to_all | solution.py:275
  24.5 3.7 %copy-start.3 = (s32[16,256]{1,0:T(8,128)S(1)}, s32[16,256]{1,0:T(8,128)}, u32[]{:S(2)}) copy-start(s32[16,256]{1,0:T(8,128)} %param.19) | copy-start | bytes 49156
  24.5 4.6 %copy-start.18 = (s32[16]{0:T(128)S(1)}, s32[16]{0:T(128)}, u32[]{:S(2)}) copy-start(s32[16]{0:T(128)} %param.20) | copy-start | bytes 196
  70.9 5.3 %copy-start.15 = (f32[256]{0:T(256)S(1)}, f32[256]{0:T(256)}, u32[]{:S(2)}) copy-start(f32[256]{0:T(256)} %copy-done.14) | copy-start | bytes 3076
  70.9 5.3 %copy-start.20 = (f32[2048]{0:T(1024)S(1)}, f32[2048]{0:T(1024)}, u32[]{:S(2)}) copy-start(f32[2048]{0:T(1024)} %param.25) | copy-start | bytes 24580
  70.9 31.9 %all-to-all-start.1 = ((bf16[16,544,128]{2,1,0:T(8,128)(2,1)}), bf16[16,544,128]{2,1,0:T(8,128)(2,1)}, u32[]{:S(2)}, u32[]{:S(2)}) async-start(bf16[16,544,128]{2,1,0:T(8,128)(2,1)} %shard_map.172), calls=%async_computation.1 | async-start | bytes 4456448 | tf_op jit(solution)/shard_map/all_to_all | solution.py:287
  76.1 2.0 copy-start.5
  76.1 2.2 %copy-start.17 = (f32[128]{0:T(128)S(1)}, f32[128]{0:T(128)}, u32[]{:S(2)}) copy-start(f32[128]{0:T(128)} %param.30) | copy-start | bytes 1540
  76.2 2.3 %copy-start.7 = (f32[256]{0:T(256)S(1)}, f32[256]{0:T(256)}, u32[]{:S(2)}) copy-start(f32[256]{0:T(256)} %copy-done.6) | copy-start | bytes 3076
  76.2 2.3 %copy-start.12 = (f32[64]{0:T(128)S(1)}, f32[64]{0:T(128)}, u32[]{:S(2)}) copy-start(f32[64]{0:T(128)} %copy-done.11) | copy-start | bytes 772
  78.3 4.9 %copy-start.2 = (pred[256,256]{0,1:T(8,128)(4,1)}, pred[256,256]{0,1:T(8,128)(4,1)S(1)}, u32[]{:S(2)}) copy-start(pred[256,256]{0,1:T(8,128)(4,1)S(1)} %compare_and_fusion) | copy-start | bytes 196612
  104.5 9.7 %copy-start.8 = (f32[2,256]{1,0:T(2,128)S(1)}, f32[2,256]{1,0:T(2,128)}, u32[]{:S(2)}) copy-start(f32[2,256]{1,0:T(2,128)} %fusion.8) | copy-start | bytes 6148
  121.4 27.8 %copy-start.9 = (f32[2048]{0:T(1024)S(1)}, f32[2048]{0:T(1024)}, u32[]{:S(2)}) copy-start(f32[2048]{0:T(1024)} %param.32) | copy-start | bytes 24580
  121.4 25.1 %all-to-all-start.2 = ((bf16[8,32,2048]{2,1,0:T(8,128)(2,1)}), bf16[8,32,2048]{2,1,0:T(8,128)(2,1)}, u32[]{:S(2)}, u32[]{:S(2)}) async-start(bf16[8,32,2048]{2,1,0:T(8,128)(2,1)} %bitcast.98), calls=%async_computation.2 | async-start | bytes 2097152 | tf_op jit(solution)/shard_map/all_to_all | solution.py:191
  147.9 20.8 %copy-start.19 = (bf16[2048,768]{1,0:T(8,128)(2,1)S(1)}, bf16[2048,768]{1,0:T(8,128)(2,1)}, u32[]{:S(2)}) copy-start(bf16[2048,768]{1,0:T(8,128)(2,1)} %param.33) | copy-start | bytes 9437188
  167.7 1.0 copy-start.1

commit v13 on v11

--- a/solution.py
+++ b/solution.py
@@ -268,7 +268,8 @@
     sin_table = jnp.sin(held_angle)
     cos_table = jnp.concatenate([cos_table, cos_table], axis=-1)[:, :, None, :]
     sin_table = jnp.concatenate([-sin_table, sin_table], axis=-1)[:, :, None, :]
-    query_copies = jnp.broadcast_to(queries[None], (req_count,) + queries.shape)
+    query_rows = queries.reshape(count_of_rows * query_heads, head_size)
+    query_copies = jnp.broadcast_to(query_rows[None], (req_count,) + query_rows.shape)
     all_queries = lax.all_to_all(query_copies, "req", 0, 0, tiled=False)
     all_queries = all_queries.reshape(request_count, req_rows * groups, head_size)
     query_pos = jnp.repeat(recompute_pos, groups, axis=1)[:, :, None]

time: 218 us -> 224 us (1.028)
  local copies, waits for them, and re-layouts: 33 us -> 41.2 us
  waiting for transfers between devices: 39 us -> 32.4 us
  other arithmetic: 20.7 us -> 23.9 us
    all_to_all x1, waiting for transfers between devices: 7.14 us -> 0.01 us  [on_device(): all_queries = lax.all_to_all(query_copies, 'req', 0, 0, tiled=False)]
  transfers between devices with their start and end apart: 3 -> 3, of which waited for: 3 -> 2; matrix products, arithmetic and copies ran while one was open for 14% -> 20% of each run, Pallas kernels for 0% -> 0%
where the time goes in v13:
time: 224 us; the launch traced here: 221 us
  blocking collectives  56.2 us (25%)
  local copies, waits for them, and re-layouts  41.2 us (18%)
  waiting for transfers between devices  32.4 us (14%)
  starting transfers between devices  24.6 us (11%)
  other arithmetic  23.9 us (11%)
  Pallas kernels  23.3 us (10%)
  matrix products  19 us (8%)
    all_to_all x2, blocking collectives, gather_rows(): got = lax.all_to_all(copies, 'tp', 0, 0, tiled=False)  36.7 us
    pallas_call x1, Pallas kernels, held_blocks(): pl.pallas_call(held_block_kernel, grid_spec=grid_spec, out_shape=jax.Shap...  23.3 us
    all_to_all x1, blocking collectives, reduce_rows(): got = lax.all_to_all(blocks, 'tp', 0, 0, tiled=False)  19.4 us
    all_to_all x1, waiting for transfers between devices, on_device(): got = lax.all_to_all(held, 'req', 0, 0, tiled=False)  17.3 us
    all_to_all x1, waiting for transfers between devices, reduce_rows(): got = lax.all_to_all(blocks, 'tp', 0, 0, tiled=False)  15.1 us
    all_to_all x1, starting transfers between devices, reduce_rows(): got = lax.all_to_all(blocks, 'tp', 0, 0, tiled=False)  9.75 us
    all_to_all x1, starting transfers between devices, on_device(): all_queries = lax.all_to_all(query_copies, 'req', 0, 0, tiled=False)  8.77 us
    all_to_all x1, starting transfers between devices, on_device(): got = lax.all_to_all(held, 'req', 0, 0, tiled=False)  6.13 us
  transfers between devices with their start and end apart: 3, of which 2 were waited for; matrix products, arithmetic and copies ran while one was open for 20% of the time, Pallas kernels for 0%

profile of v13, /device:TPU:1, one launch (start us, length us, event | category | flops | bytes accessed | tf_op | source)
XLA Modules:
  0.0 221.0 jit_solution(2215695761868877642)
XLA Ops:
  1.5 1.5 fusion
  3.0 2.9 %multiply_reduce_fusion.1 = (f32[256,2]{0,1:T(2,128)S(1)}, f32[256,256]{0,1:T(8,128)}) fusion(bf16[2048,256]{1,0:T(8,128)(2,1)} %param.26, bf16[256,2048]{1,0:T(8,128)(2,1)} %param.18, f32[2048]{0:T(1024)} %param.25, f32[256]{0:T(256)S(1)} %add_rsqrt_fusion.2), kind=kOutput, calls=%fused_computation.44 | convolution fusion | flops 270663168 | bytes 2370560 | tf_op jit(solution)/shard_map/dot_general | solution.py:233
  8.3 1.7 broadcast_in_dim.69
  10.0 8.8 %all-to-all-start = ((bf16[16,512,128]{2,1,0:T(8,128)(2,1)}), bf16[16,512,128]{2,1,0:T(8,128)(2,1)}, u32[]{:S(2)}, u32[]{:S(2)}) async-start(bf16[16,512,128]{2,1,0:T(8,128)(2,1)} %broadcast_in_dim.69), calls=%async_computation | async-start | bytes 4194304 | tf_op jit(solution)/shard_map/all_to_all | solution.py:273
  19.8 3.5 %gather_fusion = s32[512]{0:T(512)S(1)} fusion(s32[512]{0:T(512)S(1)} %bitcast.93, s32[1024]{0:T(1024)S(1)} %pad_clamp_fusion), kind=kCustom, calls=%fused_computation | custom fusion | bytes 6144 | tf_op jit(solution)/shard_map/gather | solution.py:253
  23.9 1.4 copy.55
  25.3 2.2 fusion.59
  27.5 1.4 copy.56
  28.8 3.5 %gather_fusion.1 = s32[512]{0:T(512)S(1)} fusion(s32[512]{0:T(512)S(1)} %bitcast.92, s32[1024]{0:T(1024)S(1)} %pad_clamp_fusion), kind=kCustom, calls=%fused_computation.1 | custom fusion | bytes 6144 | tf_op jit(solution)/shard_map/gather | solution.py:254
  38.0 1.3 copy.57
  39.3 1.4 min.12.slot_ref
  40.7 1.3 copy.58
  42.0 1.4 reshape.410.alive_ref
  44.2 5.7 %copy.67.qpos_ref = s32[16,512,1]{2,1,0:T(8,128)} copy(s32[16,512,1]{0,1,2:T(8,128)} %bitcast.98) | data formatting | bytes 65536 | tf_op jit(solution)/shard_map/broadcast_in_dim;reshape | solution.py:275
  52.3 23.3 %shard_map.172 = bf16[16,544,128]{2,1,0:T(8,128)(2,1)} custom-call(s32[32]{0:T(128)} %min.12.slot_ref, s32[32]{0:T(128)} %reshape.410.alive_ref, bf16[16,512,128]{2,1,0:T(8,128)(2,1)} %all-to-all-done.q_ref, bf16[32,512,128]{2,1,0:T(8,128)(2,1)} %k1_ref.1, bf16[32,512,128]{2,1,0:T(8,128)(2,1)} %k1_ref.1, bf16[32,512,128]{2,1,0:T(8,128)(2,1)} %v1_ref.1, ...), custom_call_target="tpu_custom_call" | custom-call | tf_op jit(solution)/shard_map/pallas_call | solution.py:181
  75.6 6.1 %all-to-all-start.1 = ((bf16[16,544,128]{2,1,0:T(8,128)(2,1)}), bf16[16,544,128]{2,1,0:T(8,128)(2,1)}, u32[]{:S(2)}, u32[]{:S(2)}) async-start(bf16[16,544,128]{2,1,0:T(8,128)(2,1)} %shard_map.172), calls=%async_computation.1 | async-start | bytes 4456448 | tf_op jit(solution)/shard_map/all_to_all | solution.py:285
  81.8 1.9 multiply_reduce_fusion.2
  85.9 2.9 %fusion.7 = f32[128,2,256]{2,0,1:T(8,128)} fusion(bf16[2048,128]{1,0:T(8,128)(2,1)} %param.28, f32[1,2,256,256]{2,3,1,0:T(8,128)} %get-tuple-element.33, f32[2,256]{1,0:T(2,128)S(1)} %get-tuple-element.32, pred[256,256]{0,1:T(8,128)(4,1)S(1)} %compare_and_fusion, bf16[256,2048]{1,0:T(8,128)(2,1)} %param.18, f32[2048]{0:T(1024)S(1)} %copy-done.19, ...), kind=kOutput, calls=%fused_computation.20 | convolution fusion | flops 170295296 | bytes 2436096 | tf_op jit(solution)/shard_map/hgmk,khd->mhgd/dot_general | solution.py:61
  89.9 1.7 fusion.8
  91.7 17.3 %all-to-all-done.1 = bf16[16,544,128]{2,1,0:T(8,128)(2,1)} async-done(((bf16[16,544,128]{2,1,0:T(8,128)(2,1)}), bf16[16,544,128]{2,1,0:T(8,128)(2,1)}, u32[]{:S(2)}, u32[]{:S(2)}) %all-to-all-start.1) | async-done | bytes 2228256 | tf_op jit(solution)/shard_map/all_to_all | solution.py:285
  109.0 1.5 fusion.56
  111.4 3.9 %multiply_reduce_fusion = f32[512,128]{1,0:T(8,128)} fusion(bf16[16,544,128]{2,1,0:T(8,128)(2,1)} %all-to-all-done.1, f32[16,512]{1,0:T(8,128)S(1)} %fusion.38), kind=kLoop, calls=%fused_computation.2 | loop fusion | flops 3080192 | bytes 2392064 | tf_op jit(solution)/shard_map/reduce_sum | solution.py:302
  115.3 1.7 reduce_sum.121
  124.8 2.7 %convolution_convert_fusion = bf16[256,2048]{1,0:T(8,128)(2,1)} fusion(bf16[256,2048]{1,0:T(8,128)(2,1)} %param.31, f32[32,8,2,128]{3,2,1,0:T(2,128)S(1)} %bitcast.97, f32[256,256]{1,0:T(8,128)} %reduce_sum.121, f32[256,256]{1,0:T(8,128)S(1)} %copy.74, f32[32,8,2,128]{3,2,1,0:T(2,128)S(1)} %bitcast.96), kind=kOutput, calls=%fused_computation.5 | convolution fusion | flops 269221888 | bytes 3145728 | tf_op jit(solution)/shard_map/dot_general | solution.py:308
  127.5 9.8 %all-to-all-start.2 = ((bf16[8,32,2048]{2,1,0:T(8,128)(2,1)}), bf16[8,32,2048]{2,1,0:T(8,128)(2,1)}, u32[]{:S(2)}, u32[]{:S(2)}) async-start(bf16[8,32,2048]{2,1,0:T(8,128)(2,1)} %bitcast.94), calls=%async_computation.2 | async-start | bytes 2097152 | tf_op jit(solution)/shard_map/all_to_all | solution.py:191
  137.3 15.1 %all-to-all-done.2 = bf16[8,32,2048]{2,1,0:T(8,128)(2,1)} async-done(((bf16[8,32,2048]{2,1,0:T(8,128)(2,1)}), bf16[8,32,2048]{2,1,0:T(8,128)(2,1)}, u32[]{:S(2)}, u32[]{:S(2)}) %all-to-all-start.2) | async-done | bytes 1048608 | tf_op jit(solution)/shard_map/all_to_all | solution.py:191
  152.3 1.4 convert_reduce_fusion.1
  155.2 18.3 %all_to_all.30 = bf16[8,32,2048]{2,1,0:T(8,128)(2,1)S(1)} all-to-all(bf16[8,32,2048]{2,1,0:T(8,128)(2,1)S(1)} %broadcast_in_dim.78), channel_id=1, replica_groups=mesh['req'=16,'tp'=8] {'tp'}, dimensions={0} | all-to-all | bytes 2097152 | tf_op jit(solution)/shard_map/all_to_all | solution.py:197
  174.5 1.9 fusion.60
  176.4 5.5 %convolution_convert_fusion.1 = bf16[256,2048]{1,0:T(8,128)(2,1)} fusion(bf16[768,2048]{1,0:T(8,128)(2,1)S(1)} %copy-done, bf16[256,2048]{1,0:T(8,128)(2,1)} %bitcast.100, bf16[2048,768]{1,0:T(8,128)(2,1)} %param.34, f32[256,768]{1,0:T(8,128)} %fusion.60), kind=kOutput, calls=%fused_computation.6 | convolution fusion | flops 1612316672 | bytes 9175040 | tf_op jit(solution)/shard_map/dot_general | solution.py:314
  181.9 19.4 %all_to_all.31 = bf16[8,32,2048]{2,1,0:T(8,128)(2,1)S(1)} all-to-all(bf16[8,32,2048]{2,1,0:T(8,128)(2,1)} %bitcast.101), channel_id=1, replica_groups=mesh['req'=16,'tp'=8] {'tp'}, dimensions={0} | all-to-all | bytes 2097152 | tf_op jit(solution)/shard_map/all_to_all | solution.py:191
  201.6 18.4 %all_to_all.32 = bf16[8,32,2048]{2,1,0:T(8,128)(2,1)S(1)} all-to-all(bf16[8,32,2048]{2,1,0:T(8,128)(2,1)S(1)} %broadcast_in_dim.79), channel_id=1, replica_groups=mesh['req'=16,'tp'=8] {'tp'}, dimensions={0} | all-to-all | bytes 2097152 | tf_op jit(solution)/shard_map/all_to_all | solution.py:197
  (103 shorter events, 29.7 us)
Async XLA Ops:
  0.0 176.4 %copy-start = (bf16[768,2048]{1,0:T(8,128)(2,1)S(1)}, bf16[768,2048]{1,0:T(8,128)(2,1)}, u32[]{:S(2)}) copy-start(bf16[768,2048]{1,0:T(8,128)(2,1)} %param.35) | copy-start | bytes 9437188
  0.0 7.0 %copy-start.11 = (f32[64]{0:T(128)}, f32[64]{0:T(128)S(1)}, u32[]{:S(2)}) copy-start(f32[64]{0:T(128)S(1)} %multiply_power_fusion) | copy-start | bytes 772
  0.9 0.6 copy-start.2
  1.5 5.6 %copy-start.4 = (f32[256]{0:T(256)}, f32[256]{0:T(256)S(1)}, u32[]{:S(2)}) copy-start(f32[256]{0:T(256)S(1)} %convert_element_type.108) | copy-start | bytes 3076
  1.5 6.1 %copy-start.16 = (f32[128]{0:T(128)S(1)}, f32[128]{0:T(128)}, u32[]{:S(2)}) copy-start(f32[128]{0:T(128)} %param.29) | copy-start | bytes 1540
  3.0 2.9 %copy-start.14 = (f32[256]{0:T(256)}, f32[256]{0:T(256)S(1)}, u32[]{:S(2)}) copy-start(f32[256]{0:T(256)S(1)} %add_rsqrt_fusion.2) | copy-start | bytes 3076
  10.0 8.8 %copy-start.10 = (s32[16,32]{1,0:T(8,128)S(1)}, s32[16,32]{1,0:T(8,128)}, u32[]{:S(2)}) copy-start(s32[16,32]{1,0:T(8,128)} %param.21) | copy-start | bytes 6148
  10.0 9.7 %copy-start.13 = (s32[2,512]{1,0:T(2,128)S(1)}, s32[2,512]{1,0:T(2,128)}, u32[]{:S(2)}) copy-start(s32[2,512]{1,0:T(2,128)} %param.22) | copy-start | bytes 12292
  10.0 42.3 %all-to-all-start = ((bf16[16,512,128]{2,1,0:T(8,128)(2,1)}), bf16[16,512,128]{2,1,0:T(8,128)(2,1)}, u32[]{:S(2)}, u32[]{:S(2)}) async-start(bf16[16,512,128]{2,1,0:T(8,128)(2,1)} %broadcast_in_dim.69), calls=%async_computation | async-start | bytes 4194304 | tf_op jit(solution)/shard_map/all_to_all | solution.py:273
  34.0 0.6 copy-start.6
  44.1 5.7 %copy-start.12 = (f32[64]{0:T(128)S(1)}, f32[64]{0:T(128)}, u32[]{:S(2)}) copy-start(f32[64]{0:T(128)} %copy-done.11) | copy-start | bytes 772
  44.2 7.4 %copy-start.9 = (pred[16,2]{1,0:T(8,128)(4,1)S(1)}, pred[16,2]{1,0:T(8,128)(4,1)}, u32[]{:S(2)}) copy-start(pred[16,2]{1,0:T(8,128)(4,1)} %copy.64) | copy-start | bytes 100
  75.6 6.2 %copy-start.15 = (f32[256]{0:T(256)S(1)}, f32[256]{0:T(256)}, u32[]{:S(2)}) copy-start(f32[256]{0:T(256)} %copy-done.14) | copy-start | bytes 3076
  75.6 6.2 %copy-start.19 = (f32[2048]{0:T(1024)S(1)}, f32[2048]{0:T(1024)}, u32[]{:S(2)}) copy-start(f32[2048]{0:T(1024)} %param.25) | copy-start | bytes 24580
  75.6 33.4 %all-to-all-start.1 = ((bf16[16,544,128]{2,1,0:T(8,128)(2,1)}), bf16[16,544,128]{2,1,0:T(8,128)(2,1)}, u32[]{:S(2)}, u32[]{:S(2)}) async-start(bf16[16,544,128]{2,1,0:T(8,128)(2,1)} %shard_map.172), calls=%async_computation.1 | async-start | bytes 4456448 | tf_op jit(solution)/shard_map/all_to_all | solution.py:285
  81.8 2.0 copy-start.3
  81.8 2.2 copy-start.17
  81.8 2.3 %copy-start.5 = (f32[256]{0:T(256)S(1)}, f32[256]{0:T(256)}, u32[]{:S(2)}) copy-start(f32[256]{0:T(256)} %copy-done.4) | copy-start | bytes 3076
  110.6 9.7 %copy-start.7 = (f32[2,256]{1,0:T(2,128)S(1)}, f32[2,256]{1,0:T(2,128)}, u32[]{:S(2)}) copy-start(f32[2,256]{1,0:T(2,128)} %fusion.8) | copy-start | bytes 6148
  127.5 27.5 %copy-start.8 = (f32[2048]{0:T(1024)S(1)}, f32[2048]{0:T(1024)}, u32[]{:S(2)}) copy-start(f32[2048]{0:T(1024)} %param.32) | copy-start | bytes 24580
  127.5 24.8 %all-to-all-start.2 = ((bf16[8,32,2048]{2,1,0:T(8,128)(2,1)}), bf16[8,32,2048]{2,1,0:T(8,128)(2,1)}, u32[]{:S(2)}, u32[]{:S(2)}) async-start(bf16[8,32,2048]{2,1,0:T(8,128)(2,1)} %bitcast.94), calls=%async_computation.2 | async-start | bytes 2097152 | tf_op jit(solution)/shard_map/all_to_all | solution.py:191
  153.7 20.8 %copy-start.18 = (bf16[2048,768]{1,0:T(8,128)(2,1)S(1)}, bf16[2048,768]{1,0:T(8,128)(2,1)}, u32[]{:S(2)}) copy-start(bf16[2048,768]{1,0:T(8,128)(2,1)} %param.33) | copy-start | bytes 9437188
  173.5 1.0 copy-start.1
